TPU v7x, 256 devices: a whole 4x4x8 slice. The times are simulated.
256 devices in a mesh: seq: 32 (over x, y, core), head: 8 (over z).
Axes of the slice: x: 4, y: 4, z: 8, core: 2. Of those that a mesh axis runs over, the one named last changes fastest.
Arguments:
- positions: int32 [16384], P('seq'), may hold values from 65535 to 98301, as said below
- queries: bfloat16 [16384, 32, 128], P('seq', 'head'), may hold values from -16 to 16
- keys: bfloat16 [16384, 16, 128], P('seq', 'head'), may hold values from -16 to 16
- values: bfloat16 [16384, 16, 128], P('seq', 'head'), may hold values from -6 to 6
- out_weight: bfloat16 [4096, 5376], P('head', 'seq'), may hold values from -0.1875 to 0.1875
- post_gain: float32 [5376], P('head'), may hold values from 0.25 to 1.75
- residual: bfloat16 [16384, 5376], P('seq', 'head'), may hold values from -6 to 6
Outputs:
- layer_out: bfloat16 [16384, 5376], P('seq', 'head')
Inputs may be any that keep to these rules, and one draw needn't show every extreme that they name: `positions`: strictly rising, by 1 or 2 from one token to the next; the last token's position is the most.
All inputs are finite; a program needn't handle non-finite values.
Results may differ from a plain program's by a relative error of at most 0.015.
Values may be sent and summed in bfloat16 or wider, within the bound.
No kernel may reach another device: no remote copies, remote signals or barrier semaphores. Data moves between devices by JAX's collectives and lax.ppermute only.
A program may use at most 64 MiB of HBM per device.

v0:
```python
import jax
import jax.numpy as jnp
from jax import lax
from jax.sharding import PartitionSpec as P

D = 5376
QUERY_HEADS = 32
KEY_VALUE_HEADS = 16
VISIBLE_SPAN = 1024


EPS = 1e-06
SCALE = 168.0 ** (-0.5)


def passed_along(value, axis, steps):
    count = lax.axis_size(axis)
    initial, last = (max(0, -steps), min(count, count - steps))
    return lax.ppermute(value, axis, [(source, source + steps) for source in range(initial, last)])


def copy_for_each(array, axis):
    length = lax.axis_size(axis)
    return lax.all_to_all(
        jnp.broadcast_to(array[None], (length, *array.shape)), axis, 0, 0, tiled=True
    )


def of_everyone(array, axis):
    return copy_for_each(array, axis).sum(axis=0)


def rotate(x, positions):
    half = x.shape[-1] // 2
    inverse = 10000.0 ** (-2.0 * jnp.arange(half, dtype=jnp.float32) / x.shape[-1])
    angle = positions.astype(jnp.float32)[:, None] * inverse[None, :]
    cosine = jnp.concatenate([jnp.cos(angle), jnp.cos(angle)], -1)[:, None, :]
    sine = jnp.concatenate([jnp.sin(angle), jnp.sin(angle)], -1)[:, None, :]
    source = x.astype(jnp.float32)
    turned = jnp.concatenate([-source[..., half:], source[..., :half]], -1)
    return (source * cosine + turned * sine).astype(jnp.bfloat16)


def on_device(positions, queries, keys, values, out_weight, post_gain, residual):
    rows = queries.shape[0]
    kv_heads = keys.shape[1]
    query_groups = QUERY_HEADS // KEY_VALUE_HEADS
    q_rot = rotate(queries, positions)
    stacked = jnp.stack([rotate(keys, positions), values], 0)
    reach = (VISIBLE_SPAN + rows - 2) // rows
    pieces = []
    carried = stacked
    for hop in range(reach):
        carried = passed_along(carried, "seq", 1)
        pieces.insert(0, carried)
    extended = jnp.concatenate(pieces + [stacked], axis=1)
    extra = extended.shape[1] - rows
    anchor = lax.axis_index("seq") * rows
    block_length = min(512, rows)
    query_tile_rows = q_rot.reshape(block_length, kv_heads, query_groups, -1)
    key_block = extended[0, 0 : extra + block_length]
    value_block = extended[1, 0 : extra + block_length]
    scores = (
        jnp.einsum("qhgd,khd->hgqk", query_tile_rows, key_block, preferred_element_type=jnp.float32)
        * SCALE
    )
    query_index = anchor + 0 + jnp.arange(block_length, dtype=jnp.int32)
    key_index = anchor - extra + 0 + jnp.arange(extra + block_length, dtype=jnp.int32)
    gap = query_index[:, None] - key_index[None, :]
    allowed = (gap >= 0) & (gap < VISIBLE_SPAN) & (key_index[None, :] >= 0)
    scores = jnp.where(allowed, scores, -1e30)
    top = jnp.max(scores, axis=-1, keepdims=True)
    weights = jnp.exp(scores - top)
    probs = (weights / jnp.sum(weights, axis=-1, keepdims=True)).astype(jnp.bfloat16)
    context = jnp.einsum("hgqk,khd->qhgd", probs, value_block, preferred_element_type=jnp.float32)
    outputs = context.astype(jnp.bfloat16).reshape(block_length, -1)
    context = outputs
    partial_value = jnp.dot(
        context,
        lax.all_gather(out_weight, "seq", axis=1, tiled=True),
        preferred_element_type=jnp.float32,
    )
    attended = lax.psum_scatter(
        partial_value.astype(jnp.bfloat16), "head", scatter_dimension=1, tiled=True
    ).astype(jnp.float32)
    squares = of_everyone(jnp.sum(attended * attended, axis=1), "head")
    scaled = attended * lax.rsqrt(squares / D + EPS)[:, None]
    result = residual.astype(jnp.float32) + post_gain[None, :] * scaled
    return result.astype(jnp.bfloat16)


def solution(mesh):
    return jax.shard_map(
        on_device,
        mesh=mesh,
        in_specs=(
            P("seq"),
            P("seq", "head", None),
            P("seq", "head", None),
            P("seq", "head", None),
            P("head", "seq"),
            P("head"),
            P("seq", "head"),
        ),
        out_specs=P("seq", "head"),
        check_vma=False,
    )
```

profile of v0, /device:TPU:6, one launch (start us, length us, event | category | flops | bytes accessed | tf_op | source)
XLA Modules:
  0.0 164.7 jit_solution(17591090239701363710)
XLA Ops:
  6.5 0.7 all-gather.2.cloned.1.call-update
  7.3 0.7 convert_element_type.39
  8.0 1.0 copy.44
  9.0 1.0 multiply_cosine_fusion
  10.0 0.2 pad_maximum_fusion.1
  10.2 1.0 copy_convert_fusion
  11.5 0.2 fusion.24
  11.7 0.9 pad_maximum_fusion
  12.6 1.9 %collective-permute-start = (bf16[2,512,2,128]{3,1,2,0:T(8,128)(2,1)}, bf16[2,512,2,128]{3,1,2,0:T(8,128)(2,1)}, u32[]{:S(2)}, u32[]{:S(2)}) collective-permute-start(bf16[2,512,2,128]{3,1,2,0:T(8,128)(2,1)} %pad_maximum_fusion), channel_id=1, source_target_pairs={{0,8},{8,16},{16,24},{24,32},{32,40},{40,48},{48,56},{56,64},{64,7... | collective-permute-start | bytes 1572872 | tf_op jit(solution)/shard_map/ppermute | solution.py:19
  14.8 0.6 slice_negate_fusion
  15.4 1.6 fusion.16
  17.1 8.4 %collective-permute-done = bf16[2,512,2,128]{3,1,2,0:T(8,128)(2,1)} collective-permute-done((bf16[2,512,2,128]{3,1,2,0:T(8,128)(2,1)}, bf16[2,512,2,128]{3,1,2,0:T(8,128)(2,1)}, u32[]{:S(2)}, u32[]{:S(2)}) %collective-permute-start) | collective-permute-done | bytes 524320 | tf_op jit(solution)/shard_map/ppermute | solution.py:19
  25.5 1.9 %collective-permute-start.1 = (bf16[2,512,2,128]{3,1,2,0:T(8,128)(2,1)}, bf16[2,512,2,128]{3,1,2,0:T(8,128)(2,1)S(1)}, u32[]{:S(2)}, u32[]{:S(2)}) collective-permute-start(bf16[2,512,2,128]{3,1,2,0:T(8,128)(2,1)} %collective-permute-done), channel_id=1, source_target_pairs={{0,8},{8,16},{16,24},{24,32},{32,40},{40,48},{48,56},{56,64},{64,7... | collective-permute-start | bytes 1572872 | tf_op jit(solution)/shard_map/ppermute | solution.py:19
  27.4 1.2 fusion.7
  28.6 11.0 %collective-permute-done.1 = bf16[2,512,2,128]{3,1,2,0:T(8,128)(2,1)S(1)} collective-permute-done((bf16[2,512,2,128]{3,1,2,0:T(8,128)(2,1)}, bf16[2,512,2,128]{3,1,2,0:T(8,128)(2,1)S(1)}, u32[]{:S(2)}, u32[]{:S(2)}) %collective-permute-start.1) | collective-permute-done | bytes 524320 | tf_op jit(solution)/shard_map/ppermute | solution.py:19
  39.6 1.2 maximum_maximum_fusion
  40.8 7.4 %fusion.27 = (f32[2,2,512]{2,1,0:T(2,128)S(1)}, f32[2,2,512,1536]{2,3,1,0:T(8,128)}) fusion(pred[512,1536]{0,1:T(8,128)(4,1)S(1)} %fusion.7, bf16[2,1536,2,128]{3,1,2,0:T(8,128)(2,1)S(1)} %maximum_maximum_fusion, bf16[512,2,2,128]{3,2,1,0:T(2,128)(2,1)S(1)} %bitcast.46), kind=kOutput, calls=%fused_computation.51 | convolution fusion | flops 817890816 | bytes 14688256 | tf_op jit(solution)/shard_map/sub | solution.py:73
  48.2 6.1 %fusion.14 = bf16[2,128,2,512]{3,1,2,0:T(8,128)(2,1)S(1)} fusion(f32[2,2,512,1536]{2,3,1,0:T(8,128)} %get-tuple-element.10, f32[2,2,512]{2,1,0:T(2,128)S(1)} %get-tuple-element.9, bf16[2,1536,2,128]{3,1,2,0:T(8,128)(2,1)S(1)} %maximum_maximum_fusion), kind=kOutput, calls=%fused_computation.22 | convolution fusion | flops 811859968 | bytes 13901824 | tf_op jit(solution)/shard_map/hgqk,khd->qhgd/dot_general | solution.py:75
  54.4 13.0 %all-gather.2.cloned.1.call-done = bf16[512,5376]{0,1:T(8,128)(2,1)} async-done(((bf16[512,168]{0,1:T(8,128)(2,1)}), bf16[512,5376]{0,1:T(8,128)(2,1)}) %all-gather.2.cloned.1.call-update) | async-done | bytes 5505040 | tf_op jit(solution)/shard_map/all_gather | solution.py:80
  67.3 7.3 %convolution_convert_fusion = bf16[512,5376]{0,1:T(8,128)(2,1)} fusion(bf16[512,5376]{0,1:T(8,128)(2,1)} %all-gather.2.cloned.1.call-done, bf16[512,512]{0,1:T(8,128)(2,1)S(1)} %bitcast.47), kind=kOutput, calls=%fused_computation.5 | convolution fusion | flops 2821324800 | bytes 11534336 | tf_op jit(solution)/shard_map/dot_general | solution.py:78
  74.7 67.6 %reduce-scatter.2.cloned.1.call-done = bf16[512,672]{0,1:T(8,128)(2,1)} async-done(((bf16[512,5376]{0,1:T(8,128)(2,1)}), bf16[512,672]{0,1:T(8,128)(2,1)}) %reduce-scatter.2.cloned.1.call-update) | async-done | bytes 688144 | tf_op jit(solution)/shard_map/reduce_scatter | solution.py:83
  142.3 1.3 fusion.8
  143.6 11.9 %all_to_all.6 = f32[8,1,512]{2,1,0:T(1,128)S(1)} all-to-all(f32[8,1,512]{2,1,0:T(1,128)S(1)} %broadcast_in_dim.10), channel_id=1, replica_groups=mesh['seq'=32,'head'=8] {'head'}, dimensions={0} | all-to-all | bytes 32768 | tf_op jit(solution)/shard_map/all_to_all | solution.py:24
  155.6 2.2 %fusion.11 = bf16[512,672]{0,1:T(8,128)(2,1)} fusion(bf16[512,672]{0,1:T(8,128)(2,1)} %reduce-scatter.2.cloned.1.call-done, bf16[512,672]{0,1:T(8,128)(2,1)S(1)} %copy-done.4, f32[512]{0:T(512)S(1)} %add_rsqrt_fusion, f32[672]{0:T(1024)S(1)} %copy-done.6), kind=kLoop, calls=%fused_computation.20 | loop fusion | flops 2064384 | bytes 2069120 | tf_op jit(solution)/shard_map/convert_element_type | solution.py:89
  (27 shorter events, 0.6 us)
Async XLA Ops:
  6.5 4.9 %copy-start.3 = (bf16[512,2,128]{2,1,0:T(2,128)(2,1)S(1)}, bf16[512,2,128]{2,1,0:T(2,128)(2,1)}, u32[]{:S(2)}) copy-start(bf16[512,2,128]{2,1,0:T(2,128)(2,1)} %param.9) | copy-start | bytes 786436
  6.5 60.8 %all-gather.2.cloned.1.call-start = ((), (), s32[]{:S(2)}) async-start(), calls=%async_computation.2 | async-start | bytes 5677056 | tf_op jit(solution)/shard_map/all_gather | solution.py:80
  7.3 135.1 %reduce-scatter.2.cloned.1.call-start = ((), (), s32[]{:S(2)}) async-start(), calls=%async_computation.3 | async-start | bytes 6193152 | tf_op jit(solution)/shard_map/reduce_scatter | solution.py:83
  10.2 4.3 %copy-start = (bf16[512,4,128]{2,1,0:T(4,128)(2,1)S(1)}, bf16[512,4,128]{2,1,0:T(4,128)(2,1)}, u32[]{:S(2)}) copy-start(bf16[512,4,128]{2,1,0:T(4,128)(2,1)} %param.8) | copy-start | bytes 1572868
  11.7 2.8 %copy-start.1 = (bf16[1,512,2,128]{3,1,2,0:T(8,128)(2,1)}, bf16[1,512,2,128]{3,1,2,0:T(8,128)(2,1)S(1)}, u32[]{:S(2)}) copy-start(bf16[1,512,2,128]{3,1,2,0:T(8,128)(2,1)S(1)} %fusion.24) | copy-start | bytes 786436
  12.6 12.9 %collective-permute-start = (bf16[2,512,2,128]{3,1,2,0:T(8,128)(2,1)}, bf16[2,512,2,128]{3,1,2,0:T(8,128)(2,1)}, u32[]{:S(2)}, u32[]{:S(2)}) collective-permute-start(bf16[2,512,2,128]{3,1,2,0:T(8,128)(2,1)} %pad_maximum_fusion), channel_id=1, source_target_pairs={{0,8},{8,16},{16,24},{24,32},{32,40},{40,48},{48,56},{56,64},{64,7... | collective-permute-start | bytes 1572872 | tf_op jit(solution)/shard_map/ppermute | solution.py:19
  14.8 24.8 %copy-start.2 = (bf16[1,512,2,128]{3,1,2,0:T(8,128)(2,1)S(1)}, bf16[1,512,2,128]{3,1,2,0:T(8,128)(2,1)}, u32[]{:S(2)}) copy-start(bf16[1,512,2,128]{3,1,2,0:T(8,128)(2,1)} %copy-done.1) | copy-start | bytes 786436
  17.1 23.7 %copy-start.5 = (bf16[512,4,128]{2,1,0:T(4,128)(2,1)S(1)}, bf16[512,4,128]{2,1,0:T(4,128)(2,1)}, u32[]{:S(2)}) copy-start(bf16[512,4,128]{2,1,0:T(4,128)(2,1)} %fusion.16) | copy-start | bytes 1572868
  25.5 14.1 %collective-permute-start.1 = (bf16[2,512,2,128]{3,1,2,0:T(8,128)(2,1)}, bf16[2,512,2,128]{3,1,2,0:T(8,128)(2,1)S(1)}, u32[]{:S(2)}, u32[]{:S(2)}) collective-permute-start(bf16[2,512,2,128]{3,1,2,0:T(8,128)(2,1)} %collective-permute-done), channel_id=1, source_target_pairs={{0,8},{8,16},{16,24},{24,32},{32,40},{40,48},{48,56},{56,64},{64,7... | collective-permute-start | bytes 1572872 | tf_op jit(solution)/shard_map/ppermute | solution.py:19
  74.7 80.9 %copy-start.4 = (bf16[512,672]{0,1:T(8,128)(2,1)S(1)}, bf16[512,672]{0,1:T(8,128)(2,1)}, u32[]{:S(2)}) copy-start(bf16[512,672]{0,1:T(8,128)(2,1)} %param.13) | copy-start | bytes 2064388
  74.7 80.9 %copy-start.6 = (f32[672]{0:T(1024)S(1)}, f32[672]{0:T(1024)}, u32[]{:S(2)}) copy-start(f32[672]{0:T(1024)} %param.12) | copy-start | bytes 8068
Sparse Core Ops, SparseCore 0:
  9.9 57.3 all-gather.1
  74.8 67.4 reduce-scatter.1
where the time goes:
time: 165 us
  waiting for transfers between devices  101 us (61%)
  matrix products  20.9 us (13%)
  between operations  13.6 us (8%)
  other arithmetic  12.5 us (8%)
  blocking collectives  11.9 us (7%)
  starting transfers between devices  3.86 us (2%)
    reduce_scatter x1, waiting for transfers between devices, on_device(): lax.psum_scatter(partial_value.astype(jnp.bfloat16), 'head', scatter_dime...  67.6 us
    ppermute x2, waiting for transfers between devices, passed_along(): lax.ppermute(value, axis, [(source, source + steps) for source in range(i...  19.4 us
    all_gather x1, waiting for transfers between devices, on_device(): lax.all_gather(out_weight, 'seq', axis=1, tiled=True)  13 us
    all_to_all x1, blocking collectives, copy_for_each(): lax.all_to_all(jnp.broadcast_to(array[None], (length, *array.shape)), axi...  11.9 us
    sub x1, matrix products, on_device(): weights = jnp.exp(scores - top)  7.44 us
    dot_general x1, matrix products, on_device(): jnp.dot(context, lax.all_gather(out_weight, 'seq', axis=1, tiled=True), p...  7.32 us
    dot_general x1, matrix products, on_device(): jnp.einsum('hgqk,khd->qhgd', probs, value_block, preferred_element_type=j...  6.11 us
    ppermute x2, starting transfers between devices, passed_along(): lax.ppermute(value, axis, [(source, source + steps) for source in range(i...  3.82 us
  transfers between devices with their start and end apart: 4, of which 4 were waited for; matrix products, arithmetic and copies ran while one was open for 14% of the time, Pallas kernels for 0%

commit v1 on v0

v1 whole, which is shorter than its diff:
```python
import math

import jax
import jax.numpy as jnp
from jax import lax
from jax.experimental import pallas as pl
from jax.experimental.pallas import tpu as pltpu
from jax.sharding import PartitionSpec as P

D = 5376
HEAD_SIZE = 128
VISIBLE_SPAN = 1024
EPS = 1e-06
SCALE = 168.0 ** (-0.5)
LOG2E = math.log2(math.e)
ROWS = 512
KV = 2
GROUP = 2
N_SEQ = 32
N_HEAD = 8
FEATURES = D // N_HEAD
SHARD = D // N_SEQ
QB = 256
LOW = -1e30


def rotated(x, cosine, sine):
    x = x.astype(jnp.float32)
    return (x * cosine + pltpu.roll(x, 64, 1) * sine).astype(jnp.bfloat16)


def prepare_kernel(k_ref, v_ref, cos_ref, sin_ref, *out_refs):
    cosine = cos_ref[...]
    sine = sin_ref[...]
    for g in range(KV):
        out_refs[g][0] = rotated(k_ref[g], cosine, sine)
        out_refs[g][1] = v_ref[g]


def prepare(k, v, cosine, sine):
    shape = jax.ShapeDtypeStruct((2, ROWS, HEAD_SIZE), jnp.bfloat16)
    return pl.pallas_call(
        prepare_kernel,
        out_shape=[shape] * KV,
        name="rotate_keys",
    )(k, v, cosine, sine)


def dot_nt(a, b):
    return lax.dot_general(a, b, (((1,), (1,)), ((), ())), preferred_element_type=jnp.float32)


def attend_kernel(place_ref, q_ref, cos_ref, sin_ref, own_ref, prev_ref, far_ref, out_ref):
    place = place_ref[0]
    prev_bias = jnp.where(place >= 1, 0.0, LOW)
    far_bias = jnp.where(place >= 2, 0.0, LOW)
    c = SCALE * LOG2E
    cosine = cos_ref[...]
    sine = sin_ref[...]
    v_own = own_ref[1].T
    v_prev = prev_ref[1].T
    v_far = far_ref[1].T
    row = lax.broadcasted_iota(jnp.int32, (QB, QB), 0)
    col = lax.broadcasted_iota(jnp.int32, (QB, QB), 1)
    seen = row <= col
    blocks = ROWS // QB
    for n in range(GROUP):
        q_all = rotated(q_ref[:, n * HEAD_SIZE : (n + 1) * HEAD_SIZE], cosine, sine)
        for b in range(blocks):
            q = q_all[b * QB : (b + 1) * QB]
            lo, hi = b * QB, (b + 1) * QB
            prev = dot_nt(prev_ref[0], q)
            own = dot_nt(own_ref[0, 0:hi, :], q)
            far = dot_nt(far_ref[0, lo:ROWS, :], q)
            mixed = jnp.where(seen, own[lo:hi], far[0:QB] + far_bias)
            top = jnp.maximum(
                jnp.max(prev, axis=0, keepdims=True) + prev_bias,
                jnp.max(mixed, axis=0, keepdims=True),
            )
            if lo > 0:
                top = jnp.maximum(top, jnp.max(own[0:lo], axis=0, keepdims=True))
            if hi < ROWS:
                top = jnp.maximum(top, jnp.max(far[QB:], axis=0, keepdims=True) + far_bias)
            top = top * c
            p_prev = jnp.exp2(prev * c - (top - prev_bias))
            p_mixed = jnp.exp2(mixed * c - top)
            total = jnp.sum(p_prev, axis=0, keepdims=True) + jnp.sum(p_mixed, axis=0, keepdims=True)
            own_parts = [jnp.where(seen, p_mixed, 0.0).astype(jnp.bfloat16)]
            far_parts = [jnp.where(seen, 0.0, p_mixed).astype(jnp.bfloat16)]
            if lo > 0:
                p = jnp.exp2(own[0:lo] * c - top)
                total = total + jnp.sum(p, axis=0, keepdims=True)
                own_parts.insert(0, p.astype(jnp.bfloat16))
            if hi < ROWS:
                p = jnp.exp2(far[QB:] * c - (top - far_bias))
                total = total + jnp.sum(p, axis=0, keepdims=True)
                far_parts.append(p.astype(jnp.bfloat16))
            context = jnp.dot(v_prev, p_prev.astype(jnp.bfloat16), preferred_element_type=jnp.float32)
            context += jnp.dot(
                v_own[:, 0:hi], jnp.concatenate(own_parts, 0), preferred_element_type=jnp.float32
            )
            context += jnp.dot(
                v_far[:, lo:], jnp.concatenate(far_parts, 0), preferred_element_type=jnp.float32
            )
            out_ref[n * HEAD_SIZE : (n + 1) * HEAD_SIZE, lo:hi] = (context / total).astype(jnp.bfloat16)


def attend(g, place, q, cosine, sine, own, prev, far):
    whole = lambda *shape: pl.BlockSpec(shape, lambda _: (0,) * len(shape))
    width = GROUP * HEAD_SIZE
    kv = whole(2, ROWS, HEAD_SIZE)
    return pl.pallas_call(
        attend_kernel,
        grid=(1,),
        in_specs=[
            pl.BlockSpec(memory_space=pltpu.SMEM),
            pl.BlockSpec((ROWS, width), lambda _: (0, g)),
            whole(ROWS, HEAD_SIZE),
            whole(ROWS, HEAD_SIZE),
            kv,
            kv,
            kv,
        ],
        out_specs=whole(width, ROWS),
        out_shape=jax.ShapeDtypeStruct((width, ROWS), jnp.bfloat16),
        compiler_params=pltpu.CompilerParams(vmem_limit_bytes=32 * 1024 * 1024),
        name="attend",
    )(place, q, cosine, sine, own, prev, far)


def project_kernel(order_ref, w_ref, *refs):
    ctx_refs, (acc_ref, sq_ref) = refs[: KV * N_HEAD], refs[KV * N_HEAD :]
    step = pl.program_id(0)
    width = GROUP * HEAD_SIZE
    for k in range(N_HEAD):

        @pl.when(step == k)
        def _(k=k):
            value = sum(
                jnp.dot(
                    w_ref[0, :, g * width : (g + 1) * width],
                    ctx_refs[k * KV + g][...],
                    preferred_element_type=jnp.float32,
                )
                for g in range(KV)
            )
            if k > 0:
                value = acc_ref[...] + value
            acc_ref[...] = value
            if k == N_HEAD - 1:
                sq_ref[...] = jnp.sum(value * value, axis=0, keepdims=True)


def project(order, weights, blocks):
    width = GROUP * HEAD_SIZE
    return pl.pallas_call(
        project_kernel,
        grid_spec=pltpu.PrefetchScalarGridSpec(
            num_scalar_prefetch=1,
            grid=(N_HEAD,),
            in_specs=[pl.BlockSpec((1, FEATURES, KV * width), lambda k, order: (order[k], 0, 0))]
            + [pl.BlockSpec((width, ROWS), lambda k, order: (0, 0))] * (KV * N_HEAD),
            out_specs=[
                pl.BlockSpec((FEATURES, ROWS), lambda k, order: (0, 0)),
                pl.BlockSpec((1, ROWS), lambda k, order: (0, 0)),
            ],
        ),
        out_shape=[
            jax.ShapeDtypeStruct((FEATURES, ROWS), jnp.float32),
            jax.ShapeDtypeStruct((1, ROWS), jnp.float32),
        ],
        compiler_params=pltpu.CompilerParams(vmem_limit_bytes=40 * 1024 * 1024),
        name="project",
    )(order, weights, *blocks)


def of_everyone(array, axis):
    length = lax.axis_size(axis)
    return lax.all_to_all(
        jnp.broadcast_to(array[None], (length, *array.shape)), axis, 0, 0, tiled=True
    ).sum(axis=0)


def on_device(positions, queries, keys, values, out_weight, post_gain, residual):
    seq = lax.axis_index("seq")
    head = lax.axis_index("head")
    spread = [
        (s * N_HEAD + h, (h * 4 + s % 4) * N_HEAD + s // 4)
        for s in range(N_SEQ)
        for h in range(N_HEAD)
    ]
    shard = lax.ppermute(out_weight.T, ("seq", "head"), spread)
    weights = lax.all_gather(shard, "seq", axis=0).reshape(N_HEAD, FEATURES, KV * GROUP * HEAD_SIZE)

    half = HEAD_SIZE // 2
    inverse = 10000.0 ** (-2.0 * jnp.arange(half, dtype=jnp.float32) / HEAD_SIZE)
    angle = positions.astype(jnp.float32)[:, None] * inverse[None, :]
    cosine, sine = jnp.cos(angle), jnp.sin(angle)
    cosine = jnp.concatenate([cosine, cosine], -1)
    sine = jnp.concatenate([-sine, sine], -1)

    own = prepare(keys.transpose(1, 0, 2), values.transpose(1, 0, 2), cosine, sine)
    onward = [(i, i + 1) for i in range(N_SEQ - 1)]
    prev = [lax.ppermute(x, "seq", onward) for x in own]
    far = [lax.ppermute(x, "seq", onward) for x in prev]
    place = seq.astype(jnp.int32).reshape(1)
    q = queries.reshape(ROWS, KV * GROUP * HEAD_SIZE)

    ring = [
        (s * N_HEAD + h, s * N_HEAD + (h + (1 if s % 2 == 0 else -1)) % N_HEAD)
        for s in range(N_SEQ)
        for h in range(N_HEAD)
    ]
    blocks = [[None] * KV for _ in range(N_HEAD)]
    for g in range(KV):
        carried = attend(g, place, q, cosine, sine, own[g], prev[g], far[g])
        blocks[0][g] = carried
        for k in range(1, N_HEAD):
            carried = lax.ppermute(carried, ("seq", "head"), ring)
            blocks[k][g] = carried
    sign = jnp.where(seq % 2 == 0, -1, 1)
    order = ((head + sign * jnp.arange(N_HEAD, dtype=jnp.int32)) % N_HEAD).astype(jnp.int32)
    attended, squares = project(order, weights, [x for pair in blocks for x in pair])
    squares = of_everyone(squares, "head")
    scaled = attended * lax.rsqrt(squares / D + EPS)
    result = residual.T.astype(jnp.float32) + post_gain[:, None] * scaled
    return result.astype(jnp.bfloat16).T


def solution(mesh):
    return jax.shard_map(
        on_device,
        mesh=mesh,
        in_specs=(
            P("seq"),
            P("seq", "head", None),
            P("seq", "head", None),
            P("seq", "head", None),
            P("head", "seq"),
            P("head"),
            P("seq", "head"),
        ),
        out_specs=P("seq", "head"),
        check_vma=False,
    )
```

time: 165 us -> 159 us (0.964)
  waiting for transfers between devices: 101 us -> 65.4 us
  starting transfers between devices: 3.86 us -> 26 us
  matrix products: 20.9 us -> 0 us
  local copies, waits for them, and re-layouts: 1.14 us -> 18.4 us
  Pallas kernels: 0 us -> 12.9 us
  other arithmetic: 12.5 us -> 4.95 us
  blocking collectives: 11.9 us -> 16.8 us
    reduce_scatter x1 -> x0, waiting for transfers between devices: 67.6 us -> none  [on_device(): lax.psum_scatter(partial_value.astype(jnp.bfloat16), 'head', scatter_dime...]
    ppermute x2 -> x19, waiting for transfers between devices: 19.4 us -> 65.4 us  [the longest x14 39.8 us: on_device(): carried = lax.ppermute(carried, ('seq', 'head'), ring)]
    ppermute x2 -> x19, starting transfers between devices: 3.82 us -> 26 us  [the longest x14 8.41 us: on_device(): carried = lax.ppermute(carried, ('seq', 'head'), ring)]
    unnamed x15 -> x53, local copies, waits for them, and re-layouts: 1.01 us -> 17.6 us
    dot_general x2 -> x0, matrix products: 13.4 us -> none  [the longest x1 7.32 us: on_device(): jnp.dot(context, lax.all_gather(out_weight, 'seq', axis=1, tiled=True), p...]
    all_gather x1, waiting for transfers between devices: 13 us -> 0.01 us  [on_device(): lax.all_gather(shard, 'seq', axis=0)]
    pallas_call x0 -> x4, Pallas kernels: none -> 12.9 us  [the longest x2 5.73 us: attend(): pl.pallas_call(attend_kernel, grid=(1,), in_specs=[pl.BlockSpec(memory_sp...]
    sub x1 -> x0, matrix products: 7.44 us -> none  [on_device(): weights = jnp.exp(scores - top)]
  transfers between devices with their start and end apart: 4 -> 20, of which waited for: 4 -> 18; matrix products, arithmetic and copies ran while one was open for 14% -> 2% of each run, Pallas kernels for 0% -> 5%
where the time goes in v1:
time: 159 us; the launch traced here: 158 us
  waiting for transfers between devices  65.4 us (41%)
  starting transfers between devices  26 us (16%)
  local copies, waits for them, and re-layouts  18.4 us (12%)
  blocking collectives  16.8 us (11%)
  between operations  13.6 us (9%)
  Pallas kernels  12.9 us (8%)
  other arithmetic  4.95 us (3%)
    ppermute x14, waiting for transfers between devices, on_device(): carried = lax.ppermute(carried, ('seq', 'head'), ring)  39.8 us
    unnamed x53, local copies, waits for them, and re-layouts  17.6 us
    all_to_all x1, blocking collectives, of_everyone(): lax.all_to_all(jnp.broadcast_to(array[None], (length, *array.shape)), axi...  16.8 us
    ppermute x1, waiting for transfers between devices, on_device(): shard = lax.ppermute(out_weight.T, ('seq', 'head'), spread)  14.7 us
    ppermute x14, starting transfers between devices, on_device(): carried = lax.ppermute(carried, ('seq', 'head'), ring)  8.41 us
    ppermute x1, starting transfers between devices, on_device(): shard = lax.ppermute(out_weight.T, ('seq', 'head'), spread)  8.24 us
    pallas_call x2, Pallas kernels, attend(): pl.pallas_call(attend_kernel, grid=(1,), in_specs=[pl.BlockSpec(memory_sp...  5.73 us
    ppermute x2, waiting for transfers between devices, on_device(): prev = [lax.ppermute(x, 'seq', onward) for x in own]  5.66 us
  transfers between devices with their start and end apart: 20, of which 18 were waited for; matrix products, arithmetic and copies ran while one was open for 2% of the time, Pallas kernels for 5%

profile of v1, /device:TPU:6, one launch (start us, length us, event | category | flops | bytes accessed | tf_op | source)
XLA Modules:
  0.0 158.1 jit_solution(14180648685153872632)
XLA Ops:
  6.5 8.2 %collective-permute-start = (bf16[168,512]{1,0:T(8,128)(2,1)}, bf16[168,512]{1,0:T(8,128)(2,1)S(1)}, u32[]{:S(2)}, u32[]{:S(2)}) collective-permute-start(bf16[168,512]{1,0:T(8,128)(2,1)} %bitcast.25), channel_id=1, source_target_pairs={{0,0},{1,32},{2,64},{3,96},{4,128},{5,160},{6,192},{7,224},{8,8},{... | collective-permute-start | bytes 516104 | tf_op jit(solution)/shard_map/ppermute | solution.py:192
  14.8 14.7 %collective-permute-done = bf16[168,512]{1,0:T(8,128)(2,1)S(1)} collective-permute-done((bf16[168,512]{1,0:T(8,128)(2,1)}, bf16[168,512]{1,0:T(8,128)(2,1)S(1)}, u32[]{:S(2)}, u32[]{:S(2)}) %collective-permute-start) | collective-permute-done | bytes 172064 | tf_op jit(solution)/shard_map/ppermute | solution.py:192
  33.8 2.1 %rotate_keys.1 = (bf16[2,512,128]{2,1,0:T(8,128)(2,1)}, bf16[2,512,128]{2,1,0:T(8,128)(2,1)}) custom-call(bf16[2,512,128]{2,1,0:T(8,128)(2,1)} %get-tuple-element.19.k_ref, bf16[2,512,128]{2,1,0:T(8,128)(2,1)} %get-tuple-element.18.v_ref, f32[512,128]{1,0:T(8,128)} %get-tuple-element.16.cos_ref, f32[512,128]{1,0:T(8,128)} %get-tuple-element.17.sin_ref), custom_call_target="tpu_custom_call" | custom-call | tf_op jit(solution)/shard_map/rotate_keys/pallas_call | solution.py:42
  37.8 3.6 %collective-permute-start.3 = (bf16[2,512,128]{2,1,0:T(8,128)(2,1)}, bf16[2,512,128]{2,1,0:T(8,128)(2,1)S(1)}, u32[]{:S(2)}, u32[]{:S(2)}) collective-permute-start(bf16[2,512,128]{2,1,0:T(8,128)(2,1)} %get-tuple-element.10.own_ref), channel_id=1, source_target_pairs={{0,8},{8,16},{16,24},{24,32},{32,40},{40,48},{48,56},{56,64},{64,7... | collective-permute-start | bytes 786440 | tf_op jit(solution)/shard_map/ppermute | solution.py:204
  41.4 4.5 %collective-permute-done.1.prev_ref = bf16[2,512,128]{2,1,0:T(8,128)(2,1)S(1)} collective-permute-done((bf16[2,512,128]{2,1,0:T(8,128)(2,1)}, bf16[2,512,128]{2,1,0:T(8,128)(2,1)S(1)}, u32[]{:S(2)}, u32[]{:S(2)}) %collective-permute-start.1) | collective-permute-done | bytes 262176 | tf_op jit(solution)/shard_map/ppermute | solution.py:204
  51.0 5.2 %collective-permute-done.2.far_ref = bf16[2,512,128]{2,1,0:T(8,128)(2,1)S(1)} collective-permute-done((bf16[2,512,128]{2,1,0:T(8,128)(2,1)S(1)}, bf16[2,512,128]{2,1,0:T(8,128)(2,1)S(1)}, u32[]{:S(2)}, u32[]{:S(2)}) %collective-permute-start.2) | collective-permute-done | bytes 262176 | tf_op jit(solution)/shard_map/ppermute | solution.py:205
  57.2 2.9 %attend.2.refs_0_ = bf16[256,512]{1,0:T(8,128)(2,1)S(1)} custom-call(s32[1]{0:T(128)} %bitcast.3.place_ref, bf16[512,512]{1,0:T(8,128)(2,1)S(1)} %bitcast.21, f32[512,128]{1,0:T(8,128)S(1)} %copy-done.1, f32[512,128]{1,0:T(8,128)S(1)} %copy-done.2, bf16[2,512,128]{2,1,0:T(8,128)(2,1)S(1)} %copy-done.20, ...), custom_call_target="tpu_custom_call" | custom-call | tf_op jit(solution)/shard_map/attend/pallas_call | solution.py:112
  60.2 2.9 %attend.3.refs_1_ = bf16[256,512]{1,0:T(8,128)(2,1)S(1)} custom-call(s32[1]{0:T(128)} %bitcast.3.place_ref, bf16[512,512]{1,0:T(8,128)(2,1)S(1)} %bitcast.22, f32[512,128]{1,0:T(8,128)S(1)} %copy-done.1, f32[512,128]{1,0:T(8,128)S(1)} %copy-done.2, bf16[2,512,128]{2,1,0:T(8,128)(2,1)S(1)} %copy-done.19, ...), custom_call_target="tpu_custom_call" | custom-call | tf_op jit(solution)/shard_map/attend/pallas_call | solution.py:112
  63.1 4.6 %collective-permute-done.5.refs_2_ = bf16[256,512]{1,0:T(8,128)(2,1)S(1)} collective-permute-done((bf16[256,512]{1,0:T(8,128)(2,1)S(1)}, bf16[256,512]{1,0:T(8,128)(2,1)S(1)}, u32[]{:S(2)}, u32[]{:S(2)}) %collective-permute-start.5) | collective-permute-done | bytes 262176 | tf_op jit(solution)/shard_map/ppermute | solution.py:219
  70.7 2.9 %collective-permute-start.8 = (bf16[256,512]{1,0:T(8,128)(2,1)S(1)}, bf16[256,512]{1,0:T(8,128)(2,1)S(1)}, u32[]{:S(2)}, u32[]{:S(2)}) collective-permute-start(bf16[256,512]{1,0:T(8,128)(2,1)S(1)} %collective-permute-done.6.refs_3_), channel_id=1, source_target_pairs={{0,1},{1,2},{2,3},{3,4},{4,5},{5,6},{6,7},{7,0},{8,15},{9,8},{10,9... | collective-permute-start | bytes 786440 | tf_op jit(solution)/shard_map/ppermute | solution.py:219
  80.0 2.9 %collective-permute-done.9.refs_6_ = bf16[256,512]{1,0:T(8,128)(2,1)S(1)} collective-permute-done((bf16[256,512]{1,0:T(8,128)(2,1)S(1)}, bf16[256,512]{1,0:T(8,128)(2,1)S(1)}, u32[]{:S(2)}, u32[]{:S(2)}) %collective-permute-start.9) | collective-permute-done | bytes 262176 | tf_op jit(solution)/shard_map/ppermute | solution.py:219
  82.9 3.0 %collective-permute-done.10.refs_7_ = bf16[256,512]{1,0:T(8,128)(2,1)S(1)} collective-permute-done((bf16[256,512]{1,0:T(8,128)(2,1)S(1)}, bf16[256,512]{1,0:T(8,128)(2,1)S(1)}, u32[]{:S(2)}, u32[]{:S(2)}) %collective-permute-start.10) | collective-permute-done | bytes 262176 | tf_op jit(solution)/shard_map/ppermute | solution.py:219
  86.3 4.1 %collective-permute-done.11.refs_8_ = bf16[256,512]{1,0:T(8,128)(2,1)S(1)} collective-permute-done((bf16[256,512]{1,0:T(8,128)(2,1)S(1)}, bf16[256,512]{1,0:T(8,128)(2,1)S(1)}, u32[]{:S(2)}, u32[]{:S(2)}) %collective-permute-start.11) | collective-permute-done | bytes 262176 | tf_op jit(solution)/shard_map/ppermute | solution.py:219
  91.2 2.3 %collective-permute-done.12.refs_9_ = bf16[256,512]{1,0:T(8,128)(2,1)S(1)} collective-permute-done((bf16[256,512]{1,0:T(8,128)(2,1)S(1)}, bf16[256,512]{1,0:T(8,128)(2,1)S(1)}, u32[]{:S(2)}, u32[]{:S(2)}) %collective-permute-start.12) | collective-permute-done | bytes 262176 | tf_op jit(solution)/shard_map/ppermute | solution.py:219
  94.2 3.9 %collective-permute-done.13.refs_10_ = bf16[256,512]{1,0:T(8,128)(2,1)S(1)} collective-permute-done((bf16[256,512]{1,0:T(8,128)(2,1)S(1)}, bf16[256,512]{1,0:T(8,128)(2,1)S(1)}, u32[]{:S(2)}, u32[]{:S(2)}) %collective-permute-start.13) | collective-permute-done | bytes 262176 | tf_op jit(solution)/shard_map/ppermute | solution.py:219
  98.8 2.3 %collective-permute-done.14.refs_11_ = bf16[256,512]{1,0:T(8,128)(2,1)S(1)} collective-permute-done((bf16[256,512]{1,0:T(8,128)(2,1)S(1)}, bf16[256,512]{1,0:T(8,128)(2,1)S(1)}, u32[]{:S(2)}, u32[]{:S(2)}) %collective-permute-start.14) | collective-permute-done | bytes 262176 | tf_op jit(solution)/shard_map/ppermute | solution.py:219
  101.7 3.9 %collective-permute-done.15.refs_12_ = bf16[256,512]{1,0:T(8,128)(2,1)S(1)} collective-permute-done((bf16[256,512]{1,0:T(8,128)(2,1)S(1)}, bf16[256,512]{1,0:T(8,128)(2,1)S(1)}, u32[]{:S(2)}, u32[]{:S(2)}) %collective-permute-start.15) | collective-permute-done | bytes 262176 | tf_op jit(solution)/shard_map/ppermute | solution.py:219
  106.3 2.3 %collective-permute-done.16.refs_13_ = bf16[256,512]{1,0:T(8,128)(2,1)S(1)} collective-permute-done((bf16[256,512]{1,0:T(8,128)(2,1)S(1)}, bf16[256,512]{1,0:T(8,128)(2,1)S(1)}, u32[]{:S(2)}, u32[]{:S(2)}) %collective-permute-start.16) | collective-permute-done | bytes 262176 | tf_op jit(solution)/shard_map/ppermute | solution.py:219
  109.3 3.9 %collective-permute-done.17.refs_14_ = bf16[256,512]{1,0:T(8,128)(2,1)S(1)} collective-permute-done((bf16[256,512]{1,0:T(8,128)(2,1)S(1)}, bf16[256,512]{1,0:T(8,128)(2,1)S(1)}, u32[]{:S(2)}, u32[]{:S(2)}) %collective-permute-start.17) | collective-permute-done | bytes 262176 | tf_op jit(solution)/shard_map/ppermute | solution.py:219
  113.9 2.3 %collective-permute-done.18.refs_15_ = bf16[256,512]{1,0:T(8,128)(2,1)S(1)} collective-permute-done((bf16[256,512]{1,0:T(8,128)(2,1)S(1)}, bf16[256,512]{1,0:T(8,128)(2,1)S(1)}, u32[]{:S(2)}, u32[]{:S(2)}) %collective-permute-start.18) | collective-permute-done | bytes 262176 | tf_op jit(solution)/shard_map/ppermute | solution.py:219
  116.9 2.6 %copy-done = bf16[5376,512]{1,0:T(8,128)(2,1)S(1)} copy-done((bf16[5376,512]{1,0:T(8,128)(2,1)S(1)}, bf16[5376,512]{1,0:T(8,128)(2,1)}, u32[]{:S(2)}) %copy-start) | copy-done | bytes 5505048
  127.1 5.1 %project.1 = (f32[672,512]{1,0:T(8,128)S(1)}, f32[1,512]{1,0:T(1,128)S(1)}) custom-call(s32[8]{0:T(128)S(1)} %and_select_fusion.order_ref, bf16[8,672,512]{2,1,0:T(8,128)(2,1)S(1)} %bitcast.20, bf16[256,512]{1,0:T(8,128)(2,1)S(1)} %attend.2.refs_0_, bf16[256,512]{1,0:T(8,128)(2,1)S(1)} %attend.3.refs_1_, ...), custom_call_target="tpu_custom_call" | custom-call | tf_op jit(solution)/shard_map/project/pallas_call | solution.py:156
  132.2 16.8 %all_to_all.5 = f32[8,1,512]{2,1,0:T(1,128)S(1)} all-to-all(f32[8,1,512]{2,1,0:T(1,128)S(1)} %broadcast_in_dim.5), channel_id=1, replica_groups=mesh['seq'=32,'head'=8] {'head'}, dimensions={0} | all-to-all | bytes 32768 | tf_op jit(solution)/shard_map/all_to_all | solution.py:179
  149.0 2.2 %fusion.1 = bf16[512,672]{0,1:T(8,128)(2,1)} fusion(f32[672,512]{1,0:T(8,128)S(1)} %get-tuple-element.11, bf16[512,672]{0,1:T(8,128)(2,1)} %param.13, f32[512]{0:T(512)S(1)} %add_rsqrt_fusion, f32[672]{0:T(1024)S(1)} %copy-done.25), kind=kLoop, calls=%fused_computation.2 | loop fusion | flops 1720320 | bytes 2757248 | tf_op jit(solution)/shard_map/transpose | solution.py:227
  (85 shorter events, 35.6 us)
Async XLA Ops:
  6.5 26.4 %copy-start.22 = (bf16[512,2,128]{2,1,0:T(2,128)(2,1)S(1)}, bf16[512,2,128]{2,1,0:T(2,128)(2,1)}, u32[]{:S(2)}) copy-start(bf16[512,2,128]{2,1,0:T(2,128)(2,1)} %param.10) | copy-start | bytes 786436
  6.5 26.4 %copy-start.23 = (bf16[512,2,128]{2,1,0:T(2,128)(2,1)S(1)}, bf16[512,2,128]{2,1,0:T(2,128)(2,1)}, u32[]{:S(2)}) copy-start(bf16[512,2,128]{2,1,0:T(2,128)(2,1)} %param.9) | copy-start | bytes 786436
  6.5 110.4 %all-gather.3.cloned.1.call-start = ((), (), s32[]{:S(2)}) async-start(), calls=%async_computation.1 | async-start | bytes 5677056 | tf_op jit(solution)/shard_map/all_gather | solution.py:193
  6.5 23.0 %collective-permute-start = (bf16[168,512]{1,0:T(8,128)(2,1)}, bf16[168,512]{1,0:T(8,128)(2,1)S(1)}, u32[]{:S(2)}, u32[]{:S(2)}) collective-permute-start(bf16[168,512]{1,0:T(8,128)(2,1)} %bitcast.25), channel_id=1, source_target_pairs={{0,0},{1,32},{2,64},{3,96},{4,128},{5,160},{6,192},{7,224},{8,8},{... | collective-permute-start | bytes 516104 | tf_op jit(solution)/shard_map/ppermute | solution.py:192
  32.9 23.3 %copy-start.1 = (f32[512,128]{1,0:T(8,128)S(1)}, f32[512,128]{1,0:T(8,128)}, u32[]{:S(2)}) copy-start(f32[512,128]{1,0:T(8,128)} %get-tuple-element.16.cos_ref) | copy-start | bytes 786436
  32.9 23.3 %copy-start.2 = (f32[512,128]{1,0:T(8,128)S(1)}, f32[512,128]{1,0:T(8,128)}, u32[]{:S(2)}) copy-start(f32[512,128]{1,0:T(8,128)} %get-tuple-element.17.sin_ref) | copy-start | bytes 786436
  35.9 10.0 %collective-permute-start.1 = (bf16[2,512,128]{2,1,0:T(8,128)(2,1)}, bf16[2,512,128]{2,1,0:T(8,128)(2,1)S(1)}, u32[]{:S(2)}, u32[]{:S(2)}) collective-permute-start(bf16[2,512,128]{2,1,0:T(8,128)(2,1)} %get-tuple-element.9.own_ref), channel_id=1, source_target_pairs={{0,8},{8,16},{16,24},{24,32},{32,40},{40,48},{48,56},{56,64},{64,7... | collective-permute-start | bytes 786440 | tf_op jit(solution)/shard_map/ppermute | solution.py:204
  37.8 11.2 %collective-permute-start.3 = (bf16[2,512,128]{2,1,0:T(8,128)(2,1)}, bf16[2,512,128]{2,1,0:T(8,128)(2,1)S(1)}, u32[]{:S(2)}, u32[]{:S(2)}) collective-permute-start(bf16[2,512,128]{2,1,0:T(8,128)(2,1)} %get-tuple-element.10.own_ref), channel_id=1, source_target_pairs={{0,8},{8,16},{16,24},{24,32},{32,40},{40,48},{48,56},{56,64},{64,7... | collective-permute-start | bytes 786440 | tf_op jit(solution)/shard_map/ppermute | solution.py:204
  45.9 10.3 %collective-permute-start.2 = (bf16[2,512,128]{2,1,0:T(8,128)(2,1)S(1)}, bf16[2,512,128]{2,1,0:T(8,128)(2,1)S(1)}, u32[]{:S(2)}, u32[]{:S(2)}) collective-permute-start(bf16[2,512,128]{2,1,0:T(8,128)(2,1)S(1)} %collective-permute-done.1.prev_ref), channel_id=1, source_target_pairs={{0,8},{8,16},{16,24},{24,32},{32,40},{40,48},{48,56},{56,64},{64,7... | collective-permute-start | bytes 786440 | tf_op jit(solution)/shard_map/ppermute | solution.py:205
  49.0 11.1 %collective-permute-start.4 = (bf16[2,512,128]{2,1,0:T(8,128)(2,1)S(1)}, bf16[2,512,128]{2,1,0:T(8,128)(2,1)S(1)}, u32[]{:S(2)}, u32[]{:S(2)}) collective-permute-start(bf16[2,512,128]{2,1,0:T(8,128)(2,1)S(1)} %collective-permute-done.3.prev_ref), channel_id=1, source_target_pairs={{0,8},{8,16},{16,24},{24,32},{32,40},{40,48},{48,56},{56,64},{64,7... | collective-permute-start | bytes 786440 | tf_op jit(solution)/shard_map/ppermute | solution.py:205
  60.0 7.7 %collective-permute-start.5 = (bf16[256,512]{1,0:T(8,128)(2,1)S(1)}, bf16[256,512]{1,0:T(8,128)(2,1)S(1)}, u32[]{:S(2)}, u32[]{:S(2)}) collective-permute-start(bf16[256,512]{1,0:T(8,128)(2,1)S(1)} %attend.2.refs_0_), channel_id=1, source_target_pairs={{0,1},{1,2},{2,3},{3,4},{4,5},{5,6},{6,7},{7,0},{8,15},{9,8},{10,9... | collective-permute-start | bytes 786440 | tf_op jit(solution)/shard_map/ppermute | solution.py:219
  63.0 7.7 %collective-permute-start.6 = (bf16[256,512]{1,0:T(8,128)(2,1)S(1)}, bf16[256,512]{1,0:T(8,128)(2,1)S(1)}, u32[]{:S(2)}, u32[]{:S(2)}) collective-permute-start(bf16[256,512]{1,0:T(8,128)(2,1)S(1)} %attend.3.refs_1_), channel_id=1, source_target_pairs={{0,1},{1,2},{2,3},{3,4},{4,5},{5,6},{6,7},{7,0},{8,15},{9,8},{10,9... | collective-permute-start | bytes 786440 | tf_op jit(solution)/shard_map/ppermute | solution.py:219
  67.7 7.6 %collective-permute-start.7 = (bf16[256,512]{1,0:T(8,128)(2,1)S(1)}, bf16[256,512]{1,0:T(8,128)(2,1)S(1)}, u32[]{:S(2)}, u32[]{:S(2)}) collective-permute-start(bf16[256,512]{1,0:T(8,128)(2,1)S(1)} %collective-permute-done.5.refs_2_), channel_id=1, source_target_pairs={{0,1},{1,2},{2,3},{3,4},{4,5},{5,6},{6,7},{7,0},{8,15},{9,8},{10,9... | collective-permute-start | bytes 786440 | tf_op jit(solution)/shard_map/ppermute | solution.py:219
  70.7 7.6 %collective-permute-start.8 = (bf16[256,512]{1,0:T(8,128)(2,1)S(1)}, bf16[256,512]{1,0:T(8,128)(2,1)S(1)}, u32[]{:S(2)}, u32[]{:S(2)}) collective-permute-start(bf16[256,512]{1,0:T(8,128)(2,1)S(1)} %collective-permute-done.6.refs_3_), channel_id=1, source_target_pairs={{0,1},{1,2},{2,3},{3,4},{4,5},{5,6},{6,7},{7,0},{8,15},{9,8},{10,9... | collective-permute-start | bytes 786440 | tf_op jit(solution)/shard_map/ppermute | solution.py:219
  75.3 7.6 %collective-permute-start.9 = (bf16[256,512]{1,0:T(8,128)(2,1)S(1)}, bf16[256,512]{1,0:T(8,128)(2,1)S(1)}, u32[]{:S(2)}, u32[]{:S(2)}) collective-permute-start(bf16[256,512]{1,0:T(8,128)(2,1)S(1)} %collective-permute-done.7.refs_4_), channel_id=1, source_target_pairs={{0,1},{1,2},{2,3},{3,4},{4,5},{5,6},{6,7},{7,0},{8,15},{9,8},{10,9... | collective-permute-start | bytes 786440 | tf_op jit(solution)/shard_map/ppermute | solution.py:219
  78.3 7.6 %collective-permute-start.10 = (bf16[256,512]{1,0:T(8,128)(2,1)S(1)}, bf16[256,512]{1,0:T(8,128)(2,1)S(1)}, u32[]{:S(2)}, u32[]{:S(2)}) collective-permute-start(bf16[256,512]{1,0:T(8,128)(2,1)S(1)} %collective-permute-done.8.refs_5_), channel_id=1, source_target_pairs={{0,1},{1,2},{2,3},{3,4},{4,5},{5,6},{6,7},{7,0},{8,15},{9,8},{10,9... | collective-permute-start | bytes 786440 | tf_op jit(solution)/shard_map/ppermute | solution.py:219
  82.9 7.6 %collective-permute-start.11 = (bf16[256,512]{1,0:T(8,128)(2,1)S(1)}, bf16[256,512]{1,0:T(8,128)(2,1)S(1)}, u32[]{:S(2)}, u32[]{:S(2)}) collective-permute-start(bf16[256,512]{1,0:T(8,128)(2,1)S(1)} %collective-permute-done.9.refs_6_), channel_id=1, source_target_pairs={{0,1},{1,2},{2,3},{3,4},{4,5},{5,6},{6,7},{7,0},{8,15},{9,8},{10,9... | collective-permute-start | bytes 786440 | tf_op jit(solution)/shard_map/ppermute | solution.py:219
  85.9 7.6 %collective-permute-start.12 = (bf16[256,512]{1,0:T(8,128)(2,1)S(1)}, bf16[256,512]{1,0:T(8,128)(2,1)S(1)}, u32[]{:S(2)}, u32[]{:S(2)}) collective-permute-start(bf16[256,512]{1,0:T(8,128)(2,1)S(1)} %collective-permute-done.10.refs_7_), channel_id=1, source_target_pairs={{0,1},{1,2},{2,3},{3,4},{4,5},{5,6},{6,7},{7,0},{8,15},{9,8},{10,9... | collective-permute-start | bytes 786440 | tf_op jit(solution)/shard_map/ppermute | solution.py:219
  90.5 7.6 %collective-permute-start.13 = (bf16[256,512]{1,0:T(8,128)(2,1)S(1)}, bf16[256,512]{1,0:T(8,128)(2,1)S(1)}, u32[]{:S(2)}, u32[]{:S(2)}) collective-permute-start(bf16[256,512]{1,0:T(8,128)(2,1)S(1)} %collective-permute-done.11.refs_8_), channel_id=1, source_target_pairs={{0,1},{1,2},{2,3},{3,4},{4,5},{5,6},{6,7},{7,0},{8,15},{9,8},{10,9... | collective-permute-start | bytes 786440 | tf_op jit(solution)/shard_map/ppermute | solution.py:219
  93.4 7.6 %collective-permute-start.14 = (bf16[256,512]{1,0:T(8,128)(2,1)S(1)}, bf16[256,512]{1,0:T(8,128)(2,1)S(1)}, u32[]{:S(2)}, u32[]{:S(2)}) collective-permute-start(bf16[256,512]{1,0:T(8,128)(2,1)S(1)} %collective-permute-done.12.refs_9_), channel_id=1, source_target_pairs={{0,1},{1,2},{2,3},{3,4},{4,5},{5,6},{6,7},{7,0},{8,15},{9,8},{10,9... | collective-permute-start | bytes 786440 | tf_op jit(solution)/shard_map/ppermute | solution.py:219
  98.0 7.6 %collective-permute-start.15 = (bf16[256,512]{1,0:T(8,128)(2,1)S(1)}, bf16[256,512]{1,0:T(8,128)(2,1)S(1)}, u32[]{:S(2)}, u32[]{:S(2)}) collective-permute-start(bf16[256,512]{1,0:T(8,128)(2,1)S(1)} %collective-permute-done.13.refs_10_), channel_id=1, source_target_pairs={{0,1},{1,2},{2,3},{3,4},{4,5},{5,6},{6,7},{7,0},{8,15},{9,8},{10,9... | collective-permute-start | bytes 786440 | tf_op jit(solution)/shard_map/ppermute | solution.py:219
  101.0 7.6 %collective-permute-start.16 = (bf16[256,512]{1,0:T(8,128)(2,1)S(1)}, bf16[256,512]{1,0:T(8,128)(2,1)S(1)}, u32[]{:S(2)}, u32[]{:S(2)}) collective-permute-start(bf16[256,512]{1,0:T(8,128)(2,1)S(1)} %collective-permute-done.14.refs_11_), channel_id=1, source_target_pairs={{0,1},{1,2},{2,3},{3,4},{4,5},{5,6},{6,7},{7,0},{8,15},{9,8},{10,9... | collective-permute-start | bytes 786440 | tf_op jit(solution)/shard_map/ppermute | solution.py:219
  105.6 7.6 %collective-permute-start.17 = (bf16[256,512]{1,0:T(8,128)(2,1)S(1)}, bf16[256,512]{1,0:T(8,128)(2,1)S(1)}, u32[]{:S(2)}, u32[]{:S(2)}) collective-permute-start(bf16[256,512]{1,0:T(8,128)(2,1)S(1)} %collective-permute-done.15.refs_12_), channel_id=1, source_target_pairs={{0,1},{1,2},{2,3},{3,4},{4,5},{5,6},{6,7},{7,0},{8,15},{9,8},{10,9... | collective-permute-start | bytes 786440 | tf_op jit(solution)/shard_map/ppermute | solution.py:219
  108.6 7.6 %collective-permute-start.18 = (bf16[256,512]{1,0:T(8,128)(2,1)S(1)}, bf16[256,512]{1,0:T(8,128)(2,1)S(1)}, u32[]{:S(2)}, u32[]{:S(2)}) collective-permute-start(bf16[256,512]{1,0:T(8,128)(2,1)S(1)} %collective-permute-done.16.refs_13_), channel_id=1, source_target_pairs={{0,1},{1,2},{2,3},{3,4},{4,5},{5,6},{6,7},{7,0},{8,15},{9,8},{10,9... | collective-permute-start | bytes 786440 | tf_op jit(solution)/shard_map/ppermute | solution.py:219
  (22 other events, 66.6 us)
Sparse Core Ops, SparseCore 0:
  30.3 56.4 all-gather.2

commit v2 on v1

--- a/solution.py
+++ b/solution.py
@@ -29,21 +29,8 @@
     return (x * cosine + pltpu.roll(x, 64, 1) * sine).astype(jnp.bfloat16)
 
 
-def prepare_kernel(k_ref, v_ref, cos_ref, sin_ref, *out_refs):
-    cosine = cos_ref[...]
-    sine = sin_ref[...]
-    for g in range(KV):
-        out_refs[g][0] = rotated(k_ref[g], cosine, sine)
-        out_refs[g][1] = v_ref[g]
-
-
-def prepare(k, v, cosine, sine):
-    shape = jax.ShapeDtypeStruct((2, ROWS, HEAD_SIZE), jnp.bfloat16)
-    return pl.pallas_call(
-        prepare_kernel,
-        out_shape=[shape] * KV,
-        name="rotate_keys",
-    )(k, v, cosine, sine)
+def twice(x, sign):
+    return jnp.concatenate([sign * x, x], -1)
 
 
 def dot_nt(a, b):
@@ -55,8 +42,11 @@
     prev_bias = jnp.where(place >= 1, 0.0, LOW)
     far_bias = jnp.where(place >= 2, 0.0, LOW)
     c = SCALE * LOG2E
-    cosine = cos_ref[...]
-    sine = sin_ref[...]
+    cosine = twice(cos_ref[0], 1.0)
+    sine = twice(sin_ref[0], -1.0)
+    k_own = rotated(own_ref[0], cosine, sine)
+    k_prev = rotated(prev_ref[0], twice(cos_ref[1], 1.0), twice(sin_ref[1], -1.0))
+    k_far = rotated(far_ref[0], twice(cos_ref[2], 1.0), twice(sin_ref[2], -1.0))
     v_own = own_ref[1].T
     v_prev = prev_ref[1].T
     v_far = far_ref[1].T
@@ -69,9 +59,9 @@
         for b in range(blocks):
             q = q_all[b * QB : (b + 1) * QB]
             lo, hi = b * QB, (b + 1) * QB
-            prev = dot_nt(prev_ref[0], q)
-            own = dot_nt(own_ref[0, 0:hi, :], q)
-            far = dot_nt(far_ref[0, lo:ROWS, :], q)
+            prev = dot_nt(k_prev, q)
+            own = dot_nt(k_own[0:hi], q)
+            far = dot_nt(k_far[lo:ROWS], q)
             mixed = jnp.where(seen, own[lo:hi], far[0:QB] + far_bias)
             top = jnp.maximum(
                 jnp.max(prev, axis=0, keepdims=True) + prev_bias,
@@ -115,94 +105,114 @@
         in_specs=[
             pl.BlockSpec(memory_space=pltpu.SMEM),
             pl.BlockSpec((ROWS, width), lambda _: (0, g)),
-            whole(ROWS, HEAD_SIZE),
-            whole(ROWS, HEAD_SIZE),
+            whole(3, ROWS, HEAD_SIZE // 2),
+            whole(3, ROWS, HEAD_SIZE // 2),
             kv,
             kv,
             kv,
         ],
         out_specs=whole(width, ROWS),
         out_shape=jax.ShapeDtypeStruct((width, ROWS), jnp.bfloat16),
-        compiler_params=pltpu.CompilerParams(vmem_limit_bytes=32 * 1024 * 1024),
+        compiler_params=pltpu.CompilerParams(vmem_limit_bytes=24 * 1024 * 1024),
         name="attend",
     )(place, q, cosine, sine, own, prev, far)
 
 
 def project_kernel(order_ref, w_ref, *refs):
-    ctx_refs, (acc_ref, sq_ref) = refs[: KV * N_HEAD], refs[KV * N_HEAD :]
-    step = pl.program_id(0)
+    ctx_refs = refs[: KV * N_HEAD]
+    acc_ref, sq_ref, buffer, arrived = refs[KV * N_HEAD :]
     width = GROUP * HEAD_SIZE
+    copies = [
+        pltpu.make_async_copy(w_ref.at[order_ref[k]], buffer.at[k], arrived.at[k])
+        for k in range(N_HEAD)
+    ]
+    for copy in copies:
+        copy.start()
     for k in range(N_HEAD):
-
-        @pl.when(step == k)
-        def _(k=k):
-            value = sum(
-                jnp.dot(
-                    w_ref[0, :, g * width : (g + 1) * width],
-                    ctx_refs[k * KV + g][...],
-                    preferred_element_type=jnp.float32,
-                )
-                for g in range(KV)
-            )
-            if k > 0:
-                value = acc_ref[...] + value
-            acc_ref[...] = value
-            if k == N_HEAD - 1:
-                sq_ref[...] = jnp.sum(value * value, axis=0, keepdims=True)
+        copies[k].wait()
+        value = sum(
+            jnp.dot(
+                buffer[k, :, g * width : (g + 1) * width],
+                ctx_refs[k * KV + g][...],
+                preferred_element_type=jnp.float32,
+            )
+            for g in range(KV)
+        )
+        if k > 0:
+            value = acc_ref[...] + value
+        acc_ref[...] = value
+        if k == N_HEAD - 1:
+            sq_ref[...] = jnp.sum(value * value, axis=0, keepdims=True)
 
 
 def project(order, weights, blocks):
     width = GROUP * HEAD_SIZE
+    vmem = pl.BlockSpec(memory_space=pltpu.VMEM)
     return pl.pallas_call(
         project_kernel,
-        grid_spec=pltpu.PrefetchScalarGridSpec(
-            num_scalar_prefetch=1,
-            grid=(N_HEAD,),
-            in_specs=[pl.BlockSpec((1, FEATURES, KV * width), lambda k, order: (order[k], 0, 0))]
-            + [pl.BlockSpec((width, ROWS), lambda k, order: (0, 0))] * (KV * N_HEAD),
-            out_specs=[
-                pl.BlockSpec((FEATURES, ROWS), lambda k, order: (0, 0)),
-                pl.BlockSpec((1, ROWS), lambda k, order: (0, 0)),
-            ],
-        ),
+        in_specs=[pl.BlockSpec(memory_space=pltpu.SMEM), pl.BlockSpec(memory_space=pltpu.HBM)]
+        + [vmem] * (KV * N_HEAD),
+        out_specs=[vmem, vmem],
         out_shape=[
             jax.ShapeDtypeStruct((FEATURES, ROWS), jnp.float32),
             jax.ShapeDtypeStruct((1, ROWS), jnp.float32),
         ],
-        compiler_params=pltpu.CompilerParams(vmem_limit_bytes=40 * 1024 * 1024),
+        scratch_shapes=[
+            pltpu.VMEM((N_HEAD, FEATURES, KV * width), jnp.bfloat16),
+            pltpu.SemaphoreType.DMA((N_HEAD,)),
+        ],
+        compiler_params=pltpu.CompilerParams(vmem_limit_bytes=16 * 1024 * 1024),
         name="project",
     )(order, weights, *blocks)
 
 
-def of_everyone(array, axis):
+def finish_kernel(acc_ref, sq_ref, gain_ref, res_ref, out_ref):
+    squares = jnp.sum(sq_ref[...], axis=0)
+    scale = lax.rsqrt(squares / D + EPS)
+    value = res_ref[...].astype(jnp.float32) + gain_ref[...] * (acc_ref[...] * scale)
+    out_ref[...] = value.astype(jnp.bfloat16)
+
+
+def finish(attended, squares, gain, residual):
+    return pl.pallas_call(
+        finish_kernel,
+        out_shape=jax.ShapeDtypeStruct((FEATURES, ROWS), jnp.bfloat16),
+        compiler_params=pltpu.CompilerParams(vmem_limit_bytes=12 * 1024 * 1024),
+        name="finish",
+    )(attended, squares, gain, residual)
+
+
+def for_everyone(array, axis):
     length = lax.axis_size(axis)
     return lax.all_to_all(
         jnp.broadcast_to(array[None], (length, *array.shape)), axis, 0, 0, tiled=True
-    ).sum(axis=0)
+    )
 
 
 def on_device(positions, queries, keys, values, out_weight, post_gain, residual):
     seq = lax.axis_index("seq")
     head = lax.axis_index("head")
     spread = [
-        (s * N_HEAD + h, (h * 4 + s % 4) * N_HEAD + s // 4)
+        (s * N_HEAD + h, ((s // 4 + h) % N_HEAD * 4 + s % 4) * N_HEAD + s // 4)
         for s in range(N_SEQ)
         for h in range(N_HEAD)
     ]
     shard = lax.ppermute(out_weight.T, ("seq", "head"), spread)
+
+    onward = [(i, i + 1) for i in range(N_SEQ - 1)]
+    beyond = [(i, i + 2) for i in range(N_SEQ - 2)]
+    places = jnp.stack(
+        [positions, lax.ppermute(positions, "seq", onward), lax.ppermute(positions, "seq", beyond)]
+    )
+    own = [jnp.stack([keys[:, g], values[:, g]]) for g in range(KV)]
+    prev = [lax.ppermute(x, "seq", onward) for x in own]
+    far = [lax.ppermute(x, "seq", onward) for x in prev]
     weights = lax.all_gather(shard, "seq", axis=0).reshape(N_HEAD, FEATURES, KV * GROUP * HEAD_SIZE)
 
     half = HEAD_SIZE // 2
     inverse = 10000.0 ** (-2.0 * jnp.arange(half, dtype=jnp.float32) / HEAD_SIZE)
-    angle = positions.astype(jnp.float32)[:, None] * inverse[None, :]
+    angle = places.astype(jnp.float32)[:, :, None] * inverse[None, None, :]
     cosine, sine = jnp.cos(angle), jnp.sin(angle)
-    cosine = jnp.concatenate([cosine, cosine], -1)
-    sine = jnp.concatenate([-sine, sine], -1)
-
-    own = prepare(keys.transpose(1, 0, 2), values.transpose(1, 0, 2), cosine, sine)
-    onward = [(i, i + 1) for i in range(N_SEQ - 1)]
-    prev = [lax.ppermute(x, "seq", onward) for x in own]
-    far = [lax.ppermute(x, "seq", onward) for x in prev]
     place = seq.astype(jnp.int32).reshape(1)
     q = queries.reshape(ROWS, KV * GROUP * HEAD_SIZE)
 
@@ -219,12 +229,11 @@
             carried = lax.ppermute(carried, ("seq", "head"), ring)
             blocks[k][g] = carried
     sign = jnp.where(seq % 2 == 0, -1, 1)
-    order = ((head + sign * jnp.arange(N_HEAD, dtype=jnp.int32)) % N_HEAD).astype(jnp.int32)
+    source = head + sign * jnp.arange(N_HEAD, dtype=jnp.int32)
+    order = ((source + head) % N_HEAD).astype(jnp.int32)
     attended, squares = project(order, weights, [x for pair in blocks for x in pair])
-    squares = of_everyone(squares, "head")
-    scaled = attended * lax.rsqrt(squares / D + EPS)
-    result = residual.T.astype(jnp.float32) + post_gain[:, None] * scaled
-    return result.astype(jnp.bfloat16).T
+    squares = for_everyone(squares, "head")
+    return finish(attended, squares, post_gain[:, None], residual.T).T
 
 
 def solution(mesh):

time: 159 us -> 165 us (1.038); the launches traced: 158 us -> 162 us
  blocking collectives: 16.8 us -> 0 us
  local copies, waits for them, and re-layouts: 18.4 us -> 26.5 us
  starting transfers between devices: 26 us -> 33.7 us
  waiting for transfers between devices: 65.4 us -> 72.2 us
  other arithmetic: 4.95 us -> 2.88 us
    all_to_all x1 -> x0, blocking collectives: 16.8 us -> none  [of_everyone(): lax.all_to_all(jnp.broadcast_to(array[None], (length, *array.shape)), axi...]
    all_to_all x0 -> x1, waiting for transfers between devices: none -> 7.62 us  [for_everyone(): lax.all_to_all(jnp.broadcast_to(array[None], (length, *array.shape)), axi...]
    all_to_all x0 -> x1, starting transfers between devices: none -> 7.02 us  [for_everyone(): lax.all_to_all(jnp.broadcast_to(array[None], (length, *array.shape)), axi...]
    ppermute x14, starting transfers between devices: 8.41 us -> 1.58 us  [on_device(): carried = lax.ppermute(carried, ('seq', 'head'), ring)]
    ppermute x0 -> x2, starting transfers between devices: none -> 6.1 us  [the longest x1 4.17 us: on_device(): lax.ppermute(positions, 'seq', beyond)]
    ppermute x2, waiting for transfers between devices: 5.66 us -> 0.01 us  [on_device(): prev = [lax.ppermute(x, 'seq', onward) for x in own]]
    unnamed x53 -> x55, local copies, waits for them, and re-layouts: 17.6 us -> 22.7 us
    ppermute x14, waiting for transfers between devices: 39.8 us -> 44.7 us  [on_device(): carried = lax.ppermute(carried, ('seq', 'head'), ring)]
  transfers between devices with their start and end apart: 20 -> 23, of which waited for: 18 -> 18; matrix products, arithmetic and copies ran while one was open for 2% -> 4% of each run, Pallas kernels for 5% -> 4%
where the time goes in v2:
time: 165 us; the launch traced here: 162 us
  waiting for transfers between devices  72.2 us (44%)
  starting transfers between devices  33.7 us (20%)
  local copies, waits for them, and re-layouts  26.5 us (16%)
  between operations  13.6 us (8%)
  Pallas kernels  13.2 us (8%)
  other arithmetic  2.88 us (2%)
    ppermute x14, waiting for transfers between devices, on_device(): carried = lax.ppermute(carried, ('seq', 'head'), ring)  44.7 us
    unnamed x55, local copies, waits for them, and re-layouts  22.7 us
    ppermute x1, waiting for transfers between devices, on_device(): shard = lax.ppermute(out_weight.T, ('seq', 'head'), spread)  14.6 us
    ppermute x1, starting transfers between devices, on_device(): shard = lax.ppermute(out_weight.T, ('seq', 'head'), spread)  8.33 us
    all_to_all x1, waiting for transfers between devices, for_everyone(): lax.all_to_all(jnp.broadcast_to(array[None], (length, *array.shape)), axi...  7.62 us
    all_to_all x1, starting transfers between devices, for_everyone(): lax.all_to_all(jnp.broadcast_to(array[None], (length, *array.shape)), axi...  7.02 us
    pallas_call x2, Pallas kernels, attend(): pl.pallas_call(attend_kernel, grid=(1,), in_specs=[pl.BlockSpec(memory_sp...  6.12 us
    pallas_call x1, Pallas kernels, project(): pl.pallas_call(project_kernel, in_specs=[pl.BlockSpec(memory_space=pltpu....  6 us
  transfers between devices with their start and end apart: 23, of which 18 were waited for; matrix products, arithmetic and copies ran while one was open for 4% of the time, Pallas kernels for 4%

profile of v2, /device:TPU:6, one launch (start us, length us, event | category | flops | bytes accessed | tf_op | source)
XLA Modules:
  0.0 162.1 jit_solution(14763431017580700620)
XLA Ops:
  6.5 8.3 %collective-permute-start = (bf16[168,512]{1,0:T(8,128)(2,1)}, bf16[168,512]{1,0:T(8,128)(2,1)S(1)}, u32[]{:S(2)}, u32[]{:S(2)}) collective-permute-start(bf16[168,512]{1,0:T(8,128)(2,1)} %bitcast.30), channel_id=1, source_target_pairs={{0,0},{1,32},{2,64},{3,96},{4,128},{5,160},{6,192},{7,224},{8,8},{... | collective-permute-start | bytes 516104 | tf_op jit(solution)/shard_map/ppermute | solution.py:200
  14.9 14.6 %collective-permute-done = bf16[168,512]{1,0:T(8,128)(2,1)S(1)} collective-permute-done((bf16[168,512]{1,0:T(8,128)(2,1)}, bf16[168,512]{1,0:T(8,128)(2,1)S(1)}, u32[]{:S(2)}, u32[]{:S(2)}) %collective-permute-start) | collective-permute-done | bytes 172064 | tf_op jit(solution)/shard_map/ppermute | solution.py:200
  35.3 3.6 %collective-permute-start.3 = (bf16[2,512,128]{2,1,0:T(8,128)(2,1)S(1)}, bf16[2,512,128]{2,1,0:T(8,128)(2,1)S(1)}, u32[]{:S(2)}, u32[]{:S(2)}) collective-permute-start(bf16[2,512,128]{2,1,0:T(8,128)(2,1)S(1)} %pad_maximum_fusion.own_ref), channel_id=1, source_target_pairs={{0,8},{8,16},{16,24},{24,32},{32,40},{40,48},{48,56},{56,64},{64,7... | collective-permute-start | bytes 786440 | tf_op jit(solution)/shard_map/ppermute | solution.py:208
  40.9 4.2 %collective-permute-start.2 = (s32[512]{0:T(512)}, s32[512]{0:T(512)S(1)}, u32[]{:S(2)}, u32[]{:S(2)}) collective-permute-start(s32[512]{0:T(512)} %param.7), channel_id=1, source_target_pairs={{0,16},{8,24},{16,32},{24,40},{32,48},{40,56},{48,64},{56,72},{64,... | collective-permute-start | bytes 6152 | tf_op jit(solution)/shard_map/ppermute | solution.py:205
  48.7 3.2 %collective-permute-start.6 = (bf16[2,512,128]{2,1,0:T(8,128)(2,1)S(1)}, bf16[2,512,128]{2,1,0:T(8,128)(2,1)S(1)}, u32[]{:S(2)}, u32[]{:S(2)}) collective-permute-start(bf16[2,512,128]{2,1,0:T(8,128)(2,1)S(1)} %collective-permute-done.5.prev_ref), channel_id=1, source_target_pairs={{0,8},{8,16},{16,24},{24,32},{32,40},{40,48},{48,56},{56,64},{64,7... | collective-permute-start | bytes 786440 | tf_op jit(solution)/shard_map/ppermute | solution.py:209
  53.9 2.8 %multiply_sine_fusion = (f32[3,512,64]{2,1,0:T(8,128)S(1)}, f32[3,512,64]{2,1,0:T(8,128)S(1)}) fusion(f32[64]{0:T(128)S(1)} %multiply_power_fusion, f32[3,512]{1,0:T(4,128)S(1)} %add_convert_fusion), kind=kLoop, calls=%fused_computation | loop fusion | flops 98304 | bytes 792832 | tf_op jit(solution)/shard_map/sin | solution.py:215
  56.6 2.7 %collective-permute-done.6.far_ref = bf16[2,512,128]{2,1,0:T(8,128)(2,1)S(1)} collective-permute-done((bf16[2,512,128]{2,1,0:T(8,128)(2,1)S(1)}, bf16[2,512,128]{2,1,0:T(8,128)(2,1)S(1)}, u32[]{:S(2)}, u32[]{:S(2)}) %collective-permute-start.6) | collective-permute-done | bytes 262176 | tf_op jit(solution)/shard_map/ppermute | solution.py:209
  59.3 3.1 %attend.3.refs_1_ = bf16[256,512]{1,0:T(8,128)(2,1)S(1)} custom-call(s32[1]{0:T(128)} %bitcast.2.place_ref, bf16[512,512]{1,0:T(8,128)(2,1)S(1)} %bitcast.22, f32[3,512,64]{2,1,0:T(8,128)S(1)} %get-tuple-element.14.cos_ref, f32[3,512,64]{2,1,0:T(8,128)S(1)} %get-tuple-element.13.sin_ref, bf16[2,512,128]{2,1,0:T(8,128)(2,1)S(1)} %pad_maximum_fusion.1.own_ref, ...), custom_call_target="tpu_custom_call" | custom-call | tf_op jit(solution)/shard_map/attend/pallas_call | solution.py:102
  62.5 3.1 %attend.2.refs_0_ = bf16[256,512]{1,0:T(8,128)(2,1)S(1)} custom-call(s32[1]{0:T(128)} %bitcast.2.place_ref, bf16[512,512]{1,0:T(8,128)(2,1)S(1)} %bitcast.23, f32[3,512,64]{2,1,0:T(8,128)S(1)} %get-tuple-element.14.cos_ref, f32[3,512,64]{2,1,0:T(8,128)S(1)} %get-tuple-element.13.sin_ref, bf16[2,512,128]{2,1,0:T(8,128)(2,1)S(1)} %pad_maximum_fusion.own_ref, ...), custom_call_target="tpu_custom_call" | custom-call | tf_op jit(solution)/shard_map/attend/pallas_call | solution.py:102
  67.1 3.0 %collective-permute-done.8.refs_3_ = bf16[256,512]{1,0:T(8,128)(2,1)S(1)} collective-permute-done((bf16[256,512]{1,0:T(8,128)(2,1)S(1)}, bf16[256,512]{1,0:T(8,128)(2,1)S(1)}, u32[]{:S(2)}, u32[]{:S(2)}) %collective-permute-start.8) | collective-permute-done | bytes 262176 | tf_op jit(solution)/shard_map/ppermute | solution.py:229
  70.1 3.4 %collective-permute-done.7.refs_2_ = bf16[256,512]{1,0:T(8,128)(2,1)S(1)} collective-permute-done((bf16[256,512]{1,0:T(8,128)(2,1)S(1)}, bf16[256,512]{1,0:T(8,128)(2,1)S(1)}, u32[]{:S(2)}, u32[]{:S(2)}) %collective-permute-start.7) | collective-permute-done | bytes 262176 | tf_op jit(solution)/shard_map/ppermute | solution.py:229
  73.4 4.2 %collective-permute-done.10.refs_5_ = bf16[256,512]{1,0:T(8,128)(2,1)S(1)} collective-permute-done((bf16[256,512]{1,0:T(8,128)(2,1)S(1)}, bf16[256,512]{1,0:T(8,128)(2,1)S(1)}, u32[]{:S(2)}, u32[]{:S(2)}) %collective-permute-start.10) | collective-permute-done | bytes 262176 | tf_op jit(solution)/shard_map/ppermute | solution.py:229
  77.7 3.4 %collective-permute-done.9.refs_4_ = bf16[256,512]{1,0:T(8,128)(2,1)S(1)} collective-permute-done((bf16[256,512]{1,0:T(8,128)(2,1)S(1)}, bf16[256,512]{1,0:T(8,128)(2,1)S(1)}, u32[]{:S(2)}, u32[]{:S(2)}) %collective-permute-start.9) | collective-permute-done | bytes 262176 | tf_op jit(solution)/shard_map/ppermute | solution.py:229
  81.7 3.5 %collective-permute-done.12.refs_7_ = bf16[256,512]{1,0:T(8,128)(2,1)S(1)} collective-permute-done((bf16[256,512]{1,0:T(8,128)(2,1)S(1)}, bf16[256,512]{1,0:T(8,128)(2,1)S(1)}, u32[]{:S(2)}, u32[]{:S(2)}) %collective-permute-start.12) | collective-permute-done | bytes 262176 | tf_op jit(solution)/shard_map/ppermute | solution.py:229
  89.3 3.5 %collective-permute-done.14.refs_9_ = bf16[256,512]{1,0:T(8,128)(2,1)S(1)} collective-permute-done((bf16[256,512]{1,0:T(8,128)(2,1)S(1)}, bf16[256,512]{1,0:T(8,128)(2,1)S(1)}, u32[]{:S(2)}, u32[]{:S(2)}) %collective-permute-start.14) | collective-permute-done | bytes 262176 | tf_op jit(solution)/shard_map/ppermute | solution.py:229
  93.5 2.7 %collective-permute-done.13.refs_8_ = bf16[256,512]{1,0:T(8,128)(2,1)S(1)} collective-permute-done((bf16[256,512]{1,0:T(8,128)(2,1)S(1)}, bf16[256,512]{1,0:T(8,128)(2,1)S(1)}, u32[]{:S(2)}, u32[]{:S(2)}) %collective-permute-start.13) | collective-permute-done | bytes 262176 | tf_op jit(solution)/shard_map/ppermute | solution.py:229
  96.9 3.5 %collective-permute-done.16.refs_11_ = bf16[256,512]{1,0:T(8,128)(2,1)S(1)} collective-permute-done((bf16[256,512]{1,0:T(8,128)(2,1)S(1)}, bf16[256,512]{1,0:T(8,128)(2,1)S(1)}, u32[]{:S(2)}, u32[]{:S(2)}) %collective-permute-start.16) | collective-permute-done | bytes 262176 | tf_op jit(solution)/shard_map/ppermute | solution.py:229
  101.1 2.7 %collective-permute-done.15.refs_10_ = bf16[256,512]{1,0:T(8,128)(2,1)S(1)} collective-permute-done((bf16[256,512]{1,0:T(8,128)(2,1)S(1)}, bf16[256,512]{1,0:T(8,128)(2,1)S(1)}, u32[]{:S(2)}, u32[]{:S(2)}) %collective-permute-start.15) | collective-permute-done | bytes 262176 | tf_op jit(solution)/shard_map/ppermute | solution.py:229
  104.5 3.5 %collective-permute-done.18.refs_13_ = bf16[256,512]{1,0:T(8,128)(2,1)S(1)} collective-permute-done((bf16[256,512]{1,0:T(8,128)(2,1)S(1)}, bf16[256,512]{1,0:T(8,128)(2,1)S(1)}, u32[]{:S(2)}, u32[]{:S(2)}) %collective-permute-start.18) | collective-permute-done | bytes 262176 | tf_op jit(solution)/shard_map/ppermute | solution.py:229
  112.1 3.5 %collective-permute-done.20.refs_15_ = bf16[256,512]{1,0:T(8,128)(2,1)S(1)} collective-permute-done((bf16[256,512]{1,0:T(8,128)(2,1)S(1)}, bf16[256,512]{1,0:T(8,128)(2,1)S(1)}, u32[]{:S(2)}, u32[]{:S(2)}) %collective-permute-start.20) | collective-permute-done | bytes 262176 | tf_op jit(solution)/shard_map/ppermute | solution.py:229
  116.3 2.7 %collective-permute-done.19.refs_14_ = bf16[256,512]{1,0:T(8,128)(2,1)S(1)} collective-permute-done((bf16[256,512]{1,0:T(8,128)(2,1)S(1)}, bf16[256,512]{1,0:T(8,128)(2,1)S(1)}, u32[]{:S(2)}, u32[]{:S(2)}) %collective-permute-start.19) | collective-permute-done | bytes 262176 | tf_op jit(solution)/shard_map/ppermute | solution.py:229
  132.7 6.0 %project.1 = (f32[672,512]{1,0:T(8,128)S(1)}, f32[1,512]{1,0:T(1,128)S(1)}) custom-call(s32[8]{0:T(128)S(1)} %and_select_fusion.order_ref, bf16[8,672,512]{2,1,0:T(8,128)(2,1)S(1)} %bitcast.21, bf16[256,512]{1,0:T(8,128)(2,1)S(1)} %attend.2.refs_0_, bf16[256,512]{1,0:T(8,128)(2,1)S(1)} %attend.3.refs_1_, ...), custom_call_target="tpu_custom_call" | custom-call | tf_op jit(solution)/shard_map/project/pallas_call | solution.py:151
  139.3 7.0 %all-to-all-start = ((f32[8,1,512]{2,1,0:T(1,128)}), f32[8,1,512]{2,1,0:T(1,128)S(1)}, u32[]{:S(2)}, u32[]{:S(2)}) async-start(f32[8,1,512]{2,1,0:T(1,128)} %broadcast_in_dim.14), calls=%async_computation | async-start | bytes 32768 | tf_op jit(solution)/shard_map/all_to_all | solution.py:187
  146.5 7.6 %all-to-all-done.sq_ref = f32[8,1,512]{2,1,0:T(1,128)S(1)} async-done(((f32[8,1,512]{2,1,0:T(1,128)}), f32[8,1,512]{2,1,0:T(1,128)S(1)}, u32[]{:S(2)}, u32[]{:S(2)}) %all-to-all-start) | async-done | bytes 16416 | tf_op jit(solution)/shard_map/all_to_all | solution.py:187
  (94 shorter events, 42.8 us)
Async XLA Ops:
  6.5 113.2 %all-gather.3.cloned.1.call-start = ((), (), s32[]{:S(2)}) async-start(), calls=%async_computation.1 | async-start | bytes 5677056 | tf_op jit(solution)/shard_map/all_gather | solution.py:210
  6.5 23.0 %collective-permute-start = (bf16[168,512]{1,0:T(8,128)(2,1)}, bf16[168,512]{1,0:T(8,128)(2,1)S(1)}, u32[]{:S(2)}, u32[]{:S(2)}) collective-permute-start(bf16[168,512]{1,0:T(8,128)(2,1)} %bitcast.30), channel_id=1, source_target_pairs={{0,0},{1,32},{2,64},{3,96},{4,128},{5,160},{6,192},{7,224},{8,8},{... | collective-permute-start | bytes 516104 | tf_op jit(solution)/shard_map/ppermute | solution.py:200
  33.3 15.4 %collective-permute-start.5 = (bf16[2,512,128]{2,1,0:T(8,128)(2,1)S(1)}, bf16[2,512,128]{2,1,0:T(8,128)(2,1)S(1)}, u32[]{:S(2)}, u32[]{:S(2)}) collective-permute-start(bf16[2,512,128]{2,1,0:T(8,128)(2,1)S(1)} %pad_maximum_fusion.1.own_ref), channel_id=1, source_target_pairs={{0,8},{8,16},{16,24},{24,32},{32,40},{40,48},{48,56},{56,64},{64,7... | collective-permute-start | bytes 786440 | tf_op jit(solution)/shard_map/ppermute | solution.py:208
  35.3 16.6 %collective-permute-start.3 = (bf16[2,512,128]{2,1,0:T(8,128)(2,1)S(1)}, bf16[2,512,128]{2,1,0:T(8,128)(2,1)S(1)}, u32[]{:S(2)}, u32[]{:S(2)}) collective-permute-start(bf16[2,512,128]{2,1,0:T(8,128)(2,1)S(1)} %pad_maximum_fusion.own_ref), channel_id=1, source_target_pairs={{0,8},{8,16},{16,24},{24,32},{32,40},{40,48},{48,56},{56,64},{64,7... | collective-permute-start | bytes 786440 | tf_op jit(solution)/shard_map/ppermute | solution.py:208
  38.9 7.3 %collective-permute-start.1 = (s32[512]{0:T(512)}, s32[512]{0:T(512)S(1)}, u32[]{:S(2)}, u32[]{:S(2)}) collective-permute-start(s32[512]{0:T(512)} %param.7), channel_id=1, source_target_pairs={{0,8},{8,16},{16,24},{24,32},{32,40},{40,48},{48,56},{56,64},{64,7... | collective-permute-start | bytes 6152 | tf_op jit(solution)/shard_map/ppermute | solution.py:205
  40.9 7.8 %collective-permute-start.2 = (s32[512]{0:T(512)}, s32[512]{0:T(512)S(1)}, u32[]{:S(2)}, u32[]{:S(2)}) collective-permute-start(s32[512]{0:T(512)} %param.7), channel_id=1, source_target_pairs={{0,16},{8,24},{16,32},{24,40},{32,48},{40,56},{48,64},{56,72},{64,... | collective-permute-start | bytes 6152 | tf_op jit(solution)/shard_map/ppermute | solution.py:205
  48.7 10.7 %collective-permute-start.6 = (bf16[2,512,128]{2,1,0:T(8,128)(2,1)S(1)}, bf16[2,512,128]{2,1,0:T(8,128)(2,1)S(1)}, u32[]{:S(2)}, u32[]{:S(2)}) collective-permute-start(bf16[2,512,128]{2,1,0:T(8,128)(2,1)S(1)} %collective-permute-done.5.prev_ref), channel_id=1, source_target_pairs={{0,8},{8,16},{16,24},{24,32},{32,40},{40,48},{48,56},{56,64},{64,7... | collective-permute-start | bytes 786440 | tf_op jit(solution)/shard_map/ppermute | solution.py:209
  51.9 10.6 %collective-permute-start.4 = (bf16[2,512,128]{2,1,0:T(8,128)(2,1)S(1)}, bf16[2,512,128]{2,1,0:T(8,128)(2,1)S(1)}, u32[]{:S(2)}, u32[]{:S(2)}) collective-permute-start(bf16[2,512,128]{2,1,0:T(8,128)(2,1)S(1)} %collective-permute-done.3.prev_ref), channel_id=1, source_target_pairs={{0,8},{8,16},{16,24},{24,32},{32,40},{40,48},{48,56},{56,64},{64,7... | collective-permute-start | bytes 786440 | tf_op jit(solution)/shard_map/ppermute | solution.py:209
  62.4 7.7 %collective-permute-start.8 = (bf16[256,512]{1,0:T(8,128)(2,1)S(1)}, bf16[256,512]{1,0:T(8,128)(2,1)S(1)}, u32[]{:S(2)}, u32[]{:S(2)}) collective-permute-start(bf16[256,512]{1,0:T(8,128)(2,1)S(1)} %attend.3.refs_1_), channel_id=1, source_target_pairs={{0,1},{1,2},{2,3},{3,4},{4,5},{5,6},{6,7},{7,0},{8,15},{9,8},{10,9... | collective-permute-start | bytes 786440 | tf_op jit(solution)/shard_map/ppermute | solution.py:229
  62.5 91.6 %copy-start.1 = (bf16[512,672]{0,1:T(8,128)(2,1)S(1)}, bf16[512,672]{0,1:T(8,128)(2,1)}, u32[]{:S(2)}) copy-start(bf16[512,672]{0,1:T(8,128)(2,1)} %param.13) | copy-start | bytes 2064388
  65.6 7.8 %collective-permute-start.7 = (bf16[256,512]{1,0:T(8,128)(2,1)S(1)}, bf16[256,512]{1,0:T(8,128)(2,1)S(1)}, u32[]{:S(2)}, u32[]{:S(2)}) collective-permute-start(bf16[256,512]{1,0:T(8,128)(2,1)S(1)} %attend.2.refs_0_), channel_id=1, source_target_pairs={{0,1},{1,2},{2,3},{3,4},{4,5},{5,6},{6,7},{7,0},{8,15},{9,8},{10,9... | collective-permute-start | bytes 786440 | tf_op jit(solution)/shard_map/ppermute | solution.py:229
  70.1 7.6 %collective-permute-start.10 = (bf16[256,512]{1,0:T(8,128)(2,1)S(1)}, bf16[256,512]{1,0:T(8,128)(2,1)S(1)}, u32[]{:S(2)}, u32[]{:S(2)}) collective-permute-start(bf16[256,512]{1,0:T(8,128)(2,1)S(1)} %collective-permute-done.8.refs_3_), channel_id=1, source_target_pairs={{0,1},{1,2},{2,3},{3,4},{4,5},{5,6},{6,7},{7,0},{8,15},{9,8},{10,9... | collective-permute-start | bytes 786440 | tf_op jit(solution)/shard_map/ppermute | solution.py:229
  73.4 7.6 %collective-permute-start.9 = (bf16[256,512]{1,0:T(8,128)(2,1)S(1)}, bf16[256,512]{1,0:T(8,128)(2,1)S(1)}, u32[]{:S(2)}, u32[]{:S(2)}) collective-permute-start(bf16[256,512]{1,0:T(8,128)(2,1)S(1)} %collective-permute-done.7.refs_2_), channel_id=1, source_target_pairs={{0,1},{1,2},{2,3},{3,4},{4,5},{5,6},{6,7},{7,0},{8,15},{9,8},{10,9... | collective-permute-start | bytes 786440 | tf_op jit(solution)/shard_map/ppermute | solution.py:229
  77.7 7.6 %collective-permute-start.12 = (bf16[256,512]{1,0:T(8,128)(2,1)S(1)}, bf16[256,512]{1,0:T(8,128)(2,1)S(1)}, u32[]{:S(2)}, u32[]{:S(2)}) collective-permute-start(bf16[256,512]{1,0:T(8,128)(2,1)S(1)} %collective-permute-done.10.refs_5_), channel_id=1, source_target_pairs={{0,1},{1,2},{2,3},{3,4},{4,5},{5,6},{6,7},{7,0},{8,15},{9,8},{10,9... | collective-permute-start | bytes 786440 | tf_op jit(solution)/shard_map/ppermute | solution.py:229
  81.0 7.6 %collective-permute-start.11 = (bf16[256,512]{1,0:T(8,128)(2,1)S(1)}, bf16[256,512]{1,0:T(8,128)(2,1)S(1)}, u32[]{:S(2)}, u32[]{:S(2)}) collective-permute-start(bf16[256,512]{1,0:T(8,128)(2,1)S(1)} %collective-permute-done.9.refs_4_), channel_id=1, source_target_pairs={{0,1},{1,2},{2,3},{3,4},{4,5},{5,6},{6,7},{7,0},{8,15},{9,8},{10,9... | collective-permute-start | bytes 786440 | tf_op jit(solution)/shard_map/ppermute | solution.py:229
  85.2 7.6 %collective-permute-start.14 = (bf16[256,512]{1,0:T(8,128)(2,1)S(1)}, bf16[256,512]{1,0:T(8,128)(2,1)S(1)}, u32[]{:S(2)}, u32[]{:S(2)}) collective-permute-start(bf16[256,512]{1,0:T(8,128)(2,1)S(1)} %collective-permute-done.12.refs_7_), channel_id=1, source_target_pairs={{0,1},{1,2},{2,3},{3,4},{4,5},{5,6},{6,7},{7,0},{8,15},{9,8},{10,9... | collective-permute-start | bytes 786440 | tf_op jit(solution)/shard_map/ppermute | solution.py:229
  88.6 7.6 %collective-permute-start.13 = (bf16[256,512]{1,0:T(8,128)(2,1)S(1)}, bf16[256,512]{1,0:T(8,128)(2,1)S(1)}, u32[]{:S(2)}, u32[]{:S(2)}) collective-permute-start(bf16[256,512]{1,0:T(8,128)(2,1)S(1)} %collective-permute-done.11.refs_6_), channel_id=1, source_target_pairs={{0,1},{1,2},{2,3},{3,4},{4,5},{5,6},{6,7},{7,0},{8,15},{9,8},{10,9... | collective-permute-start | bytes 786440 | tf_op jit(solution)/shard_map/ppermute | solution.py:229
  92.8 7.6 %collective-permute-start.16 = (bf16[256,512]{1,0:T(8,128)(2,1)S(1)}, bf16[256,512]{1,0:T(8,128)(2,1)S(1)}, u32[]{:S(2)}, u32[]{:S(2)}) collective-permute-start(bf16[256,512]{1,0:T(8,128)(2,1)S(1)} %collective-permute-done.14.refs_9_), channel_id=1, source_target_pairs={{0,1},{1,2},{2,3},{3,4},{4,5},{5,6},{6,7},{7,0},{8,15},{9,8},{10,9... | collective-permute-start | bytes 786440 | tf_op jit(solution)/shard_map/ppermute | solution.py:229
  96.2 7.6 %collective-permute-start.15 = (bf16[256,512]{1,0:T(8,128)(2,1)S(1)}, bf16[256,512]{1,0:T(8,128)(2,1)S(1)}, u32[]{:S(2)}, u32[]{:S(2)}) collective-permute-start(bf16[256,512]{1,0:T(8,128)(2,1)S(1)} %collective-permute-done.13.refs_8_), channel_id=1, source_target_pairs={{0,1},{1,2},{2,3},{3,4},{4,5},{5,6},{6,7},{7,0},{8,15},{9,8},{10,9... | collective-permute-start | bytes 786440 | tf_op jit(solution)/shard_map/ppermute | solution.py:229
  100.4 7.6 %collective-permute-start.18 = (bf16[256,512]{1,0:T(8,128)(2,1)S(1)}, bf16[256,512]{1,0:T(8,128)(2,1)S(1)}, u32[]{:S(2)}, u32[]{:S(2)}) collective-permute-start(bf16[256,512]{1,0:T(8,128)(2,1)S(1)} %collective-permute-done.16.refs_11_), channel_id=1, source_target_pairs={{0,1},{1,2},{2,3},{3,4},{4,5},{5,6},{6,7},{7,0},{8,15},{9,8},{10,9... | collective-permute-start | bytes 786440 | tf_op jit(solution)/shard_map/ppermute | solution.py:229
  103.8 7.6 %collective-permute-start.17 = (bf16[256,512]{1,0:T(8,128)(2,1)S(1)}, bf16[256,512]{1,0:T(8,128)(2,1)S(1)}, u32[]{:S(2)}, u32[]{:S(2)}) collective-permute-start(bf16[256,512]{1,0:T(8,128)(2,1)S(1)} %collective-permute-done.15.refs_10_), channel_id=1, source_target_pairs={{0,1},{1,2},{2,3},{3,4},{4,5},{5,6},{6,7},{7,0},{8,15},{9,8},{10,9... | collective-permute-start | bytes 786440 | tf_op jit(solution)/shard_map/ppermute | solution.py:229
  108.0 7.6 %collective-permute-start.20 = (bf16[256,512]{1,0:T(8,128)(2,1)S(1)}, bf16[256,512]{1,0:T(8,128)(2,1)S(1)}, u32[]{:S(2)}, u32[]{:S(2)}) collective-permute-start(bf16[256,512]{1,0:T(8,128)(2,1)S(1)} %collective-permute-done.18.refs_13_), channel_id=1, source_target_pairs={{0,1},{1,2},{2,3},{3,4},{4,5},{5,6},{6,7},{7,0},{8,15},{9,8},{10,9... | collective-permute-start | bytes 786440 | tf_op jit(solution)/shard_map/ppermute | solution.py:229
  111.4 7.6 %collective-permute-start.19 = (bf16[256,512]{1,0:T(8,128)(2,1)S(1)}, bf16[256,512]{1,0:T(8,128)(2,1)S(1)}, u32[]{:S(2)}, u32[]{:S(2)}) collective-permute-start(bf16[256,512]{1,0:T(8,128)(2,1)S(1)} %collective-permute-done.17.refs_12_), channel_id=1, source_target_pairs={{0,1},{1,2},{2,3},{3,4},{4,5},{5,6},{6,7},{7,0},{8,15},{9,8},{10,9... | collective-permute-start | bytes 786440 | tf_op jit(solution)/shard_map/ppermute | solution.py:229
  139.3 14.8 %all-to-all-start = ((f32[8,1,512]{2,1,0:T(1,128)}), f32[8,1,512]{2,1,0:T(1,128)S(1)}, u32[]{:S(2)}, u32[]{:S(2)}) async-start(f32[8,1,512]{2,1,0:T(1,128)} %broadcast_in_dim.14), calls=%async_computation | async-start | bytes 32768 | tf_op jit(solution)/shard_map/all_to_all | solution.py:187
  (26 other events, 144.4 us)
Sparse Core Ops, SparseCore 0:
  30.3 57.2 all-gather.2

commit v3 on v2

--- a/solution.py
+++ b/solution.py
@@ -35,6 +35,22 @@
 
 def dot_nt(a, b):
     return lax.dot_general(a, b, (((1,), (1,)), ((), ())), preferred_element_type=jnp.float32)
+
+
+def hold_kernel(first_ref, *refs):
+    pass
+
+
+def held(array, *others):
+    hbm = pl.BlockSpec(memory_space=pl.ANY)
+    return pl.pallas_call(
+        hold_kernel,
+        in_specs=[hbm] * (1 + len(others)),
+        out_specs=hbm,
+        out_shape=jax.ShapeDtypeStruct(array.shape, array.dtype),
+        input_output_aliases={0: 0},
+        name="hold",
+    )(array, *others)
 
 
 def attend_kernel(place_ref, q_ref, cos_ref, sin_ref, own_ref, prev_ref, far_ref, out_ref):
@@ -120,24 +136,27 @@
 
 def project_kernel(order_ref, w_ref, *refs):
     ctx_refs = refs[: KV * N_HEAD]
-    acc_ref, sq_ref, buffer, arrived = refs[KV * N_HEAD :]
+    acc_ref, sq_ref, w_buffer, ctx_buffer, arrived = refs[KV * N_HEAD :]
     width = GROUP * HEAD_SIZE
-    copies = [
-        pltpu.make_async_copy(w_ref.at[order_ref[k]], buffer.at[k], arrived.at[k])
-        for k in range(N_HEAD)
-    ]
-    for copy in copies:
-        copy.start()
+    copies = []
     for k in range(N_HEAD):
-        copies[k].wait()
-        value = sum(
-            jnp.dot(
-                buffer[k, :, g * width : (g + 1) * width],
-                ctx_refs[k * KV + g][...],
-                preferred_element_type=jnp.float32,
-            )
-            for g in range(KV)
+        copies.append(
+            [pltpu.make_async_copy(w_ref.at[order_ref[k]], w_buffer.at[k], arrived.at[k, KV])]
+            + [
+                pltpu.make_async_copy(
+                    ctx_refs[k * KV + g],
+                    ctx_buffer.at[k, g * width : (g + 1) * width],
+                    arrived.at[k, g],
+                )
+                for g in range(KV)
+            ]
         )
+        for copy in copies[k]:
+            copy.start()
+    for k in range(N_HEAD):
+        for copy in copies[k]:
+            copy.wait()
+        value = jnp.dot(w_buffer[k], ctx_buffer[k], preferred_element_type=jnp.float32)
         if k > 0:
             value = acc_ref[...] + value
         acc_ref[...] = value
@@ -146,22 +165,25 @@
 
 
 def project(order, weights, blocks):
-    width = GROUP * HEAD_SIZE
+    width = KV * GROUP * HEAD_SIZE
     vmem = pl.BlockSpec(memory_space=pltpu.VMEM)
+    hbm = pl.BlockSpec(memory_space=pltpu.HBM)
+    weights = pltpu.with_memory_space_constraint(weights, pltpu.HBM)
+    blocks = [pltpu.with_memory_space_constraint(x, pltpu.HBM) for x in blocks]
     return pl.pallas_call(
         project_kernel,
-        in_specs=[pl.BlockSpec(memory_space=pltpu.SMEM), pl.BlockSpec(memory_space=pltpu.HBM)]
-        + [vmem] * (KV * N_HEAD),
+        in_specs=[pl.BlockSpec(memory_space=pltpu.SMEM), hbm] + [hbm] * (KV * N_HEAD),
         out_specs=[vmem, vmem],
         out_shape=[
             jax.ShapeDtypeStruct((FEATURES, ROWS), jnp.float32),
             jax.ShapeDtypeStruct((1, ROWS), jnp.float32),
         ],
         scratch_shapes=[
-            pltpu.VMEM((N_HEAD, FEATURES, KV * width), jnp.bfloat16),
-            pltpu.SemaphoreType.DMA((N_HEAD,)),
+            pltpu.VMEM((N_HEAD, FEATURES, width), jnp.bfloat16),
+            pltpu.VMEM((N_HEAD, width, ROWS), jnp.bfloat16),
+            pltpu.SemaphoreType.DMA((N_HEAD, KV + 1)),
         ],
-        compiler_params=pltpu.CompilerParams(vmem_limit_bytes=16 * 1024 * 1024),
+        compiler_params=pltpu.CompilerParams(vmem_limit_bytes=24 * 1024 * 1024),
         name="project",
     )(order, weights, *blocks)
 
@@ -207,6 +229,7 @@
     own = [jnp.stack([keys[:, g], values[:, g]]) for g in range(KV)]
     prev = [lax.ppermute(x, "seq", onward) for x in own]
     far = [lax.ppermute(x, "seq", onward) for x in prev]
+    shard = held(shard, *prev)
     weights = lax.all_gather(shard, "seq", axis=0).reshape(N_HEAD, FEATURES, KV * GROUP * HEAD_SIZE)
 
     half = HEAD_SIZE // 2

time: 165 us -> 154 us (0.933)
  the two profiles are of different devices: /device:TPU:6 before, /device:TPU:4 now
where the time goes in v3:
time: 154 us
  waiting for transfers between devices  73.3 us (48%)
  starting transfers between devices  44.6 us (29%)
  between operations  13.7 us (9%)
  Pallas kernels  12.6 us (8%)
  local copies, waits for them, and re-layouts  6.43 us (4%)
  other arithmetic  2.87 us (2%)
    ppermute x14, waiting for transfers between devices, on_device(): carried = lax.ppermute(carried, ('seq', 'head'), ring)  51.9 us
    ppermute x14, starting transfers between devices, on_device(): carried = lax.ppermute(carried, ('seq', 'head'), ring)  9.26 us
    all_to_all x1, starting transfers between devices, for_everyone(): lax.all_to_all(jnp.broadcast_to(array[None], (length, *array.shape)), axi...  9.15 us
    ppermute x1, starting transfers between devices, on_device(): shard = lax.ppermute(out_weight.T, ('seq', 'head'), spread)  9.1 us
    ppermute x1, waiting for transfers between devices, on_device(): shard = lax.ppermute(out_weight.T, ('seq', 'head'), spread)  8.63 us
    all_to_all x1, waiting for transfers between devices, for_everyone(): lax.all_to_all(jnp.broadcast_to(array[None], (length, *array.shape)), axi...  7.62 us
    pallas_call x2, Pallas kernels, attend(): pl.pallas_call(attend_kernel, grid=(1,), in_specs=[pl.BlockSpec(memory_sp...  6.11 us
    ppermute x2, starting transfers between devices, on_device(): far = [lax.ppermute(x, 'seq', onward) for x in prev]  6.06 us
  transfers between devices with their start and end apart: 23, of which 19 were waited for; matrix products, arithmetic and copies ran while one was open for 2% of the time, Pallas kernels for 4%

profile of v3, /device:TPU:4, one launch (start us, length us, event | category | flops | bytes accessed | tf_op | source)
XLA Modules:
  0.0 153.5 jit_solution(13330449358886069992)
XLA Ops:
  11.7 3.6 %collective-permute-start.1 = (bf16[2,512,128]{2,1,0:T(8,128)(2,1)S(1)}, bf16[2,512,128]{2,1,0:T(8,128)(2,1)S(1)}, u32[]{:S(2)}, u32[]{:S(2)}) collective-permute-start(bf16[2,512,128]{2,1,0:T(8,128)(2,1)S(1)} %pad_maximum_fusion.own_ref), channel_id=1, source_target_pairs={{0,8},{8,16},{16,24},{24,32},{32,40},{40,48},{48,56},{56,64},{64,7... | collective-permute-start | bytes 786440 | tf_op jit(solution)/shard_map/ppermute | solution.py:230
  15.3 9.1 %collective-permute-start = (bf16[168,512]{1,0:T(8,128)(2,1)}, bf16[168,512]{1,0:T(8,128)(2,1)S(1)}, u32[]{:S(2)}, u32[]{:S(2)}) collective-permute-start(bf16[168,512]{1,0:T(8,128)(2,1)} %bitcast.30), channel_id=1, source_target_pairs={{0,0},{1,32},{2,64},{3,96},{4,128},{5,160},{6,192},{7,224},{8,8},{... | collective-permute-start | bytes 516104 | tf_op jit(solution)/shard_map/ppermute | solution.py:222
  24.4 8.6 %collective-permute-done.first_ref = bf16[168,512]{1,0:T(8,128)(2,1)S(1)} collective-permute-done((bf16[168,512]{1,0:T(8,128)(2,1)}, bf16[168,512]{1,0:T(8,128)(2,1)S(1)}, u32[]{:S(2)}, u32[]{:S(2)}) %collective-permute-start) | collective-permute-done | bytes 172064 | tf_op jit(solution)/shard_map/ppermute | solution.py:222
  36.6 3.5 %collective-permute-start.4 = (s32[512]{0:T(512)S(1)}, s32[512]{0:T(512)S(1)}, u32[]{:S(2)}, u32[]{:S(2)}) collective-permute-start(s32[512]{0:T(512)S(1)} %copy-done.20), channel_id=1, source_target_pairs={{0,16},{8,24},{16,32},{24,40},{32,48},{40,56},{48,64},{56,72},{64,... | collective-permute-start | bytes 6152 | tf_op jit(solution)/shard_map/ppermute | solution.py:227
  44.2 3.3 %collective-permute-start.6 = (bf16[2,512,128]{2,1,0:T(8,128)(2,1)}, bf16[2,512,128]{2,1,0:T(8,128)(2,1)S(1)}, u32[]{:S(2)}, u32[]{:S(2)}) collective-permute-start(bf16[2,512,128]{2,1,0:T(8,128)(2,1)} %copy-done.2), channel_id=1, source_target_pairs={{0,8},{8,16},{16,24},{24,32},{32,40},{40,48},{48,56},{56,64},{64,7... | collective-permute-start | bytes 786440 | tf_op jit(solution)/shard_map/ppermute | solution.py:231
  55.1 3.1 %attend.3.refs_1_ = bf16[256,512]{1,0:T(8,128)(2,1)S(1)} custom-call(s32[1]{0:T(128)} %bitcast.6.place_ref, bf16[512,512]{1,0:T(8,128)(2,1)S(1)} %bitcast.21, f32[3,512,64]{2,1,0:T(8,128)S(1)} %get-tuple-element.14.cos_ref, f32[3,512,64]{2,1,0:T(8,128)S(1)} %get-tuple-element.13.sin_ref, bf16[2,512,128]{2,1,0:T(8,128)(2,1)S(1)} %pad_maximum_fusion.1.own_ref, ...), custom_call_target="tpu_custom_call" | custom-call | tf_op jit(solution)/shard_map/attend/pallas_call | solution.py:118
  58.2 6.4 %collective-permute-start.8 = (bf16[256,512]{1,0:T(8,128)(2,1)S(1)}, bf16[256,512]{1,0:T(8,128)(2,1)S(1)}, u32[]{:S(2)}, u32[]{:S(2)}) collective-permute-start(bf16[256,512]{1,0:T(8,128)(2,1)S(1)} %attend.3.refs_1_), channel_id=1, source_target_pairs={{0,1},{1,2},{2,3},{3,4},{4,5},{5,6},{6,7},{7,0},{8,15},{9,8},{10,9... | collective-permute-start | bytes 786440 | tf_op jit(solution)/shard_map/ppermute | solution.py:252
  64.7 3.1 %attend.2.refs_0_ = bf16[256,512]{1,0:T(8,128)(2,1)S(1)} custom-call(s32[1]{0:T(128)} %bitcast.6.place_ref, bf16[512,512]{1,0:T(8,128)(2,1)S(1)} %bitcast.22, f32[3,512,64]{2,1,0:T(8,128)S(1)} %get-tuple-element.14.cos_ref, f32[3,512,64]{2,1,0:T(8,128)S(1)} %get-tuple-element.13.sin_ref, bf16[2,512,128]{2,1,0:T(8,128)(2,1)S(1)} %pad_maximum_fusion.own_ref, ...), custom_call_target="tpu_custom_call" | custom-call | tf_op jit(solution)/shard_map/attend/pallas_call | solution.py:118
  68.4 3.2 %collective-permute-done.8.refs_3_ = bf16[256,512]{1,0:T(8,128)(2,1)S(1)} collective-permute-done((bf16[256,512]{1,0:T(8,128)(2,1)S(1)}, bf16[256,512]{1,0:T(8,128)(2,1)S(1)}, u32[]{:S(2)}, u32[]{:S(2)}) %collective-permute-start.8) | collective-permute-done | bytes 262176 | tf_op jit(solution)/shard_map/ppermute | solution.py:252
  76.6 4.1 %collective-permute-done.10.refs_5_ = bf16[256,512]{1,0:T(8,128)(2,1)S(1)} collective-permute-done((bf16[256,512]{1,0:T(8,128)(2,1)S(1)}, bf16[256,512]{1,0:T(8,128)(2,1)S(1)}, u32[]{:S(2)}, u32[]{:S(2)}) %collective-permute-start.10) | collective-permute-done | bytes 262176 | tf_op jit(solution)/shard_map/ppermute | solution.py:252
  80.8 3.4 %collective-permute-done.9.refs_4_ = bf16[256,512]{1,0:T(8,128)(2,1)S(1)} collective-permute-done((bf16[256,512]{1,0:T(8,128)(2,1)S(1)}, bf16[256,512]{1,0:T(8,128)(2,1)S(1)}, u32[]{:S(2)}, u32[]{:S(2)}) %collective-permute-start.9) | collective-permute-done | bytes 262176 | tf_op jit(solution)/shard_map/ppermute | solution.py:252
  84.2 4.2 %collective-permute-done.12.refs_7_ = bf16[256,512]{1,0:T(8,128)(2,1)S(1)} collective-permute-done((bf16[256,512]{1,0:T(8,128)(2,1)S(1)}, bf16[256,512]{1,0:T(8,128)(2,1)S(1)}, u32[]{:S(2)}, u32[]{:S(2)}) %collective-permute-start.12) | collective-permute-done | bytes 262176 | tf_op jit(solution)/shard_map/ppermute | solution.py:252
  88.4 3.4 %collective-permute-done.11.refs_6_ = bf16[256,512]{1,0:T(8,128)(2,1)S(1)} collective-permute-done((bf16[256,512]{1,0:T(8,128)(2,1)S(1)}, bf16[256,512]{1,0:T(8,128)(2,1)S(1)}, u32[]{:S(2)}, u32[]{:S(2)}) %collective-permute-start.11) | collective-permute-done | bytes 262176 | tf_op jit(solution)/shard_map/ppermute | solution.py:252
  91.8 4.2 %collective-permute-done.14.refs_9_ = bf16[256,512]{1,0:T(8,128)(2,1)S(1)} collective-permute-done((bf16[256,512]{1,0:T(8,128)(2,1)S(1)}, bf16[256,512]{1,0:T(8,128)(2,1)S(1)}, u32[]{:S(2)}, u32[]{:S(2)}) %collective-permute-start.14) | collective-permute-done | bytes 262176 | tf_op jit(solution)/shard_map/ppermute | solution.py:252
  96.0 3.4 %collective-permute-done.13.refs_8_ = bf16[256,512]{1,0:T(8,128)(2,1)S(1)} collective-permute-done((bf16[256,512]{1,0:T(8,128)(2,1)S(1)}, bf16[256,512]{1,0:T(8,128)(2,1)S(1)}, u32[]{:S(2)}, u32[]{:S(2)}) %collective-permute-start.13) | collective-permute-done | bytes 262176 | tf_op jit(solution)/shard_map/ppermute | solution.py:252
  99.4 4.2 %collective-permute-done.16.refs_11_ = bf16[256,512]{1,0:T(8,128)(2,1)S(1)} collective-permute-done((bf16[256,512]{1,0:T(8,128)(2,1)S(1)}, bf16[256,512]{1,0:T(8,128)(2,1)S(1)}, u32[]{:S(2)}, u32[]{:S(2)}) %collective-permute-start.16) | collective-permute-done | bytes 262176 | tf_op jit(solution)/shard_map/ppermute | solution.py:252
  103.6 3.4 %collective-permute-done.15.refs_10_ = bf16[256,512]{1,0:T(8,128)(2,1)S(1)} collective-permute-done((bf16[256,512]{1,0:T(8,128)(2,1)S(1)}, bf16[256,512]{1,0:T(8,128)(2,1)S(1)}, u32[]{:S(2)}, u32[]{:S(2)}) %collective-permute-start.15) | collective-permute-done | bytes 262176 | tf_op jit(solution)/shard_map/ppermute | solution.py:252
  107.0 4.3 %collective-permute-done.18.refs_13_ = bf16[256,512]{1,0:T(8,128)(2,1)} collective-permute-done((bf16[256,512]{1,0:T(8,128)(2,1)S(1)}, bf16[256,512]{1,0:T(8,128)(2,1)}, u32[]{:S(2)}, u32[]{:S(2)}) %collective-permute-start.18) | collective-permute-done | bytes 262176 | tf_op jit(solution)/shard_map/ppermute | solution.py:252
  111.2 3.4 %collective-permute-done.17.refs_12_ = bf16[256,512]{1,0:T(8,128)(2,1)} collective-permute-done((bf16[256,512]{1,0:T(8,128)(2,1)S(1)}, bf16[256,512]{1,0:T(8,128)(2,1)}, u32[]{:S(2)}, u32[]{:S(2)}) %collective-permute-start.17) | collective-permute-done | bytes 262176 | tf_op jit(solution)/shard_map/ppermute | solution.py:252
  114.7 4.5 %collective-permute-done.20.refs_15_ = bf16[256,512]{1,0:T(8,128)(2,1)} collective-permute-done((bf16[256,512]{1,0:T(8,128)(2,1)}, bf16[256,512]{1,0:T(8,128)(2,1)}, u32[]{:S(2)}, u32[]{:S(2)}) %collective-permute-start.20) | collective-permute-done | bytes 262176 | tf_op jit(solution)/shard_map/ppermute | solution.py:252
  119.1 3.4 %collective-permute-done.19.refs_14_ = bf16[256,512]{1,0:T(8,128)(2,1)} collective-permute-done((bf16[256,512]{1,0:T(8,128)(2,1)}, bf16[256,512]{1,0:T(8,128)(2,1)}, u32[]{:S(2)}, u32[]{:S(2)}) %collective-permute-start.19) | collective-permute-done | bytes 262176 | tf_op jit(solution)/shard_map/ppermute | solution.py:252
  122.6 5.4 %project.1 = (f32[672,512]{1,0:T(8,128)S(1)}, f32[1,512]{1,0:T(1,128)S(1)}) custom-call(s32[8]{0:T(128)S(1)} %and_select_fusion.order_ref, bf16[8,672,512]{2,1,0:T(8,128)(2,1)} %bitcast.25, bf16[256,512]{1,0:T(8,128)(2,1)} %copy-done.1, bf16[256,512]{1,0:T(8,128)(2,1)} %copy-done, bf16[256,512]{1,0:T(8,128)(2,1)} %copy-done.10, bf16[256,512]{1,0:T(8,128)(2,1)} %copy-done.9, ...), custom_call_target="tpu_custom_call" | custom-call | tf_op jit(solution)/shard_map/project/pallas_call | solution.py:173
  128.6 9.1 %all-to-all-start = ((f32[8,1,512]{2,1,0:T(1,128)}), f32[8,1,512]{2,1,0:T(1,128)S(1)}, u32[]{:S(2)}, u32[]{:S(2)}) async-start(f32[8,1,512]{2,1,0:T(1,128)} %broadcast_in_dim.14), calls=%async_computation | async-start | bytes 32768 | tf_op jit(solution)/shard_map/all_to_all | solution.py:209
  137.9 7.6 %all-to-all-done.sq_ref = f32[8,1,512]{2,1,0:T(1,128)S(1)} async-done(((f32[8,1,512]{2,1,0:T(1,128)}), f32[8,1,512]{2,1,0:T(1,128)S(1)}, u32[]{:S(2)}, u32[]{:S(2)}) %all-to-all-start) | async-done | bytes 16416 | tf_op jit(solution)/shard_map/all_to_all | solution.py:209
  (83 shorter events, 28.0 us)
Async XLA Ops:
  6.5 116.0 %all-gather.3.cloned.1.call-start = ((), (), s32[]{:S(2)}) async-start(), calls=%async_computation.1 | async-start | bytes 5677056 | tf_op jit(solution)/shard_map/all_gather | solution.py:233
  9.7 23.3 %collective-permute-start.2 = (bf16[2,512,128]{2,1,0:T(8,128)(2,1)S(1)}, bf16[2,512,128]{2,1,0:T(8,128)(2,1)S(1)}, u32[]{:S(2)}, u32[]{:S(2)}) collective-permute-start(bf16[2,512,128]{2,1,0:T(8,128)(2,1)S(1)} %pad_maximum_fusion.1.own_ref), channel_id=1, source_target_pairs={{0,8},{8,16},{16,24},{24,32},{32,40},{40,48},{48,56},{56,64},{64,7... | collective-permute-start | bytes 786440 | tf_op jit(solution)/shard_map/ppermute | solution.py:230
  11.7 21.3 %collective-permute-start.1 = (bf16[2,512,128]{2,1,0:T(8,128)(2,1)S(1)}, bf16[2,512,128]{2,1,0:T(8,128)(2,1)S(1)}, u32[]{:S(2)}, u32[]{:S(2)}) collective-permute-start(bf16[2,512,128]{2,1,0:T(8,128)(2,1)S(1)} %pad_maximum_fusion.own_ref), channel_id=1, source_target_pairs={{0,8},{8,16},{16,24},{24,32},{32,40},{40,48},{48,56},{56,64},{64,7... | collective-permute-start | bytes 786440 | tf_op jit(solution)/shard_map/ppermute | solution.py:230
  15.3 17.7 %collective-permute-start = (bf16[168,512]{1,0:T(8,128)(2,1)}, bf16[168,512]{1,0:T(8,128)(2,1)S(1)}, u32[]{:S(2)}, u32[]{:S(2)}) collective-permute-start(bf16[168,512]{1,0:T(8,128)(2,1)} %bitcast.30), channel_id=1, source_target_pairs={{0,0},{1,32},{2,64},{3,96},{4,128},{5,160},{6,192},{7,224},{8,8},{... | collective-permute-start | bytes 516104 | tf_op jit(solution)/shard_map/ppermute | solution.py:222
  34.5 7.1 %collective-permute-start.3 = (s32[512]{0:T(512)S(1)}, s32[512]{0:T(512)S(1)}, u32[]{:S(2)}, u32[]{:S(2)}) collective-permute-start(s32[512]{0:T(512)S(1)} %copy-done.20), channel_id=1, source_target_pairs={{0,8},{8,16},{16,24},{24,32},{32,40},{40,48},{48,56},{56,64},{64,7... | collective-permute-start | bytes 6152 | tf_op jit(solution)/shard_map/ppermute | solution.py:227
  36.6 7.6 %collective-permute-start.4 = (s32[512]{0:T(512)S(1)}, s32[512]{0:T(512)S(1)}, u32[]{:S(2)}, u32[]{:S(2)}) collective-permute-start(s32[512]{0:T(512)S(1)} %copy-done.20), channel_id=1, source_target_pairs={{0,16},{8,24},{16,32},{24,40},{32,48},{40,56},{48,64},{56,72},{64,... | collective-permute-start | bytes 6152 | tf_op jit(solution)/shard_map/ppermute | solution.py:227
  44.2 10.0 %collective-permute-start.6 = (bf16[2,512,128]{2,1,0:T(8,128)(2,1)}, bf16[2,512,128]{2,1,0:T(8,128)(2,1)S(1)}, u32[]{:S(2)}, u32[]{:S(2)}) collective-permute-start(bf16[2,512,128]{2,1,0:T(8,128)(2,1)} %copy-done.2), channel_id=1, source_target_pairs={{0,8},{8,16},{16,24},{24,32},{32,40},{40,48},{48,56},{56,64},{64,7... | collective-permute-start | bytes 786440 | tf_op jit(solution)/shard_map/ppermute | solution.py:231
  47.5 17.2 %collective-permute-start.5 = (bf16[2,512,128]{2,1,0:T(8,128)(2,1)}, bf16[2,512,128]{2,1,0:T(8,128)(2,1)S(1)}, u32[]{:S(2)}, u32[]{:S(2)}) collective-permute-start(bf16[2,512,128]{2,1,0:T(8,128)(2,1)} %copy-done.4), channel_id=1, source_target_pairs={{0,8},{8,16},{16,24},{24,32},{32,40},{40,48},{48,56},{56,64},{64,7... | collective-permute-start | bytes 786440 | tf_op jit(solution)/shard_map/ppermute | solution.py:231
  58.2 13.4 %collective-permute-start.8 = (bf16[256,512]{1,0:T(8,128)(2,1)S(1)}, bf16[256,512]{1,0:T(8,128)(2,1)S(1)}, u32[]{:S(2)}, u32[]{:S(2)}) collective-permute-start(bf16[256,512]{1,0:T(8,128)(2,1)S(1)} %attend.3.refs_1_), channel_id=1, source_target_pairs={{0,1},{1,2},{2,3},{3,4},{4,5},{5,6},{6,7},{7,0},{8,15},{9,8},{10,9... | collective-permute-start | bytes 786440 | tf_op jit(solution)/shard_map/ppermute | solution.py:252
  67.8 77.8 %copy-start.6 = (bf16[512,672]{0,1:T(8,128)(2,1)S(1)}, bf16[512,672]{0,1:T(8,128)(2,1)}, u32[]{:S(2)}) copy-start(bf16[512,672]{0,1:T(8,128)(2,1)} %param.13) | copy-start | bytes 2064388
  67.8 7.8 %collective-permute-start.7 = (bf16[256,512]{1,0:T(8,128)(2,1)S(1)}, bf16[256,512]{1,0:T(8,128)(2,1)S(1)}, u32[]{:S(2)}, u32[]{:S(2)}) collective-permute-start(bf16[256,512]{1,0:T(8,128)(2,1)S(1)} %attend.2.refs_0_), channel_id=1, source_target_pairs={{0,1},{1,2},{2,3},{3,4},{4,5},{5,6},{6,7},{7,0},{8,15},{9,8},{10,9... | collective-permute-start | bytes 786440 | tf_op jit(solution)/shard_map/ppermute | solution.py:252
  71.7 9.1 %collective-permute-start.10 = (bf16[256,512]{1,0:T(8,128)(2,1)S(1)}, bf16[256,512]{1,0:T(8,128)(2,1)S(1)}, u32[]{:S(2)}, u32[]{:S(2)}) collective-permute-start(bf16[256,512]{1,0:T(8,128)(2,1)S(1)} %collective-permute-done.8.refs_3_), channel_id=1, source_target_pairs={{0,1},{1,2},{2,3},{3,4},{4,5},{5,6},{6,7},{7,0},{8,15},{9,8},{10,9... | collective-permute-start | bytes 786440 | tf_op jit(solution)/shard_map/ppermute | solution.py:252
  75.6 8.6 %collective-permute-start.9 = (bf16[256,512]{1,0:T(8,128)(2,1)S(1)}, bf16[256,512]{1,0:T(8,128)(2,1)S(1)}, u32[]{:S(2)}, u32[]{:S(2)}) collective-permute-start(bf16[256,512]{1,0:T(8,128)(2,1)S(1)} %collective-permute-done.7.refs_2_), channel_id=1, source_target_pairs={{0,1},{1,2},{2,3},{3,4},{4,5},{5,6},{6,7},{7,0},{8,15},{9,8},{10,9... | collective-permute-start | bytes 786440 | tf_op jit(solution)/shard_map/ppermute | solution.py:252
  80.8 7.6 %collective-permute-start.12 = (bf16[256,512]{1,0:T(8,128)(2,1)S(1)}, bf16[256,512]{1,0:T(8,128)(2,1)S(1)}, u32[]{:S(2)}, u32[]{:S(2)}) collective-permute-start(bf16[256,512]{1,0:T(8,128)(2,1)S(1)} %collective-permute-done.10.refs_5_), channel_id=1, source_target_pairs={{0,1},{1,2},{2,3},{3,4},{4,5},{5,6},{6,7},{7,0},{8,15},{9,8},{10,9... | collective-permute-start | bytes 786440 | tf_op jit(solution)/shard_map/ppermute | solution.py:252
  84.2 7.6 %collective-permute-start.11 = (bf16[256,512]{1,0:T(8,128)(2,1)S(1)}, bf16[256,512]{1,0:T(8,128)(2,1)S(1)}, u32[]{:S(2)}, u32[]{:S(2)}) collective-permute-start(bf16[256,512]{1,0:T(8,128)(2,1)S(1)} %collective-permute-done.9.refs_4_), channel_id=1, source_target_pairs={{0,1},{1,2},{2,3},{3,4},{4,5},{5,6},{6,7},{7,0},{8,15},{9,8},{10,9... | collective-permute-start | bytes 786440 | tf_op jit(solution)/shard_map/ppermute | solution.py:252
  88.4 7.6 %collective-permute-start.14 = (bf16[256,512]{1,0:T(8,128)(2,1)S(1)}, bf16[256,512]{1,0:T(8,128)(2,1)S(1)}, u32[]{:S(2)}, u32[]{:S(2)}) collective-permute-start(bf16[256,512]{1,0:T(8,128)(2,1)S(1)} %collective-permute-done.12.refs_7_), channel_id=1, source_target_pairs={{0,1},{1,2},{2,3},{3,4},{4,5},{5,6},{6,7},{7,0},{8,15},{9,8},{10,9... | collective-permute-start | bytes 786440 | tf_op jit(solution)/shard_map/ppermute | solution.py:252
  91.8 7.6 %collective-permute-start.13 = (bf16[256,512]{1,0:T(8,128)(2,1)S(1)}, bf16[256,512]{1,0:T(8,128)(2,1)S(1)}, u32[]{:S(2)}, u32[]{:S(2)}) collective-permute-start(bf16[256,512]{1,0:T(8,128)(2,1)S(1)} %collective-permute-done.11.refs_6_), channel_id=1, source_target_pairs={{0,1},{1,2},{2,3},{3,4},{4,5},{5,6},{6,7},{7,0},{8,15},{9,8},{10,9... | collective-permute-start | bytes 786440 | tf_op jit(solution)/shard_map/ppermute | solution.py:252
  96.0 7.6 %collective-permute-start.16 = (bf16[256,512]{1,0:T(8,128)(2,1)S(1)}, bf16[256,512]{1,0:T(8,128)(2,1)S(1)}, u32[]{:S(2)}, u32[]{:S(2)}) collective-permute-start(bf16[256,512]{1,0:T(8,128)(2,1)S(1)} %collective-permute-done.14.refs_9_), channel_id=1, source_target_pairs={{0,1},{1,2},{2,3},{3,4},{4,5},{5,6},{6,7},{7,0},{8,15},{9,8},{10,9... | collective-permute-start | bytes 786440 | tf_op jit(solution)/shard_map/ppermute | solution.py:252
  99.4 7.6 %collective-permute-start.15 = (bf16[256,512]{1,0:T(8,128)(2,1)S(1)}, bf16[256,512]{1,0:T(8,128)(2,1)S(1)}, u32[]{:S(2)}, u32[]{:S(2)}) collective-permute-start(bf16[256,512]{1,0:T(8,128)(2,1)S(1)} %collective-permute-done.13.refs_8_), channel_id=1, source_target_pairs={{0,1},{1,2},{2,3},{3,4},{4,5},{5,6},{6,7},{7,0},{8,15},{9,8},{10,9... | collective-permute-start | bytes 786440 | tf_op jit(solution)/shard_map/ppermute | solution.py:252
  103.5 7.7 %collective-permute-start.18 = (bf16[256,512]{1,0:T(8,128)(2,1)S(1)}, bf16[256,512]{1,0:T(8,128)(2,1)}, u32[]{:S(2)}, u32[]{:S(2)}) collective-permute-start(bf16[256,512]{1,0:T(8,128)(2,1)S(1)} %collective-permute-done.16.refs_11_), channel_id=1, source_target_pairs={{0,1},{1,2},{2,3},{3,4},{4,5},{5,6},{6,7},{7,0},{8,15},{9,8},{10,9... | collective-permute-start | bytes 786440 | tf_op jit(solution)/shard_map/ppermute | solution.py:252
  106.9 7.7 %collective-permute-start.17 = (bf16[256,512]{1,0:T(8,128)(2,1)S(1)}, bf16[256,512]{1,0:T(8,128)(2,1)}, u32[]{:S(2)}, u32[]{:S(2)}) collective-permute-start(bf16[256,512]{1,0:T(8,128)(2,1)S(1)} %collective-permute-done.15.refs_10_), channel_id=1, source_target_pairs={{0,1},{1,2},{2,3},{3,4},{4,5},{5,6},{6,7},{7,0},{8,15},{9,8},{10,9... | collective-permute-start | bytes 786440 | tf_op jit(solution)/shard_map/ppermute | solution.py:252
  111.2 7.9 %collective-permute-start.20 = (bf16[256,512]{1,0:T(8,128)(2,1)}, bf16[256,512]{1,0:T(8,128)(2,1)}, u32[]{:S(2)}, u32[]{:S(2)}) collective-permute-start(bf16[256,512]{1,0:T(8,128)(2,1)} %collective-permute-done.18.refs_13_), channel_id=1, source_target_pairs={{0,1},{1,2},{2,3},{3,4},{4,5},{5,6},{6,7},{7,0},{8,15},{9,8},{10,9... | collective-permute-start | bytes 786440 | tf_op jit(solution)/shard_map/ppermute | solution.py:252
  114.6 7.9 %collective-permute-start.19 = (bf16[256,512]{1,0:T(8,128)(2,1)}, bf16[256,512]{1,0:T(8,128)(2,1)}, u32[]{:S(2)}, u32[]{:S(2)}) collective-permute-start(bf16[256,512]{1,0:T(8,128)(2,1)} %collective-permute-done.17.refs_12_), channel_id=1, source_target_pairs={{0,1},{1,2},{2,3},{3,4},{4,5},{5,6},{6,7},{7,0},{8,15},{9,8},{10,9... | collective-permute-start | bytes 786440 | tf_op jit(solution)/shard_map/ppermute | solution.py:252
  128.6 16.9 %all-to-all-start = ((f32[8,1,512]{2,1,0:T(1,128)}), f32[8,1,512]{2,1,0:T(1,128)S(1)}, u32[]{:S(2)}, u32[]{:S(2)}) async-start(f32[8,1,512]{2,1,0:T(1,128)} %broadcast_in_dim.14), calls=%async_computation | async-start | bytes 32768 | tf_op jit(solution)/shard_map/all_to_all | solution.py:209
  (20 other events, 576.6 us)
Sparse Core Ops, SparseCore 0:
  34.6 60.1 all-gather.2

commit v4 on v3

v4 whole, which is shorter than its diff:
```python
import functools
import math

import jax
import jax.numpy as jnp
from jax import lax
from jax.experimental import pallas as pl
from jax.experimental.pallas import tpu as pltpu
from jax.sharding import PartitionSpec as P

D = 5376
HEAD_SIZE = 128
VISIBLE_SPAN = 1024
EPS = 1e-06
SCALE = 168.0 ** (-0.5)
LOG2E = math.log2(math.e)
ROWS = 512
KV = 2
GROUP = 2
N_SEQ = 32
N_HEAD = 8
FEATURES = D // N_HEAD
SHARD = D // N_SEQ
QB = 256
WIDTH = KV * GROUP * HEAD_SIZE
PIECE = 128
PIECES = WIDTH // PIECE
LOW = -1e30
VMEM = pl.BlockSpec(memory_space=pltpu.VMEM)


def cos_and_sin(angle):
    turns = jnp.floor(angle * (2.0 / math.pi) + 0.5)
    x = angle - turns * 1.5703125
    x = x - turns * 4.8351287841796875e-4
    x = x - turns * 3.1385570764541626e-07
    x = x - turns * 6.0771005065061922e-11
    z = x * x
    sine = ((-1.9515295891e-4 * z + 8.3321608736e-3) * z - 1.6666654611e-1) * z * x + x
    cosine = ((2.443315711809948e-5 * z - 1.388731625493765e-3) * z + 4.166664568298827e-2) * z * z
    cosine = cosine - 0.5 * z + 1.0
    quadrant = turns.astype(jnp.int32) & 3
    odd = (quadrant & 1) == 1
    first = jnp.where(odd, sine, cosine)
    second = jnp.where(odd, cosine, sine)
    first = jnp.where((quadrant == 1) | (quadrant == 2), -first, first)
    second = jnp.where(quadrant >= 2, -second, second)
    return first, second


def rotated(x, cosine, sine):
    x = x.astype(jnp.float32)
    return (x * cosine + pltpu.roll(x, 64, 1) * sine).astype(jnp.bfloat16)


def prepare_kernel(pos_ref, inverse_ref, k_ref, v_ref, kv_ref, cos_ref, sin_ref):
    place = jnp.broadcast_to(pos_ref[...].astype(jnp.float32), (HEAD_SIZE, ROWS)).T
    cosine, sine = cos_and_sin(place * inverse_ref[...])
    lane = lax.broadcasted_iota(jnp.int32, (ROWS, HEAD_SIZE), 1)
    sine = jnp.where(lane < HEAD_SIZE // 2, -sine, sine)
    cos_ref[...] = cosine
    sin_ref[...] = sine
    for g in range(KV):
        kv_ref[g, 0] = rotated(k_ref[g], cosine, sine)
        kv_ref[g, 1] = v_ref[g]


def prepare(positions, inverse, k, v):
    payload = jax.ShapeDtypeStruct((KV, 2, ROWS, HEAD_SIZE), jnp.bfloat16)
    table = jax.ShapeDtypeStruct((ROWS, HEAD_SIZE), jnp.float32)
    return pl.pallas_call(
        prepare_kernel,
        in_specs=[VMEM] * 4,
        out_specs=[VMEM] * 3,
        out_shape=[payload, table, table],
        compiler_params=pltpu.CompilerParams(vmem_limit_bytes=8 * 1024 * 1024),
        name="prepare",
    )(positions, inverse, k, v)


def dot_nt(a, b):
    return lax.dot_general(a, b, (((1,), (1,)), ((), ())), preferred_element_type=jnp.float32)


def hold_kernel(first_ref, *refs):
    pass


def held(array, *others):
    hbm = pl.BlockSpec(memory_space=pltpu.HBM)
    others = [pltpu.with_memory_space_constraint(x, pltpu.VMEM) for x in others]
    return pl.pallas_call(
        hold_kernel,
        in_specs=[hbm] + [VMEM] * len(others),
        out_specs=hbm,
        out_shape=jax.ShapeDtypeStruct(array.shape, array.dtype),
        input_output_aliases={0: 0},
        compiler_params=pltpu.CompilerParams(vmem_limit_bytes=1024 * 1024),
        name="hold",
    )(array, *others)


def attend_kernel(g, place_ref, q_ref, cos_ref, sin_ref, own_ref, prev_ref, far_ref, *out_refs):
    place = place_ref[0]
    prev_bias = jnp.where(place >= 1, 0.0, LOW)
    far_bias = jnp.where(place >= 2, 0.0, LOW)
    c = SCALE * LOG2E
    cosine = cos_ref[...]
    sine = sin_ref[...]
    k_own, k_prev, k_far = own_ref[g, 0], prev_ref[g, 0], far_ref[g, 0]
    v_own = own_ref[g, 1].T
    v_prev = prev_ref[g, 1].T
    v_far = far_ref[g, 1].T
    row = lax.broadcasted_iota(jnp.int32, (QB, QB), 0)
    col = lax.broadcasted_iota(jnp.int32, (QB, QB), 1)
    seen = row <= col
    blocks = ROWS // QB
    for n in range(GROUP):
        head = g * GROUP + n
        q_all = rotated(q_ref[:, head * HEAD_SIZE : (head + 1) * HEAD_SIZE], cosine, sine)
        for b in range(blocks):
            q = q_all[b * QB : (b + 1) * QB]
            lo, hi = b * QB, (b + 1) * QB
            prev = dot_nt(k_prev, q)
            own = dot_nt(k_own[0:hi], q)
            far = dot_nt(k_far[lo:ROWS], q)
            mixed = jnp.where(seen, own[lo:hi], far[0:QB] + far_bias)
            top = jnp.maximum(
                jnp.max(prev, axis=0, keepdims=True) + prev_bias,
                jnp.max(mixed, axis=0, keepdims=True),
            )
            if lo > 0:
                top = jnp.maximum(top, jnp.max(own[0:lo], axis=0, keepdims=True))
            if hi < ROWS:
                top = jnp.maximum(top, jnp.max(far[QB:], axis=0, keepdims=True) + far_bias)
            top = top * c
            p_prev = jnp.exp2(prev * c - (top - prev_bias))
            p_mixed = jnp.exp2(mixed * c - top)
            total = jnp.sum(p_prev, axis=0, keepdims=True) + jnp.sum(p_mixed, axis=0, keepdims=True)
            own_parts = [jnp.where(seen, p_mixed, 0.0).astype(jnp.bfloat16)]
            far_parts = [jnp.where(seen, 0.0, p_mixed).astype(jnp.bfloat16)]
            if lo > 0:
                p = jnp.exp2(own[0:lo] * c - top)
                total = total + jnp.sum(p, axis=0, keepdims=True)
                own_parts.insert(0, p.astype(jnp.bfloat16))
            if hi < ROWS:
                p = jnp.exp2(far[QB:] * c - (top - far_bias))
                total = total + jnp.sum(p, axis=0, keepdims=True)
                far_parts.append(p.astype(jnp.bfloat16))
            context = jnp.dot(v_prev, p_prev.astype(jnp.bfloat16), preferred_element_type=jnp.float32)
            context += jnp.dot(
                v_own[:, 0:hi], jnp.concatenate(own_parts, 0), preferred_element_type=jnp.float32
            )
            context += jnp.dot(
                v_far[:, lo:], jnp.concatenate(far_parts, 0), preferred_element_type=jnp.float32
            )
            first = n * HEAD_SIZE % PIECE
            out_refs[n * HEAD_SIZE // PIECE][first : first + HEAD_SIZE, lo:hi] = (
                context / total
            ).astype(jnp.bfloat16)


def attend(g, place, *arrays):
    width = GROUP * HEAD_SIZE
    arrays = [pltpu.with_memory_space_constraint(x, pltpu.VMEM) for x in arrays]
    return pl.pallas_call(
        functools.partial(attend_kernel, g),
        in_specs=[pl.BlockSpec(memory_space=pltpu.SMEM)] + [VMEM] * len(arrays),
        out_specs=[VMEM] * (width // PIECE),
        out_shape=[jax.ShapeDtypeStruct((PIECE, ROWS), jnp.bfloat16)] * (width // PIECE),
        compiler_params=pltpu.CompilerParams(vmem_limit_bytes=20 * 1024 * 1024),
        name="attend",
    )(place, *arrays)


def project_kernel(order_ref, w_ref, *refs):
    ctx_refs = refs[: PIECES * N_HEAD]
    acc_ref, sq_ref, w_buffer, ctx_buffer, arrived = refs[PIECES * N_HEAD :]
    copies = []
    for k in range(N_HEAD):
        copies.append(
            [pltpu.make_async_copy(w_ref.at[order_ref[k]], w_buffer.at[k], arrived.at[k, PIECES])]
            + [
                pltpu.make_async_copy(
                    ctx_refs[k * PIECES + g],
                    ctx_buffer.at[k, g * PIECE : (g + 1) * PIECE],
                    arrived.at[k, g],
                )
                for g in range(PIECES)
            ]
        )
        for copy in copies[k]:
            copy.start()
    for k in range(N_HEAD):
        for copy in copies[k]:
            copy.wait()
        value = jnp.dot(w_buffer[k], ctx_buffer[k], preferred_element_type=jnp.float32)
        if k > 0:
            value = acc_ref[...] + value
        acc_ref[...] = value
        if k == N_HEAD - 1:
            sq_ref[...] = jnp.sum(value * value, axis=0, keepdims=True)


def project(order, weights, blocks):
    hbm = pl.BlockSpec(memory_space=pltpu.HBM)
    weights = pltpu.with_memory_space_constraint(weights, pltpu.HBM)
    blocks = [pltpu.with_memory_space_constraint(x, pltpu.HBM) for x in blocks]
    return pl.pallas_call(
        project_kernel,
        in_specs=[pl.BlockSpec(memory_space=pltpu.SMEM), hbm] + [hbm] * (PIECES * N_HEAD),
        out_specs=[VMEM, VMEM],
        out_shape=[
            jax.ShapeDtypeStruct((FEATURES, ROWS), jnp.float32),
            jax.ShapeDtypeStruct((1, ROWS), jnp.float32),
        ],
        scratch_shapes=[
            pltpu.VMEM((N_HEAD, FEATURES, WIDTH), jnp.bfloat16),
            pltpu.VMEM((N_HEAD, WIDTH, ROWS), jnp.bfloat16),
            pltpu.SemaphoreType.DMA((N_HEAD, PIECES + 1)),
        ],
        compiler_params=pltpu.CompilerParams(vmem_limit_bytes=24 * 1024 * 1024),
        name="project",
    )(order, weights, *blocks)


def finish_kernel(acc_ref, sq_ref, gain_ref, res_ref, out_ref):
    squares = jnp.sum(sq_ref[...], axis=0)
    scale = lax.rsqrt(squares / D + EPS)
    value = res_ref[...].astype(jnp.float32) + gain_ref[...] * (acc_ref[...] * scale)
    out_ref[...] = value.astype(jnp.bfloat16)


def finish(attended, squares, gain, residual):
    return pl.pallas_call(
        finish_kernel,
        in_specs=[VMEM] * 4,
        out_shape=jax.ShapeDtypeStruct((FEATURES, ROWS), jnp.bfloat16),
        compiler_params=pltpu.CompilerParams(vmem_limit_bytes=12 * 1024 * 1024),
        name="finish",
    )(attended, squares, gain, residual)


def for_everyone(array, axis):
    length = lax.axis_size(axis)
    return lax.all_to_all(
        jnp.broadcast_to(array[None], (length, *array.shape)), axis, 0, 0, tiled=True
    )


def on_device(positions, queries, keys, values, out_weight, post_gain, residual):
    seq = lax.axis_index("seq")
    head = lax.axis_index("head")
    spread = [
        (s * N_HEAD + h, ((s // 4 + h) % N_HEAD * 4 + s % 4) * N_HEAD + s // 4)
        for s in range(N_SEQ)
        for h in range(N_HEAD)
    ]
    shard = lax.ppermute(out_weight.T, ("seq", "head"), spread)

    half = HEAD_SIZE // 2
    inverse = 10000.0 ** (-2.0 * jnp.arange(half, dtype=jnp.float32) / HEAD_SIZE)
    inverse = jnp.concatenate([inverse, inverse])[None]
    own, cosine, sine = prepare(
        positions[None], inverse, keys.transpose(1, 0, 2), values.transpose(1, 0, 2)
    )
    onward = [(i, i + 1) for i in range(N_SEQ - 1)]
    beyond = [(i, i + 2) for i in range(N_SEQ - 2)]
    prev = lax.ppermute(own, "seq", onward)
    far = lax.ppermute(own, "seq", beyond)
    shard = held(shard, prev, far)
    weights = lax.all_gather(shard, "seq", axis=0).reshape(N_HEAD, FEATURES, WIDTH)
    place = seq.astype(jnp.int32).reshape(1)
    q = queries.reshape(ROWS, WIDTH)

    ring = [
        (s * N_HEAD + h, s * N_HEAD + (h + (1 if s % 2 == 0 else -1)) % N_HEAD)
        for s in range(N_SEQ)
        for h in range(N_HEAD)
    ]
    blocks = [[] for _ in range(N_HEAD)]
    for g in range(KV):
        pieces = attend(g, place, q, cosine, sine, own, prev, far)
        for carried in pieces:
            blocks[0].append(carried)
            for k in range(1, N_HEAD):
                carried = lax.ppermute(carried, ("seq", "head"), ring)
                blocks[k].append(carried)
    sign = jnp.where(seq % 2 == 0, -1, 1)
    source = head + sign * jnp.arange(N_HEAD, dtype=jnp.int32)
    order = ((source + head) % N_HEAD).astype(jnp.int32)
    attended, squares = project(order, weights, [x for row in blocks for x in row])
    squares = for_everyone(squares, "head")
    return finish(attended, squares, post_gain[:, None], residual.T).T


def solution(mesh):
    return jax.shard_map(
        on_device,
        mesh=mesh,
        in_specs=(
            P("seq"),
            P("seq", "head", None),
            P("seq", "head", None),
            P("seq", "head", None),
            P("head", "seq"),
            P("head"),
            P("seq", "head"),
        ),
        out_specs=P("seq", "head"),
        check_vma=False,
    )
```

time: 154 us -> 129 us (0.84)
  the two profiles are of different devices: /device:TPU:4 before, /device:TPU:6 now
where the time goes in v4:
time: 129 us; the launch traced here: 128 us
  waiting for transfers between devices  55.9 us (43%)
  starting transfers between devices  42 us (33%)
  between operations  13.7 us (11%)
  Pallas kernels  13 us (10%)
  local copies, waits for them, and re-layouts  3.76 us (3%)
    ppermute x28, waiting for transfers between devices, on_device(): carried = lax.ppermute(carried, ('seq', 'head'), ring)  33.3 us
    ppermute x28, starting transfers between devices, on_device(): carried = lax.ppermute(carried, ('seq', 'head'), ring)  23.9 us
    ppermute x1, waiting for transfers between devices, on_device(): shard = lax.ppermute(out_weight.T, ('seq', 'head'), spread)  14.9 us
    ppermute x1, starting transfers between devices, on_device(): shard = lax.ppermute(out_weight.T, ('seq', 'head'), spread)  8.21 us
    all_to_all x1, waiting for transfers between devices, for_everyone(): lax.all_to_all(jnp.broadcast_to(array[None], (length, *array.shape)), axi...  7.62 us
    pallas_call x2, Pallas kernels, attend(): pl.pallas_call(functools.partial(attend_kernel, g), in_specs=[pl.BlockSpe...  5.71 us
    pallas_call x1, Pallas kernels, project(): pl.pallas_call(project_kernel, in_specs=[pl.BlockSpec(memory_space=pltpu....  5.61 us
    all_to_all x1, starting transfers between devices, for_everyone(): lax.all_to_all(jnp.broadcast_to(array[None], (length, *array.shape)), axi...  4.44 us
  transfers between devices with their start and end apart: 33, of which 25 were waited for; matrix products, arithmetic and copies ran while one was open for 1% of the time, Pallas kernels for 4%

profile of v4, /device:TPU:6, one launch (start us, length us, event | category | flops | bytes accessed | tf_op | source)
XLA Modules:
  0.0 128.5 jit_solution(11757907361430249709)
XLA Ops:
  9.0 1.9 %collective-permute-start.1 = (bf16[2,2,512,128]{3,2,1,0:T(8,128)(2,1)S(1)}, bf16[2,2,512,128]{3,2,1,0:T(8,128)(2,1)S(1)}, u32[]{:S(2)}, u32[]{:S(2)}) collective-permute-start(bf16[2,2,512,128]{3,2,1,0:T(8,128)(2,1)S(1)} %get-tuple-element.14.own_ref), channel_id=1, source_target_pairs={{0,8},{8,16},{16,24},{24,32},{32,40},{40,48},{48,56},{56,64},{64,7... | collective-permute-start | bytes 1572872 | tf_op jit(solution)/shard_map/ppermute | solution.py:269
  10.9 3.5 %collective-permute-start.2 = (bf16[2,2,512,128]{3,2,1,0:T(8,128)(2,1)S(1)}, bf16[2,2,512,128]{3,2,1,0:T(8,128)(2,1)S(1)}, u32[]{:S(2)}, u32[]{:S(2)}) collective-permute-start(bf16[2,2,512,128]{3,2,1,0:T(8,128)(2,1)S(1)} %get-tuple-element.14.own_ref), channel_id=1, source_target_pairs={{0,16},{8,24},{16,32},{24,40},{32,48},{40,56},{48,64},{56,72},{64,... | collective-permute-start | bytes 1572872 | tf_op jit(solution)/shard_map/ppermute | solution.py:270
  14.4 8.2 %collective-permute-start = (bf16[168,512]{1,0:T(8,128)(2,1)}, bf16[168,512]{1,0:T(8,128)(2,1)}, u32[]{:S(2)}, u32[]{:S(2)}) collective-permute-start(bf16[168,512]{1,0:T(8,128)(2,1)} %bitcast.24), channel_id=1, source_target_pairs={{0,0},{1,32},{2,64},{3,96},{4,128},{5,160},{6,192},{7,224},{8,8},{... | collective-permute-start | bytes 516104 | tf_op jit(solution)/shard_map/ppermute | solution.py:259
  22.6 14.9 %collective-permute-done.first_ref = bf16[168,512]{1,0:T(8,128)(2,1)} collective-permute-done((bf16[168,512]{1,0:T(8,128)(2,1)}, bf16[168,512]{1,0:T(8,128)(2,1)}, u32[]{:S(2)}, u32[]{:S(2)}) %collective-permute-start) | collective-permute-done | bytes 172064 | tf_op jit(solution)/shard_map/ppermute | solution.py:259
  38.7 2.9 %attend.3 = (bf16[128,512]{1,0:T(8,128)(2,1)S(1)}, bf16[128,512]{1,0:T(8,128)(2,1)S(1)}) custom-call(s32[1]{0:T(128)} %bitcast.6.place_ref, bf16[512,512]{1,0:T(8,128)(2,1)S(1)} %bitcast.17, f32[512,128]{1,0:T(8,128)S(1)} %get-tuple-element.15.cos_ref, f32[512,128]{1,0:T(8,128)S(1)} %get-tuple-element.16.sin_ref, ...), custom_call_target="tpu_custom_call" | custom-call | tf_op jit(solution)/shard_map/attend/pallas_call | solution.py:166
  42.9 2.9 %attend.2 = (bf16[128,512]{1,0:T(8,128)(2,1)S(1)}, bf16[128,512]{1,0:T(8,128)(2,1)S(1)}) custom-call(s32[1]{0:T(128)} %bitcast.6.place_ref, bf16[512,512]{1,0:T(8,128)(2,1)S(1)} %bitcast.18, f32[512,128]{1,0:T(8,128)S(1)} %get-tuple-element.15.cos_ref, f32[512,128]{1,0:T(8,128)S(1)} %get-tuple-element.16.sin_ref, ...), custom_call_target="tpu_custom_call" | custom-call | tf_op jit(solution)/shard_map/attend/pallas_call | solution.py:166
  46.3 4.2 %collective-permute-start.4 = (bf16[128,512]{1,0:T(8,128)(2,1)S(1)}, bf16[128,512]{1,0:T(8,128)(2,1)S(1)}, u32[]{:S(2)}, u32[]{:S(2)}) collective-permute-start(bf16[128,512]{1,0:T(8,128)(2,1)S(1)} %get-tuple-element.18.refs_1_), channel_id=1, source_target_pairs={{0,1},{1,2},{2,3},{3,4},{4,5},{5,6},{6,7},{7,0},{8,15},{9,8},{10,9... | collective-permute-start | bytes 393224 | tf_op jit(solution)/shard_map/ppermute | solution.py:287
  50.5 11.0 %collective-permute-start.9 = (bf16[128,512]{1,0:T(8,128)(2,1)S(1)}, bf16[128,512]{1,0:T(8,128)(2,1)S(1)}, u32[]{:S(2)}, u32[]{:S(2)}) collective-permute-start(bf16[128,512]{1,0:T(8,128)(2,1)S(1)} %collective-permute-done.5.refs_6_), channel_id=1, source_target_pairs={{0,1},{1,2},{2,3},{3,4},{4,5},{5,6},{6,7},{7,0},{8,15},{9,8},{10,9... | collective-permute-start | bytes 393224 | tf_op jit(solution)/shard_map/ppermute | solution.py:287
  61.8 2.3 %collective-permute-start.8 = (bf16[128,512]{1,0:T(8,128)(2,1)S(1)}, bf16[128,512]{1,0:T(8,128)(2,1)S(1)}, u32[]{:S(2)}, u32[]{:S(2)}) collective-permute-start(bf16[128,512]{1,0:T(8,128)(2,1)S(1)} %collective-permute-done.4.refs_5_), channel_id=1, source_target_pairs={{0,1},{1,2},{2,3},{3,4},{4,5},{5,6},{6,7},{7,0},{8,15},{9,8},{10,9... | collective-permute-start | bytes 393224 | tf_op jit(solution)/shard_map/ppermute | solution.py:287
  64.1 2.4 %collective-permute-start.13 = (bf16[128,512]{1,0:T(8,128)(2,1)S(1)}, bf16[128,512]{1,0:T(8,128)(2,1)S(1)}, u32[]{:S(2)}, u32[]{:S(2)}) collective-permute-start(bf16[128,512]{1,0:T(8,128)(2,1)S(1)} %collective-permute-done.9.refs_10_), channel_id=1, source_target_pairs={{0,1},{1,2},{2,3},{3,4},{4,5},{5,6},{6,7},{7,0},{8,15},{9,8},{10,9... | collective-permute-start | bytes 393224 | tf_op jit(solution)/shard_map/ppermute | solution.py:287
  72.1 1.8 %collective-permute-done.14.refs_15_ = bf16[128,512]{1,0:T(8,128)(2,1)S(1)} collective-permute-done((bf16[128,512]{1,0:T(8,128)(2,1)S(1)}, bf16[128,512]{1,0:T(8,128)(2,1)S(1)}, u32[]{:S(2)}, u32[]{:S(2)}) %collective-permute-start.14) | collective-permute-done | bytes 131104 | tf_op jit(solution)/shard_map/ppermute | solution.py:287
  78.2 1.9 %collective-permute-done.18.refs_19_ = bf16[128,512]{1,0:T(8,128)(2,1)S(1)} collective-permute-done((bf16[128,512]{1,0:T(8,128)(2,1)S(1)}, bf16[128,512]{1,0:T(8,128)(2,1)S(1)}, u32[]{:S(2)}, u32[]{:S(2)}) %collective-permute-start.18) | collective-permute-done | bytes 131104 | tf_op jit(solution)/shard_map/ppermute | solution.py:287
  84.4 1.9 %collective-permute-done.22.refs_23_ = bf16[128,512]{1,0:T(8,128)(2,1)S(1)} collective-permute-done((bf16[128,512]{1,0:T(8,128)(2,1)S(1)}, bf16[128,512]{1,0:T(8,128)(2,1)S(1)}, u32[]{:S(2)}, u32[]{:S(2)}) %collective-permute-start.22) | collective-permute-done | bytes 131104 | tf_op jit(solution)/shard_map/ppermute | solution.py:287
  89.2 1.4 %collective-permute-done.25.refs_26_ = bf16[128,512]{1,0:T(8,128)(2,1)} collective-permute-done((bf16[128,512]{1,0:T(8,128)(2,1)S(1)}, bf16[128,512]{1,0:T(8,128)(2,1)}, u32[]{:S(2)}, u32[]{:S(2)}) %collective-permute-start.25) | collective-permute-done | bytes 131104 | tf_op jit(solution)/shard_map/ppermute | solution.py:287
  90.6 2.0 %collective-permute-done.26.refs_27_ = bf16[128,512]{1,0:T(8,128)(2,1)} collective-permute-done((bf16[128,512]{1,0:T(8,128)(2,1)S(1)}, bf16[128,512]{1,0:T(8,128)(2,1)}, u32[]{:S(2)}, u32[]{:S(2)}) %collective-permute-start.26) | collective-permute-done | bytes 131104 | tf_op jit(solution)/shard_map/ppermute | solution.py:287
  92.6 1.4 %collective-permute-done.23.refs_24_ = bf16[128,512]{1,0:T(8,128)(2,1)} collective-permute-done((bf16[128,512]{1,0:T(8,128)(2,1)S(1)}, bf16[128,512]{1,0:T(8,128)(2,1)}, u32[]{:S(2)}, u32[]{:S(2)}) %collective-permute-start.23) | collective-permute-done | bytes 131104 | tf_op jit(solution)/shard_map/ppermute | solution.py:287
  94.0 1.4 %collective-permute-done.24.refs_25_ = bf16[128,512]{1,0:T(8,128)(2,1)} collective-permute-done((bf16[128,512]{1,0:T(8,128)(2,1)S(1)}, bf16[128,512]{1,0:T(8,128)(2,1)}, u32[]{:S(2)}, u32[]{:S(2)}) %collective-permute-start.24) | collective-permute-done | bytes 131104 | tf_op jit(solution)/shard_map/ppermute | solution.py:287
  95.5 1.6 %collective-permute-done.29.refs_30_ = bf16[128,512]{1,0:T(8,128)(2,1)} collective-permute-done((bf16[128,512]{1,0:T(8,128)(2,1)}, bf16[128,512]{1,0:T(8,128)(2,1)}, u32[]{:S(2)}, u32[]{:S(2)}) %collective-permute-start.29) | collective-permute-done | bytes 131104 | tf_op jit(solution)/shard_map/ppermute | solution.py:287
  97.1 2.0 %collective-permute-done.30.refs_31_ = bf16[128,512]{1,0:T(8,128)(2,1)} collective-permute-done((bf16[128,512]{1,0:T(8,128)(2,1)}, bf16[128,512]{1,0:T(8,128)(2,1)}, u32[]{:S(2)}, u32[]{:S(2)}) %collective-permute-start.30) | collective-permute-done | bytes 131104 | tf_op jit(solution)/shard_map/ppermute | solution.py:287
  99.1 1.4 %collective-permute-done.27.refs_28_ = bf16[128,512]{1,0:T(8,128)(2,1)} collective-permute-done((bf16[128,512]{1,0:T(8,128)(2,1)}, bf16[128,512]{1,0:T(8,128)(2,1)}, u32[]{:S(2)}, u32[]{:S(2)}) %collective-permute-start.27) | collective-permute-done | bytes 131104 | tf_op jit(solution)/shard_map/ppermute | solution.py:287
  100.5 1.4 %collective-permute-done.28.refs_29_ = bf16[128,512]{1,0:T(8,128)(2,1)} collective-permute-done((bf16[128,512]{1,0:T(8,128)(2,1)}, bf16[128,512]{1,0:T(8,128)(2,1)}, u32[]{:S(2)}, u32[]{:S(2)}) %collective-permute-start.28) | collective-permute-done | bytes 131104 | tf_op jit(solution)/shard_map/ppermute | solution.py:287
  102.1 5.6 %project.1 = (f32[672,512]{1,0:T(8,128)S(1)}, f32[1,512]{1,0:T(1,128)S(1)}) custom-call(s32[8]{0:T(128)S(1)} %and_select_fusion.order_ref, bf16[8,672,512]{2,1,0:T(8,128)(2,1)} %bitcast.22, bf16[128,512]{1,0:T(8,128)(2,1)} %copy-done.3, bf16[128,512]{1,0:T(8,128)(2,1)} %copy-done.4, bf16[128,512]{1,0:T(8,128)(2,1)} %copy-done.1, bf16[128,512]{1,0:T(8,128)(2,1)} %copy-done.2, ...), custom_call_target="tpu_custom_call" | custom-call | tf_op jit(solution)/shard_map/project/pallas_call | solution.py:209
  108.3 4.4 %all-to-all-start = ((f32[8,1,512]{2,1,0:T(1,128)}), f32[8,1,512]{2,1,0:T(1,128)S(1)}, u32[]{:S(2)}, u32[]{:S(2)}) async-start(f32[8,1,512]{2,1,0:T(1,128)} %broadcast_in_dim.20), calls=%async_computation | async-start | bytes 32768 | tf_op jit(solution)/shard_map/all_to_all | solution.py:246
  112.9 7.6 %all-to-all-done.sq_ref = f32[8,1,512]{2,1,0:T(1,128)S(1)} async-done(((f32[8,1,512]{2,1,0:T(1,128)}), f32[8,1,512]{2,1,0:T(1,128)S(1)}, u32[]{:S(2)}, u32[]{:S(2)}) %all-to-all-start) | async-done | bytes 16416 | tf_op jit(solution)/shard_map/all_to_all | solution.py:246
  (110 shorter events, 24.8 us)
Async XLA Ops:
  6.5 95.3 %all-gather.3.cloned.1.call-start = ((), (), s32[]{:S(2)}) async-start(), calls=%async_computation.1 | async-start | bytes 5677056 | tf_op jit(solution)/shard_map/all_gather | solution.py:272
  9.0 28.6 %collective-permute-start.1 = (bf16[2,2,512,128]{3,2,1,0:T(8,128)(2,1)S(1)}, bf16[2,2,512,128]{3,2,1,0:T(8,128)(2,1)S(1)}, u32[]{:S(2)}, u32[]{:S(2)}) collective-permute-start(bf16[2,2,512,128]{3,2,1,0:T(8,128)(2,1)S(1)} %get-tuple-element.14.own_ref), channel_id=1, source_target_pairs={{0,8},{8,16},{16,24},{24,32},{32,40},{40,48},{48,56},{56,64},{64,7... | collective-permute-start | bytes 1572872 | tf_op jit(solution)/shard_map/ppermute | solution.py:269
  10.9 26.7 %collective-permute-start.2 = (bf16[2,2,512,128]{3,2,1,0:T(8,128)(2,1)S(1)}, bf16[2,2,512,128]{3,2,1,0:T(8,128)(2,1)S(1)}, u32[]{:S(2)}, u32[]{:S(2)}) collective-permute-start(bf16[2,2,512,128]{3,2,1,0:T(8,128)(2,1)S(1)} %get-tuple-element.14.own_ref), channel_id=1, source_target_pairs={{0,16},{8,24},{16,32},{24,40},{32,48},{40,56},{48,64},{56,72},{64,... | collective-permute-start | bytes 1572872 | tf_op jit(solution)/shard_map/ppermute | solution.py:270
  14.4 23.2 %collective-permute-start = (bf16[168,512]{1,0:T(8,128)(2,1)}, bf16[168,512]{1,0:T(8,128)(2,1)}, u32[]{:S(2)}, u32[]{:S(2)}) collective-permute-start(bf16[168,512]{1,0:T(8,128)(2,1)} %bitcast.24), channel_id=1, source_target_pairs={{0,0},{1,32},{2,64},{3,96},{4,128},{5,160},{6,192},{7,224},{8,8},{... | collective-permute-start | bytes 516104 | tf_op jit(solution)/shard_map/ppermute | solution.py:259
  41.6 8.9 %collective-permute-start.5 = (bf16[128,512]{1,0:T(8,128)(2,1)S(1)}, bf16[128,512]{1,0:T(8,128)(2,1)S(1)}, u32[]{:S(2)}, u32[]{:S(2)}) collective-permute-start(bf16[128,512]{1,0:T(8,128)(2,1)S(1)} %get-tuple-element.19.refs_2_), channel_id=1, source_target_pairs={{0,1},{1,2},{2,3},{3,4},{4,5},{5,6},{6,7},{7,0},{8,15},{9,8},{10,9... | collective-permute-start | bytes 393224 | tf_op jit(solution)/shard_map/ppermute | solution.py:287
  41.7 19.8 %collective-permute-start.6 = (bf16[128,512]{1,0:T(8,128)(2,1)S(1)}, bf16[128,512]{1,0:T(8,128)(2,1)S(1)}, u32[]{:S(2)}, u32[]{:S(2)}) collective-permute-start(bf16[128,512]{1,0:T(8,128)(2,1)S(1)} %get-tuple-element.20.refs_3_), channel_id=1, source_target_pairs={{0,1},{1,2},{2,3},{3,4},{4,5},{5,6},{6,7},{7,0},{8,15},{9,8},{10,9... | collective-permute-start | bytes 393224 | tf_op jit(solution)/shard_map/ppermute | solution.py:287
  45.8 15.8 %collective-permute-start.3 = (bf16[128,512]{1,0:T(8,128)(2,1)S(1)}, bf16[128,512]{1,0:T(8,128)(2,1)S(1)}, u32[]{:S(2)}, u32[]{:S(2)}) collective-permute-start(bf16[128,512]{1,0:T(8,128)(2,1)S(1)} %get-tuple-element.17.refs_0_), channel_id=1, source_target_pairs={{0,1},{1,2},{2,3},{3,4},{4,5},{5,6},{6,7},{7,0},{8,15},{9,8},{10,9... | collective-permute-start | bytes 393224 | tf_op jit(solution)/shard_map/ppermute | solution.py:287
  46.3 15.4 %collective-permute-start.4 = (bf16[128,512]{1,0:T(8,128)(2,1)S(1)}, bf16[128,512]{1,0:T(8,128)(2,1)S(1)}, u32[]{:S(2)}, u32[]{:S(2)}) collective-permute-start(bf16[128,512]{1,0:T(8,128)(2,1)S(1)} %get-tuple-element.18.refs_1_), channel_id=1, source_target_pairs={{0,1},{1,2},{2,3},{3,4},{4,5},{5,6},{6,7},{7,0},{8,15},{9,8},{10,9... | collective-permute-start | bytes 393224 | tf_op jit(solution)/shard_map/ppermute | solution.py:287
  50.5 13.6 %collective-permute-start.9 = (bf16[128,512]{1,0:T(8,128)(2,1)S(1)}, bf16[128,512]{1,0:T(8,128)(2,1)S(1)}, u32[]{:S(2)}, u32[]{:S(2)}) collective-permute-start(bf16[128,512]{1,0:T(8,128)(2,1)S(1)} %collective-permute-done.5.refs_6_), channel_id=1, source_target_pairs={{0,1},{1,2},{2,3},{3,4},{4,5},{5,6},{6,7},{7,0},{8,15},{9,8},{10,9... | collective-permute-start | bytes 393224 | tf_op jit(solution)/shard_map/ppermute | solution.py:287
  61.6 6.2 %collective-permute-start.10 = (bf16[128,512]{1,0:T(8,128)(2,1)S(1)}, bf16[128,512]{1,0:T(8,128)(2,1)S(1)}, u32[]{:S(2)}, u32[]{:S(2)}) collective-permute-start(bf16[128,512]{1,0:T(8,128)(2,1)S(1)} %collective-permute-done.6.refs_7_), channel_id=1, source_target_pairs={{0,1},{1,2},{2,3},{3,4},{4,5},{5,6},{6,7},{7,0},{8,15},{9,8},{10,9... | collective-permute-start | bytes 393224 | tf_op jit(solution)/shard_map/ppermute | solution.py:287
  61.7 7.5 %collective-permute-start.7 = (bf16[128,512]{1,0:T(8,128)(2,1)S(1)}, bf16[128,512]{1,0:T(8,128)(2,1)S(1)}, u32[]{:S(2)}, u32[]{:S(2)}) collective-permute-start(bf16[128,512]{1,0:T(8,128)(2,1)S(1)} %collective-permute-done.3.refs_4_), channel_id=1, source_target_pairs={{0,1},{1,2},{2,3},{3,4},{4,5},{5,6},{6,7},{7,0},{8,15},{9,8},{10,9... | collective-permute-start | bytes 393224 | tf_op jit(solution)/shard_map/ppermute | solution.py:287
  61.8 8.8 %collective-permute-start.8 = (bf16[128,512]{1,0:T(8,128)(2,1)S(1)}, bf16[128,512]{1,0:T(8,128)(2,1)S(1)}, u32[]{:S(2)}, u32[]{:S(2)}) collective-permute-start(bf16[128,512]{1,0:T(8,128)(2,1)S(1)} %collective-permute-done.4.refs_5_), channel_id=1, source_target_pairs={{0,1},{1,2},{2,3},{3,4},{4,5},{5,6},{6,7},{7,0},{8,15},{9,8},{10,9... | collective-permute-start | bytes 393224 | tf_op jit(solution)/shard_map/ppermute | solution.py:287
  64.1 7.9 %collective-permute-start.13 = (bf16[128,512]{1,0:T(8,128)(2,1)S(1)}, bf16[128,512]{1,0:T(8,128)(2,1)S(1)}, u32[]{:S(2)}, u32[]{:S(2)}) collective-permute-start(bf16[128,512]{1,0:T(8,128)(2,1)S(1)} %collective-permute-done.9.refs_10_), channel_id=1, source_target_pairs={{0,1},{1,2},{2,3},{3,4},{4,5},{5,6},{6,7},{7,0},{8,15},{9,8},{10,9... | collective-permute-start | bytes 393224 | tf_op jit(solution)/shard_map/ppermute | solution.py:287
  73.9 6.2 %collective-permute-start.18 = (bf16[128,512]{1,0:T(8,128)(2,1)S(1)}, bf16[128,512]{1,0:T(8,128)(2,1)S(1)}, u32[]{:S(2)}, u32[]{:S(2)}) collective-permute-start(bf16[128,512]{1,0:T(8,128)(2,1)S(1)} %collective-permute-done.14.refs_15_), channel_id=1, source_target_pairs={{0,1},{1,2},{2,3},{3,4},{4,5},{5,6},{6,7},{7,0},{8,15},{9,8},{10,9... | collective-permute-start | bytes 393224 | tf_op jit(solution)/shard_map/ppermute | solution.py:287
  82.9 6.2 %collective-permute-start.20 = (bf16[128,512]{1,0:T(8,128)(2,1)S(1)}, bf16[128,512]{1,0:T(8,128)(2,1)S(1)}, u32[]{:S(2)}, u32[]{:S(2)}) collective-permute-start(bf16[128,512]{1,0:T(8,128)(2,1)S(1)} %collective-permute-done.16.refs_17_), channel_id=1, source_target_pairs={{0,1},{1,2},{2,3},{3,4},{4,5},{5,6},{6,7},{7,0},{8,15},{9,8},{10,9... | collective-permute-start | bytes 393224 | tf_op jit(solution)/shard_map/ppermute | solution.py:287
  84.3 6.3 %collective-permute-start.25 = (bf16[128,512]{1,0:T(8,128)(2,1)S(1)}, bf16[128,512]{1,0:T(8,128)(2,1)}, u32[]{:S(2)}, u32[]{:S(2)}) collective-permute-start(bf16[128,512]{1,0:T(8,128)(2,1)S(1)} %collective-permute-done.21.refs_22_), channel_id=1, source_target_pairs={{0,1},{1,2},{2,3},{3,4},{4,5},{5,6},{6,7},{7,0},{8,15},{9,8},{10,9... | collective-permute-start | bytes 393224 | tf_op jit(solution)/shard_map/ppermute | solution.py:287
  86.3 6.3 %collective-permute-start.26 = (bf16[128,512]{1,0:T(8,128)(2,1)S(1)}, bf16[128,512]{1,0:T(8,128)(2,1)}, u32[]{:S(2)}, u32[]{:S(2)}) collective-permute-start(bf16[128,512]{1,0:T(8,128)(2,1)S(1)} %collective-permute-done.22.refs_23_), channel_id=1, source_target_pairs={{0,1},{1,2},{2,3},{3,4},{4,5},{5,6},{6,7},{7,0},{8,15},{9,8},{10,9... | collective-permute-start | bytes 393224 | tf_op jit(solution)/shard_map/ppermute | solution.py:287
  87.7 6.3 %collective-permute-start.23 = (bf16[128,512]{1,0:T(8,128)(2,1)S(1)}, bf16[128,512]{1,0:T(8,128)(2,1)}, u32[]{:S(2)}, u32[]{:S(2)}) collective-permute-start(bf16[128,512]{1,0:T(8,128)(2,1)S(1)} %collective-permute-done.19.refs_20_), channel_id=1, source_target_pairs={{0,1},{1,2},{2,3},{3,4},{4,5},{5,6},{6,7},{7,0},{8,15},{9,8},{10,9... | collective-permute-start | bytes 393224 | tf_op jit(solution)/shard_map/ppermute | solution.py:287
  89.1 6.3 %collective-permute-start.24 = (bf16[128,512]{1,0:T(8,128)(2,1)S(1)}, bf16[128,512]{1,0:T(8,128)(2,1)}, u32[]{:S(2)}, u32[]{:S(2)}) collective-permute-start(bf16[128,512]{1,0:T(8,128)(2,1)S(1)} %collective-permute-done.20.refs_21_), channel_id=1, source_target_pairs={{0,1},{1,2},{2,3},{3,4},{4,5},{5,6},{6,7},{7,0},{8,15},{9,8},{10,9... | collective-permute-start | bytes 393224 | tf_op jit(solution)/shard_map/ppermute | solution.py:287
  90.6 6.5 %collective-permute-start.29 = (bf16[128,512]{1,0:T(8,128)(2,1)}, bf16[128,512]{1,0:T(8,128)(2,1)}, u32[]{:S(2)}, u32[]{:S(2)}) collective-permute-start(bf16[128,512]{1,0:T(8,128)(2,1)} %collective-permute-done.25.refs_26_), channel_id=1, source_target_pairs={{0,1},{1,2},{2,3},{3,4},{4,5},{5,6},{6,7},{7,0},{8,15},{9,8},{10,9... | collective-permute-start | bytes 393224 | tf_op jit(solution)/shard_map/ppermute | solution.py:287
  92.6 6.5 %collective-permute-start.30 = (bf16[128,512]{1,0:T(8,128)(2,1)}, bf16[128,512]{1,0:T(8,128)(2,1)}, u32[]{:S(2)}, u32[]{:S(2)}) collective-permute-start(bf16[128,512]{1,0:T(8,128)(2,1)} %collective-permute-done.26.refs_27_), channel_id=1, source_target_pairs={{0,1},{1,2},{2,3},{3,4},{4,5},{5,6},{6,7},{7,0},{8,15},{9,8},{10,9... | collective-permute-start | bytes 393224 | tf_op jit(solution)/shard_map/ppermute | solution.py:287
  94.0 6.5 %collective-permute-start.27 = (bf16[128,512]{1,0:T(8,128)(2,1)}, bf16[128,512]{1,0:T(8,128)(2,1)}, u32[]{:S(2)}, u32[]{:S(2)}) collective-permute-start(bf16[128,512]{1,0:T(8,128)(2,1)} %collective-permute-done.23.refs_24_), channel_id=1, source_target_pairs={{0,1},{1,2},{2,3},{3,4},{4,5},{5,6},{6,7},{7,0},{8,15},{9,8},{10,9... | collective-permute-start | bytes 393224 | tf_op jit(solution)/shard_map/ppermute | solution.py:287
  95.4 6.5 %collective-permute-start.28 = (bf16[128,512]{1,0:T(8,128)(2,1)}, bf16[128,512]{1,0:T(8,128)(2,1)}, u32[]{:S(2)}, u32[]{:S(2)}) collective-permute-start(bf16[128,512]{1,0:T(8,128)(2,1)} %collective-permute-done.24.refs_25_), channel_id=1, source_target_pairs={{0,1},{1,2},{2,3},{3,4},{4,5},{5,6},{6,7},{7,0},{8,15},{9,8},{10,9... | collective-permute-start | bytes 393224 | tf_op jit(solution)/shard_map/ppermute | solution.py:287
  108.3 12.2 %all-to-all-start = ((f32[8,1,512]{2,1,0:T(1,128)}), f32[8,1,512]{2,1,0:T(1,128)S(1)}, u32[]{:S(2)}, u32[]{:S(2)}) async-start(f32[8,1,512]{2,1,0:T(1,128)} %broadcast_in_dim.20), calls=%async_computation | async-start | bytes 32768 | tf_op jit(solution)/shard_map/all_to_all | solution.py:246
  (36 other events, 966.4 us)
Sparse Core Ops, SparseCore 0:
  37.7 61.3 all-gather.2

commit v5 on v4

--- a/solution.py
+++ b/solution.py
@@ -78,6 +78,23 @@
     )(positions, inverse, k, v)
 
 
+def rotate_kernel(q_ref, cos_ref, sin_ref, out_ref):
+    for n in range(KV * GROUP):
+        part = slice(n * HEAD_SIZE, (n + 1) * HEAD_SIZE)
+        out_ref[:, part] = rotated(q_ref[:, part], cos_ref[...], sin_ref[...])
+
+
+def rotate(q, cosine, sine):
+    return pl.pallas_call(
+        rotate_kernel,
+        in_specs=[VMEM] * 3,
+        out_specs=VMEM,
+        out_shape=jax.ShapeDtypeStruct(q.shape, q.dtype),
+        compiler_params=pltpu.CompilerParams(vmem_limit_bytes=4 * 1024 * 1024),
+        name="rotate",
+    )(q, cosine, sine)
+
+
 def dot_nt(a, b):
     return lax.dot_general(a, b, (((1,), (1,)), ((), ())), preferred_element_type=jnp.float32)
 
@@ -100,13 +117,12 @@
     )(array, *others)
 
 
-def attend_kernel(g, place_ref, q_ref, cos_ref, sin_ref, own_ref, prev_ref, far_ref, *out_refs):
+def attend_kernel(n, place_ref, q_ref, own_ref, prev_ref, far_ref, out_ref):
+    g = n // GROUP
     place = place_ref[0]
     prev_bias = jnp.where(place >= 1, 0.0, LOW)
     far_bias = jnp.where(place >= 2, 0.0, LOW)
     c = SCALE * LOG2E
-    cosine = cos_ref[...]
-    sine = sin_ref[...]
     k_own, k_prev, k_far = own_ref[g, 0], prev_ref[g, 0], far_ref[g, 0]
     v_own = own_ref[g, 1].T
     v_prev = prev_ref[g, 1].T
@@ -115,60 +131,54 @@
     col = lax.broadcasted_iota(jnp.int32, (QB, QB), 1)
     seen = row <= col
     blocks = ROWS // QB
-    for n in range(GROUP):
-        head = g * GROUP + n
-        q_all = rotated(q_ref[:, head * HEAD_SIZE : (head + 1) * HEAD_SIZE], cosine, sine)
-        for b in range(blocks):
-            q = q_all[b * QB : (b + 1) * QB]
-            lo, hi = b * QB, (b + 1) * QB
-            prev = dot_nt(k_prev, q)
-            own = dot_nt(k_own[0:hi], q)
-            far = dot_nt(k_far[lo:ROWS], q)
-            mixed = jnp.where(seen, own[lo:hi], far[0:QB] + far_bias)
-            top = jnp.maximum(
-                jnp.max(prev, axis=0, keepdims=True) + prev_bias,
-                jnp.max(mixed, axis=0, keepdims=True),
-            )
-            if lo > 0:
-                top = jnp.maximum(top, jnp.max(own[0:lo], axis=0, keepdims=True))
-            if hi < ROWS:
-                top = jnp.maximum(top, jnp.max(far[QB:], axis=0, keepdims=True) + far_bias)
-            top = top * c
-            p_prev = jnp.exp2(prev * c - (top - prev_bias))
-            p_mixed = jnp.exp2(mixed * c - top)
-            total = jnp.sum(p_prev, axis=0, keepdims=True) + jnp.sum(p_mixed, axis=0, keepdims=True)
-            own_parts = [jnp.where(seen, p_mixed, 0.0).astype(jnp.bfloat16)]
-            far_parts = [jnp.where(seen, 0.0, p_mixed).astype(jnp.bfloat16)]
-            if lo > 0:
-                p = jnp.exp2(own[0:lo] * c - top)
-                total = total + jnp.sum(p, axis=0, keepdims=True)
-                own_parts.insert(0, p.astype(jnp.bfloat16))
-            if hi < ROWS:
-                p = jnp.exp2(far[QB:] * c - (top - far_bias))
-                total = total + jnp.sum(p, axis=0, keepdims=True)
-                far_parts.append(p.astype(jnp.bfloat16))
-            context = jnp.dot(v_prev, p_prev.astype(jnp.bfloat16), preferred_element_type=jnp.float32)
-            context += jnp.dot(
-                v_own[:, 0:hi], jnp.concatenate(own_parts, 0), preferred_element_type=jnp.float32
-            )
-            context += jnp.dot(
-                v_far[:, lo:], jnp.concatenate(far_parts, 0), preferred_element_type=jnp.float32
-            )
-            first = n * HEAD_SIZE % PIECE
-            out_refs[n * HEAD_SIZE // PIECE][first : first + HEAD_SIZE, lo:hi] = (
-                context / total
-            ).astype(jnp.bfloat16)
-
-
-def attend(g, place, *arrays):
-    width = GROUP * HEAD_SIZE
+    q_all = q_ref[:, n * HEAD_SIZE : (n + 1) * HEAD_SIZE]
+    for b in range(blocks):
+        q = q_all[b * QB : (b + 1) * QB]
+        lo, hi = b * QB, (b + 1) * QB
+        prev = dot_nt(k_prev, q)
+        own = dot_nt(k_own[0:hi], q)
+        far = dot_nt(k_far[lo:ROWS], q)
+        mixed = jnp.where(seen, own[lo:hi], far[0:QB] + far_bias)
+        top = jnp.maximum(
+            jnp.max(prev, axis=0, keepdims=True) + prev_bias,
+            jnp.max(mixed, axis=0, keepdims=True),
+        )
+        if lo > 0:
+            top = jnp.maximum(top, jnp.max(own[0:lo], axis=0, keepdims=True))
+        if hi < ROWS:
+            top = jnp.maximum(top, jnp.max(far[QB:], axis=0, keepdims=True) + far_bias)
+        top = top * c
+        p_prev = jnp.exp2(prev * c - (top - prev_bias))
+        p_mixed = jnp.exp2(mixed * c - top)
+        total = jnp.sum(p_prev, axis=0, keepdims=True) + jnp.sum(p_mixed, axis=0, keepdims=True)
+        own_parts = [jnp.where(seen, p_mixed, 0.0).astype(jnp.bfloat16)]
+        far_parts = [jnp.where(seen, 0.0, p_mixed).astype(jnp.bfloat16)]
+        if lo > 0:
+            p = jnp.exp2(own[0:lo] * c - top)
+            total = total + jnp.sum(p, axis=0, keepdims=True)
+            own_parts.insert(0, p.astype(jnp.bfloat16))
+        if hi < ROWS:
+            p = jnp.exp2(far[QB:] * c - (top - far_bias))
+            total = total + jnp.sum(p, axis=0, keepdims=True)
+            far_parts.append(p.astype(jnp.bfloat16))
+        context = jnp.dot(v_prev, p_prev.astype(jnp.bfloat16), preferred_element_type=jnp.float32)
+        context += jnp.dot(
+            v_own[:, 0:hi], jnp.concatenate(own_parts, 0), preferred_element_type=jnp.float32
+        )
+        context += jnp.dot(
+            v_far[:, lo:], jnp.concatenate(far_parts, 0), preferred_element_type=jnp.float32
+        )
+        out_ref[:, lo:hi] = (context / total).astype(jnp.bfloat16)
+
+
+def attend(n, place, *arrays):
     arrays = [pltpu.with_memory_space_constraint(x, pltpu.VMEM) for x in arrays]
     return pl.pallas_call(
-        functools.partial(attend_kernel, g),
+        functools.partial(attend_kernel, n),
         in_specs=[pl.BlockSpec(memory_space=pltpu.SMEM)] + [VMEM] * len(arrays),
-        out_specs=[VMEM] * (width // PIECE),
-        out_shape=[jax.ShapeDtypeStruct((PIECE, ROWS), jnp.bfloat16)] * (width // PIECE),
-        compiler_params=pltpu.CompilerParams(vmem_limit_bytes=20 * 1024 * 1024),
+        out_specs=VMEM,
+        out_shape=jax.ShapeDtypeStruct((PIECE, ROWS), jnp.bfloat16),
+        compiler_params=pltpu.CompilerParams(vmem_limit_bytes=16 * 1024 * 1024),
         name="attend",
     )(place, *arrays)
 
@@ -179,7 +189,14 @@
     copies = []
     for k in range(N_HEAD):
         copies.append(
-            [pltpu.make_async_copy(w_ref.at[order_ref[k]], w_buffer.at[k], arrived.at[k, PIECES])]
+            [
+                pltpu.make_async_copy(
+                    w_ref.at[order_ref[0, k], order_ref[1, k] ^ part],
+                    w_buffer.at[k, part],
+                    arrived.at[k, PIECES + part],
+                )
+                for part in range(2)
+            ]
             + [
                 pltpu.make_async_copy(
                     ctx_refs[k * PIECES + g],
@@ -194,12 +211,17 @@
     for k in range(N_HEAD):
         for copy in copies[k]:
             copy.wait()
-        value = jnp.dot(w_buffer[k], ctx_buffer[k], preferred_element_type=jnp.float32)
-        if k > 0:
-            value = acc_ref[...] + value
-        acc_ref[...] = value
+        total = 0.0
+        for part in range(2):
+            rows = slice(part * FEATURES // 2, (part + 1) * FEATURES // 2)
+            value = jnp.dot(w_buffer[k, part], ctx_buffer[k], preferred_element_type=jnp.float32)
+            if k > 0:
+                value = acc_ref[rows] + value
+            acc_ref[rows] = value
+            if k == N_HEAD - 1:
+                total = total + jnp.sum(value * value, axis=0, keepdims=True)
         if k == N_HEAD - 1:
-            sq_ref[...] = jnp.sum(value * value, axis=0, keepdims=True)
+            sq_ref[...] = jnp.broadcast_to(total[None], sq_ref.shape)
 
 
 def project(order, weights, blocks):
@@ -212,12 +234,12 @@
         out_specs=[VMEM, VMEM],
         out_shape=[
             jax.ShapeDtypeStruct((FEATURES, ROWS), jnp.float32),
-            jax.ShapeDtypeStruct((1, ROWS), jnp.float32),
+            jax.ShapeDtypeStruct((N_HEAD, 1, ROWS), jnp.float32),
         ],
         scratch_shapes=[
-            pltpu.VMEM((N_HEAD, FEATURES, WIDTH), jnp.bfloat16),
+            pltpu.VMEM((N_HEAD, 2, FEATURES // 2, WIDTH), jnp.bfloat16),
             pltpu.VMEM((N_HEAD, WIDTH, ROWS), jnp.bfloat16),
-            pltpu.SemaphoreType.DMA((N_HEAD, PIECES + 1)),
+            pltpu.SemaphoreType.DMA((N_HEAD, PIECES + 2)),
         ],
         compiler_params=pltpu.CompilerParams(vmem_limit_bytes=24 * 1024 * 1024),
         name="project",
@@ -241,22 +263,18 @@
     )(attended, squares, gain, residual)
 
 
-def for_everyone(array, axis):
-    length = lax.axis_size(axis)
-    return lax.all_to_all(
-        jnp.broadcast_to(array[None], (length, *array.shape)), axis, 0, 0, tiled=True
-    )
-
-
 def on_device(positions, queries, keys, values, out_weight, post_gain, residual):
     seq = lax.axis_index("seq")
     head = lax.axis_index("head")
-    spread = [
-        (s * N_HEAD + h, ((s // 4 + h) % N_HEAD * 4 + s % 4) * N_HEAD + s // 4)
-        for s in range(N_SEQ)
-        for h in range(N_HEAD)
-    ]
-    shard = lax.ppermute(out_weight.T, ("seq", "head"), spread)
+    across, along = [], []
+    for s in range(N_SEQ):
+        for h in range(N_HEAD):
+            group = s // 4
+            middle = (group + h) % N_HEAD * 4 + (s % 4 if (h % 2 == 0) else s % 4 ^ 2)
+            across.append((s * N_HEAD + h, middle * N_HEAD + h))
+            along.append((middle * N_HEAD + h, middle * N_HEAD + group))
+    shard = lax.ppermute(out_weight.T, ("seq", "head"), across)
+    shard = lax.ppermute(shard, ("seq", "head"), along)
 
     half = HEAD_SIZE // 2
     inverse = 10000.0 ** (-2.0 * jnp.arange(half, dtype=jnp.float32) / HEAD_SIZE)
@@ -268,10 +286,10 @@
     beyond = [(i, i + 2) for i in range(N_SEQ - 2)]
     prev = lax.ppermute(own, "seq", onward)
     far = lax.ppermute(own, "seq", beyond)
-    shard = held(shard, prev, far)
-    weights = lax.all_gather(shard, "seq", axis=0).reshape(N_HEAD, FEATURES, WIDTH)
+    q = rotate(queries.reshape(ROWS, WIDTH), cosine, sine)
+    shard = held(shard, prev, far, q)
+    weights = lax.all_gather(shard, "seq", axis=0).reshape(N_HEAD, 2, FEATURES // 2, WIDTH)
     place = seq.astype(jnp.int32).reshape(1)
-    q = queries.reshape(ROWS, WIDTH)
 
     ring = [
         (s * N_HEAD + h, s * N_HEAD + (h + (1 if s % 2 == 0 else -1)) % N_HEAD)
@@ -279,18 +297,18 @@
         for h in range(N_HEAD)
     ]
     blocks = [[] for _ in range(N_HEAD)]
-    for g in range(KV):
-        pieces = attend(g, place, q, cosine, sine, own, prev, far)
-        for carried in pieces:
-            blocks[0].append(carried)
-            for k in range(1, N_HEAD):
-                carried = lax.ppermute(carried, ("seq", "head"), ring)
-                blocks[k].append(carried)
+    for n in range(PIECES):
+        carried = attend(n, place, q, own, prev, far)
+        blocks[0].append(carried)
+        for k in range(1, N_HEAD):
+            carried = lax.ppermute(carried, ("seq", "head"), ring)
+            blocks[k].append(carried)
     sign = jnp.where(seq % 2 == 0, -1, 1)
     source = head + sign * jnp.arange(N_HEAD, dtype=jnp.int32)
-    order = ((source + head) % N_HEAD).astype(jnp.int32)
+    source = source % N_HEAD
+    order = jnp.stack([(source + head) % N_HEAD, source % 2]).astype(jnp.int32)
     attended, squares = project(order, weights, [x for row in blocks for x in row])
-    squares = for_everyone(squares, "head")
+    squares = lax.all_to_all(squares, "head", 0, 0, tiled=True)
     return finish(attended, squares, post_gain[:, None], residual.T).T
 
 

time: 129 us -> 133 us (1.031)
  the two profiles are of different devices: /device:TPU:6 before, /device:TPU:2 now
where the time goes in v5:
time: 133 us
  starting transfers between devices  79.2 us (60%)
  waiting for transfers between devices  22.5 us (17%)
  Pallas kernels  14.3 us (11%)
  between operations  13.7 us (10%)
  local copies, waits for them, and re-layouts  3.14 us (2%)
    ppermute x28, starting transfers between devices, on_device(): carried = lax.ppermute(carried, ('seq', 'head'), ring)  53.8 us
    ppermute x1, starting transfers between devices, on_device(): shard = lax.ppermute(shard, ('seq', 'head'), along)  12.6 us
    ppermute x28, waiting for transfers between devices, on_device(): carried = lax.ppermute(carried, ('seq', 'head'), ring)  11.2 us
    all_to_all x1, waiting for transfers between devices, on_device(): squares = lax.all_to_all(squares, 'head', 0, 0, tiled=True)  7.62 us
    pallas_call x1, Pallas kernels, project(): pl.pallas_call(project_kernel, in_specs=[pl.BlockSpec(memory_space=pltpu....  6.3 us
    pallas_call x4, Pallas kernels, attend(): pl.pallas_call(functools.partial(attend_kernel, n), in_specs=[pl.BlockSpe...  6 us
    all_to_all x1, starting transfers between devices, on_device(): squares = lax.all_to_all(squares, 'head', 0, 0, tiled=True)  5.75 us
    ppermute x1, waiting for transfers between devices, on_device(): shard = lax.ppermute(shard, ('seq', 'head'), along)  3.65 us
  transfers between devices with their start and end apart: 34, of which 17 were waited for; matrix products, arithmetic and copies ran while one was open for 1% of the time, Pallas kernels for 5%

profile of v5, /device:TPU:2, one launch (start us, length us, event | category | flops | bytes accessed | tf_op | source)
XLA Modules:
  0.0 133.0 jit_solution(13162779921256775450)
XLA Ops:
  9.0 1.9 %collective-permute-start.2 = (bf16[2,2,512,128]{3,2,1,0:T(8,128)(2,1)S(1)}, bf16[2,2,512,128]{3,2,1,0:T(8,128)(2,1)S(1)}, u32[]{:S(2)}, u32[]{:S(2)}) collective-permute-start(bf16[2,2,512,128]{3,2,1,0:T(8,128)(2,1)S(1)} %get-tuple-element.10.own_ref), channel_id=1, source_target_pairs={{0,8},{8,16},{16,24},{24,32},{32,40},{40,48},{48,56},{56,64},{64,7... | collective-permute-start | bytes 1572872 | tf_op jit(solution)/shard_map/ppermute | solution.py:287
  10.9 3.5 %collective-permute-start.3 = (bf16[2,2,512,128]{3,2,1,0:T(8,128)(2,1)S(1)}, bf16[2,2,512,128]{3,2,1,0:T(8,128)(2,1)S(1)}, u32[]{:S(2)}, u32[]{:S(2)}) collective-permute-start(bf16[2,2,512,128]{3,2,1,0:T(8,128)(2,1)S(1)} %get-tuple-element.10.own_ref), channel_id=1, source_target_pairs={{0,16},{8,24},{16,32},{24,40},{32,48},{40,56},{48,64},{56,72},{64,... | collective-permute-start | bytes 1572872 | tf_op jit(solution)/shard_map/ppermute | solution.py:288
  14.4 1.6 %collective-permute-start = (bf16[168,512]{1,0:T(8,128)(2,1)}, bf16[168,512]{1,0:T(8,128)(2,1)S(1)}, u32[]{:S(2)}, u32[]{:S(2)}) collective-permute-start(bf16[168,512]{1,0:T(8,128)(2,1)} %bitcast.21), channel_id=1, source_target_pairs={{0,0},{1,49},{2,66},{3,115},{4,132},{5,181},{6,198},{7,247},{8,8},... | collective-permute-start | bytes 516104 | tf_op jit(solution)/shard_map/ppermute | solution.py:276
  16.0 12.6 %collective-permute-start.1 = (bf16[168,512]{1,0:T(8,128)(2,1)S(1)}, bf16[168,512]{1,0:T(8,128)(2,1)}, u32[]{:S(2)}, u32[]{:S(2)}) collective-permute-start(bf16[168,512]{1,0:T(8,128)(2,1)S(1)} %collective-permute-done), channel_id=1, source_target_pairs={{0,0},{49,48},{66,64},{115,112},{132,128},{181,176},{198,192},{247... | collective-permute-start | bytes 516104 | tf_op jit(solution)/shard_map/ppermute | solution.py:277
  30.0 3.7 %collective-permute-done.1.first_ref = bf16[168,512]{1,0:T(8,128)(2,1)} collective-permute-done((bf16[168,512]{1,0:T(8,128)(2,1)S(1)}, bf16[168,512]{1,0:T(8,128)(2,1)}, u32[]{:S(2)}, u32[]{:S(2)}) %collective-permute-start.1) | collective-permute-done | bytes 172064 | tf_op jit(solution)/shard_map/ppermute | solution.py:277
  33.7 1.5 %attend.7.refs_3_ = bf16[128,512]{1,0:T(8,128)(2,1)S(1)} custom-call(s32[1]{0:T(128)} %bitcast.6.place_ref, bf16[512,512]{1,0:T(8,128)(2,1)S(1)} %rotate.1.refs_2_.q_ref, bf16[2,2,512,128]{3,2,1,0:T(8,128)(2,1)S(1)} %get-tuple-element.10.own_ref, bf16[2,2,512,128]{3,2,1,0:T(8,128)(2,1)S(1)} %collective-permute-done.2.refs_0_.prev_ref, ...), custom_call_target="tpu_custom_call" | custom-call | tf_op jit(solution)/shard_map/attend/pallas_call | solution.py:176
  35.3 4.6 %collective-permute-start.7 = (bf16[128,512]{1,0:T(8,128)(2,1)S(1)}, bf16[128,512]{1,0:T(8,128)(2,1)S(1)}, u32[]{:S(2)}, u32[]{:S(2)}) collective-permute-start(bf16[128,512]{1,0:T(8,128)(2,1)S(1)} %attend.7.refs_3_), channel_id=1, source_target_pairs={{0,1},{1,2},{2,3},{3,4},{4,5},{5,6},{6,7},{7,0},{8,15},{9,8},{10,9... | collective-permute-start | bytes 393224 | tf_op jit(solution)/shard_map/ppermute | solution.py:304
  39.8 1.5 %attend.6.refs_2_ = bf16[128,512]{1,0:T(8,128)(2,1)S(1)} custom-call(s32[1]{0:T(128)} %bitcast.6.place_ref, bf16[512,512]{1,0:T(8,128)(2,1)S(1)} %rotate.1.refs_2_.q_ref, bf16[2,2,512,128]{3,2,1,0:T(8,128)(2,1)S(1)} %get-tuple-element.10.own_ref, bf16[2,2,512,128]{3,2,1,0:T(8,128)(2,1)S(1)} %collective-permute-done.2.refs_0_.prev_ref, ...), custom_call_target="tpu_custom_call" | custom-call | tf_op jit(solution)/shard_map/attend/pallas_call | solution.py:176
  41.4 1.5 %attend.5.refs_1_ = bf16[128,512]{1,0:T(8,128)(2,1)S(1)} custom-call(s32[1]{0:T(128)} %bitcast.6.place_ref, bf16[512,512]{1,0:T(8,128)(2,1)S(1)} %rotate.1.refs_2_.q_ref, bf16[2,2,512,128]{3,2,1,0:T(8,128)(2,1)S(1)} %get-tuple-element.10.own_ref, bf16[2,2,512,128]{3,2,1,0:T(8,128)(2,1)S(1)} %collective-permute-done.2.refs_0_.prev_ref, ...), custom_call_target="tpu_custom_call" | custom-call | tf_op jit(solution)/shard_map/attend/pallas_call | solution.py:176
  43.0 15.4 %collective-permute-start.5 = (bf16[128,512]{1,0:T(8,128)(2,1)S(1)}, bf16[128,512]{1,0:T(8,128)(2,1)S(1)}, u32[]{:S(2)}, u32[]{:S(2)}) collective-permute-start(bf16[128,512]{1,0:T(8,128)(2,1)S(1)} %attend.5.refs_1_), channel_id=1, source_target_pairs={{0,1},{1,2},{2,3},{3,4},{4,5},{5,6},{6,7},{7,0},{8,15},{9,8},{10,9... | collective-permute-start | bytes 393224 | tf_op jit(solution)/shard_map/ppermute | solution.py:304
  58.3 1.5 %attend.4.refs_0_ = bf16[128,512]{1,0:T(8,128)(2,1)S(1)} custom-call(s32[1]{0:T(128)} %bitcast.6.place_ref, bf16[512,512]{1,0:T(8,128)(2,1)S(1)} %rotate.1.refs_2_.q_ref, bf16[2,2,512,128]{3,2,1,0:T(8,128)(2,1)S(1)} %get-tuple-element.10.own_ref, bf16[2,2,512,128]{3,2,1,0:T(8,128)(2,1)S(1)} %collective-permute-done.2.refs_0_.prev_ref, ...), custom_call_target="tpu_custom_call" | custom-call | tf_op jit(solution)/shard_map/attend/pallas_call | solution.py:176
  60.8 1.6 %collective-permute-done.5.refs_5_ = bf16[128,512]{1,0:T(8,128)(2,1)S(1)} collective-permute-done((bf16[128,512]{1,0:T(8,128)(2,1)S(1)}, bf16[128,512]{1,0:T(8,128)(2,1)S(1)}, u32[]{:S(2)}, u32[]{:S(2)}) %collective-permute-start.5) | collective-permute-done | bytes 131104 | tf_op jit(solution)/shard_map/ppermute | solution.py:304
  62.5 4.7 %collective-permute-start.9 = (bf16[128,512]{1,0:T(8,128)(2,1)S(1)}, bf16[128,512]{1,0:T(8,128)(2,1)S(1)}, u32[]{:S(2)}, u32[]{:S(2)}) collective-permute-start(bf16[128,512]{1,0:T(8,128)(2,1)S(1)} %collective-permute-done.5.refs_5_), channel_id=1, source_target_pairs={{0,1},{1,2},{2,3},{3,4},{4,5},{5,6},{6,7},{7,0},{8,15},{9,8},{10,9... | collective-permute-start | bytes 393224 | tf_op jit(solution)/shard_map/ppermute | solution.py:304
  70.3 3.0 %collective-permute-start.13 = (bf16[128,512]{1,0:T(8,128)(2,1)S(1)}, bf16[128,512]{1,0:T(8,128)(2,1)S(1)}, u32[]{:S(2)}, u32[]{:S(2)}) collective-permute-start(bf16[128,512]{1,0:T(8,128)(2,1)S(1)} %collective-permute-done.9.refs_9_), channel_id=1, source_target_pairs={{0,1},{1,2},{2,3},{3,4},{4,5},{5,6},{6,7},{7,0},{8,15},{9,8},{10,9... | collective-permute-start | bytes 393224 | tf_op jit(solution)/shard_map/ppermute | solution.py:304
  77.6 2.0 %collective-permute-start.17 = (bf16[128,512]{1,0:T(8,128)(2,1)S(1)}, bf16[128,512]{1,0:T(8,128)(2,1)S(1)}, u32[]{:S(2)}, u32[]{:S(2)}) collective-permute-start(bf16[128,512]{1,0:T(8,128)(2,1)S(1)} %collective-permute-done.13.refs_13_), channel_id=1, source_target_pairs={{0,1},{1,2},{2,3},{3,4},{4,5},{5,6},{6,7},{7,0},{8,15},{9,8},{10,9... | collective-permute-start | bytes 393224 | tf_op jit(solution)/shard_map/ppermute | solution.py:304
  83.8 2.0 %collective-permute-start.21 = (bf16[128,512]{1,0:T(8,128)(2,1)S(1)}, bf16[128,512]{1,0:T(8,128)(2,1)}, u32[]{:S(2)}, u32[]{:S(2)}) collective-permute-start(bf16[128,512]{1,0:T(8,128)(2,1)S(1)} %collective-permute-done.17.refs_17_), channel_id=1, source_target_pairs={{0,1},{1,2},{2,3},{3,4},{4,5},{5,6},{6,7},{7,0},{8,15},{9,8},{10,9... | collective-permute-start | bytes 393224 | tf_op jit(solution)/shard_map/ppermute | solution.py:304
  90.1 1.9 %collective-permute-start.25 = (bf16[128,512]{1,0:T(8,128)(2,1)}, bf16[128,512]{1,0:T(8,128)(2,1)}, u32[]{:S(2)}, u32[]{:S(2)}) collective-permute-start(bf16[128,512]{1,0:T(8,128)(2,1)} %collective-permute-done.21.refs_21_), channel_id=1, source_target_pairs={{0,1},{1,2},{2,3},{3,4},{4,5},{5,6},{6,7},{7,0},{8,15},{9,8},{10,9... | collective-permute-start | bytes 393224 | tf_op jit(solution)/shard_map/ppermute | solution.py:304
  96.5 1.6 %collective-permute-start.29 = (bf16[128,512]{1,0:T(8,128)(2,1)}, bf16[128,512]{1,0:T(8,128)(2,1)}, u32[]{:S(2)}, u32[]{:S(2)}) collective-permute-start(bf16[128,512]{1,0:T(8,128)(2,1)} %collective-permute-done.25.refs_25_), channel_id=1, source_target_pairs={{0,1},{1,2},{2,3},{3,4},{4,5},{5,6},{6,7},{7,0},{8,15},{9,8},{10,9... | collective-permute-start | bytes 393224 | tf_op jit(solution)/shard_map/ppermute | solution.py:304
  99.9 1.7 %collective-permute-done.30.refs_30_ = bf16[128,512]{1,0:T(8,128)(2,1)} collective-permute-done((bf16[128,512]{1,0:T(8,128)(2,1)}, bf16[128,512]{1,0:T(8,128)(2,1)}, u32[]{:S(2)}, u32[]{:S(2)}) %collective-permute-start.30) | collective-permute-done | bytes 131104 | tf_op jit(solution)/shard_map/ppermute | solution.py:304
  101.6 1.4 %collective-permute-done.29.refs_29_ = bf16[128,512]{1,0:T(8,128)(2,1)} collective-permute-done((bf16[128,512]{1,0:T(8,128)(2,1)}, bf16[128,512]{1,0:T(8,128)(2,1)}, u32[]{:S(2)}, u32[]{:S(2)}) %collective-permute-start.29) | collective-permute-done | bytes 131104 | tf_op jit(solution)/shard_map/ppermute | solution.py:304
  103.0 2.0 %collective-permute-done.28.refs_28_ = bf16[128,512]{1,0:T(8,128)(2,1)} collective-permute-done((bf16[128,512]{1,0:T(8,128)(2,1)}, bf16[128,512]{1,0:T(8,128)(2,1)}, u32[]{:S(2)}, u32[]{:S(2)}) %collective-permute-start.28) | collective-permute-done | bytes 131104 | tf_op jit(solution)/shard_map/ppermute | solution.py:304
  105.2 6.3 %project.1 = (f32[672,512]{1,0:T(8,128)S(1)}, f32[8,1,512]{2,1,0:T(1,128)}) custom-call(s32[2,8]{1,0:T(2,128)S(1)} %pad_add_fusion.order_ref, bf16[8,2,336,512]{3,2,1,0:T(8,128)(2,1)} %bitcast.19, bf16[128,512]{1,0:T(8,128)(2,1)} %copy-done.4, bf16[128,512]{1,0:T(8,128)(2,1)} %copy-done.3, bf16[128,512]{1,0:T(8,128)(2,1)} %copy-done.2, ...), custom_call_target="tpu_custom_call" | custom-call | tf_op jit(solution)/shard_map/project/pallas_call | solution.py:231
  111.5 5.8 %all-to-all-start = ((f32[8,1,512]{2,1,0:T(1,128)}), f32[8,1,512]{2,1,0:T(1,128)S(1)}, u32[]{:S(2)}, u32[]{:S(2)}) async-start(f32[8,1,512]{2,1,0:T(1,128)} %get-tuple-element.14), calls=%async_computation | async-start | bytes 32768 | tf_op jit(solution)/shard_map/all_to_all | solution.py:311
  117.4 7.6 %all-to-all-done.sq_ref = f32[8,1,512]{2,1,0:T(1,128)S(1)} async-done(((f32[8,1,512]{2,1,0:T(1,128)}), f32[8,1,512]{2,1,0:T(1,128)S(1)}, u32[]{:S(2)}, u32[]{:S(2)}) %all-to-all-start) | async-done | bytes 16416 | tf_op jit(solution)/shard_map/all_to_all | solution.py:311
  (109 shorter events, 28.5 us)
Async XLA Ops:
  6.5 98.5 %all-gather.3.cloned.1.call-start = ((), (), s32[]{:S(2)}) async-start(), calls=%async_computation.1 | async-start | bytes 5677056 | tf_op jit(solution)/shard_map/all_gather | solution.py:291
  9.0 24.7 %collective-permute-start.2 = (bf16[2,2,512,128]{3,2,1,0:T(8,128)(2,1)S(1)}, bf16[2,2,512,128]{3,2,1,0:T(8,128)(2,1)S(1)}, u32[]{:S(2)}, u32[]{:S(2)}) collective-permute-start(bf16[2,2,512,128]{3,2,1,0:T(8,128)(2,1)S(1)} %get-tuple-element.10.own_ref), channel_id=1, source_target_pairs={{0,8},{8,16},{16,24},{24,32},{32,40},{40,48},{48,56},{56,64},{64,7... | collective-permute-start | bytes 1572872 | tf_op jit(solution)/shard_map/ppermute | solution.py:287
  10.9 22.8 %collective-permute-start.3 = (bf16[2,2,512,128]{3,2,1,0:T(8,128)(2,1)S(1)}, bf16[2,2,512,128]{3,2,1,0:T(8,128)(2,1)S(1)}, u32[]{:S(2)}, u32[]{:S(2)}) collective-permute-start(bf16[2,2,512,128]{3,2,1,0:T(8,128)(2,1)S(1)} %get-tuple-element.10.own_ref), channel_id=1, source_target_pairs={{0,16},{8,24},{16,32},{24,40},{32,48},{40,56},{48,64},{56,72},{64,... | collective-permute-start | bytes 1572872 | tf_op jit(solution)/shard_map/ppermute | solution.py:288
  16.0 17.7 %collective-permute-start.1 = (bf16[168,512]{1,0:T(8,128)(2,1)S(1)}, bf16[168,512]{1,0:T(8,128)(2,1)}, u32[]{:S(2)}, u32[]{:S(2)}) collective-permute-start(bf16[168,512]{1,0:T(8,128)(2,1)S(1)} %collective-permute-done), channel_id=1, source_target_pairs={{0,0},{49,48},{66,64},{115,112},{132,128},{181,176},{198,192},{247... | collective-permute-start | bytes 516104 | tf_op jit(solution)/shard_map/ppermute | solution.py:277
  35.3 24.7 %collective-permute-start.7 = (bf16[128,512]{1,0:T(8,128)(2,1)S(1)}, bf16[128,512]{1,0:T(8,128)(2,1)S(1)}, u32[]{:S(2)}, u32[]{:S(2)}) collective-permute-start(bf16[128,512]{1,0:T(8,128)(2,1)S(1)} %attend.7.refs_3_), channel_id=1, source_target_pairs={{0,1},{1,2},{2,3},{3,4},{4,5},{5,6},{6,7},{7,0},{8,15},{9,8},{10,9... | collective-permute-start | bytes 393224 | tf_op jit(solution)/shard_map/ppermute | solution.py:304
  41.3 19.5 %collective-permute-start.6 = (bf16[128,512]{1,0:T(8,128)(2,1)S(1)}, bf16[128,512]{1,0:T(8,128)(2,1)S(1)}, u32[]{:S(2)}, u32[]{:S(2)}) collective-permute-start(bf16[128,512]{1,0:T(8,128)(2,1)S(1)} %attend.6.refs_2_), channel_id=1, source_target_pairs={{0,1},{1,2},{2,3},{3,4},{4,5},{5,6},{6,7},{7,0},{8,15},{9,8},{10,9... | collective-permute-start | bytes 393224 | tf_op jit(solution)/shard_map/ppermute | solution.py:304
  43.0 19.5 %collective-permute-start.5 = (bf16[128,512]{1,0:T(8,128)(2,1)S(1)}, bf16[128,512]{1,0:T(8,128)(2,1)S(1)}, u32[]{:S(2)}, u32[]{:S(2)}) collective-permute-start(bf16[128,512]{1,0:T(8,128)(2,1)S(1)} %attend.5.refs_1_), channel_id=1, source_target_pairs={{0,1},{1,2},{2,3},{3,4},{4,5},{5,6},{6,7},{7,0},{8,15},{9,8},{10,9... | collective-permute-start | bytes 393224 | tf_op jit(solution)/shard_map/ppermute | solution.py:304
  59.9 7.3 %collective-permute-start.4 = (bf16[128,512]{1,0:T(8,128)(2,1)S(1)}, bf16[128,512]{1,0:T(8,128)(2,1)S(1)}, u32[]{:S(2)}, u32[]{:S(2)}) collective-permute-start(bf16[128,512]{1,0:T(8,128)(2,1)S(1)} %attend.4.refs_0_), channel_id=1, source_target_pairs={{0,1},{1,2},{2,3},{3,4},{4,5},{5,6},{6,7},{7,0},{8,15},{9,8},{10,9... | collective-permute-start | bytes 393224 | tf_op jit(solution)/shard_map/ppermute | solution.py:304
  60.0 7.5 %collective-permute-start.11 = (bf16[128,512]{1,0:T(8,128)(2,1)S(1)}, bf16[128,512]{1,0:T(8,128)(2,1)S(1)}, u32[]{:S(2)}, u32[]{:S(2)}) collective-permute-start(bf16[128,512]{1,0:T(8,128)(2,1)S(1)} %collective-permute-done.7.refs_7_), channel_id=1, source_target_pairs={{0,1},{1,2},{2,3},{3,4},{4,5},{5,6},{6,7},{7,0},{8,15},{9,8},{10,9... | collective-permute-start | bytes 393224 | tf_op jit(solution)/shard_map/ppermute | solution.py:304
  60.8 8.1 %collective-permute-start.10 = (bf16[128,512]{1,0:T(8,128)(2,1)S(1)}, bf16[128,512]{1,0:T(8,128)(2,1)S(1)}, u32[]{:S(2)}, u32[]{:S(2)}) collective-permute-start(bf16[128,512]{1,0:T(8,128)(2,1)S(1)} %collective-permute-done.6.refs_6_), channel_id=1, source_target_pairs={{0,1},{1,2},{2,3},{3,4},{4,5},{5,6},{6,7},{7,0},{8,15},{9,8},{10,9... | collective-permute-start | bytes 393224 | tf_op jit(solution)/shard_map/ppermute | solution.py:304
  62.5 7.9 %collective-permute-start.9 = (bf16[128,512]{1,0:T(8,128)(2,1)S(1)}, bf16[128,512]{1,0:T(8,128)(2,1)S(1)}, u32[]{:S(2)}, u32[]{:S(2)}) collective-permute-start(bf16[128,512]{1,0:T(8,128)(2,1)S(1)} %collective-permute-done.5.refs_5_), channel_id=1, source_target_pairs={{0,1},{1,2},{2,3},{3,4},{4,5},{5,6},{6,7},{7,0},{8,15},{9,8},{10,9... | collective-permute-start | bytes 393224 | tf_op jit(solution)/shard_map/ppermute | solution.py:304
  67.5 7.3 %collective-permute-start.15 = (bf16[128,512]{1,0:T(8,128)(2,1)S(1)}, bf16[128,512]{1,0:T(8,128)(2,1)S(1)}, u32[]{:S(2)}, u32[]{:S(2)}) collective-permute-start(bf16[128,512]{1,0:T(8,128)(2,1)S(1)} %collective-permute-done.11.refs_11_), channel_id=1, source_target_pairs={{0,1},{1,2},{2,3},{3,4},{4,5},{5,6},{6,7},{7,0},{8,15},{9,8},{10,9... | collective-permute-start | bytes 393224 | tf_op jit(solution)/shard_map/ppermute | solution.py:304
  68.9 7.3 %collective-permute-start.14 = (bf16[128,512]{1,0:T(8,128)(2,1)S(1)}, bf16[128,512]{1,0:T(8,128)(2,1)S(1)}, u32[]{:S(2)}, u32[]{:S(2)}) collective-permute-start(bf16[128,512]{1,0:T(8,128)(2,1)S(1)} %collective-permute-done.10.refs_10_), channel_id=1, source_target_pairs={{0,1},{1,2},{2,3},{3,4},{4,5},{5,6},{6,7},{7,0},{8,15},{9,8},{10,9... | collective-permute-start | bytes 393224 | tf_op jit(solution)/shard_map/ppermute | solution.py:304
  70.3 7.3 %collective-permute-start.13 = (bf16[128,512]{1,0:T(8,128)(2,1)S(1)}, bf16[128,512]{1,0:T(8,128)(2,1)S(1)}, u32[]{:S(2)}, u32[]{:S(2)}) collective-permute-start(bf16[128,512]{1,0:T(8,128)(2,1)S(1)} %collective-permute-done.9.refs_9_), channel_id=1, source_target_pairs={{0,1},{1,2},{2,3},{3,4},{4,5},{5,6},{6,7},{7,0},{8,15},{9,8},{10,9... | collective-permute-start | bytes 393224 | tf_op jit(solution)/shard_map/ppermute | solution.py:304
  82.4 6.3 %collective-permute-start.22 = (bf16[128,512]{1,0:T(8,128)(2,1)S(1)}, bf16[128,512]{1,0:T(8,128)(2,1)}, u32[]{:S(2)}, u32[]{:S(2)}) collective-permute-start(bf16[128,512]{1,0:T(8,128)(2,1)S(1)} %collective-permute-done.18.refs_18_), channel_id=1, source_target_pairs={{0,1},{1,2},{2,3},{3,4},{4,5},{5,6},{6,7},{7,0},{8,15},{9,8},{10,9... | collective-permute-start | bytes 393224 | tf_op jit(solution)/shard_map/ppermute | solution.py:304
  83.8 6.3 %collective-permute-start.21 = (bf16[128,512]{1,0:T(8,128)(2,1)S(1)}, bf16[128,512]{1,0:T(8,128)(2,1)}, u32[]{:S(2)}, u32[]{:S(2)}) collective-permute-start(bf16[128,512]{1,0:T(8,128)(2,1)S(1)} %collective-permute-done.17.refs_17_), channel_id=1, source_target_pairs={{0,1},{1,2},{2,3},{3,4},{4,5},{5,6},{6,7},{7,0},{8,15},{9,8},{10,9... | collective-permute-start | bytes 393224 | tf_op jit(solution)/shard_map/ppermute | solution.py:304
  88.6 6.5 %collective-permute-start.26 = (bf16[128,512]{1,0:T(8,128)(2,1)}, bf16[128,512]{1,0:T(8,128)(2,1)}, u32[]{:S(2)}, u32[]{:S(2)}) collective-permute-start(bf16[128,512]{1,0:T(8,128)(2,1)} %collective-permute-done.22.refs_22_), channel_id=1, source_target_pairs={{0,1},{1,2},{2,3},{3,4},{4,5},{5,6},{6,7},{7,0},{8,15},{9,8},{10,9... | collective-permute-start | bytes 393224 | tf_op jit(solution)/shard_map/ppermute | solution.py:304
  90.1 6.5 %collective-permute-start.25 = (bf16[128,512]{1,0:T(8,128)(2,1)}, bf16[128,512]{1,0:T(8,128)(2,1)}, u32[]{:S(2)}, u32[]{:S(2)}) collective-permute-start(bf16[128,512]{1,0:T(8,128)(2,1)} %collective-permute-done.21.refs_21_), channel_id=1, source_target_pairs={{0,1},{1,2},{2,3},{3,4},{4,5},{5,6},{6,7},{7,0},{8,15},{9,8},{10,9... | collective-permute-start | bytes 393224 | tf_op jit(solution)/shard_map/ppermute | solution.py:304
  92.0 6.5 %collective-permute-start.24 = (bf16[128,512]{1,0:T(8,128)(2,1)}, bf16[128,512]{1,0:T(8,128)(2,1)}, u32[]{:S(2)}, u32[]{:S(2)}) collective-permute-start(bf16[128,512]{1,0:T(8,128)(2,1)} %collective-permute-done.20.refs_20_), channel_id=1, source_target_pairs={{0,1},{1,2},{2,3},{3,4},{4,5},{5,6},{6,7},{7,0},{8,15},{9,8},{10,9... | collective-permute-start | bytes 393224 | tf_op jit(solution)/shard_map/ppermute | solution.py:304
  93.4 6.5 %collective-permute-start.31 = (bf16[128,512]{1,0:T(8,128)(2,1)}, bf16[128,512]{1,0:T(8,128)(2,1)}, u32[]{:S(2)}, u32[]{:S(2)}) collective-permute-start(bf16[128,512]{1,0:T(8,128)(2,1)} %collective-permute-done.27.refs_27_), channel_id=1, source_target_pairs={{0,1},{1,2},{2,3},{3,4},{4,5},{5,6},{6,7},{7,0},{8,15},{9,8},{10,9... | collective-permute-start | bytes 393224 | tf_op jit(solution)/shard_map/ppermute | solution.py:304
  95.1 6.5 %collective-permute-start.30 = (bf16[128,512]{1,0:T(8,128)(2,1)}, bf16[128,512]{1,0:T(8,128)(2,1)}, u32[]{:S(2)}, u32[]{:S(2)}) collective-permute-start(bf16[128,512]{1,0:T(8,128)(2,1)} %collective-permute-done.26.refs_26_), channel_id=1, source_target_pairs={{0,1},{1,2},{2,3},{3,4},{4,5},{5,6},{6,7},{7,0},{8,15},{9,8},{10,9... | collective-permute-start | bytes 393224 | tf_op jit(solution)/shard_map/ppermute | solution.py:304
  96.5 6.5 %collective-permute-start.29 = (bf16[128,512]{1,0:T(8,128)(2,1)}, bf16[128,512]{1,0:T(8,128)(2,1)}, u32[]{:S(2)}, u32[]{:S(2)}) collective-permute-start(bf16[128,512]{1,0:T(8,128)(2,1)} %collective-permute-done.25.refs_25_), channel_id=1, source_target_pairs={{0,1},{1,2},{2,3},{3,4},{4,5},{5,6},{6,7},{7,0},{8,15},{9,8},{10,9... | collective-permute-start | bytes 393224 | tf_op jit(solution)/shard_map/ppermute | solution.py:304
  98.5 6.5 %collective-permute-start.28 = (bf16[128,512]{1,0:T(8,128)(2,1)}, bf16[128,512]{1,0:T(8,128)(2,1)}, u32[]{:S(2)}, u32[]{:S(2)}) collective-permute-start(bf16[128,512]{1,0:T(8,128)(2,1)} %collective-permute-done.24.refs_24_), channel_id=1, source_target_pairs={{0,1},{1,2},{2,3},{3,4},{4,5},{5,6},{6,7},{7,0},{8,15},{9,8},{10,9... | collective-permute-start | bytes 393224 | tf_op jit(solution)/shard_map/ppermute | solution.py:304
  111.5 13.5 %all-to-all-start = ((f32[8,1,512]{2,1,0:T(1,128)}), f32[8,1,512]{2,1,0:T(1,128)S(1)}, u32[]{:S(2)}, u32[]{:S(2)}) async-start(f32[8,1,512]{2,1,0:T(1,128)} %get-tuple-element.14), calls=%async_computation | async-start | bytes 32768 | tf_op jit(solution)/shard_map/all_to_all | solution.py:311
  (34 other events, 966.7 us)
Sparse Core Ops, SparseCore 0:
  33.9 64.9 all-gather.2

commit v6 on v5

--- a/solution.py
+++ b/solution.py
@@ -283,9 +283,8 @@
         positions[None], inverse, keys.transpose(1, 0, 2), values.transpose(1, 0, 2)
     )
     onward = [(i, i + 1) for i in range(N_SEQ - 1)]
-    beyond = [(i, i + 2) for i in range(N_SEQ - 2)]
     prev = lax.ppermute(own, "seq", onward)
-    far = lax.ppermute(own, "seq", beyond)
+    far = lax.ppermute(prev, "seq", onward)
     q = rotate(queries.reshape(ROWS, WIDTH), cosine, sine)
     shard = held(shard, prev, far, q)
     weights = lax.all_gather(shard, "seq", axis=0).reshape(N_HEAD, 2, FEATURES // 2, WIDTH)

time: 133 us -> 135 us (1.015)
  waiting for transfers between devices: 22.5 us -> 31.9 us
  starting transfers between devices: 79.2 us -> 71.1 us
    ppermute x1, waiting for transfers between devices: 0.01 us -> 10.7 us  [on_device(): prev = lax.ppermute(own, 'seq', onward)]
    ppermute x28, starting transfers between devices: 53.8 us -> 48.4 us  [on_device(): carried = lax.ppermute(carried, ('seq', 'head'), ring)]
    ppermute x1, waiting for transfers between devices: 3.65 us -> 2.03 us  [on_device(): shard = lax.ppermute(shard, ('seq', 'head'), along)]
    ppermute x1, starting transfers between devices: 3.48 us -> 1.91 us  [on_device(): far = lax.ppermute(prev, 'seq', onward)]
  transfers between devices with their start and end apart: 34 -> 34, of which waited for: 17 -> 19; matrix products, arithmetic and copies ran while one was open for 1% -> 1% of each run, Pallas kernels for 5% -> 5%
where the time goes in v6:
time: 135 us; the launch traced here: 134 us
  starting transfers between devices  71.1 us (53%)
  waiting for transfers between devices  31.9 us (24%)
  Pallas kernels  14.3 us (11%)
  between operations  13.8 us (10%)
  local copies, waits for them, and re-layouts  3.14 us (2%)
    ppermute x28, starting transfers between devices, on_device(): carried = lax.ppermute(carried, ('seq', 'head'), ring)  48.4 us
    ppermute x28, waiting for transfers between devices, on_device(): carried = lax.ppermute(carried, ('seq', 'head'), ring)  11.5 us
    ppermute x1, starting transfers between devices, on_device(): shard = lax.ppermute(shard, ('seq', 'head'), along)  11.5 us
    ppermute x1, waiting for transfers between devices, on_device(): prev = lax.ppermute(own, 'seq', onward)  10.7 us
    all_to_all x1, waiting for transfers between devices, on_device(): squares = lax.all_to_all(squares, 'head', 0, 0, tiled=True)  7.62 us
    pallas_call x1, Pallas kernels, project(): pl.pallas_call(project_kernel, in_specs=[pl.BlockSpec(memory_space=pltpu....  6.3 us
    pallas_call x4, Pallas kernels, attend(): pl.pallas_call(functools.partial(attend_kernel, n), in_specs=[pl.BlockSpe...  6.01 us
    all_to_all x1, starting transfers between devices, on_device(): squares = lax.all_to_all(squares, 'head', 0, 0, tiled=True)  5.75 us
  transfers between devices with their start and end apart: 34, of which 19 were waited for; matrix products, arithmetic and copies ran while one was open for 1% of the time, Pallas kernels for 5%

profile of v6, /device:TPU:2, one launch (start us, length us, event | category | flops | bytes accessed | tf_op | source)
XLA Modules:
  0.0 134.4 jit_solution(2584246700137923041)
XLA Ops:
  9.0 1.9 %collective-permute-start.2 = (bf16[2,2,512,128]{3,2,1,0:T(8,128)(2,1)S(1)}, bf16[2,2,512,128]{3,2,1,0:T(8,128)(2,1)S(1)}, u32[]{:S(2)}, u32[]{:S(2)}) collective-permute-start(bf16[2,2,512,128]{3,2,1,0:T(8,128)(2,1)S(1)} %get-tuple-element.10.own_ref), channel_id=1, source_target_pairs={{0,8},{8,16},{16,24},{24,32},{32,40},{40,48},{48,56},{56,64},{64,7... | collective-permute-start | bytes 1572872 | tf_op jit(solution)/shard_map/ppermute | solution.py:286
  10.9 10.7 %collective-permute-done.2.refs_0_.prev_ref = bf16[2,2,512,128]{3,2,1,0:T(8,128)(2,1)S(1)} collective-permute-done((bf16[2,2,512,128]{3,2,1,0:T(8,128)(2,1)S(1)}, bf16[2,2,512,128]{3,2,1,0:T(8,128)(2,1)S(1)}, u32[]{:S(2)}, u32[]{:S(2)}) %collective-permute-start.2) | collective-permute-done | bytes 524320 | tf_op jit(solution)/shard_map/ppermute | solution.py:286
  21.6 1.9 %collective-permute-start.3 = (bf16[2,2,512,128]{3,2,1,0:T(8,128)(2,1)S(1)}, bf16[2,2,512,128]{3,2,1,0:T(8,128)(2,1)S(1)}, u32[]{:S(2)}, u32[]{:S(2)}) collective-permute-start(bf16[2,2,512,128]{3,2,1,0:T(8,128)(2,1)S(1)} %collective-permute-done.2.refs_0_.prev_ref), channel_id=1, source_target_pairs={{0,8},{8,16},{16,24},{24,32},{32,40},{40,48},{48,56},{56,64},{64,7... | collective-permute-start | bytes 1572872 | tf_op jit(solution)/shard_map/ppermute | solution.py:287
  23.5 1.6 %collective-permute-start = (bf16[168,512]{1,0:T(8,128)(2,1)}, bf16[168,512]{1,0:T(8,128)(2,1)S(1)}, u32[]{:S(2)}, u32[]{:S(2)}) collective-permute-start(bf16[168,512]{1,0:T(8,128)(2,1)} %bitcast.21), channel_id=1, source_target_pairs={{0,0},{1,49},{2,66},{3,115},{4,132},{5,181},{6,198},{7,247},{8,8},... | collective-permute-start | bytes 516104 | tf_op jit(solution)/shard_map/ppermute | solution.py:276
  25.1 11.5 %collective-permute-start.1 = (bf16[168,512]{1,0:T(8,128)(2,1)S(1)}, bf16[168,512]{1,0:T(8,128)(2,1)}, u32[]{:S(2)}, u32[]{:S(2)}) collective-permute-start(bf16[168,512]{1,0:T(8,128)(2,1)S(1)} %collective-permute-done), channel_id=1, source_target_pairs={{0,0},{49,48},{66,64},{115,112},{132,128},{181,176},{198,192},{247... | collective-permute-start | bytes 516104 | tf_op jit(solution)/shard_map/ppermute | solution.py:277
  38.1 2.0 %collective-permute-done.1.first_ref = bf16[168,512]{1,0:T(8,128)(2,1)} collective-permute-done((bf16[168,512]{1,0:T(8,128)(2,1)S(1)}, bf16[168,512]{1,0:T(8,128)(2,1)}, u32[]{:S(2)}, u32[]{:S(2)}) %collective-permute-start.1) | collective-permute-done | bytes 172064 | tf_op jit(solution)/shard_map/ppermute | solution.py:277
  40.2 1.5 %attend.7.refs_3_ = bf16[128,512]{1,0:T(8,128)(2,1)S(1)} custom-call(s32[1]{0:T(128)} %bitcast.6.place_ref, bf16[512,512]{1,0:T(8,128)(2,1)S(1)} %rotate.1.refs_2_.q_ref, bf16[2,2,512,128]{3,2,1,0:T(8,128)(2,1)S(1)} %get-tuple-element.10.own_ref, bf16[2,2,512,128]{3,2,1,0:T(8,128)(2,1)S(1)} %collective-permute-done.2.refs_0_.prev_ref, ...), custom_call_target="tpu_custom_call" | custom-call | tf_op jit(solution)/shard_map/attend/pallas_call | solution.py:176
  41.8 1.5 %attend.6.refs_2_ = bf16[128,512]{1,0:T(8,128)(2,1)S(1)} custom-call(s32[1]{0:T(128)} %bitcast.6.place_ref, bf16[512,512]{1,0:T(8,128)(2,1)S(1)} %rotate.1.refs_2_.q_ref, bf16[2,2,512,128]{3,2,1,0:T(8,128)(2,1)S(1)} %get-tuple-element.10.own_ref, bf16[2,2,512,128]{3,2,1,0:T(8,128)(2,1)S(1)} %collective-permute-done.2.refs_0_.prev_ref, ...), custom_call_target="tpu_custom_call" | custom-call | tf_op jit(solution)/shard_map/attend/pallas_call | solution.py:176
  43.3 3.5 %collective-permute-start.6 = (bf16[128,512]{1,0:T(8,128)(2,1)S(1)}, bf16[128,512]{1,0:T(8,128)(2,1)S(1)}, u32[]{:S(2)}, u32[]{:S(2)}) collective-permute-start(bf16[128,512]{1,0:T(8,128)(2,1)S(1)} %attend.6.refs_2_), channel_id=1, source_target_pairs={{0,1},{1,2},{2,3},{3,4},{4,5},{5,6},{6,7},{7,0},{8,15},{9,8},{10,9... | collective-permute-start | bytes 393224 | tf_op jit(solution)/shard_map/ppermute | solution.py:303
  46.8 1.5 %attend.5.refs_1_ = bf16[128,512]{1,0:T(8,128)(2,1)S(1)} custom-call(s32[1]{0:T(128)} %bitcast.6.place_ref, bf16[512,512]{1,0:T(8,128)(2,1)S(1)} %rotate.1.refs_2_.q_ref, bf16[2,2,512,128]{3,2,1,0:T(8,128)(2,1)S(1)} %get-tuple-element.10.own_ref, bf16[2,2,512,128]{3,2,1,0:T(8,128)(2,1)S(1)} %collective-permute-done.2.refs_0_.prev_ref, ...), custom_call_target="tpu_custom_call" | custom-call | tf_op jit(solution)/shard_map/attend/pallas_call | solution.py:176
  48.4 11.6 %collective-permute-start.5 = (bf16[128,512]{1,0:T(8,128)(2,1)S(1)}, bf16[128,512]{1,0:T(8,128)(2,1)S(1)}, u32[]{:S(2)}, u32[]{:S(2)}) collective-permute-start(bf16[128,512]{1,0:T(8,128)(2,1)S(1)} %attend.5.refs_1_), channel_id=1, source_target_pairs={{0,1},{1,2},{2,3},{3,4},{4,5},{5,6},{6,7},{7,0},{8,15},{9,8},{10,9... | collective-permute-start | bytes 393224 | tf_op jit(solution)/shard_map/ppermute | solution.py:303
  59.9 1.5 %attend.4.refs_0_ = bf16[128,512]{1,0:T(8,128)(2,1)S(1)} custom-call(s32[1]{0:T(128)} %bitcast.6.place_ref, bf16[512,512]{1,0:T(8,128)(2,1)S(1)} %rotate.1.refs_2_.q_ref, bf16[2,2,512,128]{3,2,1,0:T(8,128)(2,1)S(1)} %get-tuple-element.10.own_ref, bf16[2,2,512,128]{3,2,1,0:T(8,128)(2,1)S(1)} %collective-permute-done.2.refs_0_.prev_ref, ...), custom_call_target="tpu_custom_call" | custom-call | tf_op jit(solution)/shard_map/attend/pallas_call | solution.py:176
  62.2 1.6 %collective-permute-done.5.refs_5_ = bf16[128,512]{1,0:T(8,128)(2,1)S(1)} collective-permute-done((bf16[128,512]{1,0:T(8,128)(2,1)S(1)}, bf16[128,512]{1,0:T(8,128)(2,1)S(1)}, u32[]{:S(2)}, u32[]{:S(2)}) %collective-permute-start.5) | collective-permute-done | bytes 131104 | tf_op jit(solution)/shard_map/ppermute | solution.py:303
  63.8 4.7 %collective-permute-start.9 = (bf16[128,512]{1,0:T(8,128)(2,1)S(1)}, bf16[128,512]{1,0:T(8,128)(2,1)S(1)}, u32[]{:S(2)}, u32[]{:S(2)}) collective-permute-start(bf16[128,512]{1,0:T(8,128)(2,1)S(1)} %collective-permute-done.5.refs_5_), channel_id=1, source_target_pairs={{0,1},{1,2},{2,3},{3,4},{4,5},{5,6},{6,7},{7,0},{8,15},{9,8},{10,9... | collective-permute-start | bytes 393224 | tf_op jit(solution)/shard_map/ppermute | solution.py:303
  71.9 2.8 %collective-permute-start.13 = (bf16[128,512]{1,0:T(8,128)(2,1)S(1)}, bf16[128,512]{1,0:T(8,128)(2,1)S(1)}, u32[]{:S(2)}, u32[]{:S(2)}) collective-permute-start(bf16[128,512]{1,0:T(8,128)(2,1)S(1)} %collective-permute-done.9.refs_9_), channel_id=1, source_target_pairs={{0,1},{1,2},{2,3},{3,4},{4,5},{5,6},{6,7},{7,0},{8,15},{9,8},{10,9... | collective-permute-start | bytes 393224 | tf_op jit(solution)/shard_map/ppermute | solution.py:303
  79.0 2.0 %collective-permute-start.17 = (bf16[128,512]{1,0:T(8,128)(2,1)S(1)}, bf16[128,512]{1,0:T(8,128)(2,1)S(1)}, u32[]{:S(2)}, u32[]{:S(2)}) collective-permute-start(bf16[128,512]{1,0:T(8,128)(2,1)S(1)} %collective-permute-done.13.refs_13_), channel_id=1, source_target_pairs={{0,1},{1,2},{2,3},{3,4},{4,5},{5,6},{6,7},{7,0},{8,15},{9,8},{10,9... | collective-permute-start | bytes 393224 | tf_op jit(solution)/shard_map/ppermute | solution.py:303
  85.1 2.0 %collective-permute-start.21 = (bf16[128,512]{1,0:T(8,128)(2,1)S(1)}, bf16[128,512]{1,0:T(8,128)(2,1)}, u32[]{:S(2)}, u32[]{:S(2)}) collective-permute-start(bf16[128,512]{1,0:T(8,128)(2,1)S(1)} %collective-permute-done.17.refs_17_), channel_id=1, source_target_pairs={{0,1},{1,2},{2,3},{3,4},{4,5},{5,6},{6,7},{7,0},{8,15},{9,8},{10,9... | collective-permute-start | bytes 393224 | tf_op jit(solution)/shard_map/ppermute | solution.py:303
  91.4 1.9 %collective-permute-start.25 = (bf16[128,512]{1,0:T(8,128)(2,1)}, bf16[128,512]{1,0:T(8,128)(2,1)}, u32[]{:S(2)}, u32[]{:S(2)}) collective-permute-start(bf16[128,512]{1,0:T(8,128)(2,1)} %collective-permute-done.21.refs_21_), channel_id=1, source_target_pairs={{0,1},{1,2},{2,3},{3,4},{4,5},{5,6},{6,7},{7,0},{8,15},{9,8},{10,9... | collective-permute-start | bytes 393224 | tf_op jit(solution)/shard_map/ppermute | solution.py:303
  97.9 1.6 %collective-permute-start.29 = (bf16[128,512]{1,0:T(8,128)(2,1)}, bf16[128,512]{1,0:T(8,128)(2,1)}, u32[]{:S(2)}, u32[]{:S(2)}) collective-permute-start(bf16[128,512]{1,0:T(8,128)(2,1)} %collective-permute-done.25.refs_25_), channel_id=1, source_target_pairs={{0,1},{1,2},{2,3},{3,4},{4,5},{5,6},{6,7},{7,0},{8,15},{9,8},{10,9... | collective-permute-start | bytes 393224 | tf_op jit(solution)/shard_map/ppermute | solution.py:303
  101.3 1.7 %collective-permute-done.30.refs_30_ = bf16[128,512]{1,0:T(8,128)(2,1)} collective-permute-done((bf16[128,512]{1,0:T(8,128)(2,1)}, bf16[128,512]{1,0:T(8,128)(2,1)}, u32[]{:S(2)}, u32[]{:S(2)}) %collective-permute-start.30) | collective-permute-done | bytes 131104 | tf_op jit(solution)/shard_map/ppermute | solution.py:303
  104.4 2.0 %collective-permute-done.28.refs_28_ = bf16[128,512]{1,0:T(8,128)(2,1)} collective-permute-done((bf16[128,512]{1,0:T(8,128)(2,1)}, bf16[128,512]{1,0:T(8,128)(2,1)}, u32[]{:S(2)}, u32[]{:S(2)}) %collective-permute-start.28) | collective-permute-done | bytes 131104 | tf_op jit(solution)/shard_map/ppermute | solution.py:303
  106.6 6.3 %project.1 = (f32[672,512]{1,0:T(8,128)S(1)}, f32[8,1,512]{2,1,0:T(1,128)}) custom-call(s32[2,8]{1,0:T(2,128)S(1)} %pad_add_fusion.order_ref, bf16[8,2,336,512]{3,2,1,0:T(8,128)(2,1)} %bitcast.19, bf16[128,512]{1,0:T(8,128)(2,1)} %copy-done.4, bf16[128,512]{1,0:T(8,128)(2,1)} %copy-done.3, bf16[128,512]{1,0:T(8,128)(2,1)} %copy-done.2, ...), custom_call_target="tpu_custom_call" | custom-call | tf_op jit(solution)/shard_map/project/pallas_call | solution.py:231
  112.9 5.8 %all-to-all-start = ((f32[8,1,512]{2,1,0:T(1,128)}), f32[8,1,512]{2,1,0:T(1,128)S(1)}, u32[]{:S(2)}, u32[]{:S(2)}) async-start(f32[8,1,512]{2,1,0:T(1,128)} %get-tuple-element.14), calls=%async_computation | async-start | bytes 32768 | tf_op jit(solution)/shard_map/all_to_all | solution.py:310
  118.8 7.6 %all-to-all-done.sq_ref = f32[8,1,512]{2,1,0:T(1,128)S(1)} async-done(((f32[8,1,512]{2,1,0:T(1,128)}), f32[8,1,512]{2,1,0:T(1,128)S(1)}, u32[]{:S(2)}, u32[]{:S(2)}) %all-to-all-start) | async-done | bytes 16416 | tf_op jit(solution)/shard_map/all_to_all | solution.py:310
  (109 shorter events, 29.9 us)
Async XLA Ops:
  6.5 99.8 %all-gather.3.cloned.1.call-start = ((), (), s32[]{:S(2)}) async-start(), calls=%async_computation.1 | async-start | bytes 5677056 | tf_op jit(solution)/shard_map/all_gather | solution.py:290
  9.0 12.6 %collective-permute-start.2 = (bf16[2,2,512,128]{3,2,1,0:T(8,128)(2,1)S(1)}, bf16[2,2,512,128]{3,2,1,0:T(8,128)(2,1)S(1)}, u32[]{:S(2)}, u32[]{:S(2)}) collective-permute-start(bf16[2,2,512,128]{3,2,1,0:T(8,128)(2,1)S(1)} %get-tuple-element.10.own_ref), channel_id=1, source_target_pairs={{0,8},{8,16},{16,24},{24,32},{32,40},{40,48},{48,56},{56,64},{64,7... | collective-permute-start | bytes 1572872 | tf_op jit(solution)/shard_map/ppermute | solution.py:286
  21.6 18.5 %collective-permute-start.3 = (bf16[2,2,512,128]{3,2,1,0:T(8,128)(2,1)S(1)}, bf16[2,2,512,128]{3,2,1,0:T(8,128)(2,1)S(1)}, u32[]{:S(2)}, u32[]{:S(2)}) collective-permute-start(bf16[2,2,512,128]{3,2,1,0:T(8,128)(2,1)S(1)} %collective-permute-done.2.refs_0_.prev_ref), channel_id=1, source_target_pairs={{0,8},{8,16},{16,24},{24,32},{32,40},{40,48},{48,56},{56,64},{64,7... | collective-permute-start | bytes 1572872 | tf_op jit(solution)/shard_map/ppermute | solution.py:287
  25.1 15.0 %collective-permute-start.1 = (bf16[168,512]{1,0:T(8,128)(2,1)S(1)}, bf16[168,512]{1,0:T(8,128)(2,1)}, u32[]{:S(2)}, u32[]{:S(2)}) collective-permute-start(bf16[168,512]{1,0:T(8,128)(2,1)S(1)} %collective-permute-done), channel_id=1, source_target_pairs={{0,0},{49,48},{66,64},{115,112},{132,128},{181,176},{198,192},{247... | collective-permute-start | bytes 516104 | tf_op jit(solution)/shard_map/ppermute | solution.py:277
  41.7 19.9 %collective-permute-start.7 = (bf16[128,512]{1,0:T(8,128)(2,1)S(1)}, bf16[128,512]{1,0:T(8,128)(2,1)S(1)}, u32[]{:S(2)}, u32[]{:S(2)}) collective-permute-start(bf16[128,512]{1,0:T(8,128)(2,1)S(1)} %attend.7.refs_3_), channel_id=1, source_target_pairs={{0,1},{1,2},{2,3},{3,4},{4,5},{5,6},{6,7},{7,0},{8,15},{9,8},{10,9... | collective-permute-start | bytes 393224 | tf_op jit(solution)/shard_map/ppermute | solution.py:303
  43.3 18.9 %collective-permute-start.6 = (bf16[128,512]{1,0:T(8,128)(2,1)S(1)}, bf16[128,512]{1,0:T(8,128)(2,1)S(1)}, u32[]{:S(2)}, u32[]{:S(2)}) collective-permute-start(bf16[128,512]{1,0:T(8,128)(2,1)S(1)} %attend.6.refs_2_), channel_id=1, source_target_pairs={{0,1},{1,2},{2,3},{3,4},{4,5},{5,6},{6,7},{7,0},{8,15},{9,8},{10,9... | collective-permute-start | bytes 393224 | tf_op jit(solution)/shard_map/ppermute | solution.py:303
  48.4 15.4 %collective-permute-start.5 = (bf16[128,512]{1,0:T(8,128)(2,1)S(1)}, bf16[128,512]{1,0:T(8,128)(2,1)S(1)}, u32[]{:S(2)}, u32[]{:S(2)}) collective-permute-start(bf16[128,512]{1,0:T(8,128)(2,1)S(1)} %attend.5.refs_1_), channel_id=1, source_target_pairs={{0,1},{1,2},{2,3},{3,4},{4,5},{5,6},{6,7},{7,0},{8,15},{9,8},{10,9... | collective-permute-start | bytes 393224 | tf_op jit(solution)/shard_map/ppermute | solution.py:303
  61.5 7.1 %collective-permute-start.4 = (bf16[128,512]{1,0:T(8,128)(2,1)S(1)}, bf16[128,512]{1,0:T(8,128)(2,1)S(1)}, u32[]{:S(2)}, u32[]{:S(2)}) collective-permute-start(bf16[128,512]{1,0:T(8,128)(2,1)S(1)} %attend.4.refs_0_), channel_id=1, source_target_pairs={{0,1},{1,2},{2,3},{3,4},{4,5},{5,6},{6,7},{7,0},{8,15},{9,8},{10,9... | collective-permute-start | bytes 393224 | tf_op jit(solution)/shard_map/ppermute | solution.py:303
  61.6 7.5 %collective-permute-start.11 = (bf16[128,512]{1,0:T(8,128)(2,1)S(1)}, bf16[128,512]{1,0:T(8,128)(2,1)S(1)}, u32[]{:S(2)}, u32[]{:S(2)}) collective-permute-start(bf16[128,512]{1,0:T(8,128)(2,1)S(1)} %collective-permute-done.7.refs_7_), channel_id=1, source_target_pairs={{0,1},{1,2},{2,3},{3,4},{4,5},{5,6},{6,7},{7,0},{8,15},{9,8},{10,9... | collective-permute-start | bytes 393224 | tf_op jit(solution)/shard_map/ppermute | solution.py:303
  62.2 8.3 %collective-permute-start.10 = (bf16[128,512]{1,0:T(8,128)(2,1)S(1)}, bf16[128,512]{1,0:T(8,128)(2,1)S(1)}, u32[]{:S(2)}, u32[]{:S(2)}) collective-permute-start(bf16[128,512]{1,0:T(8,128)(2,1)S(1)} %collective-permute-done.6.refs_6_), channel_id=1, source_target_pairs={{0,1},{1,2},{2,3},{3,4},{4,5},{5,6},{6,7},{7,0},{8,15},{9,8},{10,9... | collective-permute-start | bytes 393224 | tf_op jit(solution)/shard_map/ppermute | solution.py:303
  63.8 8.1 %collective-permute-start.9 = (bf16[128,512]{1,0:T(8,128)(2,1)S(1)}, bf16[128,512]{1,0:T(8,128)(2,1)S(1)}, u32[]{:S(2)}, u32[]{:S(2)}) collective-permute-start(bf16[128,512]{1,0:T(8,128)(2,1)S(1)} %collective-permute-done.5.refs_5_), channel_id=1, source_target_pairs={{0,1},{1,2},{2,3},{3,4},{4,5},{5,6},{6,7},{7,0},{8,15},{9,8},{10,9... | collective-permute-start | bytes 393224 | tf_op jit(solution)/shard_map/ppermute | solution.py:303
  69.1 7.0 %collective-permute-start.15 = (bf16[128,512]{1,0:T(8,128)(2,1)S(1)}, bf16[128,512]{1,0:T(8,128)(2,1)S(1)}, u32[]{:S(2)}, u32[]{:S(2)}) collective-permute-start(bf16[128,512]{1,0:T(8,128)(2,1)S(1)} %collective-permute-done.11.refs_11_), channel_id=1, source_target_pairs={{0,1},{1,2},{2,3},{3,4},{4,5},{5,6},{6,7},{7,0},{8,15},{9,8},{10,9... | collective-permute-start | bytes 393224 | tf_op jit(solution)/shard_map/ppermute | solution.py:303
  70.5 7.0 %collective-permute-start.14 = (bf16[128,512]{1,0:T(8,128)(2,1)S(1)}, bf16[128,512]{1,0:T(8,128)(2,1)S(1)}, u32[]{:S(2)}, u32[]{:S(2)}) collective-permute-start(bf16[128,512]{1,0:T(8,128)(2,1)S(1)} %collective-permute-done.10.refs_10_), channel_id=1, source_target_pairs={{0,1},{1,2},{2,3},{3,4},{4,5},{5,6},{6,7},{7,0},{8,15},{9,8},{10,9... | collective-permute-start | bytes 393224 | tf_op jit(solution)/shard_map/ppermute | solution.py:303
  71.9 7.0 %collective-permute-start.13 = (bf16[128,512]{1,0:T(8,128)(2,1)S(1)}, bf16[128,512]{1,0:T(8,128)(2,1)S(1)}, u32[]{:S(2)}, u32[]{:S(2)}) collective-permute-start(bf16[128,512]{1,0:T(8,128)(2,1)S(1)} %collective-permute-done.9.refs_9_), channel_id=1, source_target_pairs={{0,1},{1,2},{2,3},{3,4},{4,5},{5,6},{6,7},{7,0},{8,15},{9,8},{10,9... | collective-permute-start | bytes 393224 | tf_op jit(solution)/shard_map/ppermute | solution.py:303
  83.7 6.3 %collective-permute-start.22 = (bf16[128,512]{1,0:T(8,128)(2,1)S(1)}, bf16[128,512]{1,0:T(8,128)(2,1)}, u32[]{:S(2)}, u32[]{:S(2)}) collective-permute-start(bf16[128,512]{1,0:T(8,128)(2,1)S(1)} %collective-permute-done.18.refs_18_), channel_id=1, source_target_pairs={{0,1},{1,2},{2,3},{3,4},{4,5},{5,6},{6,7},{7,0},{8,15},{9,8},{10,9... | collective-permute-start | bytes 393224 | tf_op jit(solution)/shard_map/ppermute | solution.py:303
  85.1 6.3 %collective-permute-start.21 = (bf16[128,512]{1,0:T(8,128)(2,1)S(1)}, bf16[128,512]{1,0:T(8,128)(2,1)}, u32[]{:S(2)}, u32[]{:S(2)}) collective-permute-start(bf16[128,512]{1,0:T(8,128)(2,1)S(1)} %collective-permute-done.17.refs_17_), channel_id=1, source_target_pairs={{0,1},{1,2},{2,3},{3,4},{4,5},{5,6},{6,7},{7,0},{8,15},{9,8},{10,9... | collective-permute-start | bytes 393224 | tf_op jit(solution)/shard_map/ppermute | solution.py:303
  90.0 6.5 %collective-permute-start.26 = (bf16[128,512]{1,0:T(8,128)(2,1)}, bf16[128,512]{1,0:T(8,128)(2,1)}, u32[]{:S(2)}, u32[]{:S(2)}) collective-permute-start(bf16[128,512]{1,0:T(8,128)(2,1)} %collective-permute-done.22.refs_22_), channel_id=1, source_target_pairs={{0,1},{1,2},{2,3},{3,4},{4,5},{5,6},{6,7},{7,0},{8,15},{9,8},{10,9... | collective-permute-start | bytes 393224 | tf_op jit(solution)/shard_map/ppermute | solution.py:303
  91.4 6.5 %collective-permute-start.25 = (bf16[128,512]{1,0:T(8,128)(2,1)}, bf16[128,512]{1,0:T(8,128)(2,1)}, u32[]{:S(2)}, u32[]{:S(2)}) collective-permute-start(bf16[128,512]{1,0:T(8,128)(2,1)} %collective-permute-done.21.refs_21_), channel_id=1, source_target_pairs={{0,1},{1,2},{2,3},{3,4},{4,5},{5,6},{6,7},{7,0},{8,15},{9,8},{10,9... | collective-permute-start | bytes 393224 | tf_op jit(solution)/shard_map/ppermute | solution.py:303
  93.4 6.5 %collective-permute-start.24 = (bf16[128,512]{1,0:T(8,128)(2,1)}, bf16[128,512]{1,0:T(8,128)(2,1)}, u32[]{:S(2)}, u32[]{:S(2)}) collective-permute-start(bf16[128,512]{1,0:T(8,128)(2,1)} %collective-permute-done.20.refs_20_), channel_id=1, source_target_pairs={{0,1},{1,2},{2,3},{3,4},{4,5},{5,6},{6,7},{7,0},{8,15},{9,8},{10,9... | collective-permute-start | bytes 393224 | tf_op jit(solution)/shard_map/ppermute | solution.py:303
  94.8 6.5 %collective-permute-start.31 = (bf16[128,512]{1,0:T(8,128)(2,1)}, bf16[128,512]{1,0:T(8,128)(2,1)}, u32[]{:S(2)}, u32[]{:S(2)}) collective-permute-start(bf16[128,512]{1,0:T(8,128)(2,1)} %collective-permute-done.27.refs_27_), channel_id=1, source_target_pairs={{0,1},{1,2},{2,3},{3,4},{4,5},{5,6},{6,7},{7,0},{8,15},{9,8},{10,9... | collective-permute-start | bytes 393224 | tf_op jit(solution)/shard_map/ppermute | solution.py:303
  96.5 6.5 %collective-permute-start.30 = (bf16[128,512]{1,0:T(8,128)(2,1)}, bf16[128,512]{1,0:T(8,128)(2,1)}, u32[]{:S(2)}, u32[]{:S(2)}) collective-permute-start(bf16[128,512]{1,0:T(8,128)(2,1)} %collective-permute-done.26.refs_26_), channel_id=1, source_target_pairs={{0,1},{1,2},{2,3},{3,4},{4,5},{5,6},{6,7},{7,0},{8,15},{9,8},{10,9... | collective-permute-start | bytes 393224 | tf_op jit(solution)/shard_map/ppermute | solution.py:303
  97.9 6.5 %collective-permute-start.29 = (bf16[128,512]{1,0:T(8,128)(2,1)}, bf16[128,512]{1,0:T(8,128)(2,1)}, u32[]{:S(2)}, u32[]{:S(2)}) collective-permute-start(bf16[128,512]{1,0:T(8,128)(2,1)} %collective-permute-done.25.refs_25_), channel_id=1, source_target_pairs={{0,1},{1,2},{2,3},{3,4},{4,5},{5,6},{6,7},{7,0},{8,15},{9,8},{10,9... | collective-permute-start | bytes 393224 | tf_op jit(solution)/shard_map/ppermute | solution.py:303
  99.9 6.5 %collective-permute-start.28 = (bf16[128,512]{1,0:T(8,128)(2,1)}, bf16[128,512]{1,0:T(8,128)(2,1)}, u32[]{:S(2)}, u32[]{:S(2)}) collective-permute-start(bf16[128,512]{1,0:T(8,128)(2,1)} %collective-permute-done.24.refs_24_), channel_id=1, source_target_pairs={{0,1},{1,2},{2,3},{3,4},{4,5},{5,6},{6,7},{7,0},{8,15},{9,8},{10,9... | collective-permute-start | bytes 393224 | tf_op jit(solution)/shard_map/ppermute | solution.py:303
  112.9 13.5 %all-to-all-start = ((f32[8,1,512]{2,1,0:T(1,128)}), f32[8,1,512]{2,1,0:T(1,128)S(1)}, u32[]{:S(2)}, u32[]{:S(2)}) async-start(f32[8,1,512]{2,1,0:T(1,128)} %get-tuple-element.14), calls=%async_computation | async-start | bytes 32768 | tf_op jit(solution)/shard_map/all_to_all | solution.py:310
  (34 other events, 951.4 us)
Sparse Core Ops, SparseCore 0:
  40.3 60.7 all-gather.2

commit v7 on v5

--- a/solution.py
+++ b/solution.py
@@ -21,6 +21,7 @@
 N_HEAD = 8
 FEATURES = D // N_HEAD
 SHARD = D // N_SEQ
+SIDE = 4
 QB = 256
 WIDTH = KV * GROUP * HEAD_SIZE
 PIECE = 128
@@ -99,22 +100,22 @@
     return lax.dot_general(a, b, (((1,), (1,)), ((), ())), preferred_element_type=jnp.float32)
 
 
-def hold_kernel(first_ref, *refs):
+def hold_kernel(*refs):
     pass
 
 
-def held(array, *others):
+def held(array, after):
     hbm = pl.BlockSpec(memory_space=pltpu.HBM)
-    others = [pltpu.with_memory_space_constraint(x, pltpu.VMEM) for x in others]
+    after = [pltpu.with_memory_space_constraint(x, pltpu.VMEM) for x in after]
     return pl.pallas_call(
         hold_kernel,
-        in_specs=[hbm] + [VMEM] * len(others),
+        in_specs=[hbm] + [VMEM] * len(after),
         out_specs=hbm,
         out_shape=jax.ShapeDtypeStruct(array.shape, array.dtype),
         input_output_aliases={0: 0},
         compiler_params=pltpu.CompilerParams(vmem_limit_bytes=1024 * 1024),
         name="hold",
-    )(array, *others)
+    )(array, *after)
 
 
 def attend_kernel(n, place_ref, q_ref, own_ref, prev_ref, far_ref, out_ref):
@@ -183,25 +184,23 @@
     )(place, *arrays)
 
 
-def project_kernel(order_ref, w_ref, *refs):
+def project_kernel(table_ref, w_ref, *refs):
     ctx_refs = refs[: PIECES * N_HEAD]
-    acc_ref, sq_ref, w_buffer, ctx_buffer, arrived = refs[PIECES * N_HEAD :]
+    acc_ref, sq_ref, w_buffer, ctx_buffer, w_arrived, ctx_arrived = refs[PIECES * N_HEAD :]
     copies = []
     for k in range(N_HEAD):
         copies.append(
             [
                 pltpu.make_async_copy(
-                    w_ref.at[order_ref[0, k], order_ref[1, k] ^ part],
-                    w_buffer.at[k, part],
-                    arrived.at[k, PIECES + part],
+                    w_ref.at[table_ref[2 * k + pair]], w_buffer.at[k, pair], w_arrived.at[k, pair]
                 )
-                for part in range(2)
+                for pair in range(2)
             ]
             + [
                 pltpu.make_async_copy(
                     ctx_refs[k * PIECES + g],
                     ctx_buffer.at[k, g * PIECE : (g + 1) * PIECE],
-                    arrived.at[k, g],
+                    ctx_arrived.at[k, g],
                 )
                 for g in range(PIECES)
             ]
@@ -211,39 +210,38 @@
     for k in range(N_HEAD):
         for copy in copies[k]:
             copy.wait()
-        total = 0.0
-        for part in range(2):
-            rows = slice(part * FEATURES // 2, (part + 1) * FEATURES // 2)
-            value = jnp.dot(w_buffer[k, part], ctx_buffer[k], preferred_element_type=jnp.float32)
-            if k > 0:
-                value = acc_ref[rows] + value
-            acc_ref[rows] = value
-            if k == N_HEAD - 1:
-                total = total + jnp.sum(value * value, axis=0, keepdims=True)
+        value = jnp.dot(
+            w_buffer[k].reshape(FEATURES, WIDTH), ctx_buffer[k], preferred_element_type=jnp.float32
+        )
+        if k > 0:
+            value = acc_ref[...] + value
+        acc_ref[...] = value
         if k == N_HEAD - 1:
+            total = jnp.sum(value * value, axis=0, keepdims=True)
             sq_ref[...] = jnp.broadcast_to(total[None], sq_ref.shape)
 
 
-def project(order, weights, blocks):
+def project(table, weights, blocks):
     hbm = pl.BlockSpec(memory_space=pltpu.HBM)
-    weights = pltpu.with_memory_space_constraint(weights, pltpu.HBM)
-    blocks = [pltpu.with_memory_space_constraint(x, pltpu.HBM) for x in blocks]
+    weights = weights.reshape(SIDE * SIDE, 2, SHARD, WIDTH)
+    arrays = [pltpu.with_memory_space_constraint(x, pltpu.HBM) for x in [weights, *blocks]]
     return pl.pallas_call(
         project_kernel,
-        in_specs=[pl.BlockSpec(memory_space=pltpu.SMEM), hbm] + [hbm] * (PIECES * N_HEAD),
+        in_specs=[pl.BlockSpec(memory_space=pltpu.SMEM)] + [hbm] * len(arrays),
         out_specs=[VMEM, VMEM],
         out_shape=[
             jax.ShapeDtypeStruct((FEATURES, ROWS), jnp.float32),
             jax.ShapeDtypeStruct((N_HEAD, 1, ROWS), jnp.float32),
         ],
         scratch_shapes=[
-            pltpu.VMEM((N_HEAD, 2, FEATURES // 2, WIDTH), jnp.bfloat16),
+            pltpu.VMEM((N_HEAD, 2, 2, SHARD, WIDTH), jnp.bfloat16),
             pltpu.VMEM((N_HEAD, WIDTH, ROWS), jnp.bfloat16),
-            pltpu.SemaphoreType.DMA((N_HEAD, PIECES + 2)),
+            pltpu.SemaphoreType.DMA((N_HEAD, 2)),
+            pltpu.SemaphoreType.DMA((N_HEAD, PIECES)),
         ],
-        compiler_params=pltpu.CompilerParams(vmem_limit_bytes=24 * 1024 * 1024),
+        compiler_params=pltpu.CompilerParams(vmem_limit_bytes=20 * 1024 * 1024),
         name="project",
-    )(order, weights, *blocks)
+    )(table, *arrays)
 
 
 def finish_kernel(acc_ref, sq_ref, gain_ref, res_ref, out_ref):
@@ -263,18 +261,35 @@
     )(attended, squares, gain, residual)
 
 
+def device(x, y, core, head):
+    return ((x % SIDE * SIDE + y % SIDE) * 2 + core) * N_HEAD + head % N_HEAD
+
+
+def moved(array, rule):
+    pairs = [
+        (device(x, y, core, head), device(*rule(x, y, core, head)))
+        for x in range(SIDE)
+        for y in range(SIDE)
+        for core in range(2)
+        for head in range(N_HEAD)
+    ]
+    return lax.ppermute(array, ("seq", "head"), pairs)
+
+
+def sense(core):
+    return 1 - 2 * core
+
+
+def spread(x, y, core, head):
+    low = y // 2 * 2
+    to_y = low + (1 if y % 2 else -1) - head % 2
+    return x + head // 2, to_y, core, 2 * x + y // 2
+
+
 def on_device(positions, queries, keys, values, out_weight, post_gain, residual):
-    seq = lax.axis_index("seq")
-    head = lax.axis_index("head")
-    across, along = [], []
-    for s in range(N_SEQ):
-        for h in range(N_HEAD):
-            group = s // 4
-            middle = (group + h) % N_HEAD * 4 + (s % 4 if (h % 2 == 0) else s % 4 ^ 2)
-            across.append((s * N_HEAD + h, middle * N_HEAD + h))
-            along.append((middle * N_HEAD + h, middle * N_HEAD + group))
-    shard = lax.ppermute(out_weight.T, ("seq", "head"), across)
-    shard = lax.ppermute(shard, ("seq", "head"), along)
+    seq = lax.axis_index("seq").astype(jnp.int32)
+    head = lax.axis_index("head").astype(jnp.int32)
+    shard = moved(out_weight.T, spread)
 
     half = HEAD_SIZE // 2
     inverse = 10000.0 ** (-2.0 * jnp.arange(half, dtype=jnp.float32) / HEAD_SIZE)
@@ -283,31 +298,28 @@
         positions[None], inverse, keys.transpose(1, 0, 2), values.transpose(1, 0, 2)
     )
     onward = [(i, i + 1) for i in range(N_SEQ - 1)]
+    prev = lax.ppermute(own, "seq", onward)
     beyond = [(i, i + 2) for i in range(N_SEQ - 2)]
-    prev = lax.ppermute(own, "seq", onward)
     far = lax.ppermute(own, "seq", beyond)
     q = rotate(queries.reshape(ROWS, WIDTH), cosine, sine)
-    shard = held(shard, prev, far, q)
-    weights = lax.all_gather(shard, "seq", axis=0).reshape(N_HEAD, 2, FEATURES // 2, WIDTH)
-    place = seq.astype(jnp.int32).reshape(1)
-
-    ring = [
-        (s * N_HEAD + h, s * N_HEAD + (h + (1 if s % 2 == 0 else -1)) % N_HEAD)
-        for s in range(N_SEQ)
-        for h in range(N_HEAD)
-    ]
+    shard = held(shard, after=[prev, far, q])
+    weights = lax.all_gather(shard, "seq", axis=0)
+
     blocks = [[] for _ in range(N_HEAD)]
+    place = seq.reshape(1)
     for n in range(PIECES):
         carried = attend(n, place, q, own, prev, far)
         blocks[0].append(carried)
         for k in range(1, N_HEAD):
-            carried = lax.ppermute(carried, ("seq", "head"), ring)
+            carried = moved(carried, lambda x, y, core, head: (x, y, core, head + sense(core)))
             blocks[k].append(carried)
-    sign = jnp.where(seq % 2 == 0, -1, 1)
-    source = head + sign * jnp.arange(N_HEAD, dtype=jnp.int32)
-    source = source % N_HEAD
-    order = jnp.stack([(source + head) % N_HEAD, source % 2]).astype(jnp.int32)
-    attended, squares = project(order, weights, [x for row in blocks for x in row])
+
+    source = (head - sense(seq % 2) * jnp.arange(N_HEAD, dtype=jnp.int32)) % N_HEAD
+    at_x = (head // 2 + source // 2)[:, None] % SIDE
+    at_y = (head % 2 * 2 + jnp.array([-1, 1], jnp.int32)[None, :] - source[:, None] % 2) % SIDE
+    table = (at_x * SIDE + at_y).reshape(-1).astype(jnp.int32)
+
+    attended, squares = project(table, weights, [x for row in blocks for x in row])
     squares = lax.all_to_all(squares, "head", 0, 0, tiled=True)
     return finish(attended, squares, post_gain[:, None], residual.T).T
 

time: 133 us -> 131 us (0.985)
  the two profiles are of different devices: /device:TPU:2 before, /device:TPU:6 now
where the time goes in v7:
time: 131 us; the launch traced here: 130 us
  waiting for transfers between devices  55.5 us (42%)
  starting transfers between devices  42.3 us (32%)
  Pallas kernels  14.9 us (11%)
  between operations  13.8 us (11%)
  local copies, waits for them, and re-layouts  3.38 us (3%)
    ppermute x29, waiting for transfers between devices, moved(): return lax.ppermute(array, ('seq', 'head'), pairs)  45.5 us
    ppermute x29, starting transfers between devices, moved(): return lax.ppermute(array, ('seq', 'head'), pairs)  29.8 us
    all_to_all x1, waiting for transfers between devices, on_device(): squares = lax.all_to_all(squares, 'head', 0, 0, tiled=True)  7.62 us
    all_to_all x1, starting transfers between devices, on_device(): squares = lax.all_to_all(squares, 'head', 0, 0, tiled=True)  7.02 us
    pallas_call x1, Pallas kernels, project(): pl.pallas_call(project_kernel, in_specs=[pl.BlockSpec(memory_space=pltpu....  6.95 us
    pallas_call x4, Pallas kernels, attend(): pl.pallas_call(functools.partial(attend_kernel, n), in_specs=[pl.BlockSpe...  6 us
    ppermute x1, starting transfers between devices, on_device(): far = lax.ppermute(own, 'seq', beyond)  3.48 us
  transfers between devices with their start and end apart: 33, of which 26 were waited for; matrix products, arithmetic and copies ran while one was open for 1% of the time, Pallas kernels for 5%

profile of v7, /device:TPU:6, one launch (start us, length us, event | category | flops | bytes accessed | tf_op | source)
XLA Modules:
  0.0 130.1 jit_solution(17131280090092684978)
XLA Ops:
  9.0 1.9 %collective-permute-start.1 = (bf16[2,2,512,128]{3,2,1,0:T(8,128)(2,1)S(1)}, bf16[2,2,512,128]{3,2,1,0:T(8,128)(2,1)S(1)}, u32[]{:S(2)}, u32[]{:S(2)}) collective-permute-start(bf16[2,2,512,128]{3,2,1,0:T(8,128)(2,1)S(1)} %get-tuple-element.10.own_ref), channel_id=1, source_target_pairs={{0,8},{8,16},{16,24},{24,32},{32,40},{40,48},{48,56},{56,64},{64,7... | collective-permute-start | bytes 1572872 | tf_op jit(solution)/shard_map/ppermute | solution.py:301
  10.9 3.5 %collective-permute-start.2 = (bf16[2,2,512,128]{3,2,1,0:T(8,128)(2,1)S(1)}, bf16[2,2,512,128]{3,2,1,0:T(8,128)(2,1)S(1)}, u32[]{:S(2)}, u32[]{:S(2)}) collective-permute-start(bf16[2,2,512,128]{3,2,1,0:T(8,128)(2,1)S(1)} %get-tuple-element.10.own_ref), channel_id=1, source_target_pairs={{0,16},{8,24},{16,32},{24,40},{32,48},{40,56},{48,64},{56,72},{64,... | collective-permute-start | bytes 1572872 | tf_op jit(solution)/shard_map/ppermute | solution.py:303
  14.4 8.5 %collective-permute-start = (bf16[168,512]{1,0:T(8,128)(2,1)}, bf16[168,512]{1,0:T(8,128)(2,1)}, u32[]{:S(2)}, u32[]{:S(2)}) collective-permute-start(bf16[168,512]{1,0:T(8,128)(2,1)} %bitcast.21), channel_id=1, source_target_pairs={{0,48},{1,32},{2,112},{3,96},{4,176},{5,160},{6,240},{7,224},{8,56... | collective-permute-start | bytes 516104 | tf_op jit(solution)/shard_map/ppermute | solution.py:276
  24.4 11.1 %collective-permute-done.refs_0_ = bf16[168,512]{1,0:T(8,128)(2,1)} collective-permute-done((bf16[168,512]{1,0:T(8,128)(2,1)}, bf16[168,512]{1,0:T(8,128)(2,1)}, u32[]{:S(2)}, u32[]{:S(2)}) %collective-permute-start) | collective-permute-done | bytes 172064 | tf_op jit(solution)/shard_map/ppermute | solution.py:276
  35.5 1.5 %attend.7.refs_3_ = bf16[128,512]{1,0:T(8,128)(2,1)S(1)} custom-call(s32[1]{0:T(128)} %bitcast.6.place_ref, bf16[512,512]{1,0:T(8,128)(2,1)S(1)} %rotate.1.refs_3_.q_ref, bf16[2,2,512,128]{3,2,1,0:T(8,128)(2,1)S(1)} %get-tuple-element.10.own_ref, bf16[2,2,512,128]{3,2,1,0:T(8,128)(2,1)S(1)} %collective-permute-done.1.refs_1_.prev_ref, ...), custom_call_target="tpu_custom_call" | custom-call | tf_op jit(solution)/shard_map/attend/pallas_call | solution.py:177
  37.0 2.4 %collective-permute-start.6 = (bf16[128,512]{1,0:T(8,128)(2,1)S(1)}, bf16[128,512]{1,0:T(8,128)(2,1)S(1)}, u32[]{:S(2)}, u32[]{:S(2)}) collective-permute-start(bf16[128,512]{1,0:T(8,128)(2,1)S(1)} %attend.7.refs_3_), channel_id=1, source_target_pairs={{0,1},{1,2},{2,3},{3,4},{4,5},{5,6},{6,7},{7,0},{8,15},{9,8},{10,9... | collective-permute-start | bytes 393224 | tf_op jit(solution)/shard_map/ppermute | solution.py:276
  39.4 1.5 %attend.6.refs_2_ = bf16[128,512]{1,0:T(8,128)(2,1)S(1)} custom-call(s32[1]{0:T(128)} %bitcast.6.place_ref, bf16[512,512]{1,0:T(8,128)(2,1)S(1)} %rotate.1.refs_3_.q_ref, bf16[2,2,512,128]{3,2,1,0:T(8,128)(2,1)S(1)} %get-tuple-element.10.own_ref, bf16[2,2,512,128]{3,2,1,0:T(8,128)(2,1)S(1)} %collective-permute-done.1.refs_1_.prev_ref, ...), custom_call_target="tpu_custom_call" | custom-call | tf_op jit(solution)/shard_map/attend/pallas_call | solution.py:177
  40.9 1.4 %collective-permute-start.5 = (bf16[128,512]{1,0:T(8,128)(2,1)S(1)}, bf16[128,512]{1,0:T(8,128)(2,1)S(1)}, u32[]{:S(2)}, u32[]{:S(2)}) collective-permute-start(bf16[128,512]{1,0:T(8,128)(2,1)S(1)} %attend.6.refs_2_), channel_id=1, source_target_pairs={{0,1},{1,2},{2,3},{3,4},{4,5},{5,6},{6,7},{7,0},{8,15},{9,8},{10,9... | collective-permute-start | bytes 393224 | tf_op jit(solution)/shard_map/ppermute | solution.py:276
  42.3 1.5 %attend.5.refs_1_ = bf16[128,512]{1,0:T(8,128)(2,1)S(1)} custom-call(s32[1]{0:T(128)} %bitcast.6.place_ref, bf16[512,512]{1,0:T(8,128)(2,1)S(1)} %rotate.1.refs_3_.q_ref, bf16[2,2,512,128]{3,2,1,0:T(8,128)(2,1)S(1)} %get-tuple-element.10.own_ref, bf16[2,2,512,128]{3,2,1,0:T(8,128)(2,1)S(1)} %collective-permute-done.1.refs_1_.prev_ref, ...), custom_call_target="tpu_custom_call" | custom-call | tf_op jit(solution)/shard_map/attend/pallas_call | solution.py:177
  43.8 4.4 %collective-permute-start.4 = (bf16[128,512]{1,0:T(8,128)(2,1)S(1)}, bf16[128,512]{1,0:T(8,128)(2,1)S(1)}, u32[]{:S(2)}, u32[]{:S(2)}) collective-permute-start(bf16[128,512]{1,0:T(8,128)(2,1)S(1)} %attend.5.refs_1_), channel_id=1, source_target_pairs={{0,1},{1,2},{2,3},{3,4},{4,5},{5,6},{6,7},{7,0},{8,15},{9,8},{10,9... | collective-permute-start | bytes 393224 | tf_op jit(solution)/shard_map/ppermute | solution.py:276
  48.2 1.5 %attend.4.refs_0_ = bf16[128,512]{1,0:T(8,128)(2,1)S(1)} custom-call(s32[1]{0:T(128)} %bitcast.6.place_ref, bf16[512,512]{1,0:T(8,128)(2,1)S(1)} %rotate.1.refs_3_.q_ref, bf16[2,2,512,128]{3,2,1,0:T(8,128)(2,1)S(1)} %get-tuple-element.10.own_ref, bf16[2,2,512,128]{3,2,1,0:T(8,128)(2,1)S(1)} %collective-permute-done.1.refs_1_.prev_ref, ...), custom_call_target="tpu_custom_call" | custom-call | tf_op jit(solution)/shard_map/attend/pallas_call | solution.py:177
  49.8 3.6 %collective-permute-start.3 = (bf16[128,512]{1,0:T(8,128)(2,1)S(1)}, bf16[128,512]{1,0:T(8,128)(2,1)S(1)}, u32[]{:S(2)}, u32[]{:S(2)}) collective-permute-start(bf16[128,512]{1,0:T(8,128)(2,1)S(1)} %attend.4.refs_0_), channel_id=1, source_target_pairs={{0,1},{1,2},{2,3},{3,4},{4,5},{5,6},{6,7},{7,0},{8,15},{9,8},{10,9... | collective-permute-start | bytes 393224 | tf_op jit(solution)/shard_map/ppermute | solution.py:276
  53.4 3.8 %collective-permute-start.10 = (bf16[128,512]{1,0:T(8,128)(2,1)S(1)}, bf16[128,512]{1,0:T(8,128)(2,1)S(1)}, u32[]{:S(2)}, u32[]{:S(2)}) collective-permute-start(bf16[128,512]{1,0:T(8,128)(2,1)S(1)} %collective-permute-done.6.refs_7_), channel_id=1, source_target_pairs={{0,1},{1,2},{2,3},{3,4},{4,5},{5,6},{6,7},{7,0},{8,15},{9,8},{10,9... | collective-permute-start | bytes 393224 | tf_op jit(solution)/shard_map/ppermute | solution.py:276
  57.4 2.3 %collective-permute-start.7 = (bf16[128,512]{1,0:T(8,128)(2,1)S(1)}, bf16[128,512]{1,0:T(8,128)(2,1)S(1)}, u32[]{:S(2)}, u32[]{:S(2)}) collective-permute-start(bf16[128,512]{1,0:T(8,128)(2,1)S(1)} %collective-permute-done.3.refs_4_), channel_id=1, source_target_pairs={{0,1},{1,2},{2,3},{3,4},{4,5},{5,6},{6,7},{7,0},{8,15},{9,8},{10,9... | collective-permute-start | bytes 393224 | tf_op jit(solution)/shard_map/ppermute | solution.py:276
  59.7 2.4 %collective-permute-start.14 = (bf16[128,512]{1,0:T(8,128)(2,1)S(1)}, bf16[128,512]{1,0:T(8,128)(2,1)S(1)}, u32[]{:S(2)}, u32[]{:S(2)}) collective-permute-start(bf16[128,512]{1,0:T(8,128)(2,1)S(1)} %collective-permute-done.10.refs_11_), channel_id=1, source_target_pairs={{0,1},{1,2},{2,3},{3,4},{4,5},{5,6},{6,7},{7,0},{8,15},{9,8},{10,9... | collective-permute-start | bytes 393224 | tf_op jit(solution)/shard_map/ppermute | solution.py:276
  67.8 1.8 %collective-permute-done.13.refs_14_ = bf16[128,512]{1,0:T(8,128)(2,1)S(1)} collective-permute-done((bf16[128,512]{1,0:T(8,128)(2,1)S(1)}, bf16[128,512]{1,0:T(8,128)(2,1)S(1)}, u32[]{:S(2)}, u32[]{:S(2)}) %collective-permute-start.13) | collective-permute-done | bytes 131104 | tf_op jit(solution)/shard_map/ppermute | solution.py:276
  73.8 2.0 %collective-permute-done.17.refs_18_ = bf16[128,512]{1,0:T(8,128)(2,1)S(1)} collective-permute-done((bf16[128,512]{1,0:T(8,128)(2,1)S(1)}, bf16[128,512]{1,0:T(8,128)(2,1)S(1)}, u32[]{:S(2)}, u32[]{:S(2)}) %collective-permute-start.17) | collective-permute-done | bytes 131104 | tf_op jit(solution)/shard_map/ppermute | solution.py:276
  80.0 2.1 %collective-permute-done.21.refs_22_ = bf16[128,512]{1,0:T(8,128)(2,1)} collective-permute-done((bf16[128,512]{1,0:T(8,128)(2,1)S(1)}, bf16[128,512]{1,0:T(8,128)(2,1)}, u32[]{:S(2)}, u32[]{:S(2)}) %collective-permute-start.21) | collective-permute-done | bytes 131104 | tf_op jit(solution)/shard_map/ppermute | solution.py:276
  86.2 2.3 %collective-permute-done.25.refs_26_ = bf16[128,512]{1,0:T(8,128)(2,1)} collective-permute-done((bf16[128,512]{1,0:T(8,128)(2,1)}, bf16[128,512]{1,0:T(8,128)(2,1)}, u32[]{:S(2)}, u32[]{:S(2)}) %collective-permute-start.25) | collective-permute-done | bytes 131104 | tf_op jit(solution)/shard_map/ppermute | solution.py:276
  92.7 2.3 %collective-permute-done.29.refs_30_ = bf16[128,512]{1,0:T(8,128)(2,1)} collective-permute-done((bf16[128,512]{1,0:T(8,128)(2,1)}, bf16[128,512]{1,0:T(8,128)(2,1)}, u32[]{:S(2)}, u32[]{:S(2)}) %collective-permute-start.29) | collective-permute-done | bytes 131104 | tf_op jit(solution)/shard_map/ppermute | solution.py:276
  97.8 2.4 %all-gather.3.cloned.1.call-done = bf16[5376,512]{1,0:T(8,128)(2,1)} async-done(((bf16[168,512]{1,0:T(8,128)(2,1)}), bf16[5376,512]{1,0:T(8,128)(2,1)}) %all-gather.3.cloned.1.call-update) | async-done | bytes 5505040 | tf_op jit(solution)/shard_map/all_gather | solution.py:306
  100.4 7.0 %project.1 = (f32[672,512]{1,0:T(8,128)S(1)}, f32[8,1,512]{2,1,0:T(1,128)}) custom-call(s32[16]{0:T(128)S(1)} %fusion.table_ref, bf16[16,2,168,512]{3,2,1,0:T(8,128)(2,1)} %bitcast.19, bf16[128,512]{1,0:T(8,128)(2,1)} %copy-done.4, bf16[128,512]{1,0:T(8,128)(2,1)} %copy-done.3, bf16[128,512]{1,0:T(8,128)(2,1)} %copy-done.2, bf16[128,512]{1,0:T(8,128)(2,1)} %copy-done.1, ...), custom_call_target="tpu_custom_call" | custom-call | tf_op jit(solution)/shard_map/project/pallas_call | solution.py:228
  107.3 7.0 %all-to-all-start = ((f32[8,1,512]{2,1,0:T(1,128)}), f32[8,1,512]{2,1,0:T(1,128)S(1)}, u32[]{:S(2)}, u32[]{:S(2)}) async-start(f32[8,1,512]{2,1,0:T(1,128)} %get-tuple-element.14), calls=%async_computation | async-start | bytes 32768 | tf_op jit(solution)/shard_map/all_to_all | solution.py:323
  114.5 7.6 %all-to-all-done.sq_ref = f32[8,1,512]{2,1,0:T(1,128)S(1)} async-done(((f32[8,1,512]{2,1,0:T(1,128)}), f32[8,1,512]{2,1,0:T(1,128)S(1)}, u32[]{:S(2)}, u32[]{:S(2)}) %all-to-all-start) | async-done | bytes 16416 | tf_op jit(solution)/shard_map/all_to_all | solution.py:323
  (114 shorter events, 30.7 us)
Async XLA Ops:
  6.5 93.6 %all-gather.3.cloned.1.call-start = ((), (), s32[]{:S(2)}) async-start(), calls=%async_computation.1 | async-start | bytes 5677056 | tf_op jit(solution)/shard_map/all_gather | solution.py:306
  9.0 26.4 %collective-permute-start.1 = (bf16[2,2,512,128]{3,2,1,0:T(8,128)(2,1)S(1)}, bf16[2,2,512,128]{3,2,1,0:T(8,128)(2,1)S(1)}, u32[]{:S(2)}, u32[]{:S(2)}) collective-permute-start(bf16[2,2,512,128]{3,2,1,0:T(8,128)(2,1)S(1)} %get-tuple-element.10.own_ref), channel_id=1, source_target_pairs={{0,8},{8,16},{16,24},{24,32},{32,40},{40,48},{48,56},{56,64},{64,7... | collective-permute-start | bytes 1572872 | tf_op jit(solution)/shard_map/ppermute | solution.py:301
  10.9 24.5 %collective-permute-start.2 = (bf16[2,2,512,128]{3,2,1,0:T(8,128)(2,1)S(1)}, bf16[2,2,512,128]{3,2,1,0:T(8,128)(2,1)S(1)}, u32[]{:S(2)}, u32[]{:S(2)}) collective-permute-start(bf16[2,2,512,128]{3,2,1,0:T(8,128)(2,1)S(1)} %get-tuple-element.10.own_ref), channel_id=1, source_target_pairs={{0,16},{8,24},{16,32},{24,40},{32,48},{40,56},{48,64},{56,72},{64,... | collective-permute-start | bytes 1572872 | tf_op jit(solution)/shard_map/ppermute | solution.py:303
  14.4 21.0 %collective-permute-start = (bf16[168,512]{1,0:T(8,128)(2,1)}, bf16[168,512]{1,0:T(8,128)(2,1)}, u32[]{:S(2)}, u32[]{:S(2)}) collective-permute-start(bf16[168,512]{1,0:T(8,128)(2,1)} %bitcast.21), channel_id=1, source_target_pairs={{0,48},{1,32},{2,112},{3,96},{4,176},{5,160},{6,240},{7,224},{8,56... | collective-permute-start | bytes 516104 | tf_op jit(solution)/shard_map/ppermute | solution.py:276
  37.0 16.5 %collective-permute-start.6 = (bf16[128,512]{1,0:T(8,128)(2,1)S(1)}, bf16[128,512]{1,0:T(8,128)(2,1)S(1)}, u32[]{:S(2)}, u32[]{:S(2)}) collective-permute-start(bf16[128,512]{1,0:T(8,128)(2,1)S(1)} %attend.7.refs_3_), channel_id=1, source_target_pairs={{0,1},{1,2},{2,3},{3,4},{4,5},{5,6},{6,7},{7,0},{8,15},{9,8},{10,9... | collective-permute-start | bytes 393224 | tf_op jit(solution)/shard_map/ppermute | solution.py:276
  40.9 16.3 %collective-permute-start.5 = (bf16[128,512]{1,0:T(8,128)(2,1)S(1)}, bf16[128,512]{1,0:T(8,128)(2,1)S(1)}, u32[]{:S(2)}, u32[]{:S(2)}) collective-permute-start(bf16[128,512]{1,0:T(8,128)(2,1)S(1)} %attend.6.refs_2_), channel_id=1, source_target_pairs={{0,1},{1,2},{2,3},{3,4},{4,5},{5,6},{6,7},{7,0},{8,15},{9,8},{10,9... | collective-permute-start | bytes 393224 | tf_op jit(solution)/shard_map/ppermute | solution.py:276
  43.8 13.5 %collective-permute-start.4 = (bf16[128,512]{1,0:T(8,128)(2,1)S(1)}, bf16[128,512]{1,0:T(8,128)(2,1)S(1)}, u32[]{:S(2)}, u32[]{:S(2)}) collective-permute-start(bf16[128,512]{1,0:T(8,128)(2,1)S(1)} %attend.5.refs_1_), channel_id=1, source_target_pairs={{0,1},{1,2},{2,3},{3,4},{4,5},{5,6},{6,7},{7,0},{8,15},{9,8},{10,9... | collective-permute-start | bytes 393224 | tf_op jit(solution)/shard_map/ppermute | solution.py:276
  49.8 7.6 %collective-permute-start.3 = (bf16[128,512]{1,0:T(8,128)(2,1)S(1)}, bf16[128,512]{1,0:T(8,128)(2,1)S(1)}, u32[]{:S(2)}, u32[]{:S(2)}) collective-permute-start(bf16[128,512]{1,0:T(8,128)(2,1)S(1)} %attend.4.refs_0_), channel_id=1, source_target_pairs={{0,1},{1,2},{2,3},{3,4},{4,5},{5,6},{6,7},{7,0},{8,15},{9,8},{10,9... | collective-permute-start | bytes 393224 | tf_op jit(solution)/shard_map/ppermute | solution.py:276
  53.4 6.3 %collective-permute-start.10 = (bf16[128,512]{1,0:T(8,128)(2,1)S(1)}, bf16[128,512]{1,0:T(8,128)(2,1)S(1)}, u32[]{:S(2)}, u32[]{:S(2)}) collective-permute-start(bf16[128,512]{1,0:T(8,128)(2,1)S(1)} %collective-permute-done.6.refs_7_), channel_id=1, source_target_pairs={{0,1},{1,2},{2,3},{3,4},{4,5},{5,6},{6,7},{7,0},{8,15},{9,8},{10,9... | collective-permute-start | bytes 393224 | tf_op jit(solution)/shard_map/ppermute | solution.py:276
  57.3 7.5 %collective-permute-start.8 = (bf16[128,512]{1,0:T(8,128)(2,1)S(1)}, bf16[128,512]{1,0:T(8,128)(2,1)S(1)}, u32[]{:S(2)}, u32[]{:S(2)}) collective-permute-start(bf16[128,512]{1,0:T(8,128)(2,1)S(1)} %collective-permute-done.4.refs_5_), channel_id=1, source_target_pairs={{0,1},{1,2},{2,3},{3,4},{4,5},{5,6},{6,7},{7,0},{8,15},{9,8},{10,9... | collective-permute-start | bytes 393224 | tf_op jit(solution)/shard_map/ppermute | solution.py:276
  57.4 8.8 %collective-permute-start.7 = (bf16[128,512]{1,0:T(8,128)(2,1)S(1)}, bf16[128,512]{1,0:T(8,128)(2,1)S(1)}, u32[]{:S(2)}, u32[]{:S(2)}) collective-permute-start(bf16[128,512]{1,0:T(8,128)(2,1)S(1)} %collective-permute-done.3.refs_4_), channel_id=1, source_target_pairs={{0,1},{1,2},{2,3},{3,4},{4,5},{5,6},{6,7},{7,0},{8,15},{9,8},{10,9... | collective-permute-start | bytes 393224 | tf_op jit(solution)/shard_map/ppermute | solution.py:276
  59.7 7.9 %collective-permute-start.14 = (bf16[128,512]{1,0:T(8,128)(2,1)S(1)}, bf16[128,512]{1,0:T(8,128)(2,1)S(1)}, u32[]{:S(2)}, u32[]{:S(2)}) collective-permute-start(bf16[128,512]{1,0:T(8,128)(2,1)S(1)} %collective-permute-done.10.refs_11_), channel_id=1, source_target_pairs={{0,1},{1,2},{2,3},{3,4},{4,5},{5,6},{6,7},{7,0},{8,15},{9,8},{10,9... | collective-permute-start | bytes 393224 | tf_op jit(solution)/shard_map/ppermute | solution.py:276
  75.7 6.3 %collective-permute-start.21 = (bf16[128,512]{1,0:T(8,128)(2,1)S(1)}, bf16[128,512]{1,0:T(8,128)(2,1)}, u32[]{:S(2)}, u32[]{:S(2)}) collective-permute-start(bf16[128,512]{1,0:T(8,128)(2,1)S(1)} %collective-permute-done.17.refs_18_), channel_id=1, source_target_pairs={{0,1},{1,2},{2,3},{3,4},{4,5},{5,6},{6,7},{7,0},{8,15},{9,8},{10,9... | collective-permute-start | bytes 393224 | tf_op jit(solution)/shard_map/ppermute | solution.py:276
  77.1 6.3 %collective-permute-start.20 = (bf16[128,512]{1,0:T(8,128)(2,1)S(1)}, bf16[128,512]{1,0:T(8,128)(2,1)}, u32[]{:S(2)}, u32[]{:S(2)}) collective-permute-start(bf16[128,512]{1,0:T(8,128)(2,1)S(1)} %collective-permute-done.16.refs_17_), channel_id=1, source_target_pairs={{0,1},{1,2},{2,3},{3,4},{4,5},{5,6},{6,7},{7,0},{8,15},{9,8},{10,9... | collective-permute-start | bytes 393224 | tf_op jit(solution)/shard_map/ppermute | solution.py:276
  78.6 6.3 %collective-permute-start.19 = (bf16[128,512]{1,0:T(8,128)(2,1)S(1)}, bf16[128,512]{1,0:T(8,128)(2,1)}, u32[]{:S(2)}, u32[]{:S(2)}) collective-permute-start(bf16[128,512]{1,0:T(8,128)(2,1)S(1)} %collective-permute-done.15.refs_16_), channel_id=1, source_target_pairs={{0,1},{1,2},{2,3},{3,4},{4,5},{5,6},{6,7},{7,0},{8,15},{9,8},{10,9... | collective-permute-start | bytes 393224 | tf_op jit(solution)/shard_map/ppermute | solution.py:276
  80.0 6.3 %collective-permute-start.26 = (bf16[128,512]{1,0:T(8,128)(2,1)S(1)}, bf16[128,512]{1,0:T(8,128)(2,1)}, u32[]{:S(2)}, u32[]{:S(2)}) collective-permute-start(bf16[128,512]{1,0:T(8,128)(2,1)S(1)} %collective-permute-done.22.refs_23_), channel_id=1, source_target_pairs={{0,1},{1,2},{2,3},{3,4},{4,5},{5,6},{6,7},{7,0},{8,15},{9,8},{10,9... | collective-permute-start | bytes 393224 | tf_op jit(solution)/shard_map/ppermute | solution.py:276
  82.0 6.5 %collective-permute-start.25 = (bf16[128,512]{1,0:T(8,128)(2,1)}, bf16[128,512]{1,0:T(8,128)(2,1)}, u32[]{:S(2)}, u32[]{:S(2)}) collective-permute-start(bf16[128,512]{1,0:T(8,128)(2,1)} %collective-permute-done.21.refs_22_), channel_id=1, source_target_pairs={{0,1},{1,2},{2,3},{3,4},{4,5},{5,6},{6,7},{7,0},{8,15},{9,8},{10,9... | collective-permute-start | bytes 393224 | tf_op jit(solution)/shard_map/ppermute | solution.py:276
  83.4 6.5 %collective-permute-start.24 = (bf16[128,512]{1,0:T(8,128)(2,1)}, bf16[128,512]{1,0:T(8,128)(2,1)}, u32[]{:S(2)}, u32[]{:S(2)}) collective-permute-start(bf16[128,512]{1,0:T(8,128)(2,1)} %collective-permute-done.20.refs_21_), channel_id=1, source_target_pairs={{0,1},{1,2},{2,3},{3,4},{4,5},{5,6},{6,7},{7,0},{8,15},{9,8},{10,9... | collective-permute-start | bytes 393224 | tf_op jit(solution)/shard_map/ppermute | solution.py:276
  84.8 6.5 %collective-permute-start.23 = (bf16[128,512]{1,0:T(8,128)(2,1)}, bf16[128,512]{1,0:T(8,128)(2,1)}, u32[]{:S(2)}, u32[]{:S(2)}) collective-permute-start(bf16[128,512]{1,0:T(8,128)(2,1)} %collective-permute-done.19.refs_20_), channel_id=1, source_target_pairs={{0,1},{1,2},{2,3},{3,4},{4,5},{5,6},{6,7},{7,0},{8,15},{9,8},{10,9... | collective-permute-start | bytes 393224 | tf_op jit(solution)/shard_map/ppermute | solution.py:276
  86.2 6.5 %collective-permute-start.30 = (bf16[128,512]{1,0:T(8,128)(2,1)}, bf16[128,512]{1,0:T(8,128)(2,1)}, u32[]{:S(2)}, u32[]{:S(2)}) collective-permute-start(bf16[128,512]{1,0:T(8,128)(2,1)} %collective-permute-done.26.refs_27_), channel_id=1, source_target_pairs={{0,1},{1,2},{2,3},{3,4},{4,5},{5,6},{6,7},{7,0},{8,15},{9,8},{10,9... | collective-permute-start | bytes 393224 | tf_op jit(solution)/shard_map/ppermute | solution.py:276
  88.5 6.5 %collective-permute-start.29 = (bf16[128,512]{1,0:T(8,128)(2,1)}, bf16[128,512]{1,0:T(8,128)(2,1)}, u32[]{:S(2)}, u32[]{:S(2)}) collective-permute-start(bf16[128,512]{1,0:T(8,128)(2,1)} %collective-permute-done.25.refs_26_), channel_id=1, source_target_pairs={{0,1},{1,2},{2,3},{3,4},{4,5},{5,6},{6,7},{7,0},{8,15},{9,8},{10,9... | collective-permute-start | bytes 393224 | tf_op jit(solution)/shard_map/ppermute | solution.py:276
  89.9 6.5 %collective-permute-start.28 = (bf16[128,512]{1,0:T(8,128)(2,1)}, bf16[128,512]{1,0:T(8,128)(2,1)}, u32[]{:S(2)}, u32[]{:S(2)}) collective-permute-start(bf16[128,512]{1,0:T(8,128)(2,1)} %collective-permute-done.24.refs_25_), channel_id=1, source_target_pairs={{0,1},{1,2},{2,3},{3,4},{4,5},{5,6},{6,7},{7,0},{8,15},{9,8},{10,9... | collective-permute-start | bytes 393224 | tf_op jit(solution)/shard_map/ppermute | solution.py:276
  91.3 6.5 %collective-permute-start.27 = (bf16[128,512]{1,0:T(8,128)(2,1)}, bf16[128,512]{1,0:T(8,128)(2,1)}, u32[]{:S(2)}, u32[]{:S(2)}) collective-permute-start(bf16[128,512]{1,0:T(8,128)(2,1)} %collective-permute-done.23.refs_24_), channel_id=1, source_target_pairs={{0,1},{1,2},{2,3},{3,4},{4,5},{5,6},{6,7},{7,0},{8,15},{9,8},{10,9... | collective-permute-start | bytes 393224 | tf_op jit(solution)/shard_map/ppermute | solution.py:276
  107.3 14.8 %all-to-all-start = ((f32[8,1,512]{2,1,0:T(1,128)}), f32[8,1,512]{2,1,0:T(1,128)S(1)}, u32[]{:S(2)}, u32[]{:S(2)}) async-start(f32[8,1,512]{2,1,0:T(1,128)} %get-tuple-element.14), calls=%async_computation | async-start | bytes 32768 | tf_op jit(solution)/shard_map/all_to_all | solution.py:323
  (34 other events, 1042.3 us)
Sparse Core Ops, SparseCore 0:
  35.6 64.5 all-gather.2

commit v8 on v7

--- a/solution.py
+++ b/solution.py
@@ -104,18 +104,18 @@
     pass
 
 
-def held(array, after):
+def held(array, other, after):
     hbm = pl.BlockSpec(memory_space=pltpu.HBM)
-    after = [pltpu.with_memory_space_constraint(x, pltpu.VMEM) for x in after]
+    other, *after = [pltpu.with_memory_space_constraint(x, pltpu.VMEM) for x in [other, *after]]
     return pl.pallas_call(
         hold_kernel,
-        in_specs=[hbm] + [VMEM] * len(after),
-        out_specs=hbm,
-        out_shape=jax.ShapeDtypeStruct(array.shape, array.dtype),
-        input_output_aliases={0: 0},
+        in_specs=[hbm, VMEM] + [VMEM] * len(after),
+        out_specs=[hbm, VMEM],
+        out_shape=[jax.ShapeDtypeStruct(x.shape, x.dtype) for x in [array, other]],
+        input_output_aliases={0: 0, 1: 1},
         compiler_params=pltpu.CompilerParams(vmem_limit_bytes=1024 * 1024),
         name="hold",
-    )(array, *after)
+    )(array, other, *after)
 
 
 def attend_kernel(n, place_ref, q_ref, own_ref, prev_ref, far_ref, out_ref):
@@ -184,23 +184,18 @@
     )(place, *arrays)
 
 
-def project_kernel(table_ref, w_ref, *refs):
+def project_kernel(order_ref, w_ref, *refs):
     ctx_refs = refs[: PIECES * N_HEAD]
-    acc_ref, sq_ref, w_buffer, ctx_buffer, w_arrived, ctx_arrived = refs[PIECES * N_HEAD :]
+    acc_ref, sq_ref, w_buffer, ctx_buffer, arrived = refs[PIECES * N_HEAD :]
     copies = []
     for k in range(N_HEAD):
         copies.append(
-            [
-                pltpu.make_async_copy(
-                    w_ref.at[table_ref[2 * k + pair]], w_buffer.at[k, pair], w_arrived.at[k, pair]
-                )
-                for pair in range(2)
-            ]
+            [pltpu.make_async_copy(w_ref.at[order_ref[k]], w_buffer.at[k], arrived.at[k, PIECES])]
             + [
                 pltpu.make_async_copy(
                     ctx_refs[k * PIECES + g],
                     ctx_buffer.at[k, g * PIECE : (g + 1) * PIECE],
-                    ctx_arrived.at[k, g],
+                    arrived.at[k, g],
                 )
                 for g in range(PIECES)
             ]
@@ -210,9 +205,7 @@
     for k in range(N_HEAD):
         for copy in copies[k]:
             copy.wait()
-        value = jnp.dot(
-            w_buffer[k].reshape(FEATURES, WIDTH), ctx_buffer[k], preferred_element_type=jnp.float32
-        )
+        value = jnp.dot(w_buffer[k], ctx_buffer[k], preferred_element_type=jnp.float32)
         if k > 0:
             value = acc_ref[...] + value
         acc_ref[...] = value
@@ -221,9 +214,8 @@
             sq_ref[...] = jnp.broadcast_to(total[None], sq_ref.shape)
 
 
-def project(table, weights, blocks):
+def project(order, weights, blocks):
     hbm = pl.BlockSpec(memory_space=pltpu.HBM)
-    weights = weights.reshape(SIDE * SIDE, 2, SHARD, WIDTH)
     arrays = [pltpu.with_memory_space_constraint(x, pltpu.HBM) for x in [weights, *blocks]]
     return pl.pallas_call(
         project_kernel,
@@ -234,14 +226,13 @@
             jax.ShapeDtypeStruct((N_HEAD, 1, ROWS), jnp.float32),
         ],
         scratch_shapes=[
-            pltpu.VMEM((N_HEAD, 2, 2, SHARD, WIDTH), jnp.bfloat16),
+            pltpu.VMEM((N_HEAD, FEATURES, WIDTH), jnp.bfloat16),
             pltpu.VMEM((N_HEAD, WIDTH, ROWS), jnp.bfloat16),
-            pltpu.SemaphoreType.DMA((N_HEAD, 2)),
-            pltpu.SemaphoreType.DMA((N_HEAD, PIECES)),
+            pltpu.SemaphoreType.DMA((N_HEAD, PIECES + 1)),
         ],
         compiler_params=pltpu.CompilerParams(vmem_limit_bytes=20 * 1024 * 1024),
         name="project",
-    )(table, *arrays)
+    )(order, *arrays)
 
 
 def finish_kernel(acc_ref, sq_ref, gain_ref, res_ref, out_ref):
@@ -281,9 +272,9 @@
 
 
 def spread(x, y, core, head):
-    low = y // 2 * 2
-    to_y = low + (1 if y % 2 else -1) - head % 2
-    return x + head // 2, to_y, core, 2 * x + y // 2
+    feature = 2 * x + y // 2
+    group = (feature + head) % N_HEAD
+    return group // 2, group % 2 * 2 + y % 2, core, feature
 
 
 def on_device(positions, queries, keys, values, out_weight, post_gain, residual):
@@ -297,13 +288,12 @@
     own, cosine, sine = prepare(
         positions[None], inverse, keys.transpose(1, 0, 2), values.transpose(1, 0, 2)
     )
-    onward = [(i, i + 1) for i in range(N_SEQ - 1)]
-    prev = lax.ppermute(own, "seq", onward)
-    beyond = [(i, i + 2) for i in range(N_SEQ - 2)]
-    far = lax.ppermute(own, "seq", beyond)
+    far = lax.ppermute(own, "seq", [(i, i + 2) for i in range(N_SEQ - 2)])
     q = rotate(queries.reshape(ROWS, WIDTH), cosine, sine)
-    shard = held(shard, after=[prev, far, q])
-    weights = lax.all_gather(shard, "seq", axis=0)
+    shard, far = held(shard, far, after=[q])
+    given = jnp.where(seq % 2 == 0, own, far)
+    prev = lax.ppermute(given, "seq", [(i, i ^ 1) for i in range(N_SEQ)])
+    weights = lax.all_gather(shard, "seq", axis=0).reshape(N_HEAD, FEATURES, WIDTH)
 
     blocks = [[] for _ in range(N_HEAD)]
     place = seq.reshape(1)
@@ -314,12 +304,9 @@
             carried = moved(carried, lambda x, y, core, head: (x, y, core, head + sense(core)))
             blocks[k].append(carried)
 
-    source = (head - sense(seq % 2) * jnp.arange(N_HEAD, dtype=jnp.int32)) % N_HEAD
-    at_x = (head // 2 + source // 2)[:, None] % SIDE
-    at_y = (head % 2 * 2 + jnp.array([-1, 1], jnp.int32)[None, :] - source[:, None] % 2) % SIDE
-    table = (at_x * SIDE + at_y).reshape(-1).astype(jnp.int32)
-
-    attended, squares = project(table, weights, [x for row in blocks for x in row])
+    source = head - sense(seq % 2) * jnp.arange(N_HEAD, dtype=jnp.int32)
+    order = ((source + head) % N_HEAD).astype(jnp.int32)
+    attended, squares = project(order, weights, [x for row in blocks for x in row])
     squares = lax.all_to_all(squares, "head", 0, 0, tiled=True)
     return finish(attended, squares, post_gain[:, None], residual.T).T
 

time: 131 us -> 126 us (0.962)
  starting transfers between devices: 42.3 us -> 37.2 us
  waiting for transfers between devices: 55.5 us -> 57 us
    all_to_all x1, starting transfers between devices: 7.02 us -> 3.3 us  [on_device(): squares = lax.all_to_all(squares, 'head', 0, 0, tiled=True)]
    all_gather x1, waiting for transfers between devices: 2.35 us -> 0.01 us  [on_device(): lax.all_gather(shard, 'seq', axis=0).reshape(N_HEAD, FEATURES, WIDTH)]
    ppermute x29, waiting for transfers between devices: 45.5 us -> 47.5 us  [moved(): return lax.ppermute(array, ('seq', 'head'), pairs)]
    ppermute x2, waiting for transfers between devices: 0.01 us -> 1.9 us  [the longest x1 1.9 us: on_device(): prev = lax.ppermute(given, 'seq', [(i, i ^ 1) for i in range(N_SEQ)])]
    ppermute x2, starting transfers between devices: 5.41 us -> 3.58 us  [the longest x1 3.48 us: on_device(): far = lax.ppermute(own, 'seq', [(i, i + 2) for i in range(N_SEQ - 2)])]
where the time goes in v8:
time: 126 us
  waiting for transfers between devices  57 us (45%)
  starting transfers between devices  37.2 us (30%)
  Pallas kernels  14.2 us (11%)
  between operations  13.8 us (11%)
  local copies, waits for them, and re-layouts  3.15 us (2%)
    ppermute x29, waiting for transfers between devices, moved(): return lax.ppermute(array, ('seq', 'head'), pairs)  47.5 us
    ppermute x29, starting transfers between devices, moved(): return lax.ppermute(array, ('seq', 'head'), pairs)  30.4 us
    all_to_all x1, waiting for transfers between devices, on_device(): squares = lax.all_to_all(squares, 'head', 0, 0, tiled=True)  7.53 us
    pallas_call x1, Pallas kernels, project(): pl.pallas_call(project_kernel, in_specs=[pl.BlockSpec(memory_space=pltpu....  6.21 us
    pallas_call x4, Pallas kernels, attend(): pl.pallas_call(functools.partial(attend_kernel, n), in_specs=[pl.BlockSpe...  6 us
    ppermute x1, starting transfers between devices, on_device(): far = lax.ppermute(own, 'seq', [(i, i + 2) for i in range(N_SEQ - 2)])  3.48 us
    all_to_all x1, starting transfers between devices, on_device(): squares = lax.all_to_all(squares, 'head', 0, 0, tiled=True)  3.3 us
  transfers between devices with their start and end apart: 33, of which 26 were waited for; matrix products, arithmetic and copies ran while one was open for 1% of the time, Pallas kernels for 5%

profile of v8, /device:TPU:6, one launch (start us, length us, event | category | flops | bytes accessed | tf_op | source)
XLA Modules:
  0.0 125.5 jit_solution(7929111189781456542)
XLA Ops:
  9.0 3.5 %collective-permute-start.1 = (bf16[2,2,512,128]{3,2,1,0:T(8,128)(2,1)S(1)}, bf16[2,2,512,128]{3,2,1,0:T(8,128)(2,1)S(1)}, u32[]{:S(2)}, u32[]{:S(2)}) collective-permute-start(bf16[2,2,512,128]{3,2,1,0:T(8,128)(2,1)S(1)} %get-tuple-element.12.own_ref), channel_id=1, source_target_pairs={{0,16},{8,24},{16,32},{24,40},{32,48},{40,56},{48,64},{56,72},{64,... | collective-permute-start | bytes 1572872 | tf_op jit(solution)/shard_map/ppermute | solution.py:291
  12.5 8.2 %collective-permute-start = (bf16[168,512]{1,0:T(8,128)(2,1)}, bf16[168,512]{1,0:T(8,128)(2,1)}, u32[]{:S(2)}, u32[]{:S(2)}) collective-permute-start(bf16[168,512]{1,0:T(8,128)(2,1)} %bitcast.21), channel_id=1, source_target_pairs={{0,0},{1,32},{2,64},{3,96},{4,128},{5,160},{6,192},{7,224},{8,8},{... | collective-permute-start | bytes 516104 | tf_op jit(solution)/shard_map/ppermute | solution.py:267
  22.2 13.0 %collective-permute-done.refs_0_ = bf16[168,512]{1,0:T(8,128)(2,1)} collective-permute-done((bf16[168,512]{1,0:T(8,128)(2,1)}, bf16[168,512]{1,0:T(8,128)(2,1)}, u32[]{:S(2)}, u32[]{:S(2)}) %collective-permute-start) | collective-permute-done | bytes 172064 | tf_op jit(solution)/shard_map/ppermute | solution.py:267
  35.4 1.9 %collective-permute-done.2.prev_ref = bf16[2,2,512,128]{3,2,1,0:T(8,128)(2,1)S(1)} collective-permute-done((bf16[2,2,512,128]{3,2,1,0:T(8,128)(2,1)S(1)}, bf16[2,2,512,128]{3,2,1,0:T(8,128)(2,1)S(1)}, u32[]{:S(2)}, u32[]{:S(2)}) %collective-permute-start.2) | collective-permute-done | bytes 524320 | tf_op jit(solution)/shard_map/ppermute | solution.py:295
  37.3 1.5 %attend.7.refs_3_ = bf16[128,512]{1,0:T(8,128)(2,1)S(1)} custom-call(s32[1]{0:T(128)} %bitcast.6.place_ref, bf16[512,512]{1,0:T(8,128)(2,1)S(1)} %rotate.1.refs_2_.q_ref, bf16[2,2,512,128]{3,2,1,0:T(8,128)(2,1)S(1)} %get-tuple-element.12.own_ref, bf16[2,2,512,128]{3,2,1,0:T(8,128)(2,1)S(1)} %collective-permute-done.2.prev_ref, ...), custom_call_target="tpu_custom_call" | custom-call | tf_op jit(solution)/shard_map/attend/pallas_call | solution.py:177
  38.9 1.5 %attend.6.refs_2_ = bf16[128,512]{1,0:T(8,128)(2,1)S(1)} custom-call(s32[1]{0:T(128)} %bitcast.6.place_ref, bf16[512,512]{1,0:T(8,128)(2,1)S(1)} %rotate.1.refs_2_.q_ref, bf16[2,2,512,128]{3,2,1,0:T(8,128)(2,1)S(1)} %get-tuple-element.12.own_ref, bf16[2,2,512,128]{3,2,1,0:T(8,128)(2,1)S(1)} %collective-permute-done.2.prev_ref, ...), custom_call_target="tpu_custom_call" | custom-call | tf_op jit(solution)/shard_map/attend/pallas_call | solution.py:177
  40.5 1.5 %attend.5.refs_1_ = bf16[128,512]{1,0:T(8,128)(2,1)S(1)} custom-call(s32[1]{0:T(128)} %bitcast.6.place_ref, bf16[512,512]{1,0:T(8,128)(2,1)S(1)} %rotate.1.refs_2_.q_ref, bf16[2,2,512,128]{3,2,1,0:T(8,128)(2,1)S(1)} %get-tuple-element.12.own_ref, bf16[2,2,512,128]{3,2,1,0:T(8,128)(2,1)S(1)} %collective-permute-done.2.prev_ref, ...), custom_call_target="tpu_custom_call" | custom-call | tf_op jit(solution)/shard_map/attend/pallas_call | solution.py:177
  43.0 1.5 %attend.4.refs_0_ = bf16[128,512]{1,0:T(8,128)(2,1)S(1)} custom-call(s32[1]{0:T(128)} %bitcast.6.place_ref, bf16[512,512]{1,0:T(8,128)(2,1)S(1)} %rotate.1.refs_2_.q_ref, bf16[2,2,512,128]{3,2,1,0:T(8,128)(2,1)S(1)} %get-tuple-element.12.own_ref, bf16[2,2,512,128]{3,2,1,0:T(8,128)(2,1)S(1)} %collective-permute-done.2.prev_ref, ...), custom_call_target="tpu_custom_call" | custom-call | tf_op jit(solution)/shard_map/attend/pallas_call | solution.py:177
  44.5 4.5 %collective-permute-start.3 = (bf16[128,512]{1,0:T(8,128)(2,1)S(1)}, bf16[128,512]{1,0:T(8,128)(2,1)S(1)}, u32[]{:S(2)}, u32[]{:S(2)}) collective-permute-start(bf16[128,512]{1,0:T(8,128)(2,1)S(1)} %attend.4.refs_0_), channel_id=1, source_target_pairs={{0,1},{1,2},{2,3},{3,4},{4,5},{5,6},{6,7},{7,0},{8,15},{9,8},{10,9... | collective-permute-start | bytes 393224 | tf_op jit(solution)/shard_map/ppermute | solution.py:267
  49.1 10.8 %collective-permute-start.10 = (bf16[128,512]{1,0:T(8,128)(2,1)S(1)}, bf16[128,512]{1,0:T(8,128)(2,1)S(1)}, u32[]{:S(2)}, u32[]{:S(2)}) collective-permute-start(bf16[128,512]{1,0:T(8,128)(2,1)S(1)} %collective-permute-done.6.refs_7_), channel_id=1, source_target_pairs={{0,1},{1,2},{2,3},{3,4},{4,5},{5,6},{6,7},{7,0},{8,15},{9,8},{10,9... | collective-permute-start | bytes 393224 | tf_op jit(solution)/shard_map/ppermute | solution.py:267
  60.2 2.1 %collective-permute-start.7 = (bf16[128,512]{1,0:T(8,128)(2,1)S(1)}, bf16[128,512]{1,0:T(8,128)(2,1)S(1)}, u32[]{:S(2)}, u32[]{:S(2)}) collective-permute-start(bf16[128,512]{1,0:T(8,128)(2,1)S(1)} %collective-permute-done.3.refs_4_), channel_id=1, source_target_pairs={{0,1},{1,2},{2,3},{3,4},{4,5},{5,6},{6,7},{7,0},{8,15},{9,8},{10,9... | collective-permute-start | bytes 393224 | tf_op jit(solution)/shard_map/ppermute | solution.py:267
  62.4 2.4 %collective-permute-start.14 = (bf16[128,512]{1,0:T(8,128)(2,1)S(1)}, bf16[128,512]{1,0:T(8,128)(2,1)S(1)}, u32[]{:S(2)}, u32[]{:S(2)}) collective-permute-start(bf16[128,512]{1,0:T(8,128)(2,1)S(1)} %collective-permute-done.10.refs_11_), channel_id=1, source_target_pairs={{0,1},{1,2},{2,3},{3,4},{4,5},{5,6},{6,7},{7,0},{8,15},{9,8},{10,9... | collective-permute-start | bytes 393224 | tf_op jit(solution)/shard_map/ppermute | solution.py:267
  70.4 1.8 %collective-permute-done.13.refs_14_ = bf16[128,512]{1,0:T(8,128)(2,1)S(1)} collective-permute-done((bf16[128,512]{1,0:T(8,128)(2,1)S(1)}, bf16[128,512]{1,0:T(8,128)(2,1)S(1)}, u32[]{:S(2)}, u32[]{:S(2)}) %collective-permute-start.13) | collective-permute-done | bytes 131104 | tf_op jit(solution)/shard_map/ppermute | solution.py:267
  76.4 2.0 %collective-permute-done.17.refs_18_ = bf16[128,512]{1,0:T(8,128)(2,1)S(1)} collective-permute-done((bf16[128,512]{1,0:T(8,128)(2,1)S(1)}, bf16[128,512]{1,0:T(8,128)(2,1)S(1)}, u32[]{:S(2)}, u32[]{:S(2)}) %collective-permute-start.17) | collective-permute-done | bytes 131104 | tf_op jit(solution)/shard_map/ppermute | solution.py:267
  82.6 2.0 %collective-permute-done.21.refs_22_ = bf16[128,512]{1,0:T(8,128)(2,1)S(1)} collective-permute-done((bf16[128,512]{1,0:T(8,128)(2,1)S(1)}, bf16[128,512]{1,0:T(8,128)(2,1)S(1)}, u32[]{:S(2)}, u32[]{:S(2)}) %collective-permute-start.21) | collective-permute-done | bytes 131104 | tf_op jit(solution)/shard_map/ppermute | solution.py:267
  87.4 1.5 %collective-permute-done.26.refs_27_ = bf16[128,512]{1,0:T(8,128)(2,1)} collective-permute-done((bf16[128,512]{1,0:T(8,128)(2,1)S(1)}, bf16[128,512]{1,0:T(8,128)(2,1)}, u32[]{:S(2)}, u32[]{:S(2)}) %collective-permute-start.26) | collective-permute-done | bytes 131104 | tf_op jit(solution)/shard_map/ppermute | solution.py:267
  88.9 2.0 %collective-permute-done.25.refs_26_ = bf16[128,512]{1,0:T(8,128)(2,1)} collective-permute-done((bf16[128,512]{1,0:T(8,128)(2,1)S(1)}, bf16[128,512]{1,0:T(8,128)(2,1)}, u32[]{:S(2)}, u32[]{:S(2)}) %collective-permute-start.25) | collective-permute-done | bytes 131104 | tf_op jit(solution)/shard_map/ppermute | solution.py:267
  93.7 1.7 %collective-permute-done.30.refs_31_ = bf16[128,512]{1,0:T(8,128)(2,1)} collective-permute-done((bf16[128,512]{1,0:T(8,128)(2,1)}, bf16[128,512]{1,0:T(8,128)(2,1)}, u32[]{:S(2)}, u32[]{:S(2)}) %collective-permute-start.30) | collective-permute-done | bytes 131104 | tf_op jit(solution)/shard_map/ppermute | solution.py:267
  95.4 2.0 %collective-permute-done.29.refs_30_ = bf16[128,512]{1,0:T(8,128)(2,1)} collective-permute-done((bf16[128,512]{1,0:T(8,128)(2,1)}, bf16[128,512]{1,0:T(8,128)(2,1)}, u32[]{:S(2)}, u32[]{:S(2)}) %collective-permute-start.29) | collective-permute-done | bytes 131104 | tf_op jit(solution)/shard_map/ppermute | solution.py:267
  97.3 1.4 %collective-permute-done.28.refs_29_ = bf16[128,512]{1,0:T(8,128)(2,1)} collective-permute-done((bf16[128,512]{1,0:T(8,128)(2,1)}, bf16[128,512]{1,0:T(8,128)(2,1)}, u32[]{:S(2)}, u32[]{:S(2)}) %collective-permute-start.28) | collective-permute-done | bytes 131104 | tf_op jit(solution)/shard_map/ppermute | solution.py:267
  98.7 1.4 %collective-permute-done.27.refs_28_ = bf16[128,512]{1,0:T(8,128)(2,1)} collective-permute-done((bf16[128,512]{1,0:T(8,128)(2,1)}, bf16[128,512]{1,0:T(8,128)(2,1)}, u32[]{:S(2)}, u32[]{:S(2)}) %collective-permute-start.27) | collective-permute-done | bytes 131104 | tf_op jit(solution)/shard_map/ppermute | solution.py:267
  100.3 6.2 %project.1 = (f32[672,512]{1,0:T(8,128)S(1)}, f32[8,1,512]{2,1,0:T(1,128)}) custom-call(s32[8]{0:T(128)S(1)} %and_select_fusion.order_ref, bf16[8,672,512]{2,1,0:T(8,128)(2,1)} %bitcast.19, bf16[128,512]{1,0:T(8,128)(2,1)} %copy-done.4, bf16[128,512]{1,0:T(8,128)(2,1)} %copy-done.3, bf16[128,512]{1,0:T(8,128)(2,1)} %copy-done.2, bf16[128,512]{1,0:T(8,128)(2,1)} %copy-done.1, ...), custom_call_target="tpu_custom_call" | custom-call | tf_op jit(solution)/shard_map/project/pallas_call | solution.py:220
  106.6 3.3 %all-to-all-start = ((f32[8,1,512]{2,1,0:T(1,128)}), f32[8,1,512]{2,1,0:T(1,128)S(1)}, u32[]{:S(2)}, u32[]{:S(2)}) async-start(f32[8,1,512]{2,1,0:T(1,128)} %get-tuple-element.18), calls=%async_computation | async-start | bytes 32768 | tf_op jit(solution)/shard_map/all_to_all | solution.py:310
  110.0 7.5 %all-to-all-done.sq_ref = f32[8,1,512]{2,1,0:T(1,128)S(1)} async-done(((f32[8,1,512]{2,1,0:T(1,128)}), f32[8,1,512]{2,1,0:T(1,128)S(1)}, u32[]{:S(2)}, u32[]{:S(2)}) %all-to-all-start) | async-done | bytes 16416 | tf_op jit(solution)/shard_map/all_to_all | solution.py:310
  (113 shorter events, 26.6 us)
Async XLA Ops:
  6.5 93.6 %all-gather.3.cloned.1.call-start = ((), (), s32[]{:S(2)}) async-start(), calls=%async_computation.1 | async-start | bytes 5677056 | tf_op jit(solution)/shard_map/all_gather | solution.py:296
  9.0 26.2 %collective-permute-start.1 = (bf16[2,2,512,128]{3,2,1,0:T(8,128)(2,1)S(1)}, bf16[2,2,512,128]{3,2,1,0:T(8,128)(2,1)S(1)}, u32[]{:S(2)}, u32[]{:S(2)}) collective-permute-start(bf16[2,2,512,128]{3,2,1,0:T(8,128)(2,1)S(1)} %get-tuple-element.12.own_ref), channel_id=1, source_target_pairs={{0,16},{8,24},{16,32},{24,40},{32,48},{40,56},{48,64},{56,72},{64,... | collective-permute-start | bytes 1572872 | tf_op jit(solution)/shard_map/ppermute | solution.py:291
  12.5 22.7 %collective-permute-start = (bf16[168,512]{1,0:T(8,128)(2,1)}, bf16[168,512]{1,0:T(8,128)(2,1)}, u32[]{:S(2)}, u32[]{:S(2)}) collective-permute-start(bf16[168,512]{1,0:T(8,128)(2,1)} %bitcast.21), channel_id=1, source_target_pairs={{0,0},{1,32},{2,64},{3,96},{4,128},{5,160},{6,192},{7,224},{8,8},{... | collective-permute-start | bytes 516104 | tf_op jit(solution)/shard_map/ppermute | solution.py:267
  38.8 10.2 %collective-permute-start.6 = (bf16[128,512]{1,0:T(8,128)(2,1)S(1)}, bf16[128,512]{1,0:T(8,128)(2,1)S(1)}, u32[]{:S(2)}, u32[]{:S(2)}) collective-permute-start(bf16[128,512]{1,0:T(8,128)(2,1)S(1)} %attend.7.refs_3_), channel_id=1, source_target_pairs={{0,1},{1,2},{2,3},{3,4},{4,5},{5,6},{6,7},{7,0},{8,15},{9,8},{10,9... | collective-permute-start | bytes 393224 | tf_op jit(solution)/shard_map/ppermute | solution.py:267
  40.4 19.4 %collective-permute-start.5 = (bf16[128,512]{1,0:T(8,128)(2,1)S(1)}, bf16[128,512]{1,0:T(8,128)(2,1)S(1)}, u32[]{:S(2)}, u32[]{:S(2)}) collective-permute-start(bf16[128,512]{1,0:T(8,128)(2,1)S(1)} %attend.6.refs_2_), channel_id=1, source_target_pairs={{0,1},{1,2},{2,3},{3,4},{4,5},{5,6},{6,7},{7,0},{8,15},{9,8},{10,9... | collective-permute-start | bytes 393224 | tf_op jit(solution)/shard_map/ppermute | solution.py:267
  42.1 17.9 %collective-permute-start.4 = (bf16[128,512]{1,0:T(8,128)(2,1)S(1)}, bf16[128,512]{1,0:T(8,128)(2,1)S(1)}, u32[]{:S(2)}, u32[]{:S(2)}) collective-permute-start(bf16[128,512]{1,0:T(8,128)(2,1)S(1)} %attend.5.refs_1_), channel_id=1, source_target_pairs={{0,1},{1,2},{2,3},{3,4},{4,5},{5,6},{6,7},{7,0},{8,15},{9,8},{10,9... | collective-permute-start | bytes 393224 | tf_op jit(solution)/shard_map/ppermute | solution.py:267
  44.5 15.7 %collective-permute-start.3 = (bf16[128,512]{1,0:T(8,128)(2,1)S(1)}, bf16[128,512]{1,0:T(8,128)(2,1)S(1)}, u32[]{:S(2)}, u32[]{:S(2)}) collective-permute-start(bf16[128,512]{1,0:T(8,128)(2,1)S(1)} %attend.4.refs_0_), channel_id=1, source_target_pairs={{0,1},{1,2},{2,3},{3,4},{4,5},{5,6},{6,7},{7,0},{8,15},{9,8},{10,9... | collective-permute-start | bytes 393224 | tf_op jit(solution)/shard_map/ppermute | solution.py:267
  49.1 13.3 %collective-permute-start.10 = (bf16[128,512]{1,0:T(8,128)(2,1)S(1)}, bf16[128,512]{1,0:T(8,128)(2,1)S(1)}, u32[]{:S(2)}, u32[]{:S(2)}) collective-permute-start(bf16[128,512]{1,0:T(8,128)(2,1)S(1)} %collective-permute-done.6.refs_7_), channel_id=1, source_target_pairs={{0,1},{1,2},{2,3},{3,4},{4,5},{5,6},{6,7},{7,0},{8,15},{9,8},{10,9... | collective-permute-start | bytes 393224 | tf_op jit(solution)/shard_map/ppermute | solution.py:267
  59.8 6.2 %collective-permute-start.9 = (bf16[128,512]{1,0:T(8,128)(2,1)S(1)}, bf16[128,512]{1,0:T(8,128)(2,1)S(1)}, u32[]{:S(2)}, u32[]{:S(2)}) collective-permute-start(bf16[128,512]{1,0:T(8,128)(2,1)S(1)} %collective-permute-done.5.refs_6_), channel_id=1, source_target_pairs={{0,1},{1,2},{2,3},{3,4},{4,5},{5,6},{6,7},{7,0},{8,15},{9,8},{10,9... | collective-permute-start | bytes 393224 | tf_op jit(solution)/shard_map/ppermute | solution.py:267
  59.9 7.5 %collective-permute-start.8 = (bf16[128,512]{1,0:T(8,128)(2,1)S(1)}, bf16[128,512]{1,0:T(8,128)(2,1)S(1)}, u32[]{:S(2)}, u32[]{:S(2)}) collective-permute-start(bf16[128,512]{1,0:T(8,128)(2,1)S(1)} %collective-permute-done.4.refs_5_), channel_id=1, source_target_pairs={{0,1},{1,2},{2,3},{3,4},{4,5},{5,6},{6,7},{7,0},{8,15},{9,8},{10,9... | collective-permute-start | bytes 393224 | tf_op jit(solution)/shard_map/ppermute | solution.py:267
  60.2 8.6 %collective-permute-start.7 = (bf16[128,512]{1,0:T(8,128)(2,1)S(1)}, bf16[128,512]{1,0:T(8,128)(2,1)S(1)}, u32[]{:S(2)}, u32[]{:S(2)}) collective-permute-start(bf16[128,512]{1,0:T(8,128)(2,1)S(1)} %collective-permute-done.3.refs_4_), channel_id=1, source_target_pairs={{0,1},{1,2},{2,3},{3,4},{4,5},{5,6},{6,7},{7,0},{8,15},{9,8},{10,9... | collective-permute-start | bytes 393224 | tf_op jit(solution)/shard_map/ppermute | solution.py:267
  62.4 7.9 %collective-permute-start.14 = (bf16[128,512]{1,0:T(8,128)(2,1)S(1)}, bf16[128,512]{1,0:T(8,128)(2,1)S(1)}, u32[]{:S(2)}, u32[]{:S(2)}) collective-permute-start(bf16[128,512]{1,0:T(8,128)(2,1)S(1)} %collective-permute-done.10.refs_11_), channel_id=1, source_target_pairs={{0,1},{1,2},{2,3},{3,4},{4,5},{5,6},{6,7},{7,0},{8,15},{9,8},{10,9... | collective-permute-start | bytes 393224 | tf_op jit(solution)/shard_map/ppermute | solution.py:267
  66.0 6.2 %collective-permute-start.13 = (bf16[128,512]{1,0:T(8,128)(2,1)S(1)}, bf16[128,512]{1,0:T(8,128)(2,1)S(1)}, u32[]{:S(2)}, u32[]{:S(2)}) collective-permute-start(bf16[128,512]{1,0:T(8,128)(2,1)S(1)} %collective-permute-done.9.refs_10_), channel_id=1, source_target_pairs={{0,1},{1,2},{2,3},{3,4},{4,5},{5,6},{6,7},{7,0},{8,15},{9,8},{10,9... | collective-permute-start | bytes 393224 | tf_op jit(solution)/shard_map/ppermute | solution.py:267
  67.4 6.2 %collective-permute-start.12 = (bf16[128,512]{1,0:T(8,128)(2,1)S(1)}, bf16[128,512]{1,0:T(8,128)(2,1)S(1)}, u32[]{:S(2)}, u32[]{:S(2)}) collective-permute-start(bf16[128,512]{1,0:T(8,128)(2,1)S(1)} %collective-permute-done.8.refs_9_), channel_id=1, source_target_pairs={{0,1},{1,2},{2,3},{3,4},{4,5},{5,6},{6,7},{7,0},{8,15},{9,8},{10,9... | collective-permute-start | bytes 393224 | tf_op jit(solution)/shard_map/ppermute | solution.py:267
  78.4 6.2 %collective-permute-start.21 = (bf16[128,512]{1,0:T(8,128)(2,1)S(1)}, bf16[128,512]{1,0:T(8,128)(2,1)S(1)}, u32[]{:S(2)}, u32[]{:S(2)}) collective-permute-start(bf16[128,512]{1,0:T(8,128)(2,1)S(1)} %collective-permute-done.17.refs_18_), channel_id=1, source_target_pairs={{0,1},{1,2},{2,3},{3,4},{4,5},{5,6},{6,7},{7,0},{8,15},{9,8},{10,9... | collective-permute-start | bytes 393224 | tf_op jit(solution)/shard_map/ppermute | solution.py:267
  82.6 6.3 %collective-permute-start.26 = (bf16[128,512]{1,0:T(8,128)(2,1)S(1)}, bf16[128,512]{1,0:T(8,128)(2,1)}, u32[]{:S(2)}, u32[]{:S(2)}) collective-permute-start(bf16[128,512]{1,0:T(8,128)(2,1)S(1)} %collective-permute-done.22.refs_23_), channel_id=1, source_target_pairs={{0,1},{1,2},{2,3},{3,4},{4,5},{5,6},{6,7},{7,0},{8,15},{9,8},{10,9... | collective-permute-start | bytes 393224 | tf_op jit(solution)/shard_map/ppermute | solution.py:267
  84.6 6.3 %collective-permute-start.25 = (bf16[128,512]{1,0:T(8,128)(2,1)S(1)}, bf16[128,512]{1,0:T(8,128)(2,1)}, u32[]{:S(2)}, u32[]{:S(2)}) collective-permute-start(bf16[128,512]{1,0:T(8,128)(2,1)S(1)} %collective-permute-done.21.refs_22_), channel_id=1, source_target_pairs={{0,1},{1,2},{2,3},{3,4},{4,5},{5,6},{6,7},{7,0},{8,15},{9,8},{10,9... | collective-permute-start | bytes 393224 | tf_op jit(solution)/shard_map/ppermute | solution.py:267
  86.0 6.3 %collective-permute-start.24 = (bf16[128,512]{1,0:T(8,128)(2,1)S(1)}, bf16[128,512]{1,0:T(8,128)(2,1)}, u32[]{:S(2)}, u32[]{:S(2)}) collective-permute-start(bf16[128,512]{1,0:T(8,128)(2,1)S(1)} %collective-permute-done.20.refs_21_), channel_id=1, source_target_pairs={{0,1},{1,2},{2,3},{3,4},{4,5},{5,6},{6,7},{7,0},{8,15},{9,8},{10,9... | collective-permute-start | bytes 393224 | tf_op jit(solution)/shard_map/ppermute | solution.py:267
  87.4 6.3 %collective-permute-start.23 = (bf16[128,512]{1,0:T(8,128)(2,1)S(1)}, bf16[128,512]{1,0:T(8,128)(2,1)}, u32[]{:S(2)}, u32[]{:S(2)}) collective-permute-start(bf16[128,512]{1,0:T(8,128)(2,1)S(1)} %collective-permute-done.19.refs_20_), channel_id=1, source_target_pairs={{0,1},{1,2},{2,3},{3,4},{4,5},{5,6},{6,7},{7,0},{8,15},{9,8},{10,9... | collective-permute-start | bytes 393224 | tf_op jit(solution)/shard_map/ppermute | solution.py:267
  88.9 6.5 %collective-permute-start.30 = (bf16[128,512]{1,0:T(8,128)(2,1)}, bf16[128,512]{1,0:T(8,128)(2,1)}, u32[]{:S(2)}, u32[]{:S(2)}) collective-permute-start(bf16[128,512]{1,0:T(8,128)(2,1)} %collective-permute-done.26.refs_27_), channel_id=1, source_target_pairs={{0,1},{1,2},{2,3},{3,4},{4,5},{5,6},{6,7},{7,0},{8,15},{9,8},{10,9... | collective-permute-start | bytes 393224 | tf_op jit(solution)/shard_map/ppermute | solution.py:267
  90.8 6.5 %collective-permute-start.29 = (bf16[128,512]{1,0:T(8,128)(2,1)}, bf16[128,512]{1,0:T(8,128)(2,1)}, u32[]{:S(2)}, u32[]{:S(2)}) collective-permute-start(bf16[128,512]{1,0:T(8,128)(2,1)} %collective-permute-done.25.refs_26_), channel_id=1, source_target_pairs={{0,1},{1,2},{2,3},{3,4},{4,5},{5,6},{6,7},{7,0},{8,15},{9,8},{10,9... | collective-permute-start | bytes 393224 | tf_op jit(solution)/shard_map/ppermute | solution.py:267
  92.2 6.5 %collective-permute-start.28 = (bf16[128,512]{1,0:T(8,128)(2,1)}, bf16[128,512]{1,0:T(8,128)(2,1)}, u32[]{:S(2)}, u32[]{:S(2)}) collective-permute-start(bf16[128,512]{1,0:T(8,128)(2,1)} %collective-permute-done.24.refs_25_), channel_id=1, source_target_pairs={{0,1},{1,2},{2,3},{3,4},{4,5},{5,6},{6,7},{7,0},{8,15},{9,8},{10,9... | collective-permute-start | bytes 393224 | tf_op jit(solution)/shard_map/ppermute | solution.py:267
  93.7 6.5 %collective-permute-start.27 = (bf16[128,512]{1,0:T(8,128)(2,1)}, bf16[128,512]{1,0:T(8,128)(2,1)}, u32[]{:S(2)}, u32[]{:S(2)}) collective-permute-start(bf16[128,512]{1,0:T(8,128)(2,1)} %collective-permute-done.23.refs_24_), channel_id=1, source_target_pairs={{0,1},{1,2},{2,3},{3,4},{4,5},{5,6},{6,7},{7,0},{8,15},{9,8},{10,9... | collective-permute-start | bytes 393224 | tf_op jit(solution)/shard_map/ppermute | solution.py:267
  106.6 11.0 %all-to-all-start = ((f32[8,1,512]{2,1,0:T(1,128)}), f32[8,1,512]{2,1,0:T(1,128)S(1)}, u32[]{:S(2)}, u32[]{:S(2)}) async-start(f32[8,1,512]{2,1,0:T(1,128)} %get-tuple-element.18), calls=%async_computation | async-start | bytes 32768 | tf_op jit(solution)/shard_map/all_to_all | solution.py:310
  (36 other events, 963.2 us)
Sparse Core Ops, SparseCore 0:
  35.3 58.1 all-gather.2

commit v9 on v8

--- a/solution.py
+++ b/solution.py
@@ -104,81 +104,82 @@
     pass
 
 
-def held(array, other, after):
+def held(array, after):
     hbm = pl.BlockSpec(memory_space=pltpu.HBM)
-    other, *after = [pltpu.with_memory_space_constraint(x, pltpu.VMEM) for x in [other, *after]]
+    after = [pltpu.with_memory_space_constraint(x, pltpu.VMEM) for x in after]
     return pl.pallas_call(
         hold_kernel,
-        in_specs=[hbm, VMEM] + [VMEM] * len(after),
-        out_specs=[hbm, VMEM],
-        out_shape=[jax.ShapeDtypeStruct(x.shape, x.dtype) for x in [array, other]],
-        input_output_aliases={0: 0, 1: 1},
+        in_specs=[hbm] + [VMEM] * len(after),
+        out_specs=hbm,
+        out_shape=jax.ShapeDtypeStruct(array.shape, array.dtype),
+        input_output_aliases={0: 0},
         compiler_params=pltpu.CompilerParams(vmem_limit_bytes=1024 * 1024),
         name="hold",
-    )(array, other, *after)
-
-
-def attend_kernel(n, place_ref, q_ref, own_ref, prev_ref, far_ref, out_ref):
-    g = n // GROUP
+    )(array, *after)
+
+
+def attend_kernel(place_ref, q_ref, own_ref, prev_ref, far_ref, *out_refs):
     place = place_ref[0]
     prev_bias = jnp.where(place >= 1, 0.0, LOW)
     far_bias = jnp.where(place >= 2, 0.0, LOW)
     c = SCALE * LOG2E
-    k_own, k_prev, k_far = own_ref[g, 0], prev_ref[g, 0], far_ref[g, 0]
-    v_own = own_ref[g, 1].T
-    v_prev = prev_ref[g, 1].T
-    v_far = far_ref[g, 1].T
     row = lax.broadcasted_iota(jnp.int32, (QB, QB), 0)
     col = lax.broadcasted_iota(jnp.int32, (QB, QB), 1)
     seen = row <= col
     blocks = ROWS // QB
-    q_all = q_ref[:, n * HEAD_SIZE : (n + 1) * HEAD_SIZE]
-    for b in range(blocks):
-        q = q_all[b * QB : (b + 1) * QB]
-        lo, hi = b * QB, (b + 1) * QB
-        prev = dot_nt(k_prev, q)
-        own = dot_nt(k_own[0:hi], q)
-        far = dot_nt(k_far[lo:ROWS], q)
-        mixed = jnp.where(seen, own[lo:hi], far[0:QB] + far_bias)
-        top = jnp.maximum(
-            jnp.max(prev, axis=0, keepdims=True) + prev_bias,
-            jnp.max(mixed, axis=0, keepdims=True),
-        )
-        if lo > 0:
-            top = jnp.maximum(top, jnp.max(own[0:lo], axis=0, keepdims=True))
-        if hi < ROWS:
-            top = jnp.maximum(top, jnp.max(far[QB:], axis=0, keepdims=True) + far_bias)
-        top = top * c
-        p_prev = jnp.exp2(prev * c - (top - prev_bias))
-        p_mixed = jnp.exp2(mixed * c - top)
-        total = jnp.sum(p_prev, axis=0, keepdims=True) + jnp.sum(p_mixed, axis=0, keepdims=True)
-        own_parts = [jnp.where(seen, p_mixed, 0.0).astype(jnp.bfloat16)]
-        far_parts = [jnp.where(seen, 0.0, p_mixed).astype(jnp.bfloat16)]
-        if lo > 0:
-            p = jnp.exp2(own[0:lo] * c - top)
-            total = total + jnp.sum(p, axis=0, keepdims=True)
-            own_parts.insert(0, p.astype(jnp.bfloat16))
-        if hi < ROWS:
-            p = jnp.exp2(far[QB:] * c - (top - far_bias))
-            total = total + jnp.sum(p, axis=0, keepdims=True)
-            far_parts.append(p.astype(jnp.bfloat16))
-        context = jnp.dot(v_prev, p_prev.astype(jnp.bfloat16), preferred_element_type=jnp.float32)
-        context += jnp.dot(
-            v_own[:, 0:hi], jnp.concatenate(own_parts, 0), preferred_element_type=jnp.float32
-        )
-        context += jnp.dot(
-            v_far[:, lo:], jnp.concatenate(far_parts, 0), preferred_element_type=jnp.float32
-        )
-        out_ref[:, lo:hi] = (context / total).astype(jnp.bfloat16)
-
-
-def attend(n, place, *arrays):
+    for n in range(PIECES):
+        g = n // GROUP
+        k_own, k_prev, k_far = own_ref[g, 0], prev_ref[g, 0], far_ref[g, 0]
+        v_own = own_ref[g, 1].T
+        v_prev = prev_ref[g, 1].T
+        v_far = far_ref[g, 1].T
+        q_all = q_ref[:, n * HEAD_SIZE : (n + 1) * HEAD_SIZE]
+        for b in range(blocks):
+            q = q_all[b * QB : (b + 1) * QB]
+            lo, hi = b * QB, (b + 1) * QB
+            prev = dot_nt(k_prev, q)
+            own = dot_nt(k_own[0:hi], q)
+            far = dot_nt(k_far[lo:ROWS], q)
+            mixed = jnp.where(seen, own[lo:hi], far[0:QB] + far_bias)
+            top = jnp.maximum(
+                jnp.max(prev, axis=0, keepdims=True) + prev_bias,
+                jnp.max(mixed, axis=0, keepdims=True),
+            )
+            if lo > 0:
+                top = jnp.maximum(top, jnp.max(own[0:lo], axis=0, keepdims=True))
+            if hi < ROWS:
+                top = jnp.maximum(top, jnp.max(far[QB:], axis=0, keepdims=True) + far_bias)
+            top = top * c
+            p_prev = jnp.exp2(prev * c - (top - prev_bias))
+            p_mixed = jnp.exp2(mixed * c - top)
+            total = jnp.sum(p_prev, axis=0, keepdims=True) + jnp.sum(p_mixed, axis=0, keepdims=True)
+            own_parts = [jnp.where(seen, p_mixed, 0.0).astype(jnp.bfloat16)]
+            far_parts = [jnp.where(seen, 0.0, p_mixed).astype(jnp.bfloat16)]
+            if lo > 0:
+                p = jnp.exp2(own[0:lo] * c - top)
+                total = total + jnp.sum(p, axis=0, keepdims=True)
+                own_parts.insert(0, p.astype(jnp.bfloat16))
+            if hi < ROWS:
+                p = jnp.exp2(far[QB:] * c - (top - far_bias))
+                total = total + jnp.sum(p, axis=0, keepdims=True)
+                far_parts.append(p.astype(jnp.bfloat16))
+            context = jnp.dot(v_prev, p_prev.astype(jnp.bfloat16), preferred_element_type=jnp.float32)
+            context += jnp.dot(
+                v_own[:, 0:hi], jnp.concatenate(own_parts, 0), preferred_element_type=jnp.float32
+            )
+            context += jnp.dot(
+                v_far[:, lo:], jnp.concatenate(far_parts, 0), preferred_element_type=jnp.float32
+            )
+            out_refs[n][:, lo:hi] = (context / total).astype(jnp.bfloat16)
+
+
+def attend(place, *arrays):
     arrays = [pltpu.with_memory_space_constraint(x, pltpu.VMEM) for x in arrays]
     return pl.pallas_call(
-        functools.partial(attend_kernel, n),
+        attend_kernel,
         in_specs=[pl.BlockSpec(memory_space=pltpu.SMEM)] + [VMEM] * len(arrays),
-        out_specs=VMEM,
-        out_shape=jax.ShapeDtypeStruct((PIECE, ROWS), jnp.bfloat16),
+        out_specs=[VMEM] * PIECES,
+        out_shape=[jax.ShapeDtypeStruct((PIECE, ROWS), jnp.bfloat16)] * PIECES,
         compiler_params=pltpu.CompilerParams(vmem_limit_bytes=16 * 1024 * 1024),
         name="attend",
     )(place, *arrays)
@@ -288,22 +289,20 @@
     own, cosine, sine = prepare(
         positions[None], inverse, keys.transpose(1, 0, 2), values.transpose(1, 0, 2)
     )
+    prev = lax.ppermute(own, "seq", [(i, i + 1) for i in range(N_SEQ - 1)])
     far = lax.ppermute(own, "seq", [(i, i + 2) for i in range(N_SEQ - 2)])
     q = rotate(queries.reshape(ROWS, WIDTH), cosine, sine)
-    shard, far = held(shard, far, after=[q])
-    given = jnp.where(seq % 2 == 0, own, far)
-    prev = lax.ppermute(given, "seq", [(i, i ^ 1) for i in range(N_SEQ)])
-    weights = lax.all_gather(shard, "seq", axis=0).reshape(N_HEAD, FEATURES, WIDTH)
 
     blocks = [[] for _ in range(N_HEAD)]
     place = seq.reshape(1)
-    for n in range(PIECES):
-        carried = attend(n, place, q, own, prev, far)
+    for carried in attend(place, q, own, prev, far):
         blocks[0].append(carried)
         for k in range(1, N_HEAD):
             carried = moved(carried, lambda x, y, core, head: (x, y, core, head + sense(core)))
             blocks[k].append(carried)
 
+    shard = held(shard, after=blocks[0])
+    weights = lax.all_gather(shard, "seq", axis=0).reshape(N_HEAD, FEATURES, WIDTH)
     source = head - sense(seq % 2) * jnp.arange(N_HEAD, dtype=jnp.int32)
     order = ((source + head) % N_HEAD).astype(jnp.int32)
     attended, squares = project(order, weights, [x for row in blocks for x in row])

time: 126 us -> 135 us (1.071)
  starting transfers between devices: 37.2 us -> 77.7 us
  waiting for transfers between devices: 57 us -> 25.6 us
    ppermute x29, waiting for transfers between devices: 47.5 us -> 7.96 us  [moved(): return lax.ppermute(array, ('seq', 'head'), pairs)]
    ppermute x29, starting transfers between devices: 30.4 us -> 65.2 us  [moved(): return lax.ppermute(array, ('seq', 'head'), pairs)]
    ppermute x1, waiting for transfers between devices: 0.01 us -> 5.14 us  [on_device(): far = lax.ppermute(own, 'seq', [(i, i + 2) for i in range(N_SEQ - 2)])]
    all_gather x1, waiting for transfers between devices: 0.01 us -> 4.29 us  [on_device(): lax.all_gather(shard, 'seq', axis=0).reshape(N_HEAD, FEATURES, WIDTH)]
    all_to_all x1, starting transfers between devices: 3.3 us -> 7.02 us  [on_device(): squares = lax.all_to_all(squares, 'head', 0, 0, tiled=True)]
    ppermute x1, starting transfers between devices: 0.09 us -> 1.92 us  [on_device(): prev = lax.ppermute(own, 'seq', [(i, i + 1) for i in range(N_SEQ - 1)])]
    pallas_call x5 -> x2, Pallas kernels: 6 us -> 5.33 us  [the longest x1 5.33 us: attend(): pl.pallas_call(attend_kernel, in_specs=[pl.BlockSpec(memory_space=pltpu.S...]
  transfers between devices with their start and end apart: 33 -> 33, of which waited for: 26 -> 13; matrix products, arithmetic and copies ran while one was open for 1% -> 1% of each run, Pallas kernels for 5% -> 4%
where the time goes in v9:
time: 135 us; the launch traced here: 134 us
  starting transfers between devices  77.7 us (58%)
  waiting for transfers between devices  25.6 us (19%)
  between operations  13.7 us (10%)
  Pallas kernels  13.5 us (10%)
  local copies, waits for them, and re-layouts  3.15 us (2%)
    ppermute x29, starting transfers between devices, moved(): return lax.ppermute(array, ('seq', 'head'), pairs)  65.2 us
    ppermute x29, waiting for transfers between devices, moved(): return lax.ppermute(array, ('seq', 'head'), pairs)  7.96 us
    all_to_all x1, waiting for transfers between devices, on_device(): squares = lax.all_to_all(squares, 'head', 0, 0, tiled=True)  7.62 us
    all_to_all x1, starting transfers between devices, on_device(): squares = lax.all_to_all(squares, 'head', 0, 0, tiled=True)  7.02 us
    pallas_call x1, Pallas kernels, project(): pl.pallas_call(project_kernel, in_specs=[pl.BlockSpec(memory_space=pltpu....  6.21 us
    pallas_call x1, Pallas kernels, attend(): pl.pallas_call(attend_kernel, in_specs=[pl.BlockSpec(memory_space=pltpu.S...  5.33 us
    ppermute x1, waiting for transfers between devices, on_device(): far = lax.ppermute(own, 'seq', [(i, i + 2) for i in range(N_SEQ - 2)])  5.14 us
    all_gather x1, waiting for transfers between devices, on_device(): lax.all_gather(shard, 'seq', axis=0).reshape(N_HEAD, FEATURES, WIDTH)  4.29 us
  transfers between devices with their start and end apart: 33, of which 13 were waited for; matrix products, arithmetic and copies ran while one was open for 1% of the time, Pallas kernels for 4%

profile of v9, /device:TPU:6, one launch (start us, length us, event | category | flops | bytes accessed | tf_op | source)
XLA Modules:
  0.0 133.7 jit_solution(10075704595285914952)
XLA Ops:
  9.0 1.9 %collective-permute-start.1 = (bf16[2,2,512,128]{3,2,1,0:T(8,128)(2,1)S(1)}, bf16[2,2,512,128]{3,2,1,0:T(8,128)(2,1)S(1)}, u32[]{:S(2)}, u32[]{:S(2)}) collective-permute-start(bf16[2,2,512,128]{3,2,1,0:T(8,128)(2,1)S(1)} %get-tuple-element.16.own_ref), channel_id=1, source_target_pairs={{0,8},{8,16},{16,24},{24,32},{32,40},{40,48},{48,56},{56,64},{64,7... | collective-permute-start | bytes 1572872 | tf_op jit(solution)/shard_map/ppermute | solution.py:292
  10.9 3.5 %collective-permute-start.2 = (bf16[2,2,512,128]{3,2,1,0:T(8,128)(2,1)S(1)}, bf16[2,2,512,128]{3,2,1,0:T(8,128)(2,1)S(1)}, u32[]{:S(2)}, u32[]{:S(2)}) collective-permute-start(bf16[2,2,512,128]{3,2,1,0:T(8,128)(2,1)S(1)} %get-tuple-element.16.own_ref), channel_id=1, source_target_pairs={{0,16},{8,24},{16,32},{24,40},{32,48},{40,56},{48,64},{56,72},{64,... | collective-permute-start | bytes 1572872 | tf_op jit(solution)/shard_map/ppermute | solution.py:293
  14.4 8.2 %collective-permute-start = (bf16[168,512]{1,0:T(8,128)(2,1)}, bf16[168,512]{1,0:T(8,128)(2,1)}, u32[]{:S(2)}, u32[]{:S(2)}) collective-permute-start(bf16[168,512]{1,0:T(8,128)(2,1)} %bitcast.21), channel_id=1, source_target_pairs={{0,0},{1,32},{2,64},{3,96},{4,128},{5,160},{6,192},{7,224},{8,8},{... | collective-permute-start | bytes 516104 | tf_op jit(solution)/shard_map/ppermute | solution.py:268
  24.6 5.1 %collective-permute-done.2.far_ref = bf16[2,2,512,128]{3,2,1,0:T(8,128)(2,1)S(1)} collective-permute-done((bf16[2,2,512,128]{3,2,1,0:T(8,128)(2,1)S(1)}, bf16[2,2,512,128]{3,2,1,0:T(8,128)(2,1)S(1)}, u32[]{:S(2)}, u32[]{:S(2)}) %collective-permute-start.2) | collective-permute-done | bytes 524320 | tf_op jit(solution)/shard_map/ppermute | solution.py:293
  29.8 5.3 %attend.1 = (bf16[128,512]{1,0:T(8,128)(2,1)S(1)}, bf16[128,512]{1,0:T(8,128)(2,1)S(1)}, bf16[128,512]{1,0:T(8,128)(2,1)S(1)}, bf16[128,512]{1,0:T(8,128)(2,1)S(1)}) custom-call(s32[1]{0:T(128)} %bitcast.1.place_ref, bf16[512,512]{1,0:T(8,128)(2,1)S(1)} %rotate.1.q_ref, bf16[2,2,512,128]{3,2,1,0:T(8,128)(2,1)S(1)} %get-tuple-element.16.own_ref, ...), custom_call_target="tpu_custom_call" | custom-call | tf_op jit(solution)/shard_map/attend/pallas_call | solution.py:178
  35.2 2.4 %collective-permute-done.refs_0_ = bf16[168,512]{1,0:T(8,128)(2,1)} collective-permute-done((bf16[168,512]{1,0:T(8,128)(2,1)}, bf16[168,512]{1,0:T(8,128)(2,1)}, u32[]{:S(2)}, u32[]{:S(2)}) %collective-permute-start) | collective-permute-done | bytes 172064 | tf_op jit(solution)/shard_map/ppermute | solution.py:268
  39.2 5.6 %collective-permute-start.5 = (bf16[128,512]{1,0:T(8,128)(2,1)S(1)}, bf16[128,512]{1,0:T(8,128)(2,1)S(1)}, u32[]{:S(2)}, u32[]{:S(2)}) collective-permute-start(bf16[128,512]{1,0:T(8,128)(2,1)S(1)} %get-tuple-element.19.refs_3_.refs_2_), channel_id=1, source_target_pairs={{0,1},{1,2},{2,3},{3,4},{4,5},{5,6},{6,7},{7,0},{8,15},{9,8},{10,9... | collective-permute-start | bytes 393224 | tf_op jit(solution)/shard_map/ppermute | solution.py:268
  44.9 15.1 %collective-permute-start.7 = (bf16[128,512]{1,0:T(8,128)(2,1)S(1)}, bf16[128,512]{1,0:T(8,128)(2,1)S(1)}, u32[]{:S(2)}, u32[]{:S(2)}) collective-permute-start(bf16[128,512]{1,0:T(8,128)(2,1)S(1)} %collective-permute-done.3.refs_4_), channel_id=1, source_target_pairs={{0,1},{1,2},{2,3},{3,4},{4,5},{5,6},{6,7},{7,0},{8,15},{9,8},{10,9... | collective-permute-start | bytes 393224 | tf_op jit(solution)/shard_map/ppermute | solution.py:268
  60.2 2.3 %collective-permute-start.10 = (bf16[128,512]{1,0:T(8,128)(2,1)S(1)}, bf16[128,512]{1,0:T(8,128)(2,1)S(1)}, u32[]{:S(2)}, u32[]{:S(2)}) collective-permute-start(bf16[128,512]{1,0:T(8,128)(2,1)S(1)} %collective-permute-done.6.refs_7_), channel_id=1, source_target_pairs={{0,1},{1,2},{2,3},{3,4},{4,5},{5,6},{6,7},{7,0},{8,15},{9,8},{10,9... | collective-permute-start | bytes 393224 | tf_op jit(solution)/shard_map/ppermute | solution.py:268
  62.5 3.6 %collective-permute-start.11 = (bf16[128,512]{1,0:T(8,128)(2,1)S(1)}, bf16[128,512]{1,0:T(8,128)(2,1)S(1)}, u32[]{:S(2)}, u32[]{:S(2)}) collective-permute-start(bf16[128,512]{1,0:T(8,128)(2,1)S(1)} %collective-permute-done.7.refs_8_), channel_id=1, source_target_pairs={{0,1},{1,2},{2,3},{3,4},{4,5},{5,6},{6,7},{7,0},{8,15},{9,8},{10,9... | collective-permute-start | bytes 393224 | tf_op jit(solution)/shard_map/ppermute | solution.py:268
  70.4 2.0 %collective-permute-start.15 = (bf16[128,512]{1,0:T(8,128)(2,1)S(1)}, bf16[128,512]{1,0:T(8,128)(2,1)S(1)}, u32[]{:S(2)}, u32[]{:S(2)}) collective-permute-start(bf16[128,512]{1,0:T(8,128)(2,1)S(1)} %collective-permute-done.11.refs_12_), channel_id=1, source_target_pairs={{0,1},{1,2},{2,3},{3,4},{4,5},{5,6},{6,7},{7,0},{8,15},{9,8},{10,9... | collective-permute-start | bytes 393224 | tf_op jit(solution)/shard_map/ppermute | solution.py:268
  76.6 2.0 %collective-permute-start.19 = (bf16[128,512]{1,0:T(8,128)(2,1)S(1)}, bf16[128,512]{1,0:T(8,128)(2,1)S(1)}, u32[]{:S(2)}, u32[]{:S(2)}) collective-permute-start(bf16[128,512]{1,0:T(8,128)(2,1)S(1)} %collective-permute-done.15.refs_16_), channel_id=1, source_target_pairs={{0,1},{1,2},{2,3},{3,4},{4,5},{5,6},{6,7},{7,0},{8,15},{9,8},{10,9... | collective-permute-start | bytes 393224 | tf_op jit(solution)/shard_map/ppermute | solution.py:268
  79.9 1.4 %collective-permute-start.21 = (bf16[128,512]{1,0:T(8,128)(2,1)S(1)}, bf16[128,512]{1,0:T(8,128)(2,1)S(1)}, u32[]{:S(2)}, u32[]{:S(2)}) collective-permute-start(bf16[128,512]{1,0:T(8,128)(2,1)S(1)} %collective-permute-done.17.refs_18_), channel_id=1, source_target_pairs={{0,1},{1,2},{2,3},{3,4},{4,5},{5,6},{6,7},{7,0},{8,15},{9,8},{10,9... | collective-permute-start | bytes 393224 | tf_op jit(solution)/shard_map/ppermute | solution.py:268
  81.3 1.4 %collective-permute-start.22 = (bf16[128,512]{1,0:T(8,128)(2,1)S(1)}, bf16[128,512]{1,0:T(8,128)(2,1)S(1)}, u32[]{:S(2)}, u32[]{:S(2)}) collective-permute-start(bf16[128,512]{1,0:T(8,128)(2,1)S(1)} %collective-permute-done.18.refs_19_), channel_id=1, source_target_pairs={{0,1},{1,2},{2,3},{3,4},{4,5},{5,6},{6,7},{7,0},{8,15},{9,8},{10,9... | collective-permute-start | bytes 393224 | tf_op jit(solution)/shard_map/ppermute | solution.py:268
  82.7 2.0 %collective-permute-start.23 = (bf16[128,512]{1,0:T(8,128)(2,1)S(1)}, bf16[128,512]{1,0:T(8,128)(2,1)}, u32[]{:S(2)}, u32[]{:S(2)}) collective-permute-start(bf16[128,512]{1,0:T(8,128)(2,1)S(1)} %collective-permute-done.19.refs_20_), channel_id=1, source_target_pairs={{0,1},{1,2},{2,3},{3,4},{4,5},{5,6},{6,7},{7,0},{8,15},{9,8},{10,9... | collective-permute-start | bytes 393224 | tf_op jit(solution)/shard_map/ppermute | solution.py:268
  86.1 1.4 %collective-permute-start.25 = (bf16[128,512]{1,0:T(8,128)(2,1)S(1)}, bf16[128,512]{1,0:T(8,128)(2,1)}, u32[]{:S(2)}, u32[]{:S(2)}) collective-permute-start(bf16[128,512]{1,0:T(8,128)(2,1)S(1)} %collective-permute-done.21.refs_22_), channel_id=1, source_target_pairs={{0,1},{1,2},{2,3},{3,4},{4,5},{5,6},{6,7},{7,0},{8,15},{9,8},{10,9... | collective-permute-start | bytes 393224 | tf_op jit(solution)/shard_map/ppermute | solution.py:268
  89.0 1.9 %collective-permute-start.27 = (bf16[128,512]{1,0:T(8,128)(2,1)}, bf16[128,512]{1,0:T(8,128)(2,1)}, u32[]{:S(2)}, u32[]{:S(2)}) collective-permute-start(bf16[128,512]{1,0:T(8,128)(2,1)} %collective-permute-done.23.refs_24_), channel_id=1, source_target_pairs={{0,1},{1,2},{2,3},{3,4},{4,5},{5,6},{6,7},{7,0},{8,15},{9,8},{10,9... | collective-permute-start | bytes 393224 | tf_op jit(solution)/shard_map/ppermute | solution.py:268
  95.5 2.0 %collective-permute-done.28.refs_29_ = bf16[128,512]{1,0:T(8,128)(2,1)} collective-permute-done((bf16[128,512]{1,0:T(8,128)(2,1)}, bf16[128,512]{1,0:T(8,128)(2,1)}, u32[]{:S(2)}, u32[]{:S(2)}) %collective-permute-start.28) | collective-permute-done | bytes 131104 | tf_op jit(solution)/shard_map/ppermute | solution.py:268
  97.5 1.4 %collective-permute-done.29.refs_30_ = bf16[128,512]{1,0:T(8,128)(2,1)} collective-permute-done((bf16[128,512]{1,0:T(8,128)(2,1)}, bf16[128,512]{1,0:T(8,128)(2,1)}, u32[]{:S(2)}, u32[]{:S(2)}) %collective-permute-start.29) | collective-permute-done | bytes 131104 | tf_op jit(solution)/shard_map/ppermute | solution.py:268
  98.9 1.4 %collective-permute-done.30.refs_31_ = bf16[128,512]{1,0:T(8,128)(2,1)} collective-permute-done((bf16[128,512]{1,0:T(8,128)(2,1)}, bf16[128,512]{1,0:T(8,128)(2,1)}, u32[]{:S(2)}, u32[]{:S(2)}) %collective-permute-start.30) | collective-permute-done | bytes 131104 | tf_op jit(solution)/shard_map/ppermute | solution.py:268
  100.3 4.3 %all-gather.3.cloned.1.call-done = bf16[5376,512]{1,0:T(8,128)(2,1)} async-done(((bf16[168,512]{1,0:T(8,128)(2,1)}), bf16[5376,512]{1,0:T(8,128)(2,1)}) %all-gather.3.cloned.1.call-update) | async-done | bytes 5505040 | tf_op jit(solution)/shard_map/all_gather | solution.py:305
  104.8 6.2 %project.1 = (f32[672,512]{1,0:T(8,128)S(1)}, f32[8,1,512]{2,1,0:T(1,128)}) custom-call(s32[8]{0:T(128)S(1)} %and_select_fusion.order_ref, bf16[8,672,512]{2,1,0:T(8,128)(2,1)} %bitcast.19, bf16[128,512]{1,0:T(8,128)(2,1)} %copy-done.1, bf16[128,512]{1,0:T(8,128)(2,1)} %copy-done.2, bf16[128,512]{1,0:T(8,128)(2,1)} %copy-done.3, bf16[128,512]{1,0:T(8,128)(2,1)} %copy-done.4, ...), custom_call_target="tpu_custom_call" | custom-call | tf_op jit(solution)/shard_map/project/pallas_call | solution.py:221
  111.0 7.0 %all-to-all-start = ((f32[8,1,512]{2,1,0:T(1,128)}), f32[8,1,512]{2,1,0:T(1,128)S(1)}, u32[]{:S(2)}, u32[]{:S(2)}) async-start(f32[8,1,512]{2,1,0:T(1,128)} %get-tuple-element.22), calls=%async_computation | async-start | bytes 32768 | tf_op jit(solution)/shard_map/all_to_all | solution.py:309
  118.2 7.6 %all-to-all-done.sq_ref = f32[8,1,512]{2,1,0:T(1,128)S(1)} async-done(((f32[8,1,512]{2,1,0:T(1,128)}), f32[8,1,512]{2,1,0:T(1,128)S(1)}, u32[]{:S(2)}, u32[]{:S(2)}) %all-to-all-start) | async-done | bytes 16416 | tf_op jit(solution)/shard_map/all_to_all | solution.py:309
  (109 shorter events, 25.0 us)
Async XLA Ops:
  6.5 98.1 %all-gather.3.cloned.1.call-start = ((), (), s32[]{:S(2)}) async-start(), calls=%async_computation.1 | async-start | bytes 5677056 | tf_op jit(solution)/shard_map/all_gather | solution.py:305
  9.0 15.7 %collective-permute-start.1 = (bf16[2,2,512,128]{3,2,1,0:T(8,128)(2,1)S(1)}, bf16[2,2,512,128]{3,2,1,0:T(8,128)(2,1)S(1)}, u32[]{:S(2)}, u32[]{:S(2)}) collective-permute-start(bf16[2,2,512,128]{3,2,1,0:T(8,128)(2,1)S(1)} %get-tuple-element.16.own_ref), channel_id=1, source_target_pairs={{0,8},{8,16},{16,24},{24,32},{32,40},{40,48},{48,56},{56,64},{64,7... | collective-permute-start | bytes 1572872 | tf_op jit(solution)/shard_map/ppermute | solution.py:292
  10.9 18.9 %collective-permute-start.2 = (bf16[2,2,512,128]{3,2,1,0:T(8,128)(2,1)S(1)}, bf16[2,2,512,128]{3,2,1,0:T(8,128)(2,1)S(1)}, u32[]{:S(2)}, u32[]{:S(2)}) collective-permute-start(bf16[2,2,512,128]{3,2,1,0:T(8,128)(2,1)S(1)} %get-tuple-element.16.own_ref), channel_id=1, source_target_pairs={{0,16},{8,24},{16,32},{24,40},{32,48},{40,56},{48,64},{56,72},{64,... | collective-permute-start | bytes 1572872 | tf_op jit(solution)/shard_map/ppermute | solution.py:293
  14.4 23.2 %collective-permute-start = (bf16[168,512]{1,0:T(8,128)(2,1)}, bf16[168,512]{1,0:T(8,128)(2,1)}, u32[]{:S(2)}, u32[]{:S(2)}) collective-permute-start(bf16[168,512]{1,0:T(8,128)(2,1)} %bitcast.21), channel_id=1, source_target_pairs={{0,0},{1,32},{2,64},{3,96},{4,128},{5,160},{6,192},{7,224},{8,8},{... | collective-permute-start | bytes 516104 | tf_op jit(solution)/shard_map/ppermute | solution.py:268
  37.6 7.2 %collective-permute-start.3 = (bf16[128,512]{1,0:T(8,128)(2,1)S(1)}, bf16[128,512]{1,0:T(8,128)(2,1)S(1)}, u32[]{:S(2)}, u32[]{:S(2)}) collective-permute-start(bf16[128,512]{1,0:T(8,128)(2,1)S(1)} %get-tuple-element.17.refs_1_.refs_0_), channel_id=1, source_target_pairs={{0,1},{1,2},{2,3},{3,4},{4,5},{5,6},{6,7},{7,0},{8,15},{9,8},{10,9... | collective-permute-start | bytes 393224 | tf_op jit(solution)/shard_map/ppermute | solution.py:268
  38.1 21.9 %collective-permute-start.4 = (bf16[128,512]{1,0:T(8,128)(2,1)S(1)}, bf16[128,512]{1,0:T(8,128)(2,1)S(1)}, u32[]{:S(2)}, u32[]{:S(2)}) collective-permute-start(bf16[128,512]{1,0:T(8,128)(2,1)S(1)} %get-tuple-element.18.refs_2_.refs_1_), channel_id=1, source_target_pairs={{0,1},{1,2},{2,3},{3,4},{4,5},{5,6},{6,7},{7,0},{8,15},{9,8},{10,9... | collective-permute-start | bytes 393224 | tf_op jit(solution)/shard_map/ppermute | solution.py:268
  39.2 20.9 %collective-permute-start.5 = (bf16[128,512]{1,0:T(8,128)(2,1)S(1)}, bf16[128,512]{1,0:T(8,128)(2,1)S(1)}, u32[]{:S(2)}, u32[]{:S(2)}) collective-permute-start(bf16[128,512]{1,0:T(8,128)(2,1)S(1)} %get-tuple-element.19.refs_3_.refs_2_), channel_id=1, source_target_pairs={{0,1},{1,2},{2,3},{3,4},{4,5},{5,6},{6,7},{7,0},{8,15},{9,8},{10,9... | collective-permute-start | bytes 393224 | tf_op jit(solution)/shard_map/ppermute | solution.py:268
  44.8 15.4 %collective-permute-start.6 = (bf16[128,512]{1,0:T(8,128)(2,1)S(1)}, bf16[128,512]{1,0:T(8,128)(2,1)S(1)}, u32[]{:S(2)}, u32[]{:S(2)}) collective-permute-start(bf16[128,512]{1,0:T(8,128)(2,1)S(1)} %get-tuple-element.20.refs_4_.refs_3_), channel_id=1, source_target_pairs={{0,1},{1,2},{2,3},{3,4},{4,5},{5,6},{6,7},{7,0},{8,15},{9,8},{10,9... | collective-permute-start | bytes 393224 | tf_op jit(solution)/shard_map/ppermute | solution.py:268
  44.9 17.7 %collective-permute-start.7 = (bf16[128,512]{1,0:T(8,128)(2,1)S(1)}, bf16[128,512]{1,0:T(8,128)(2,1)S(1)}, u32[]{:S(2)}, u32[]{:S(2)}) collective-permute-start(bf16[128,512]{1,0:T(8,128)(2,1)S(1)} %collective-permute-done.3.refs_4_), channel_id=1, source_target_pairs={{0,1},{1,2},{2,3},{3,4},{4,5},{5,6},{6,7},{7,0},{8,15},{9,8},{10,9... | collective-permute-start | bytes 393224 | tf_op jit(solution)/shard_map/ppermute | solution.py:268
  60.0 6.2 %collective-permute-start.8 = (bf16[128,512]{1,0:T(8,128)(2,1)S(1)}, bf16[128,512]{1,0:T(8,128)(2,1)S(1)}, u32[]{:S(2)}, u32[]{:S(2)}) collective-permute-start(bf16[128,512]{1,0:T(8,128)(2,1)S(1)} %collective-permute-done.4.refs_5_), channel_id=1, source_target_pairs={{0,1},{1,2},{2,3},{3,4},{4,5},{5,6},{6,7},{7,0},{8,15},{9,8},{10,9... | collective-permute-start | bytes 393224 | tf_op jit(solution)/shard_map/ppermute | solution.py:268
  60.1 7.5 %collective-permute-start.9 = (bf16[128,512]{1,0:T(8,128)(2,1)S(1)}, bf16[128,512]{1,0:T(8,128)(2,1)S(1)}, u32[]{:S(2)}, u32[]{:S(2)}) collective-permute-start(bf16[128,512]{1,0:T(8,128)(2,1)S(1)} %collective-permute-done.5.refs_6_), channel_id=1, source_target_pairs={{0,1},{1,2},{2,3},{3,4},{4,5},{5,6},{6,7},{7,0},{8,15},{9,8},{10,9... | collective-permute-start | bytes 393224 | tf_op jit(solution)/shard_map/ppermute | solution.py:268
  60.2 8.8 %collective-permute-start.10 = (bf16[128,512]{1,0:T(8,128)(2,1)S(1)}, bf16[128,512]{1,0:T(8,128)(2,1)S(1)}, u32[]{:S(2)}, u32[]{:S(2)}) collective-permute-start(bf16[128,512]{1,0:T(8,128)(2,1)S(1)} %collective-permute-done.6.refs_7_), channel_id=1, source_target_pairs={{0,1},{1,2},{2,3},{3,4},{4,5},{5,6},{6,7},{7,0},{8,15},{9,8},{10,9... | collective-permute-start | bytes 393224 | tf_op jit(solution)/shard_map/ppermute | solution.py:268
  62.5 7.9 %collective-permute-start.11 = (bf16[128,512]{1,0:T(8,128)(2,1)S(1)}, bf16[128,512]{1,0:T(8,128)(2,1)S(1)}, u32[]{:S(2)}, u32[]{:S(2)}) collective-permute-start(bf16[128,512]{1,0:T(8,128)(2,1)S(1)} %collective-permute-done.7.refs_8_), channel_id=1, source_target_pairs={{0,1},{1,2},{2,3},{3,4},{4,5},{5,6},{6,7},{7,0},{8,15},{9,8},{10,9... | collective-permute-start | bytes 393224 | tf_op jit(solution)/shard_map/ppermute | solution.py:268
  70.4 6.2 %collective-permute-start.15 = (bf16[128,512]{1,0:T(8,128)(2,1)S(1)}, bf16[128,512]{1,0:T(8,128)(2,1)S(1)}, u32[]{:S(2)}, u32[]{:S(2)}) collective-permute-start(bf16[128,512]{1,0:T(8,128)(2,1)S(1)} %collective-permute-done.11.refs_12_), channel_id=1, source_target_pairs={{0,1},{1,2},{2,3},{3,4},{4,5},{5,6},{6,7},{7,0},{8,15},{9,8},{10,9... | collective-permute-start | bytes 393224 | tf_op jit(solution)/shard_map/ppermute | solution.py:268
  76.6 6.2 %collective-permute-start.19 = (bf16[128,512]{1,0:T(8,128)(2,1)S(1)}, bf16[128,512]{1,0:T(8,128)(2,1)S(1)}, u32[]{:S(2)}, u32[]{:S(2)}) collective-permute-start(bf16[128,512]{1,0:T(8,128)(2,1)S(1)} %collective-permute-done.15.refs_16_), channel_id=1, source_target_pairs={{0,1},{1,2},{2,3},{3,4},{4,5},{5,6},{6,7},{7,0},{8,15},{9,8},{10,9... | collective-permute-start | bytes 393224 | tf_op jit(solution)/shard_map/ppermute | solution.py:268
  82.7 6.3 %collective-permute-start.23 = (bf16[128,512]{1,0:T(8,128)(2,1)S(1)}, bf16[128,512]{1,0:T(8,128)(2,1)}, u32[]{:S(2)}, u32[]{:S(2)}) collective-permute-start(bf16[128,512]{1,0:T(8,128)(2,1)S(1)} %collective-permute-done.19.refs_20_), channel_id=1, source_target_pairs={{0,1},{1,2},{2,3},{3,4},{4,5},{5,6},{6,7},{7,0},{8,15},{9,8},{10,9... | collective-permute-start | bytes 393224 | tf_op jit(solution)/shard_map/ppermute | solution.py:268
  84.7 6.3 %collective-permute-start.24 = (bf16[128,512]{1,0:T(8,128)(2,1)S(1)}, bf16[128,512]{1,0:T(8,128)(2,1)}, u32[]{:S(2)}, u32[]{:S(2)}) collective-permute-start(bf16[128,512]{1,0:T(8,128)(2,1)S(1)} %collective-permute-done.20.refs_21_), channel_id=1, source_target_pairs={{0,1},{1,2},{2,3},{3,4},{4,5},{5,6},{6,7},{7,0},{8,15},{9,8},{10,9... | collective-permute-start | bytes 393224 | tf_op jit(solution)/shard_map/ppermute | solution.py:268
  86.1 6.3 %collective-permute-start.25 = (bf16[128,512]{1,0:T(8,128)(2,1)S(1)}, bf16[128,512]{1,0:T(8,128)(2,1)}, u32[]{:S(2)}, u32[]{:S(2)}) collective-permute-start(bf16[128,512]{1,0:T(8,128)(2,1)S(1)} %collective-permute-done.21.refs_22_), channel_id=1, source_target_pairs={{0,1},{1,2},{2,3},{3,4},{4,5},{5,6},{6,7},{7,0},{8,15},{9,8},{10,9... | collective-permute-start | bytes 393224 | tf_op jit(solution)/shard_map/ppermute | solution.py:268
  87.5 6.3 %collective-permute-start.26 = (bf16[128,512]{1,0:T(8,128)(2,1)S(1)}, bf16[128,512]{1,0:T(8,128)(2,1)}, u32[]{:S(2)}, u32[]{:S(2)}) collective-permute-start(bf16[128,512]{1,0:T(8,128)(2,1)S(1)} %collective-permute-done.22.refs_23_), channel_id=1, source_target_pairs={{0,1},{1,2},{2,3},{3,4},{4,5},{5,6},{6,7},{7,0},{8,15},{9,8},{10,9... | collective-permute-start | bytes 393224 | tf_op jit(solution)/shard_map/ppermute | solution.py:268
  89.0 6.5 %collective-permute-start.27 = (bf16[128,512]{1,0:T(8,128)(2,1)}, bf16[128,512]{1,0:T(8,128)(2,1)}, u32[]{:S(2)}, u32[]{:S(2)}) collective-permute-start(bf16[128,512]{1,0:T(8,128)(2,1)} %collective-permute-done.23.refs_24_), channel_id=1, source_target_pairs={{0,1},{1,2},{2,3},{3,4},{4,5},{5,6},{6,7},{7,0},{8,15},{9,8},{10,9... | collective-permute-start | bytes 393224 | tf_op jit(solution)/shard_map/ppermute | solution.py:268
  91.0 6.5 %collective-permute-start.28 = (bf16[128,512]{1,0:T(8,128)(2,1)}, bf16[128,512]{1,0:T(8,128)(2,1)}, u32[]{:S(2)}, u32[]{:S(2)}) collective-permute-start(bf16[128,512]{1,0:T(8,128)(2,1)} %collective-permute-done.24.refs_25_), channel_id=1, source_target_pairs={{0,1},{1,2},{2,3},{3,4},{4,5},{5,6},{6,7},{7,0},{8,15},{9,8},{10,9... | collective-permute-start | bytes 393224 | tf_op jit(solution)/shard_map/ppermute | solution.py:268
  92.4 6.5 %collective-permute-start.29 = (bf16[128,512]{1,0:T(8,128)(2,1)}, bf16[128,512]{1,0:T(8,128)(2,1)}, u32[]{:S(2)}, u32[]{:S(2)}) collective-permute-start(bf16[128,512]{1,0:T(8,128)(2,1)} %collective-permute-done.25.refs_26_), channel_id=1, source_target_pairs={{0,1},{1,2},{2,3},{3,4},{4,5},{5,6},{6,7},{7,0},{8,15},{9,8},{10,9... | collective-permute-start | bytes 393224 | tf_op jit(solution)/shard_map/ppermute | solution.py:268
  93.8 6.5 %collective-permute-start.30 = (bf16[128,512]{1,0:T(8,128)(2,1)}, bf16[128,512]{1,0:T(8,128)(2,1)}, u32[]{:S(2)}, u32[]{:S(2)}) collective-permute-start(bf16[128,512]{1,0:T(8,128)(2,1)} %collective-permute-done.26.refs_27_), channel_id=1, source_target_pairs={{0,1},{1,2},{2,3},{3,4},{4,5},{5,6},{6,7},{7,0},{8,15},{9,8},{10,9... | collective-permute-start | bytes 393224 | tf_op jit(solution)/shard_map/ppermute | solution.py:268
  111.0 14.8 %all-to-all-start = ((f32[8,1,512]{2,1,0:T(1,128)}), f32[8,1,512]{2,1,0:T(1,128)S(1)}, u32[]{:S(2)}, u32[]{:S(2)}) async-start(f32[8,1,512]{2,1,0:T(1,128)} %get-tuple-element.22), calls=%async_computation | async-start | bytes 32768 | tf_op jit(solution)/shard_map/all_to_all | solution.py:309
  (36 other events, 1108.3 us)
Sparse Core Ops, SparseCore 0:
  37.7 66.8 all-gather.2

commit v10 on v9

--- a/solution.py
+++ b/solution.py
@@ -104,18 +104,18 @@
     pass
 
 
-def held(array, after):
+def held(array, other, after):
     hbm = pl.BlockSpec(memory_space=pltpu.HBM)
-    after = [pltpu.with_memory_space_constraint(x, pltpu.VMEM) for x in after]
+    other, *after = [pltpu.with_memory_space_constraint(x, pltpu.VMEM) for x in [other, *after]]
     return pl.pallas_call(
         hold_kernel,
-        in_specs=[hbm] + [VMEM] * len(after),
-        out_specs=hbm,
-        out_shape=jax.ShapeDtypeStruct(array.shape, array.dtype),
-        input_output_aliases={0: 0},
+        in_specs=[hbm, VMEM] + [VMEM] * len(after),
+        out_specs=[hbm, VMEM],
+        out_shape=[jax.ShapeDtypeStruct(x.shape, x.dtype) for x in [array, other]],
+        input_output_aliases={0: 0, 1: 1},
         compiler_params=pltpu.CompilerParams(vmem_limit_bytes=1024 * 1024),
         name="hold",
-    )(array, *after)
+    )(array, other, *after)
 
 
 def attend_kernel(place_ref, q_ref, own_ref, prev_ref, far_ref, *out_refs):
@@ -289,9 +289,12 @@
     own, cosine, sine = prepare(
         positions[None], inverse, keys.transpose(1, 0, 2), values.transpose(1, 0, 2)
     )
-    prev = lax.ppermute(own, "seq", [(i, i + 1) for i in range(N_SEQ - 1)])
     far = lax.ppermute(own, "seq", [(i, i + 2) for i in range(N_SEQ - 2)])
     q = rotate(queries.reshape(ROWS, WIDTH), cosine, sine)
+    shard, far = held(shard, far, after=[q])
+    given = jnp.where(seq % 2 == 0, own, far)
+    prev = lax.ppermute(given, "seq", [(i, i ^ 1) for i in range(N_SEQ)])
+    weights = lax.all_gather(shard, "seq", axis=0).reshape(N_HEAD, FEATURES, WIDTH)
 
     blocks = [[] for _ in range(N_HEAD)]
     place = seq.reshape(1)
@@ -301,8 +304,6 @@
             carried = moved(carried, lambda x, y, core, head: (x, y, core, head + sense(core)))
             blocks[k].append(carried)
 
-    shard = held(shard, after=blocks[0])
-    weights = lax.all_gather(shard, "seq", axis=0).reshape(N_HEAD, FEATURES, WIDTH)
     source = head - sense(seq % 2) * jnp.arange(N_HEAD, dtype=jnp.int32)
     order = ((source + head) % N_HEAD).astype(jnp.int32)
     attended, squares = project(order, weights, [x for row in blocks for x in row])

time: 135 us -> 128 us (0.948)
  starting transfers between devices: 77.7 us -> 67.6 us
  waiting for transfers between devices: 25.6 us -> 29 us
    ppermute x29, waiting for transfers between devices: 7.96 us -> 19.4 us  [moved(): return lax.ppermute(array, ('seq', 'head'), pairs)]
    ppermute x29, starting transfers between devices: 65.2 us -> 58.2 us  [moved(): return lax.ppermute(array, ('seq', 'head'), pairs)]
    ppermute x1, waiting for transfers between devices: 5.14 us -> 0.01 us  [on_device(): far = lax.ppermute(own, 'seq', [(i, i + 2) for i in range(N_SEQ - 2)])]
    all_gather x1, waiting for transfers between devices: 4.29 us -> 0.01 us  [on_device(): lax.all_gather(shard, 'seq', axis=0).reshape(N_HEAD, FEATURES, WIDTH)]
    ppermute x1, starting transfers between devices: 1.92 us -> 0.09 us  [on_device(): prev = lax.ppermute(given, 'seq', [(i, i ^ 1) for i in range(N_SEQ)])]
  transfers between devices with their start and end apart: 33 -> 33, of which waited for: 13 -> 12; matrix products, arithmetic and copies ran while one was open for 1% -> 1% of each run, Pallas kernels for 4% -> 4%
where the time goes in v10:
time: 128 us; the launch traced here: 127 us
  starting transfers between devices  67.6 us (53%)
  waiting for transfers between devices  29 us (23%)
  between operations  13.7 us (11%)
  Pallas kernels  13.5 us (11%)
  local copies, waits for them, and re-layouts  3.15 us (2%)
    ppermute x29, starting transfers between devices, moved(): return lax.ppermute(array, ('seq', 'head'), pairs)  58.2 us
    ppermute x29, waiting for transfers between devices, moved(): return lax.ppermute(array, ('seq', 'head'), pairs)  19.4 us
    all_to_all x1, waiting for transfers between devices, on_device(): squares = lax.all_to_all(squares, 'head', 0, 0, tiled=True)  7.62 us
    pallas_call x1, Pallas kernels, project(): pl.pallas_call(project_kernel, in_specs=[pl.BlockSpec(memory_space=pltpu....  6.21 us
    all_to_all x1, starting transfers between devices, on_device(): squares = lax.all_to_all(squares, 'head', 0, 0, tiled=True)  5.75 us
    pallas_call x1, Pallas kernels, attend(): pl.pallas_call(attend_kernel, in_specs=[pl.BlockSpec(memory_space=pltpu.S...  5.33 us
    ppermute x1, starting transfers between devices, on_device(): far = lax.ppermute(own, 'seq', [(i, i + 2) for i in range(N_SEQ - 2)])  3.48 us
  transfers between devices with their start and end apart: 33, of which 12 were waited for; matrix products, arithmetic and copies ran while one was open for 1% of the time, Pallas kernels for 4%

profile of v10, /device:TPU:6, one launch (start us, length us, event | category | flops | bytes accessed | tf_op | source)
XLA Modules:
  0.0 127.1 jit_solution(809228945404453081)
XLA Ops:
  9.0 3.5 %collective-permute-start.1 = (bf16[2,2,512,128]{3,2,1,0:T(8,128)(2,1)S(1)}, bf16[2,2,512,128]{3,2,1,0:T(8,128)(2,1)S(1)}, u32[]{:S(2)}, u32[]{:S(2)}) collective-permute-start(bf16[2,2,512,128]{3,2,1,0:T(8,128)(2,1)S(1)} %get-tuple-element.16.own_ref), channel_id=1, source_target_pairs={{0,16},{8,24},{16,32},{24,40},{32,48},{40,56},{48,64},{56,72},{64,... | collective-permute-start | bytes 1572872 | tf_op jit(solution)/shard_map/ppermute | solution.py:292
  12.5 8.2 %collective-permute-start = (bf16[168,512]{1,0:T(8,128)(2,1)}, bf16[168,512]{1,0:T(8,128)(2,1)}, u32[]{:S(2)}, u32[]{:S(2)}) collective-permute-start(bf16[168,512]{1,0:T(8,128)(2,1)} %bitcast.21), channel_id=1, source_target_pairs={{0,0},{1,32},{2,64},{3,96},{4,128},{5,160},{6,192},{7,224},{8,8},{... | collective-permute-start | bytes 516104 | tf_op jit(solution)/shard_map/ppermute | solution.py:268
  22.2 13.0 %collective-permute-done.refs_0_ = bf16[168,512]{1,0:T(8,128)(2,1)} collective-permute-done((bf16[168,512]{1,0:T(8,128)(2,1)}, bf16[168,512]{1,0:T(8,128)(2,1)}, u32[]{:S(2)}, u32[]{:S(2)}) %collective-permute-start) | collective-permute-done | bytes 172064 | tf_op jit(solution)/shard_map/ppermute | solution.py:268
  35.4 1.9 %collective-permute-done.2.prev_ref = bf16[2,2,512,128]{3,2,1,0:T(8,128)(2,1)S(1)} collective-permute-done((bf16[2,2,512,128]{3,2,1,0:T(8,128)(2,1)S(1)}, bf16[2,2,512,128]{3,2,1,0:T(8,128)(2,1)S(1)}, u32[]{:S(2)}, u32[]{:S(2)}) %collective-permute-start.2) | collective-permute-done | bytes 524320 | tf_op jit(solution)/shard_map/ppermute | solution.py:296
  37.3 5.3 %attend.1 = (bf16[128,512]{1,0:T(8,128)(2,1)S(1)}, bf16[128,512]{1,0:T(8,128)(2,1)S(1)}, bf16[128,512]{1,0:T(8,128)(2,1)S(1)}, bf16[128,512]{1,0:T(8,128)(2,1)S(1)}) custom-call(s32[1]{0:T(128)} %bitcast.6.place_ref, bf16[512,512]{1,0:T(8,128)(2,1)S(1)} %rotate.1.refs_2_.q_ref, bf16[2,2,512,128]{3,2,1,0:T(8,128)(2,1)S(1)} %get-tuple-element.16.own_ref, ...), custom_call_target="tpu_custom_call" | custom-call | tf_op jit(solution)/shard_map/attend/pallas_call | solution.py:178
  43.7 4.4 %collective-permute-start.6 = (bf16[128,512]{1,0:T(8,128)(2,1)S(1)}, bf16[128,512]{1,0:T(8,128)(2,1)S(1)}, u32[]{:S(2)}, u32[]{:S(2)}) collective-permute-start(bf16[128,512]{1,0:T(8,128)(2,1)S(1)} %get-tuple-element.24.refs_3_), channel_id=1, source_target_pairs={{0,1},{1,2},{2,3},{3,4},{4,5},{5,6},{6,7},{7,0},{8,15},{9,8},{10,9... | collective-permute-start | bytes 393224 | tf_op jit(solution)/shard_map/ppermute | solution.py:268
  49.0 9.9 %collective-permute-start.7 = (bf16[128,512]{1,0:T(8,128)(2,1)S(1)}, bf16[128,512]{1,0:T(8,128)(2,1)S(1)}, u32[]{:S(2)}, u32[]{:S(2)}) collective-permute-start(bf16[128,512]{1,0:T(8,128)(2,1)S(1)} %collective-permute-done.3.refs_4_), channel_id=1, source_target_pairs={{0,1},{1,2},{2,3},{3,4},{4,5},{5,6},{6,7},{7,0},{8,15},{9,8},{10,9... | collective-permute-start | bytes 393224 | tf_op jit(solution)/shard_map/ppermute | solution.py:268
  59.3 2.1 %collective-permute-start.10 = (bf16[128,512]{1,0:T(8,128)(2,1)S(1)}, bf16[128,512]{1,0:T(8,128)(2,1)S(1)}, u32[]{:S(2)}, u32[]{:S(2)}) collective-permute-start(bf16[128,512]{1,0:T(8,128)(2,1)S(1)} %collective-permute-done.6.refs_7_), channel_id=1, source_target_pairs={{0,1},{1,2},{2,3},{3,4},{4,5},{5,6},{6,7},{7,0},{8,15},{9,8},{10,9... | collective-permute-start | bytes 393224 | tf_op jit(solution)/shard_map/ppermute | solution.py:268
  61.4 3.7 %collective-permute-start.11 = (bf16[128,512]{1,0:T(8,128)(2,1)S(1)}, bf16[128,512]{1,0:T(8,128)(2,1)S(1)}, u32[]{:S(2)}, u32[]{:S(2)}) collective-permute-start(bf16[128,512]{1,0:T(8,128)(2,1)S(1)} %collective-permute-done.7.refs_8_), channel_id=1, source_target_pairs={{0,1},{1,2},{2,3},{3,4},{4,5},{5,6},{6,7},{7,0},{8,15},{9,8},{10,9... | collective-permute-start | bytes 393224 | tf_op jit(solution)/shard_map/ppermute | solution.py:268
  65.1 1.4 %collective-permute-start.12 = (bf16[128,512]{1,0:T(8,128)(2,1)S(1)}, bf16[128,512]{1,0:T(8,128)(2,1)S(1)}, u32[]{:S(2)}, u32[]{:S(2)}) collective-permute-start(bf16[128,512]{1,0:T(8,128)(2,1)S(1)} %collective-permute-done.8.refs_9_), channel_id=1, source_target_pairs={{0,1},{1,2},{2,3},{3,4},{4,5},{5,6},{6,7},{7,0},{8,15},{9,8},{10,9... | collective-permute-start | bytes 393224 | tf_op jit(solution)/shard_map/ppermute | solution.py:268
  66.5 1.4 %collective-permute-start.13 = (bf16[128,512]{1,0:T(8,128)(2,1)S(1)}, bf16[128,512]{1,0:T(8,128)(2,1)S(1)}, u32[]{:S(2)}, u32[]{:S(2)}) collective-permute-start(bf16[128,512]{1,0:T(8,128)(2,1)S(1)} %collective-permute-done.9.refs_10_), channel_id=1, source_target_pairs={{0,1},{1,2},{2,3},{3,4},{4,5},{5,6},{6,7},{7,0},{8,15},{9,8},{10,9... | collective-permute-start | bytes 393224 | tf_op jit(solution)/shard_map/ppermute | solution.py:268
  69.3 2.0 %collective-permute-start.15 = (bf16[128,512]{1,0:T(8,128)(2,1)S(1)}, bf16[128,512]{1,0:T(8,128)(2,1)S(1)}, u32[]{:S(2)}, u32[]{:S(2)}) collective-permute-start(bf16[128,512]{1,0:T(8,128)(2,1)S(1)} %collective-permute-done.11.refs_12_), channel_id=1, source_target_pairs={{0,1},{1,2},{2,3},{3,4},{4,5},{5,6},{6,7},{7,0},{8,15},{9,8},{10,9... | collective-permute-start | bytes 393224 | tf_op jit(solution)/shard_map/ppermute | solution.py:268
  71.3 1.4 %collective-permute-start.16 = (bf16[128,512]{1,0:T(8,128)(2,1)S(1)}, bf16[128,512]{1,0:T(8,128)(2,1)S(1)}, u32[]{:S(2)}, u32[]{:S(2)}) collective-permute-start(bf16[128,512]{1,0:T(8,128)(2,1)S(1)} %collective-permute-done.12.refs_13_), channel_id=1, source_target_pairs={{0,1},{1,2},{2,3},{3,4},{4,5},{5,6},{6,7},{7,0},{8,15},{9,8},{10,9... | collective-permute-start | bytes 393224 | tf_op jit(solution)/shard_map/ppermute | solution.py:268
  72.7 1.4 %collective-permute-start.17 = (bf16[128,512]{1,0:T(8,128)(2,1)S(1)}, bf16[128,512]{1,0:T(8,128)(2,1)S(1)}, u32[]{:S(2)}, u32[]{:S(2)}) collective-permute-start(bf16[128,512]{1,0:T(8,128)(2,1)S(1)} %collective-permute-done.13.refs_14_), channel_id=1, source_target_pairs={{0,1},{1,2},{2,3},{3,4},{4,5},{5,6},{6,7},{7,0},{8,15},{9,8},{10,9... | collective-permute-start | bytes 393224 | tf_op jit(solution)/shard_map/ppermute | solution.py:268
  74.1 1.4 %collective-permute-start.18 = (bf16[128,512]{1,0:T(8,128)(2,1)S(1)}, bf16[128,512]{1,0:T(8,128)(2,1)S(1)}, u32[]{:S(2)}, u32[]{:S(2)}) collective-permute-start(bf16[128,512]{1,0:T(8,128)(2,1)S(1)} %collective-permute-done.14.refs_15_), channel_id=1, source_target_pairs={{0,1},{1,2},{2,3},{3,4},{4,5},{5,6},{6,7},{7,0},{8,15},{9,8},{10,9... | collective-permute-start | bytes 393224 | tf_op jit(solution)/shard_map/ppermute | solution.py:268
  75.5 2.0 %collective-permute-start.19 = (bf16[128,512]{1,0:T(8,128)(2,1)S(1)}, bf16[128,512]{1,0:T(8,128)(2,1)S(1)}, u32[]{:S(2)}, u32[]{:S(2)}) collective-permute-start(bf16[128,512]{1,0:T(8,128)(2,1)S(1)} %collective-permute-done.15.refs_16_), channel_id=1, source_target_pairs={{0,1},{1,2},{2,3},{3,4},{4,5},{5,6},{6,7},{7,0},{8,15},{9,8},{10,9... | collective-permute-start | bytes 393224 | tf_op jit(solution)/shard_map/ppermute | solution.py:268
  81.7 2.0 %collective-permute-start.23 = (bf16[128,512]{1,0:T(8,128)(2,1)S(1)}, bf16[128,512]{1,0:T(8,128)(2,1)}, u32[]{:S(2)}, u32[]{:S(2)}) collective-permute-start(bf16[128,512]{1,0:T(8,128)(2,1)S(1)} %collective-permute-done.19.refs_20_), channel_id=1, source_target_pairs={{0,1},{1,2},{2,3},{3,4},{4,5},{5,6},{6,7},{7,0},{8,15},{9,8},{10,9... | collective-permute-start | bytes 393224 | tf_op jit(solution)/shard_map/ppermute | solution.py:268
  88.0 1.9 %collective-permute-start.27 = (bf16[128,512]{1,0:T(8,128)(2,1)}, bf16[128,512]{1,0:T(8,128)(2,1)}, u32[]{:S(2)}, u32[]{:S(2)}) collective-permute-start(bf16[128,512]{1,0:T(8,128)(2,1)} %collective-permute-done.23.refs_24_), channel_id=1, source_target_pairs={{0,1},{1,2},{2,3},{3,4},{4,5},{5,6},{6,7},{7,0},{8,15},{9,8},{10,9... | collective-permute-start | bytes 393224 | tf_op jit(solution)/shard_map/ppermute | solution.py:268
  94.5 2.0 %collective-permute-done.28.refs_29_ = bf16[128,512]{1,0:T(8,128)(2,1)} collective-permute-done((bf16[128,512]{1,0:T(8,128)(2,1)}, bf16[128,512]{1,0:T(8,128)(2,1)}, u32[]{:S(2)}, u32[]{:S(2)}) %collective-permute-start.28) | collective-permute-done | bytes 131104 | tf_op jit(solution)/shard_map/ppermute | solution.py:268
  96.4 1.4 %collective-permute-done.29.refs_30_ = bf16[128,512]{1,0:T(8,128)(2,1)} collective-permute-done((bf16[128,512]{1,0:T(8,128)(2,1)}, bf16[128,512]{1,0:T(8,128)(2,1)}, u32[]{:S(2)}, u32[]{:S(2)}) %collective-permute-start.29) | collective-permute-done | bytes 131104 | tf_op jit(solution)/shard_map/ppermute | solution.py:268
  97.8 1.4 %collective-permute-done.30.refs_31_ = bf16[128,512]{1,0:T(8,128)(2,1)} collective-permute-done((bf16[128,512]{1,0:T(8,128)(2,1)}, bf16[128,512]{1,0:T(8,128)(2,1)}, u32[]{:S(2)}, u32[]{:S(2)}) %collective-permute-start.30) | collective-permute-done | bytes 131104 | tf_op jit(solution)/shard_map/ppermute | solution.py:268
  99.4 6.2 %project.1 = (f32[672,512]{1,0:T(8,128)S(1)}, f32[8,1,512]{2,1,0:T(1,128)}) custom-call(s32[8]{0:T(128)S(1)} %and_select_fusion.order_ref, bf16[8,672,512]{2,1,0:T(8,128)(2,1)} %bitcast.19, bf16[128,512]{1,0:T(8,128)(2,1)} %copy-done.1, bf16[128,512]{1,0:T(8,128)(2,1)} %copy-done.2, bf16[128,512]{1,0:T(8,128)(2,1)} %copy-done.3, bf16[128,512]{1,0:T(8,128)(2,1)} %copy-done.4, ...), custom_call_target="tpu_custom_call" | custom-call | tf_op jit(solution)/shard_map/project/pallas_call | solution.py:221
  105.6 5.8 %all-to-all-start = ((f32[8,1,512]{2,1,0:T(1,128)}), f32[8,1,512]{2,1,0:T(1,128)S(1)}, u32[]{:S(2)}, u32[]{:S(2)}) async-start(f32[8,1,512]{2,1,0:T(1,128)} %get-tuple-element.26), calls=%async_computation | async-start | bytes 32768 | tf_op jit(solution)/shard_map/all_to_all | solution.py:310
  111.5 7.6 %all-to-all-done.sq_ref = f32[8,1,512]{2,1,0:T(1,128)S(1)} async-done(((f32[8,1,512]{2,1,0:T(1,128)}), f32[8,1,512]{2,1,0:T(1,128)S(1)}, u32[]{:S(2)}, u32[]{:S(2)}) %all-to-all-start) | async-done | bytes 16416 | tf_op jit(solution)/shard_map/all_to_all | solution.py:310
  (110 shorter events, 22.2 us)
Async XLA Ops:
  6.5 92.7 %all-gather.3.cloned.1.call-start = ((), (), s32[]{:S(2)}) async-start(), calls=%async_computation.1 | async-start | bytes 5677056 | tf_op jit(solution)/shard_map/all_gather | solution.py:297
  9.0 26.2 %collective-permute-start.1 = (bf16[2,2,512,128]{3,2,1,0:T(8,128)(2,1)S(1)}, bf16[2,2,512,128]{3,2,1,0:T(8,128)(2,1)S(1)}, u32[]{:S(2)}, u32[]{:S(2)}) collective-permute-start(bf16[2,2,512,128]{3,2,1,0:T(8,128)(2,1)S(1)} %get-tuple-element.16.own_ref), channel_id=1, source_target_pairs={{0,16},{8,24},{16,32},{24,40},{32,48},{40,56},{48,64},{56,72},{64,... | collective-permute-start | bytes 1572872 | tf_op jit(solution)/shard_map/ppermute | solution.py:292
  12.5 22.7 %collective-permute-start = (bf16[168,512]{1,0:T(8,128)(2,1)}, bf16[168,512]{1,0:T(8,128)(2,1)}, u32[]{:S(2)}, u32[]{:S(2)}) collective-permute-start(bf16[168,512]{1,0:T(8,128)(2,1)} %bitcast.21), channel_id=1, source_target_pairs={{0,0},{1,32},{2,64},{3,96},{4,128},{5,160},{6,192},{7,224},{8,8},{... | collective-permute-start | bytes 516104 | tf_op jit(solution)/shard_map/ppermute | solution.py:268
  42.7 6.3 %collective-permute-start.3 = (bf16[128,512]{1,0:T(8,128)(2,1)S(1)}, bf16[128,512]{1,0:T(8,128)(2,1)S(1)}, u32[]{:S(2)}, u32[]{:S(2)}) collective-permute-start(bf16[128,512]{1,0:T(8,128)(2,1)S(1)} %get-tuple-element.21.refs_0_), channel_id=1, source_target_pairs={{0,1},{1,2},{2,3},{3,4},{4,5},{5,6},{6,7},{7,0},{8,15},{9,8},{10,9... | collective-permute-start | bytes 393224 | tf_op jit(solution)/shard_map/ppermute | solution.py:268
  42.8 16.1 %collective-permute-start.4 = (bf16[128,512]{1,0:T(8,128)(2,1)S(1)}, bf16[128,512]{1,0:T(8,128)(2,1)S(1)}, u32[]{:S(2)}, u32[]{:S(2)}) collective-permute-start(bf16[128,512]{1,0:T(8,128)(2,1)S(1)} %get-tuple-element.22.refs_1_), channel_id=1, source_target_pairs={{0,1},{1,2},{2,3},{3,4},{4,5},{5,6},{6,7},{7,0},{8,15},{9,8},{10,9... | collective-permute-start | bytes 393224 | tf_op jit(solution)/shard_map/ppermute | solution.py:268
  42.9 16.1 %collective-permute-start.5 = (bf16[128,512]{1,0:T(8,128)(2,1)S(1)}, bf16[128,512]{1,0:T(8,128)(2,1)S(1)}, u32[]{:S(2)}, u32[]{:S(2)}) collective-permute-start(bf16[128,512]{1,0:T(8,128)(2,1)S(1)} %get-tuple-element.23.refs_2_), channel_id=1, source_target_pairs={{0,1},{1,2},{2,3},{3,4},{4,5},{5,6},{6,7},{7,0},{8,15},{9,8},{10,9... | collective-permute-start | bytes 393224 | tf_op jit(solution)/shard_map/ppermute | solution.py:268
  43.7 15.6 %collective-permute-start.6 = (bf16[128,512]{1,0:T(8,128)(2,1)S(1)}, bf16[128,512]{1,0:T(8,128)(2,1)S(1)}, u32[]{:S(2)}, u32[]{:S(2)}) collective-permute-start(bf16[128,512]{1,0:T(8,128)(2,1)S(1)} %get-tuple-element.24.refs_3_), channel_id=1, source_target_pairs={{0,1},{1,2},{2,3},{3,4},{4,5},{5,6},{6,7},{7,0},{8,15},{9,8},{10,9... | collective-permute-start | bytes 393224 | tf_op jit(solution)/shard_map/ppermute | solution.py:268
  49.0 12.5 %collective-permute-start.7 = (bf16[128,512]{1,0:T(8,128)(2,1)S(1)}, bf16[128,512]{1,0:T(8,128)(2,1)S(1)}, u32[]{:S(2)}, u32[]{:S(2)}) collective-permute-start(bf16[128,512]{1,0:T(8,128)(2,1)S(1)} %collective-permute-done.3.refs_4_), channel_id=1, source_target_pairs={{0,1},{1,2},{2,3},{3,4},{4,5},{5,6},{6,7},{7,0},{8,15},{9,8},{10,9... | collective-permute-start | bytes 393224 | tf_op jit(solution)/shard_map/ppermute | solution.py:268
  58.9 6.2 %collective-permute-start.8 = (bf16[128,512]{1,0:T(8,128)(2,1)S(1)}, bf16[128,512]{1,0:T(8,128)(2,1)S(1)}, u32[]{:S(2)}, u32[]{:S(2)}) collective-permute-start(bf16[128,512]{1,0:T(8,128)(2,1)S(1)} %collective-permute-done.4.refs_5_), channel_id=1, source_target_pairs={{0,1},{1,2},{2,3},{3,4},{4,5},{5,6},{6,7},{7,0},{8,15},{9,8},{10,9... | collective-permute-start | bytes 393224 | tf_op jit(solution)/shard_map/ppermute | solution.py:268
  59.0 7.5 %collective-permute-start.9 = (bf16[128,512]{1,0:T(8,128)(2,1)S(1)}, bf16[128,512]{1,0:T(8,128)(2,1)S(1)}, u32[]{:S(2)}, u32[]{:S(2)}) collective-permute-start(bf16[128,512]{1,0:T(8,128)(2,1)S(1)} %collective-permute-done.5.refs_6_), channel_id=1, source_target_pairs={{0,1},{1,2},{2,3},{3,4},{4,5},{5,6},{6,7},{7,0},{8,15},{9,8},{10,9... | collective-permute-start | bytes 393224 | tf_op jit(solution)/shard_map/ppermute | solution.py:268
  59.3 8.6 %collective-permute-start.10 = (bf16[128,512]{1,0:T(8,128)(2,1)S(1)}, bf16[128,512]{1,0:T(8,128)(2,1)S(1)}, u32[]{:S(2)}, u32[]{:S(2)}) collective-permute-start(bf16[128,512]{1,0:T(8,128)(2,1)S(1)} %collective-permute-done.6.refs_7_), channel_id=1, source_target_pairs={{0,1},{1,2},{2,3},{3,4},{4,5},{5,6},{6,7},{7,0},{8,15},{9,8},{10,9... | collective-permute-start | bytes 393224 | tf_op jit(solution)/shard_map/ppermute | solution.py:268
  61.4 7.9 %collective-permute-start.11 = (bf16[128,512]{1,0:T(8,128)(2,1)S(1)}, bf16[128,512]{1,0:T(8,128)(2,1)S(1)}, u32[]{:S(2)}, u32[]{:S(2)}) collective-permute-start(bf16[128,512]{1,0:T(8,128)(2,1)S(1)} %collective-permute-done.7.refs_8_), channel_id=1, source_target_pairs={{0,1},{1,2},{2,3},{3,4},{4,5},{5,6},{6,7},{7,0},{8,15},{9,8},{10,9... | collective-permute-start | bytes 393224 | tf_op jit(solution)/shard_map/ppermute | solution.py:268
  65.1 6.2 %collective-permute-start.12 = (bf16[128,512]{1,0:T(8,128)(2,1)S(1)}, bf16[128,512]{1,0:T(8,128)(2,1)S(1)}, u32[]{:S(2)}, u32[]{:S(2)}) collective-permute-start(bf16[128,512]{1,0:T(8,128)(2,1)S(1)} %collective-permute-done.8.refs_9_), channel_id=1, source_target_pairs={{0,1},{1,2},{2,3},{3,4},{4,5},{5,6},{6,7},{7,0},{8,15},{9,8},{10,9... | collective-permute-start | bytes 393224 | tf_op jit(solution)/shard_map/ppermute | solution.py:268
  69.3 6.2 %collective-permute-start.15 = (bf16[128,512]{1,0:T(8,128)(2,1)S(1)}, bf16[128,512]{1,0:T(8,128)(2,1)S(1)}, u32[]{:S(2)}, u32[]{:S(2)}) collective-permute-start(bf16[128,512]{1,0:T(8,128)(2,1)S(1)} %collective-permute-done.11.refs_12_), channel_id=1, source_target_pairs={{0,1},{1,2},{2,3},{3,4},{4,5},{5,6},{6,7},{7,0},{8,15},{9,8},{10,9... | collective-permute-start | bytes 393224 | tf_op jit(solution)/shard_map/ppermute | solution.py:268
  71.3 6.2 %collective-permute-start.16 = (bf16[128,512]{1,0:T(8,128)(2,1)S(1)}, bf16[128,512]{1,0:T(8,128)(2,1)S(1)}, u32[]{:S(2)}, u32[]{:S(2)}) collective-permute-start(bf16[128,512]{1,0:T(8,128)(2,1)S(1)} %collective-permute-done.12.refs_13_), channel_id=1, source_target_pairs={{0,1},{1,2},{2,3},{3,4},{4,5},{5,6},{6,7},{7,0},{8,15},{9,8},{10,9... | collective-permute-start | bytes 393224 | tf_op jit(solution)/shard_map/ppermute | solution.py:268
  81.7 6.3 %collective-permute-start.23 = (bf16[128,512]{1,0:T(8,128)(2,1)S(1)}, bf16[128,512]{1,0:T(8,128)(2,1)}, u32[]{:S(2)}, u32[]{:S(2)}) collective-permute-start(bf16[128,512]{1,0:T(8,128)(2,1)S(1)} %collective-permute-done.19.refs_20_), channel_id=1, source_target_pairs={{0,1},{1,2},{2,3},{3,4},{4,5},{5,6},{6,7},{7,0},{8,15},{9,8},{10,9... | collective-permute-start | bytes 393224 | tf_op jit(solution)/shard_map/ppermute | solution.py:268
  83.6 6.3 %collective-permute-start.24 = (bf16[128,512]{1,0:T(8,128)(2,1)S(1)}, bf16[128,512]{1,0:T(8,128)(2,1)}, u32[]{:S(2)}, u32[]{:S(2)}) collective-permute-start(bf16[128,512]{1,0:T(8,128)(2,1)S(1)} %collective-permute-done.20.refs_21_), channel_id=1, source_target_pairs={{0,1},{1,2},{2,3},{3,4},{4,5},{5,6},{6,7},{7,0},{8,15},{9,8},{10,9... | collective-permute-start | bytes 393224 | tf_op jit(solution)/shard_map/ppermute | solution.py:268
  85.0 6.3 %collective-permute-start.25 = (bf16[128,512]{1,0:T(8,128)(2,1)S(1)}, bf16[128,512]{1,0:T(8,128)(2,1)}, u32[]{:S(2)}, u32[]{:S(2)}) collective-permute-start(bf16[128,512]{1,0:T(8,128)(2,1)S(1)} %collective-permute-done.21.refs_22_), channel_id=1, source_target_pairs={{0,1},{1,2},{2,3},{3,4},{4,5},{5,6},{6,7},{7,0},{8,15},{9,8},{10,9... | collective-permute-start | bytes 393224 | tf_op jit(solution)/shard_map/ppermute | solution.py:268
  86.4 6.3 %collective-permute-start.26 = (bf16[128,512]{1,0:T(8,128)(2,1)S(1)}, bf16[128,512]{1,0:T(8,128)(2,1)}, u32[]{:S(2)}, u32[]{:S(2)}) collective-permute-start(bf16[128,512]{1,0:T(8,128)(2,1)S(1)} %collective-permute-done.22.refs_23_), channel_id=1, source_target_pairs={{0,1},{1,2},{2,3},{3,4},{4,5},{5,6},{6,7},{7,0},{8,15},{9,8},{10,9... | collective-permute-start | bytes 393224 | tf_op jit(solution)/shard_map/ppermute | solution.py:268
  88.0 6.5 %collective-permute-start.27 = (bf16[128,512]{1,0:T(8,128)(2,1)}, bf16[128,512]{1,0:T(8,128)(2,1)}, u32[]{:S(2)}, u32[]{:S(2)}) collective-permute-start(bf16[128,512]{1,0:T(8,128)(2,1)} %collective-permute-done.23.refs_24_), channel_id=1, source_target_pairs={{0,1},{1,2},{2,3},{3,4},{4,5},{5,6},{6,7},{7,0},{8,15},{9,8},{10,9... | collective-permute-start | bytes 393224 | tf_op jit(solution)/shard_map/ppermute | solution.py:268
  89.9 6.5 %collective-permute-start.28 = (bf16[128,512]{1,0:T(8,128)(2,1)}, bf16[128,512]{1,0:T(8,128)(2,1)}, u32[]{:S(2)}, u32[]{:S(2)}) collective-permute-start(bf16[128,512]{1,0:T(8,128)(2,1)} %collective-permute-done.24.refs_25_), channel_id=1, source_target_pairs={{0,1},{1,2},{2,3},{3,4},{4,5},{5,6},{6,7},{7,0},{8,15},{9,8},{10,9... | collective-permute-start | bytes 393224 | tf_op jit(solution)/shard_map/ppermute | solution.py:268
  91.3 6.5 %collective-permute-start.29 = (bf16[128,512]{1,0:T(8,128)(2,1)}, bf16[128,512]{1,0:T(8,128)(2,1)}, u32[]{:S(2)}, u32[]{:S(2)}) collective-permute-start(bf16[128,512]{1,0:T(8,128)(2,1)} %collective-permute-done.25.refs_26_), channel_id=1, source_target_pairs={{0,1},{1,2},{2,3},{3,4},{4,5},{5,6},{6,7},{7,0},{8,15},{9,8},{10,9... | collective-permute-start | bytes 393224 | tf_op jit(solution)/shard_map/ppermute | solution.py:268
  92.7 6.5 %collective-permute-start.30 = (bf16[128,512]{1,0:T(8,128)(2,1)}, bf16[128,512]{1,0:T(8,128)(2,1)}, u32[]{:S(2)}, u32[]{:S(2)}) collective-permute-start(bf16[128,512]{1,0:T(8,128)(2,1)} %collective-permute-done.26.refs_27_), channel_id=1, source_target_pairs={{0,1},{1,2},{2,3},{3,4},{4,5},{5,6},{6,7},{7,0},{8,15},{9,8},{10,9... | collective-permute-start | bytes 393224 | tf_op jit(solution)/shard_map/ppermute | solution.py:268
  105.6 13.5 %all-to-all-start = ((f32[8,1,512]{2,1,0:T(1,128)}), f32[8,1,512]{2,1,0:T(1,128)S(1)}, u32[]{:S(2)}, u32[]{:S(2)}) async-start(f32[8,1,512]{2,1,0:T(1,128)} %get-tuple-element.26), calls=%async_computation | async-start | bytes 32768 | tf_op jit(solution)/shard_map/all_to_all | solution.py:310
  (36 other events, 963.6 us)
Sparse Core Ops, SparseCore 0:
  35.3 58.1 all-gather.2

commit v11 on v10

--- a/solution.py
+++ b/solution.py
@@ -116,6 +116,20 @@
         compiler_params=pltpu.CompilerParams(vmem_limit_bytes=1024 * 1024),
         name="hold",
     )(array, other, *after)
+
+
+def held_alone(array, after):
+    hbm = pl.BlockSpec(memory_space=pltpu.HBM)
+    after = [pltpu.with_memory_space_constraint(x, pltpu.VMEM) for x in after]
+    return pl.pallas_call(
+        hold_kernel,
+        in_specs=[hbm] + [VMEM] * len(after),
+        out_specs=hbm,
+        out_shape=jax.ShapeDtypeStruct(array.shape, array.dtype),
+        input_output_aliases={0: 0},
+        compiler_params=pltpu.CompilerParams(vmem_limit_bytes=1024 * 1024),
+        name="hold",
+    )(array, *after)
 
 
 def attend_kernel(place_ref, q_ref, own_ref, prev_ref, far_ref, *out_refs):
@@ -191,7 +205,14 @@
     copies = []
     for k in range(N_HEAD):
         copies.append(
-            [pltpu.make_async_copy(w_ref.at[order_ref[k]], w_buffer.at[k], arrived.at[k, PIECES])]
+            [
+                pltpu.make_async_copy(
+                    w_ref.at[order_ref[0, k], order_ref[1, k] ^ part],
+                    w_buffer.at[k, part],
+                    arrived.at[k, PIECES + part],
+                )
+                for part in range(2)
+            ]
             + [
                 pltpu.make_async_copy(
                     ctx_refs[k * PIECES + g],
@@ -206,7 +227,9 @@
     for k in range(N_HEAD):
         for copy in copies[k]:
             copy.wait()
-        value = jnp.dot(w_buffer[k], ctx_buffer[k], preferred_element_type=jnp.float32)
+        value = jnp.dot(
+            w_buffer[k].reshape(FEATURES, WIDTH), ctx_buffer[k], preferred_element_type=jnp.float32
+        )
         if k > 0:
             value = acc_ref[...] + value
         acc_ref[...] = value
@@ -227,9 +250,9 @@
             jax.ShapeDtypeStruct((N_HEAD, 1, ROWS), jnp.float32),
         ],
         scratch_shapes=[
-            pltpu.VMEM((N_HEAD, FEATURES, WIDTH), jnp.bfloat16),
+            pltpu.VMEM((N_HEAD, 2, FEATURES // 2, WIDTH), jnp.bfloat16),
             pltpu.VMEM((N_HEAD, WIDTH, ROWS), jnp.bfloat16),
-            pltpu.SemaphoreType.DMA((N_HEAD, PIECES + 1)),
+            pltpu.SemaphoreType.DMA((N_HEAD, PIECES + 2)),
         ],
         compiler_params=pltpu.CompilerParams(vmem_limit_bytes=20 * 1024 * 1024),
         name="project",
@@ -273,9 +296,12 @@
 
 
 def spread(x, y, core, head):
-    feature = 2 * x + y // 2
-    group = (feature + head) % N_HEAD
-    return group // 2, group % 2 * 2 + y % 2, core, feature
+    group = (2 * x + y // 2 + head) % N_HEAD
+    return group // 2, group % 2 * 2 + (y + head) % 2, core, head
+
+
+def lifted(x, y, core, head):
+    return x, y, core, 2 * x + y // 2 - head
 
 
 def on_device(positions, queries, keys, values, out_weight, post_gain, residual):
@@ -292,9 +318,9 @@
     far = lax.ppermute(own, "seq", [(i, i + 2) for i in range(N_SEQ - 2)])
     q = rotate(queries.reshape(ROWS, WIDTH), cosine, sine)
     shard, far = held(shard, far, after=[q])
+    shard = moved(shard, lifted)
     given = jnp.where(seq % 2 == 0, own, far)
     prev = lax.ppermute(given, "seq", [(i, i ^ 1) for i in range(N_SEQ)])
-    weights = lax.all_gather(shard, "seq", axis=0).reshape(N_HEAD, FEATURES, WIDTH)
 
     blocks = [[] for _ in range(N_HEAD)]
     place = seq.reshape(1)
@@ -304,8 +330,11 @@
             carried = moved(carried, lambda x, y, core, head: (x, y, core, head + sense(core)))
             blocks[k].append(carried)
 
-    source = head - sense(seq % 2) * jnp.arange(N_HEAD, dtype=jnp.int32)
-    order = ((source + head) % N_HEAD).astype(jnp.int32)
+    shard = held_alone(shard, after=blocks[0])
+    weights = lax.all_gather(shard, "seq", axis=0).reshape(N_HEAD, 2, FEATURES // 2, WIDTH)
+
+    source = (head - sense(seq % 2) * jnp.arange(N_HEAD, dtype=jnp.int32)) % N_HEAD
+    order = jnp.stack([(source + head) % N_HEAD, source % 2]).astype(jnp.int32)
     attended, squares = project(order, weights, [x for row in blocks for x in row])
     squares = lax.all_to_all(squares, "head", 0, 0, tiled=True)
     return finish(attended, squares, post_gain[:, None], residual.T).T

time: 128 us -> 126 us (0.984)
  starting transfers between devices: 67.6 us -> 63.5 us
  waiting for transfers between devices: 29 us -> 30.7 us
    ppermute x1, waiting for transfers between devices: 0.01 us -> 11.2 us  [on_device(): far = lax.ppermute(own, 'seq', [(i, i + 2) for i in range(N_SEQ - 2)])]
    ppermute x29 -> x30, waiting for transfers between devices: 19.4 us -> 10.2 us  [moved(): return lax.ppermute(array, ('seq', 'head'), pairs)]
    ppermute x29 -> x30, starting transfers between devices: 58.2 us -> 52.9 us  [moved(): return lax.ppermute(array, ('seq', 'head'), pairs)]
    ppermute x1, waiting for transfers between devices: 1.9 us -> 0.01 us  [on_device(): prev = lax.ppermute(given, 'seq', [(i, i ^ 1) for i in range(N_SEQ)])]
    all_gather x1, waiting for transfers between devices: 0.01 us -> 1.73 us  [on_device(): lax.all_gather(shard, 'seq', axis=0)]
  transfers between devices with their start and end apart: 33 -> 34, of which waited for: 12 -> 18; matrix products, arithmetic and copies ran while one was open for 1% -> 1% of each run, Pallas kernels for 4% -> 5%
where the time goes in v11:
time: 126 us; the launch traced here: 125 us
  starting transfers between devices  63.5 us (50%)
  waiting for transfers between devices  30.7 us (24%)
  Pallas kernels  13.7 us (11%)
  between operations  13.7 us (11%)
  local copies, waits for them, and re-layouts  3.14 us (2%)
    ppermute x30, starting transfers between devices, moved(): return lax.ppermute(array, ('seq', 'head'), pairs)  52.9 us
    ppermute x1, waiting for transfers between devices, on_device(): far = lax.ppermute(own, 'seq', [(i, i + 2) for i in range(N_SEQ - 2)])  11.2 us
    ppermute x30, waiting for transfers between devices, moved(): return lax.ppermute(array, ('seq', 'head'), pairs)  10.2 us
    all_to_all x1, waiting for transfers between devices, on_device(): squares = lax.all_to_all(squares, 'head', 0, 0, tiled=True)  7.62 us
    all_to_all x1, starting transfers between devices, on_device(): squares = lax.all_to_all(squares, 'head', 0, 0, tiled=True)  7.02 us
    pallas_call x1, Pallas kernels, project(): pl.pallas_call(project_kernel, in_specs=[pl.BlockSpec(memory_space=pltpu....  6.3 us
    pallas_call x1, Pallas kernels, attend(): pl.pallas_call(attend_kernel, in_specs=[pl.BlockSpec(memory_space=pltpu.S...  5.38 us
    ppermute x1, starting transfers between devices, on_device(): far = lax.ppermute(own, 'seq', [(i, i + 2) for i in range(N_SEQ - 2)])  3.48 us
  transfers between devices with their start and end apart: 34, of which 18 were waited for; matrix products, arithmetic and copies ran while one was open for 1% of the time, Pallas kernels for 5%

profile of v11, /device:TPU:6, one launch (start us, length us, event | category | flops | bytes accessed | tf_op | source)
XLA Modules:
  0.0 124.9 jit_solution(5542632792462920915)
XLA Ops:
  9.0 3.5 %collective-permute-start.1 = (bf16[2,2,512,128]{3,2,1,0:T(8,128)(2,1)S(1)}, bf16[2,2,512,128]{3,2,1,0:T(8,128)(2,1)S(1)}, u32[]{:S(2)}, u32[]{:S(2)}) collective-permute-start(bf16[2,2,512,128]{3,2,1,0:T(8,128)(2,1)S(1)} %get-tuple-element.16.own_ref), channel_id=1, source_target_pairs={{0,16},{8,24},{16,32},{24,40},{32,48},{40,56},{48,64},{56,72},{64,... | collective-permute-start | bytes 1572872 | tf_op jit(solution)/shard_map/ppermute | solution.py:318
  12.5 1.6 %collective-permute-start = (bf16[168,512]{1,0:T(8,128)(2,1)}, bf16[168,512]{1,0:T(8,128)(2,1)S(1)}, u32[]{:S(2)}, u32[]{:S(2)}) collective-permute-start(bf16[168,512]{1,0:T(8,128)(2,1)} %bitcast.21), channel_id=1, source_target_pairs={{0,0},{1,49},{2,66},{3,115},{4,132},{5,181},{6,198},{7,247},{8,8},... | collective-permute-start | bytes 516104 | tf_op jit(solution)/shard_map/ppermute | solution.py:291
  15.5 11.2 %collective-permute-done.1.refs_1_ = bf16[2,2,512,128]{3,2,1,0:T(8,128)(2,1)S(1)} collective-permute-done((bf16[2,2,512,128]{3,2,1,0:T(8,128)(2,1)S(1)}, bf16[2,2,512,128]{3,2,1,0:T(8,128)(2,1)S(1)}, u32[]{:S(2)}, u32[]{:S(2)}) %collective-permute-start.1) | collective-permute-done | bytes 524320 | tf_op jit(solution)/shard_map/ppermute | solution.py:318
  26.8 8.2 %collective-permute-start.2 = (bf16[168,512]{1,0:T(8,128)(2,1)S(1)}, bf16[168,512]{1,0:T(8,128)(2,1)}, u32[]{:S(2)}, u32[]{:S(2)}) collective-permute-start(bf16[168,512]{1,0:T(8,128)(2,1)S(1)} %get-tuple-element.19), channel_id=1, source_target_pairs={{0,0},{1,7},{2,6},{3,5},{4,4},{5,3},{6,2},{7,1},{8,8},{9,15},{10,1... | collective-permute-start | bytes 516104 | tf_op jit(solution)/shard_map/ppermute | solution.py:291
  35.0 5.4 %attend.1 = (bf16[128,512]{1,0:T(8,128)(2,1)S(1)}, bf16[128,512]{1,0:T(8,128)(2,1)S(1)}, bf16[128,512]{1,0:T(8,128)(2,1)S(1)}, bf16[128,512]{1,0:T(8,128)(2,1)S(1)}) custom-call(s32[1]{0:T(128)} %bitcast.5.place_ref, bf16[512,512]{1,0:T(8,128)(2,1)S(1)} %rotate.1.refs_2_.q_ref, bf16[2,2,512,128]{3,2,1,0:T(8,128)(2,1)S(1)} %get-tuple-element.16.own_ref, ...), custom_call_target="tpu_custom_call" | custom-call | tf_op jit(solution)/shard_map/attend/pallas_call | solution.py:192
  40.6 5.7 %collective-permute-start.4 = (bf16[128,512]{1,0:T(8,128)(2,1)S(1)}, bf16[128,512]{1,0:T(8,128)(2,1)S(1)}, u32[]{:S(2)}, u32[]{:S(2)}) collective-permute-start(bf16[128,512]{1,0:T(8,128)(2,1)S(1)} %get-tuple-element.21.refs_1_.refs_0_), channel_id=1, source_target_pairs={{0,1},{1,2},{2,3},{3,4},{4,5},{5,6},{6,7},{7,0},{8,15},{9,8},{10,9... | collective-permute-start | bytes 393224 | tf_op jit(solution)/shard_map/ppermute | solution.py:291
  48.7 4.5 %collective-permute-start.8 = (bf16[128,512]{1,0:T(8,128)(2,1)S(1)}, bf16[128,512]{1,0:T(8,128)(2,1)S(1)}, u32[]{:S(2)}, u32[]{:S(2)}) collective-permute-start(bf16[128,512]{1,0:T(8,128)(2,1)S(1)} %collective-permute-done.4.refs_4_), channel_id=1, source_target_pairs={{0,1},{1,2},{2,3},{3,4},{4,5},{5,6},{6,7},{7,0},{8,15},{9,8},{10,9... | collective-permute-start | bytes 393224 | tf_op jit(solution)/shard_map/ppermute | solution.py:291
  56.6 2.9 %collective-permute-start.12 = (bf16[128,512]{1,0:T(8,128)(2,1)S(1)}, bf16[128,512]{1,0:T(8,128)(2,1)S(1)}, u32[]{:S(2)}, u32[]{:S(2)}) collective-permute-start(bf16[128,512]{1,0:T(8,128)(2,1)S(1)} %collective-permute-done.8.refs_8_), channel_id=1, source_target_pairs={{0,1},{1,2},{2,3},{3,4},{4,5},{5,6},{6,7},{7,0},{8,15},{9,8},{10,9... | collective-permute-start | bytes 393224 | tf_op jit(solution)/shard_map/ppermute | solution.py:291
  59.5 1.4 %collective-permute-start.13 = (bf16[128,512]{1,0:T(8,128)(2,1)S(1)}, bf16[128,512]{1,0:T(8,128)(2,1)S(1)}, u32[]{:S(2)}, u32[]{:S(2)}) collective-permute-start(bf16[128,512]{1,0:T(8,128)(2,1)S(1)} %collective-permute-done.9.refs_9_), channel_id=1, source_target_pairs={{0,1},{1,2},{2,3},{3,4},{4,5},{5,6},{6,7},{7,0},{8,15},{9,8},{10,9... | collective-permute-start | bytes 393224 | tf_op jit(solution)/shard_map/ppermute | solution.py:291
  62.3 1.4 %collective-permute-start.15 = (bf16[128,512]{1,0:T(8,128)(2,1)S(1)}, bf16[128,512]{1,0:T(8,128)(2,1)S(1)}, u32[]{:S(2)}, u32[]{:S(2)}) collective-permute-start(bf16[128,512]{1,0:T(8,128)(2,1)S(1)} %collective-permute-done.11.refs_11_), channel_id=1, source_target_pairs={{0,1},{1,2},{2,3},{3,4},{4,5},{5,6},{6,7},{7,0},{8,15},{9,8},{10,9... | collective-permute-start | bytes 393224 | tf_op jit(solution)/shard_map/ppermute | solution.py:291
  63.7 2.0 %collective-permute-start.16 = (bf16[128,512]{1,0:T(8,128)(2,1)S(1)}, bf16[128,512]{1,0:T(8,128)(2,1)S(1)}, u32[]{:S(2)}, u32[]{:S(2)}) collective-permute-start(bf16[128,512]{1,0:T(8,128)(2,1)S(1)} %collective-permute-done.12.refs_12_), channel_id=1, source_target_pairs={{0,1},{1,2},{2,3},{3,4},{4,5},{5,6},{6,7},{7,0},{8,15},{9,8},{10,9... | collective-permute-start | bytes 393224 | tf_op jit(solution)/shard_map/ppermute | solution.py:291
  65.7 1.4 %collective-permute-start.17 = (bf16[128,512]{1,0:T(8,128)(2,1)S(1)}, bf16[128,512]{1,0:T(8,128)(2,1)S(1)}, u32[]{:S(2)}, u32[]{:S(2)}) collective-permute-start(bf16[128,512]{1,0:T(8,128)(2,1)S(1)} %collective-permute-done.13.refs_13_), channel_id=1, source_target_pairs={{0,1},{1,2},{2,3},{3,4},{4,5},{5,6},{6,7},{7,0},{8,15},{9,8},{10,9... | collective-permute-start | bytes 393224 | tf_op jit(solution)/shard_map/ppermute | solution.py:291
  69.9 2.0 %collective-permute-start.20 = (bf16[128,512]{1,0:T(8,128)(2,1)S(1)}, bf16[128,512]{1,0:T(8,128)(2,1)S(1)}, u32[]{:S(2)}, u32[]{:S(2)}) collective-permute-start(bf16[128,512]{1,0:T(8,128)(2,1)S(1)} %collective-permute-done.16.refs_16_), channel_id=1, source_target_pairs={{0,1},{1,2},{2,3},{3,4},{4,5},{5,6},{6,7},{7,0},{8,15},{9,8},{10,9... | collective-permute-start | bytes 393224 | tf_op jit(solution)/shard_map/ppermute | solution.py:291
  71.9 1.4 %collective-permute-start.21 = (bf16[128,512]{1,0:T(8,128)(2,1)S(1)}, bf16[128,512]{1,0:T(8,128)(2,1)}, u32[]{:S(2)}, u32[]{:S(2)}) collective-permute-start(bf16[128,512]{1,0:T(8,128)(2,1)S(1)} %collective-permute-done.17.refs_17_), channel_id=1, source_target_pairs={{0,1},{1,2},{2,3},{3,4},{4,5},{5,6},{6,7},{7,0},{8,15},{9,8},{10,9... | collective-permute-start | bytes 393224 | tf_op jit(solution)/shard_map/ppermute | solution.py:291
  74.7 1.4 %collective-permute-start.23 = (bf16[128,512]{1,0:T(8,128)(2,1)S(1)}, bf16[128,512]{1,0:T(8,128)(2,1)}, u32[]{:S(2)}, u32[]{:S(2)}) collective-permute-start(bf16[128,512]{1,0:T(8,128)(2,1)S(1)} %collective-permute-done.19.refs_19_), channel_id=1, source_target_pairs={{0,1},{1,2},{2,3},{3,4},{4,5},{5,6},{6,7},{7,0},{8,15},{9,8},{10,9... | collective-permute-start | bytes 393224 | tf_op jit(solution)/shard_map/ppermute | solution.py:291
  76.1 2.0 %collective-permute-start.24 = (bf16[128,512]{1,0:T(8,128)(2,1)S(1)}, bf16[128,512]{1,0:T(8,128)(2,1)}, u32[]{:S(2)}, u32[]{:S(2)}) collective-permute-start(bf16[128,512]{1,0:T(8,128)(2,1)S(1)} %collective-permute-done.20.refs_20_), channel_id=1, source_target_pairs={{0,1},{1,2},{2,3},{3,4},{4,5},{5,6},{6,7},{7,0},{8,15},{9,8},{10,9... | collective-permute-start | bytes 393224 | tf_op jit(solution)/shard_map/ppermute | solution.py:291
  82.4 2.0 %collective-permute-start.28 = (bf16[128,512]{1,0:T(8,128)(2,1)}, bf16[128,512]{1,0:T(8,128)(2,1)}, u32[]{:S(2)}, u32[]{:S(2)}) collective-permute-start(bf16[128,512]{1,0:T(8,128)(2,1)} %collective-permute-done.24.refs_24_), channel_id=1, source_target_pairs={{0,1},{1,2},{2,3},{3,4},{4,5},{5,6},{6,7},{7,0},{8,15},{9,8},{10,9... | collective-permute-start | bytes 393224 | tf_op jit(solution)/shard_map/ppermute | solution.py:291
  88.8 2.3 %collective-permute-done.29.refs_29_ = bf16[128,512]{1,0:T(8,128)(2,1)} collective-permute-done((bf16[128,512]{1,0:T(8,128)(2,1)}, bf16[128,512]{1,0:T(8,128)(2,1)}, u32[]{:S(2)}, u32[]{:S(2)}) %collective-permute-start.29) | collective-permute-done | bytes 131104 | tf_op jit(solution)/shard_map/ppermute | solution.py:291
  91.1 1.4 %collective-permute-done.30.refs_30_ = bf16[128,512]{1,0:T(8,128)(2,1)} collective-permute-done((bf16[128,512]{1,0:T(8,128)(2,1)}, bf16[128,512]{1,0:T(8,128)(2,1)}, u32[]{:S(2)}, u32[]{:S(2)}) %collective-permute-start.30) | collective-permute-done | bytes 131104 | tf_op jit(solution)/shard_map/ppermute | solution.py:291
  92.5 1.4 %collective-permute-done.31.refs_31_ = bf16[128,512]{1,0:T(8,128)(2,1)} collective-permute-done((bf16[128,512]{1,0:T(8,128)(2,1)}, bf16[128,512]{1,0:T(8,128)(2,1)}, u32[]{:S(2)}, u32[]{:S(2)}) %collective-permute-start.31) | collective-permute-done | bytes 131104 | tf_op jit(solution)/shard_map/ppermute | solution.py:291
  93.9 1.7 %all-gather.3.cloned.1.call-done = bf16[5376,512]{1,0:T(8,128)(2,1)} async-done(((bf16[168,512]{1,0:T(8,128)(2,1)}), bf16[5376,512]{1,0:T(8,128)(2,1)}) %all-gather.3.cloned.1.call-update) | async-done | bytes 5505040 | tf_op jit(solution)/shard_map/all_gather | solution.py:334
  95.9 6.3 %project.1 = (f32[672,512]{1,0:T(8,128)S(1)}, f32[8,1,512]{2,1,0:T(1,128)}) custom-call(s32[2,8]{1,0:T(2,128)S(1)} %pad_add_fusion.order_ref, bf16[8,2,336,512]{3,2,1,0:T(8,128)(2,1)} %bitcast.19, bf16[128,512]{1,0:T(8,128)(2,1)} %copy-done.1, bf16[128,512]{1,0:T(8,128)(2,1)} %copy-done.2, bf16[128,512]{1,0:T(8,128)(2,1)} %copy-done.3, ...), custom_call_target="tpu_custom_call" | custom-call | tf_op jit(solution)/shard_map/project/pallas_call | solution.py:244
  102.2 7.0 %all-to-all-start = ((f32[8,1,512]{2,1,0:T(1,128)}), f32[8,1,512]{2,1,0:T(1,128)S(1)}, u32[]{:S(2)}, u32[]{:S(2)}) async-start(f32[8,1,512]{2,1,0:T(1,128)} %get-tuple-element.26), calls=%async_computation | async-start | bytes 32768 | tf_op jit(solution)/shard_map/all_to_all | solution.py:339
  109.3 7.6 %all-to-all-done.sq_ref = f32[8,1,512]{2,1,0:T(1,128)S(1)} async-done(((f32[8,1,512]{2,1,0:T(1,128)}), f32[8,1,512]{2,1,0:T(1,128)S(1)}, u32[]{:S(2)}, u32[]{:S(2)}) %all-to-all-start) | async-done | bytes 16416 | tf_op jit(solution)/shard_map/all_to_all | solution.py:339
  (108 shorter events, 25.7 us)
Async XLA Ops:
  6.5 89.1 %all-gather.3.cloned.1.call-start = ((), (), s32[]{:S(2)}) async-start(), calls=%async_computation.1 | async-start | bytes 5677056 | tf_op jit(solution)/shard_map/all_gather | solution.py:334
  9.0 17.7 %collective-permute-start.1 = (bf16[2,2,512,128]{3,2,1,0:T(8,128)(2,1)S(1)}, bf16[2,2,512,128]{3,2,1,0:T(8,128)(2,1)S(1)}, u32[]{:S(2)}, u32[]{:S(2)}) collective-permute-start(bf16[2,2,512,128]{3,2,1,0:T(8,128)(2,1)S(1)} %get-tuple-element.16.own_ref), channel_id=1, source_target_pairs={{0,16},{8,24},{16,32},{24,40},{32,48},{40,56},{48,64},{56,72},{64,... | collective-permute-start | bytes 1572872 | tf_op jit(solution)/shard_map/ppermute | solution.py:318
  26.7 8.3 %collective-permute-start.3 = (bf16[2,2,512,128]{3,2,1,0:T(8,128)(2,1)S(1)}, bf16[2,2,512,128]{3,2,1,0:T(8,128)(2,1)S(1)}, u32[]{:S(2)}, u32[]{:S(2)}) collective-permute-start(bf16[2,2,512,128]{3,2,1,0:T(8,128)(2,1)S(1)} %broadcast_select_fusion), channel_id=1, source_target_pairs={{0,8},{8,0},{16,24},{24,16},{32,40},{40,32},{48,56},{56,48},{64,72... | collective-permute-start | bytes 1572872 | tf_op jit(solution)/shard_map/ppermute | solution.py:323
  26.8 13.7 %collective-permute-start.2 = (bf16[168,512]{1,0:T(8,128)(2,1)S(1)}, bf16[168,512]{1,0:T(8,128)(2,1)}, u32[]{:S(2)}, u32[]{:S(2)}) collective-permute-start(bf16[168,512]{1,0:T(8,128)(2,1)S(1)} %get-tuple-element.19), channel_id=1, source_target_pairs={{0,0},{1,7},{2,6},{3,5},{4,4},{5,3},{6,2},{7,1},{8,8},{9,15},{10,1... | collective-permute-start | bytes 516104 | tf_op jit(solution)/shard_map/ppermute | solution.py:291
  40.6 8.2 %collective-permute-start.4 = (bf16[128,512]{1,0:T(8,128)(2,1)S(1)}, bf16[128,512]{1,0:T(8,128)(2,1)S(1)}, u32[]{:S(2)}, u32[]{:S(2)}) collective-permute-start(bf16[128,512]{1,0:T(8,128)(2,1)S(1)} %get-tuple-element.21.refs_1_.refs_0_), channel_id=1, source_target_pairs={{0,1},{1,2},{2,3},{3,4},{4,5},{5,6},{6,7},{7,0},{8,15},{9,8},{10,9... | collective-permute-start | bytes 393224 | tf_op jit(solution)/shard_map/ppermute | solution.py:291
  46.2 7.1 %collective-permute-start.5 = (bf16[128,512]{1,0:T(8,128)(2,1)S(1)}, bf16[128,512]{1,0:T(8,128)(2,1)S(1)}, u32[]{:S(2)}, u32[]{:S(2)}) collective-permute-start(bf16[128,512]{1,0:T(8,128)(2,1)S(1)} %get-tuple-element.22.refs_2_.refs_1_), channel_id=1, source_target_pairs={{0,1},{1,2},{2,3},{3,4},{4,5},{5,6},{6,7},{7,0},{8,15},{9,8},{10,9... | collective-permute-start | bytes 393224 | tf_op jit(solution)/shard_map/ppermute | solution.py:291
  47.1 6.7 %collective-permute-start.6 = (bf16[128,512]{1,0:T(8,128)(2,1)S(1)}, bf16[128,512]{1,0:T(8,128)(2,1)S(1)}, u32[]{:S(2)}, u32[]{:S(2)}) collective-permute-start(bf16[128,512]{1,0:T(8,128)(2,1)S(1)} %get-tuple-element.23.refs_3_.refs_2_), channel_id=1, source_target_pairs={{0,1},{1,2},{2,3},{3,4},{4,5},{5,6},{6,7},{7,0},{8,15},{9,8},{10,9... | collective-permute-start | bytes 393224 | tf_op jit(solution)/shard_map/ppermute | solution.py:291
  47.2 8.0 %collective-permute-start.7 = (bf16[128,512]{1,0:T(8,128)(2,1)S(1)}, bf16[128,512]{1,0:T(8,128)(2,1)S(1)}, u32[]{:S(2)}, u32[]{:S(2)}) collective-permute-start(bf16[128,512]{1,0:T(8,128)(2,1)S(1)} %get-tuple-element.24.refs_4_.refs_3_), channel_id=1, source_target_pairs={{0,1},{1,2},{2,3},{3,4},{4,5},{5,6},{6,7},{7,0},{8,15},{9,8},{10,9... | collective-permute-start | bytes 393224 | tf_op jit(solution)/shard_map/ppermute | solution.py:291
  48.7 7.9 %collective-permute-start.8 = (bf16[128,512]{1,0:T(8,128)(2,1)S(1)}, bf16[128,512]{1,0:T(8,128)(2,1)S(1)}, u32[]{:S(2)}, u32[]{:S(2)}) collective-permute-start(bf16[128,512]{1,0:T(8,128)(2,1)S(1)} %collective-permute-done.4.refs_4_), channel_id=1, source_target_pairs={{0,1},{1,2},{2,3},{3,4},{4,5},{5,6},{6,7},{7,0},{8,15},{9,8},{10,9... | collective-permute-start | bytes 393224 | tf_op jit(solution)/shard_map/ppermute | solution.py:291
  53.8 7.1 %collective-permute-start.10 = (bf16[128,512]{1,0:T(8,128)(2,1)S(1)}, bf16[128,512]{1,0:T(8,128)(2,1)S(1)}, u32[]{:S(2)}, u32[]{:S(2)}) collective-permute-start(bf16[128,512]{1,0:T(8,128)(2,1)S(1)} %collective-permute-done.6.refs_6_), channel_id=1, source_target_pairs={{0,1},{1,2},{2,3},{3,4},{4,5},{5,6},{6,7},{7,0},{8,15},{9,8},{10,9... | collective-permute-start | bytes 393224 | tf_op jit(solution)/shard_map/ppermute | solution.py:291
  55.2 7.1 %collective-permute-start.11 = (bf16[128,512]{1,0:T(8,128)(2,1)S(1)}, bf16[128,512]{1,0:T(8,128)(2,1)S(1)}, u32[]{:S(2)}, u32[]{:S(2)}) collective-permute-start(bf16[128,512]{1,0:T(8,128)(2,1)S(1)} %collective-permute-done.7.refs_7_), channel_id=1, source_target_pairs={{0,1},{1,2},{2,3},{3,4},{4,5},{5,6},{6,7},{7,0},{8,15},{9,8},{10,9... | collective-permute-start | bytes 393224 | tf_op jit(solution)/shard_map/ppermute | solution.py:291
  56.6 7.1 %collective-permute-start.12 = (bf16[128,512]{1,0:T(8,128)(2,1)S(1)}, bf16[128,512]{1,0:T(8,128)(2,1)S(1)}, u32[]{:S(2)}, u32[]{:S(2)}) collective-permute-start(bf16[128,512]{1,0:T(8,128)(2,1)S(1)} %collective-permute-done.8.refs_8_), channel_id=1, source_target_pairs={{0,1},{1,2},{2,3},{3,4},{4,5},{5,6},{6,7},{7,0},{8,15},{9,8},{10,9... | collective-permute-start | bytes 393224 | tf_op jit(solution)/shard_map/ppermute | solution.py:291
  71.9 6.3 %collective-permute-start.21 = (bf16[128,512]{1,0:T(8,128)(2,1)S(1)}, bf16[128,512]{1,0:T(8,128)(2,1)}, u32[]{:S(2)}, u32[]{:S(2)}) collective-permute-start(bf16[128,512]{1,0:T(8,128)(2,1)S(1)} %collective-permute-done.17.refs_17_), channel_id=1, source_target_pairs={{0,1},{1,2},{2,3},{3,4},{4,5},{5,6},{6,7},{7,0},{8,15},{9,8},{10,9... | collective-permute-start | bytes 393224 | tf_op jit(solution)/shard_map/ppermute | solution.py:291
  73.3 6.3 %collective-permute-start.22 = (bf16[128,512]{1,0:T(8,128)(2,1)S(1)}, bf16[128,512]{1,0:T(8,128)(2,1)}, u32[]{:S(2)}, u32[]{:S(2)}) collective-permute-start(bf16[128,512]{1,0:T(8,128)(2,1)S(1)} %collective-permute-done.18.refs_18_), channel_id=1, source_target_pairs={{0,1},{1,2},{2,3},{3,4},{4,5},{5,6},{6,7},{7,0},{8,15},{9,8},{10,9... | collective-permute-start | bytes 393224 | tf_op jit(solution)/shard_map/ppermute | solution.py:291
  74.7 6.3 %collective-permute-start.23 = (bf16[128,512]{1,0:T(8,128)(2,1)S(1)}, bf16[128,512]{1,0:T(8,128)(2,1)}, u32[]{:S(2)}, u32[]{:S(2)}) collective-permute-start(bf16[128,512]{1,0:T(8,128)(2,1)S(1)} %collective-permute-done.19.refs_19_), channel_id=1, source_target_pairs={{0,1},{1,2},{2,3},{3,4},{4,5},{5,6},{6,7},{7,0},{8,15},{9,8},{10,9... | collective-permute-start | bytes 393224 | tf_op jit(solution)/shard_map/ppermute | solution.py:291
  76.1 6.3 %collective-permute-start.24 = (bf16[128,512]{1,0:T(8,128)(2,1)S(1)}, bf16[128,512]{1,0:T(8,128)(2,1)}, u32[]{:S(2)}, u32[]{:S(2)}) collective-permute-start(bf16[128,512]{1,0:T(8,128)(2,1)S(1)} %collective-permute-done.20.refs_20_), channel_id=1, source_target_pairs={{0,1},{1,2},{2,3},{3,4},{4,5},{5,6},{6,7},{7,0},{8,15},{9,8},{10,9... | collective-permute-start | bytes 393224 | tf_op jit(solution)/shard_map/ppermute | solution.py:291
  78.1 6.5 %collective-permute-start.25 = (bf16[128,512]{1,0:T(8,128)(2,1)}, bf16[128,512]{1,0:T(8,128)(2,1)}, u32[]{:S(2)}, u32[]{:S(2)}) collective-permute-start(bf16[128,512]{1,0:T(8,128)(2,1)} %collective-permute-done.21.refs_21_), channel_id=1, source_target_pairs={{0,1},{1,2},{2,3},{3,4},{4,5},{5,6},{6,7},{7,0},{8,15},{9,8},{10,9... | collective-permute-start | bytes 393224 | tf_op jit(solution)/shard_map/ppermute | solution.py:291
  79.5 6.5 %collective-permute-start.26 = (bf16[128,512]{1,0:T(8,128)(2,1)}, bf16[128,512]{1,0:T(8,128)(2,1)}, u32[]{:S(2)}, u32[]{:S(2)}) collective-permute-start(bf16[128,512]{1,0:T(8,128)(2,1)} %collective-permute-done.22.refs_22_), channel_id=1, source_target_pairs={{0,1},{1,2},{2,3},{3,4},{4,5},{5,6},{6,7},{7,0},{8,15},{9,8},{10,9... | collective-permute-start | bytes 393224 | tf_op jit(solution)/shard_map/ppermute | solution.py:291
  81.0 6.5 %collective-permute-start.27 = (bf16[128,512]{1,0:T(8,128)(2,1)}, bf16[128,512]{1,0:T(8,128)(2,1)}, u32[]{:S(2)}, u32[]{:S(2)}) collective-permute-start(bf16[128,512]{1,0:T(8,128)(2,1)} %collective-permute-done.23.refs_23_), channel_id=1, source_target_pairs={{0,1},{1,2},{2,3},{3,4},{4,5},{5,6},{6,7},{7,0},{8,15},{9,8},{10,9... | collective-permute-start | bytes 393224 | tf_op jit(solution)/shard_map/ppermute | solution.py:291
  82.4 6.5 %collective-permute-start.28 = (bf16[128,512]{1,0:T(8,128)(2,1)}, bf16[128,512]{1,0:T(8,128)(2,1)}, u32[]{:S(2)}, u32[]{:S(2)}) collective-permute-start(bf16[128,512]{1,0:T(8,128)(2,1)} %collective-permute-done.24.refs_24_), channel_id=1, source_target_pairs={{0,1},{1,2},{2,3},{3,4},{4,5},{5,6},{6,7},{7,0},{8,15},{9,8},{10,9... | collective-permute-start | bytes 393224 | tf_op jit(solution)/shard_map/ppermute | solution.py:291
  84.6 6.5 %collective-permute-start.29 = (bf16[128,512]{1,0:T(8,128)(2,1)}, bf16[128,512]{1,0:T(8,128)(2,1)}, u32[]{:S(2)}, u32[]{:S(2)}) collective-permute-start(bf16[128,512]{1,0:T(8,128)(2,1)} %collective-permute-done.25.refs_25_), channel_id=1, source_target_pairs={{0,1},{1,2},{2,3},{3,4},{4,5},{5,6},{6,7},{7,0},{8,15},{9,8},{10,9... | collective-permute-start | bytes 393224 | tf_op jit(solution)/shard_map/ppermute | solution.py:291
  86.0 6.5 %collective-permute-start.30 = (bf16[128,512]{1,0:T(8,128)(2,1)}, bf16[128,512]{1,0:T(8,128)(2,1)}, u32[]{:S(2)}, u32[]{:S(2)}) collective-permute-start(bf16[128,512]{1,0:T(8,128)(2,1)} %collective-permute-done.26.refs_26_), channel_id=1, source_target_pairs={{0,1},{1,2},{2,3},{3,4},{4,5},{5,6},{6,7},{7,0},{8,15},{9,8},{10,9... | collective-permute-start | bytes 393224 | tf_op jit(solution)/shard_map/ppermute | solution.py:291
  87.4 6.5 %collective-permute-start.31 = (bf16[128,512]{1,0:T(8,128)(2,1)}, bf16[128,512]{1,0:T(8,128)(2,1)}, u32[]{:S(2)}, u32[]{:S(2)}) collective-permute-start(bf16[128,512]{1,0:T(8,128)(2,1)} %collective-permute-done.27.refs_27_), channel_id=1, source_target_pairs={{0,1},{1,2},{2,3},{3,4},{4,5},{5,6},{6,7},{7,0},{8,15},{9,8},{10,9... | collective-permute-start | bytes 393224 | tf_op jit(solution)/shard_map/ppermute | solution.py:291
  102.2 14.8 %all-to-all-start = ((f32[8,1,512]{2,1,0:T(1,128)}), f32[8,1,512]{2,1,0:T(1,128)S(1)}, u32[]{:S(2)}, u32[]{:S(2)}) async-start(f32[8,1,512]{2,1,0:T(1,128)} %get-tuple-element.26), calls=%async_computation | async-start | bytes 32768 | tf_op jit(solution)/shard_map/all_to_all | solution.py:339
  (34 other events, 972.3 us)
Sparse Core Ops, SparseCore 0:
  40.7 54.9 all-gather.2

commit v12 on v8

--- a/solution.py
+++ b/solution.py
@@ -116,6 +116,20 @@
         compiler_params=pltpu.CompilerParams(vmem_limit_bytes=1024 * 1024),
         name="hold",
     )(array, other, *after)
+
+
+def held_alone(array, after):
+    hbm = pl.BlockSpec(memory_space=pltpu.HBM)
+    after = [pltpu.with_memory_space_constraint(x, pltpu.VMEM) for x in after]
+    return pl.pallas_call(
+        hold_kernel,
+        in_specs=[hbm] + [VMEM] * len(after),
+        out_specs=hbm,
+        out_shape=jax.ShapeDtypeStruct(array.shape, array.dtype),
+        input_output_aliases={0: 0},
+        compiler_params=pltpu.CompilerParams(vmem_limit_bytes=1024 * 1024),
+        name="hold",
+    )(array, *after)
 
 
 def attend_kernel(n, place_ref, q_ref, own_ref, prev_ref, far_ref, out_ref):
@@ -190,7 +204,14 @@
     copies = []
     for k in range(N_HEAD):
         copies.append(
-            [pltpu.make_async_copy(w_ref.at[order_ref[k]], w_buffer.at[k], arrived.at[k, PIECES])]
+            [
+                pltpu.make_async_copy(
+                    w_ref.at[order_ref[0, k], order_ref[1, k] ^ part],
+                    w_buffer.at[k, part],
+                    arrived.at[k, PIECES + part],
+                )
+                for part in range(2)
+            ]
             + [
                 pltpu.make_async_copy(
                     ctx_refs[k * PIECES + g],
@@ -205,7 +226,9 @@
     for k in range(N_HEAD):
         for copy in copies[k]:
             copy.wait()
-        value = jnp.dot(w_buffer[k], ctx_buffer[k], preferred_element_type=jnp.float32)
+        value = jnp.dot(
+            w_buffer[k].reshape(FEATURES, WIDTH), ctx_buffer[k], preferred_element_type=jnp.float32
+        )
         if k > 0:
             value = acc_ref[...] + value
         acc_ref[...] = value
@@ -226,9 +249,9 @@
             jax.ShapeDtypeStruct((N_HEAD, 1, ROWS), jnp.float32),
         ],
         scratch_shapes=[
-            pltpu.VMEM((N_HEAD, FEATURES, WIDTH), jnp.bfloat16),
+            pltpu.VMEM((N_HEAD, 2, FEATURES // 2, WIDTH), jnp.bfloat16),
             pltpu.VMEM((N_HEAD, WIDTH, ROWS), jnp.bfloat16),
-            pltpu.SemaphoreType.DMA((N_HEAD, PIECES + 1)),
+            pltpu.SemaphoreType.DMA((N_HEAD, PIECES + 2)),
         ],
         compiler_params=pltpu.CompilerParams(vmem_limit_bytes=20 * 1024 * 1024),
         name="project",
@@ -272,9 +295,12 @@
 
 
 def spread(x, y, core, head):
-    feature = 2 * x + y // 2
-    group = (feature + head) % N_HEAD
-    return group // 2, group % 2 * 2 + y % 2, core, feature
+    group = (2 * x + y // 2 + head) % N_HEAD
+    return group // 2, group % 2 * 2 + (y + head) % 2, core, head
+
+
+def lifted(x, y, core, head):
+    return x, y, core, 2 * x + y // 2 - head
 
 
 def on_device(positions, queries, keys, values, out_weight, post_gain, residual):
@@ -291,9 +317,9 @@
     far = lax.ppermute(own, "seq", [(i, i + 2) for i in range(N_SEQ - 2)])
     q = rotate(queries.reshape(ROWS, WIDTH), cosine, sine)
     shard, far = held(shard, far, after=[q])
+    shard = moved(shard, lifted)
     given = jnp.where(seq % 2 == 0, own, far)
     prev = lax.ppermute(given, "seq", [(i, i ^ 1) for i in range(N_SEQ)])
-    weights = lax.all_gather(shard, "seq", axis=0).reshape(N_HEAD, FEATURES, WIDTH)
 
     blocks = [[] for _ in range(N_HEAD)]
     place = seq.reshape(1)
@@ -304,8 +330,11 @@
             carried = moved(carried, lambda x, y, core, head: (x, y, core, head + sense(core)))
             blocks[k].append(carried)
 
-    source = head - sense(seq % 2) * jnp.arange(N_HEAD, dtype=jnp.int32)
-    order = ((source + head) % N_HEAD).astype(jnp.int32)
+    shard = held_alone(shard, after=blocks[0][-1:])
+    weights = lax.all_gather(shard, "seq", axis=0).reshape(N_HEAD, 2, FEATURES // 2, WIDTH)
+
+    source = (head - sense(seq % 2) * jnp.arange(N_HEAD, dtype=jnp.int32)) % N_HEAD
+    order = jnp.stack([(source + head) % N_HEAD, source % 2]).astype(jnp.int32)
     attended, squares = project(order, weights, [x for row in blocks for x in row])
     squares = lax.all_to_all(squares, "head", 0, 0, tiled=True)
     return finish(attended, squares, post_gain[:, None], residual.T).T

time: 126 us -> 126 us (level)
    ppermute x1, waiting for transfers between devices: 0.01 us -> 11.2 us  [on_device(): far = lax.ppermute(own, 'seq', [(i, i + 2) for i in range(N_SEQ - 2)])]
    ppermute x29 -> x30, waiting for transfers between devices: 47.5 us -> 37.9 us  [moved(): return lax.ppermute(array, ('seq', 'head'), pairs)]
    ppermute x1, waiting for transfers between devices: 1.9 us -> 0.01 us  [on_device(): prev = lax.ppermute(given, 'seq', [(i, i ^ 1) for i in range(N_SEQ)])]
    ppermute x29 -> x30, starting transfers between devices: 30.4 us -> 29.4 us  [moved(): return lax.ppermute(array, ('seq', 'head'), pairs)]
  transfers between devices with their start and end apart: 33 -> 34, of which waited for: 26 -> 28; matrix products, arithmetic and copies ran while one was open for 1% -> 1% of each run, Pallas kernels for 5% -> 5%
where the time goes in v12:
time: 126 us; the launch traced here: 125 us
  waiting for transfers between devices  56.7 us (45%)
  starting transfers between devices  37.4 us (30%)
  Pallas kernels  14.3 us (11%)
  between operations  13.7 us (11%)
  local copies, waits for them, and re-layouts  3.14 us (2%)
    ppermute x30, waiting for transfers between devices, moved(): return lax.ppermute(array, ('seq', 'head'), pairs)  37.9 us
    ppermute x30, starting transfers between devices, moved(): return lax.ppermute(array, ('seq', 'head'), pairs)  29.4 us
    ppermute x1, waiting for transfers between devices, on_device(): far = lax.ppermute(own, 'seq', [(i, i + 2) for i in range(N_SEQ - 2)])  11.2 us
    all_to_all x1, waiting for transfers between devices, on_device(): squares = lax.all_to_all(squares, 'head', 0, 0, tiled=True)  7.62 us
    pallas_call x1, Pallas kernels, project(): pl.pallas_call(project_kernel, in_specs=[pl.BlockSpec(memory_space=pltpu....  6.3 us
    pallas_call x4, Pallas kernels, attend(): pl.pallas_call(functools.partial(attend_kernel, n), in_specs=[pl.BlockSpe...  6.01 us
    all_to_all x1, starting transfers between devices, on_device(): squares = lax.all_to_all(squares, 'head', 0, 0, tiled=True)  4.38 us
    ppermute x1, starting transfers between devices, on_device(): far = lax.ppermute(own, 'seq', [(i, i + 2) for i in range(N_SEQ - 2)])  3.48 us
  transfers between devices with their start and end apart: 34, of which 28 were waited for; matrix products, arithmetic and copies ran while one was open for 1% of the time, Pallas kernels for 5%

profile of v12, /device:TPU:6, one launch (start us, length us, event | category | flops | bytes accessed | tf_op | source)
XLA Modules:
  0.0 125.4 jit_solution(771711148792434164)
XLA Ops:
  9.0 3.5 %collective-permute-start.1 = (bf16[2,2,512,128]{3,2,1,0:T(8,128)(2,1)S(1)}, bf16[2,2,512,128]{3,2,1,0:T(8,128)(2,1)S(1)}, u32[]{:S(2)}, u32[]{:S(2)}) collective-permute-start(bf16[2,2,512,128]{3,2,1,0:T(8,128)(2,1)S(1)} %get-tuple-element.12.own_ref), channel_id=1, source_target_pairs={{0,16},{8,24},{16,32},{24,40},{32,48},{40,56},{48,64},{56,72},{64,... | collective-permute-start | bytes 1572872 | tf_op jit(solution)/shard_map/ppermute | solution.py:317
  12.5 1.6 %collective-permute-start = (bf16[168,512]{1,0:T(8,128)(2,1)}, bf16[168,512]{1,0:T(8,128)(2,1)S(1)}, u32[]{:S(2)}, u32[]{:S(2)}) collective-permute-start(bf16[168,512]{1,0:T(8,128)(2,1)} %bitcast.21), channel_id=1, source_target_pairs={{0,0},{1,49},{2,66},{3,115},{4,132},{5,181},{6,198},{7,247},{8,8},... | collective-permute-start | bytes 516104 | tf_op jit(solution)/shard_map/ppermute | solution.py:290
  15.5 11.2 %collective-permute-done.1.refs_1_ = bf16[2,2,512,128]{3,2,1,0:T(8,128)(2,1)S(1)} collective-permute-done((bf16[2,2,512,128]{3,2,1,0:T(8,128)(2,1)S(1)}, bf16[2,2,512,128]{3,2,1,0:T(8,128)(2,1)S(1)}, u32[]{:S(2)}, u32[]{:S(2)}) %collective-permute-start.1) | collective-permute-done | bytes 524320 | tf_op jit(solution)/shard_map/ppermute | solution.py:317
  26.8 8.2 %collective-permute-start.2 = (bf16[168,512]{1,0:T(8,128)(2,1)S(1)}, bf16[168,512]{1,0:T(8,128)(2,1)}, u32[]{:S(2)}, u32[]{:S(2)}) collective-permute-start(bf16[168,512]{1,0:T(8,128)(2,1)S(1)} %get-tuple-element.15), channel_id=1, source_target_pairs={{0,0},{1,7},{2,6},{3,5},{4,4},{5,3},{6,2},{7,1},{8,8},{9,15},{10,1... | collective-permute-start | bytes 516104 | tf_op jit(solution)/shard_map/ppermute | solution.py:290
  35.0 1.5 %attend.4.refs_1_.refs_3_ = bf16[128,512]{1,0:T(8,128)(2,1)S(1)} custom-call(s32[1]{0:T(128)} %bitcast.5.place_ref, bf16[512,512]{1,0:T(8,128)(2,1)S(1)} %rotate.1.refs_2_.q_ref, bf16[2,2,512,128]{3,2,1,0:T(8,128)(2,1)S(1)} %get-tuple-element.12.own_ref, bf16[2,2,512,128]{3,2,1,0:T(8,128)(2,1)S(1)} %collective-permute-done.3.prev_ref, ...), custom_call_target="tpu_custom_call" | custom-call | tf_op jit(solution)/shard_map/attend/pallas_call | solution.py:191
  36.6 3.6 %collective-permute-done.2.refs_0_ = bf16[168,512]{1,0:T(8,128)(2,1)} collective-permute-done((bf16[168,512]{1,0:T(8,128)(2,1)S(1)}, bf16[168,512]{1,0:T(8,128)(2,1)}, u32[]{:S(2)}, u32[]{:S(2)}) %collective-permute-start.2) | collective-permute-done | bytes 172064 | tf_op jit(solution)/shard_map/ppermute | solution.py:290
  40.2 1.5 %attend.7.refs_2_ = bf16[128,512]{1,0:T(8,128)(2,1)S(1)} custom-call(s32[1]{0:T(128)} %bitcast.5.place_ref, bf16[512,512]{1,0:T(8,128)(2,1)S(1)} %rotate.1.refs_2_.q_ref, bf16[2,2,512,128]{3,2,1,0:T(8,128)(2,1)S(1)} %get-tuple-element.12.own_ref, bf16[2,2,512,128]{3,2,1,0:T(8,128)(2,1)S(1)} %collective-permute-done.3.prev_ref, ...), custom_call_target="tpu_custom_call" | custom-call | tf_op jit(solution)/shard_map/attend/pallas_call | solution.py:191
  41.7 5.8 %collective-permute-start.6 = (bf16[128,512]{1,0:T(8,128)(2,1)S(1)}, bf16[128,512]{1,0:T(8,128)(2,1)S(1)}, u32[]{:S(2)}, u32[]{:S(2)}) collective-permute-start(bf16[128,512]{1,0:T(8,128)(2,1)S(1)} %attend.7.refs_2_), channel_id=1, source_target_pairs={{0,1},{1,2},{2,3},{3,4},{4,5},{5,6},{6,7},{7,0},{8,15},{9,8},{10,9... | collective-permute-start | bytes 393224 | tf_op jit(solution)/shard_map/ppermute | solution.py:290
  47.5 1.5 %attend.6.refs_1_ = bf16[128,512]{1,0:T(8,128)(2,1)S(1)} custom-call(s32[1]{0:T(128)} %bitcast.5.place_ref, bf16[512,512]{1,0:T(8,128)(2,1)S(1)} %rotate.1.refs_2_.q_ref, bf16[2,2,512,128]{3,2,1,0:T(8,128)(2,1)S(1)} %get-tuple-element.12.own_ref, bf16[2,2,512,128]{3,2,1,0:T(8,128)(2,1)S(1)} %collective-permute-done.3.prev_ref, ...), custom_call_target="tpu_custom_call" | custom-call | tf_op jit(solution)/shard_map/attend/pallas_call | solution.py:191
  50.2 1.5 %attend.5.refs_0_ = bf16[128,512]{1,0:T(8,128)(2,1)S(1)} custom-call(s32[1]{0:T(128)} %bitcast.5.place_ref, bf16[512,512]{1,0:T(8,128)(2,1)S(1)} %rotate.1.refs_2_.q_ref, bf16[2,2,512,128]{3,2,1,0:T(8,128)(2,1)S(1)} %get-tuple-element.12.own_ref, bf16[2,2,512,128]{3,2,1,0:T(8,128)(2,1)S(1)} %collective-permute-done.3.prev_ref, ...), custom_call_target="tpu_custom_call" | custom-call | tf_op jit(solution)/shard_map/attend/pallas_call | solution.py:191
  52.6 5.6 %collective-permute-start.10 = (bf16[128,512]{1,0:T(8,128)(2,1)S(1)}, bf16[128,512]{1,0:T(8,128)(2,1)S(1)}, u32[]{:S(2)}, u32[]{:S(2)}) collective-permute-start(bf16[128,512]{1,0:T(8,128)(2,1)S(1)} %collective-permute-done.6.refs_6_), channel_id=1, source_target_pairs={{0,1},{1,2},{2,3},{3,4},{4,5},{5,6},{6,7},{7,0},{8,15},{9,8},{10,9... | collective-permute-start | bytes 393224 | tf_op jit(solution)/shard_map/ppermute | solution.py:290
  60.8 2.3 %collective-permute-start.14 = (bf16[128,512]{1,0:T(8,128)(2,1)S(1)}, bf16[128,512]{1,0:T(8,128)(2,1)S(1)}, u32[]{:S(2)}, u32[]{:S(2)}) collective-permute-start(bf16[128,512]{1,0:T(8,128)(2,1)S(1)} %collective-permute-done.10.refs_10_), channel_id=1, source_target_pairs={{0,1},{1,2},{2,3},{3,4},{4,5},{5,6},{6,7},{7,0},{8,15},{9,8},{10,9... | collective-permute-start | bytes 393224 | tf_op jit(solution)/shard_map/ppermute | solution.py:290
  68.9 1.6 %collective-permute-done.13.refs_13_ = bf16[128,512]{1,0:T(8,128)(2,1)S(1)} collective-permute-done((bf16[128,512]{1,0:T(8,128)(2,1)S(1)}, bf16[128,512]{1,0:T(8,128)(2,1)S(1)}, u32[]{:S(2)}, u32[]{:S(2)}) %collective-permute-start.13) | collective-permute-done | bytes 131104 | tf_op jit(solution)/shard_map/ppermute | solution.py:290
  75.1 1.6 %collective-permute-done.17.refs_17_ = bf16[128,512]{1,0:T(8,128)(2,1)S(1)} collective-permute-done((bf16[128,512]{1,0:T(8,128)(2,1)S(1)}, bf16[128,512]{1,0:T(8,128)(2,1)S(1)}, u32[]{:S(2)}, u32[]{:S(2)}) %collective-permute-start.17) | collective-permute-done | bytes 131104 | tf_op jit(solution)/shard_map/ppermute | solution.py:290
  81.3 1.7 %collective-permute-done.21.refs_21_ = bf16[128,512]{1,0:T(8,128)(2,1)} collective-permute-done((bf16[128,512]{1,0:T(8,128)(2,1)S(1)}, bf16[128,512]{1,0:T(8,128)(2,1)}, u32[]{:S(2)}, u32[]{:S(2)}) %collective-permute-start.21) | collective-permute-done | bytes 131104 | tf_op jit(solution)/shard_map/ppermute | solution.py:290
  84.4 1.4 %collective-permute-done.23.refs_23_ = bf16[128,512]{1,0:T(8,128)(2,1)} collective-permute-done((bf16[128,512]{1,0:T(8,128)(2,1)S(1)}, bf16[128,512]{1,0:T(8,128)(2,1)}, u32[]{:S(2)}, u32[]{:S(2)}) %collective-permute-start.23) | collective-permute-done | bytes 131104 | tf_op jit(solution)/shard_map/ppermute | solution.py:290
  87.5 1.9 %collective-permute-done.25.refs_25_ = bf16[128,512]{1,0:T(8,128)(2,1)} collective-permute-done((bf16[128,512]{1,0:T(8,128)(2,1)}, bf16[128,512]{1,0:T(8,128)(2,1)}, u32[]{:S(2)}, u32[]{:S(2)}) %collective-permute-start.25) | collective-permute-done | bytes 131104 | tf_op jit(solution)/shard_map/ppermute | solution.py:290
  90.9 1.4 %collective-permute-done.27.refs_27_ = bf16[128,512]{1,0:T(8,128)(2,1)} collective-permute-done((bf16[128,512]{1,0:T(8,128)(2,1)}, bf16[128,512]{1,0:T(8,128)(2,1)}, u32[]{:S(2)}, u32[]{:S(2)}) %collective-permute-start.27) | collective-permute-done | bytes 131104 | tf_op jit(solution)/shard_map/ppermute | solution.py:290
  93.7 2.3 %collective-permute-done.29.refs_29_ = bf16[128,512]{1,0:T(8,128)(2,1)} collective-permute-done((bf16[128,512]{1,0:T(8,128)(2,1)}, bf16[128,512]{1,0:T(8,128)(2,1)}, u32[]{:S(2)}, u32[]{:S(2)}) %collective-permute-start.29) | collective-permute-done | bytes 131104 | tf_op jit(solution)/shard_map/ppermute | solution.py:290
  96.0 1.4 %collective-permute-done.28.refs_28_ = bf16[128,512]{1,0:T(8,128)(2,1)} collective-permute-done((bf16[128,512]{1,0:T(8,128)(2,1)}, bf16[128,512]{1,0:T(8,128)(2,1)}, u32[]{:S(2)}, u32[]{:S(2)}) %collective-permute-start.28) | collective-permute-done | bytes 131104 | tf_op jit(solution)/shard_map/ppermute | solution.py:290
  97.4 1.4 %collective-permute-done.31.refs_31_ = bf16[128,512]{1,0:T(8,128)(2,1)} collective-permute-done((bf16[128,512]{1,0:T(8,128)(2,1)}, bf16[128,512]{1,0:T(8,128)(2,1)}, u32[]{:S(2)}, u32[]{:S(2)}) %collective-permute-start.31) | collective-permute-done | bytes 131104 | tf_op jit(solution)/shard_map/ppermute | solution.py:290
  98.9 6.3 %project.1 = (f32[672,512]{1,0:T(8,128)S(1)}, f32[8,1,512]{2,1,0:T(1,128)}) custom-call(s32[2,8]{1,0:T(2,128)S(1)} %pad_add_fusion.order_ref, bf16[8,2,336,512]{3,2,1,0:T(8,128)(2,1)} %bitcast.19, bf16[128,512]{1,0:T(8,128)(2,1)} %copy-done.4, bf16[128,512]{1,0:T(8,128)(2,1)} %copy-done.3, bf16[128,512]{1,0:T(8,128)(2,1)} %copy-done.2, ...), custom_call_target="tpu_custom_call" | custom-call | tf_op jit(solution)/shard_map/project/pallas_call | solution.py:243
  105.2 4.4 %all-to-all-start = ((f32[8,1,512]{2,1,0:T(1,128)}), f32[8,1,512]{2,1,0:T(1,128)S(1)}, u32[]{:S(2)}, u32[]{:S(2)}) async-start(f32[8,1,512]{2,1,0:T(1,128)} %get-tuple-element.18), calls=%async_computation | async-start | bytes 32768 | tf_op jit(solution)/shard_map/all_to_all | solution.py:339
  109.8 7.6 %all-to-all-done.sq_ref = f32[8,1,512]{2,1,0:T(1,128)S(1)} async-done(((f32[8,1,512]{2,1,0:T(1,128)}), f32[8,1,512]{2,1,0:T(1,128)S(1)}, u32[]{:S(2)}, u32[]{:S(2)}) %all-to-all-start) | async-done | bytes 16416 | tf_op jit(solution)/shard_map/all_to_all | solution.py:339
  (111 shorter events, 30.9 us)
Async XLA Ops:
  6.5 92.2 %all-gather.3.cloned.1.call-start = ((), (), s32[]{:S(2)}) async-start(), calls=%async_computation.1 | async-start | bytes 5677056 | tf_op jit(solution)/shard_map/all_gather | solution.py:334
  9.0 17.7 %collective-permute-start.1 = (bf16[2,2,512,128]{3,2,1,0:T(8,128)(2,1)S(1)}, bf16[2,2,512,128]{3,2,1,0:T(8,128)(2,1)S(1)}, u32[]{:S(2)}, u32[]{:S(2)}) collective-permute-start(bf16[2,2,512,128]{3,2,1,0:T(8,128)(2,1)S(1)} %get-tuple-element.12.own_ref), channel_id=1, source_target_pairs={{0,16},{8,24},{16,32},{24,40},{32,48},{40,56},{48,64},{56,72},{64,... | collective-permute-start | bytes 1572872 | tf_op jit(solution)/shard_map/ppermute | solution.py:317
  26.7 8.3 %collective-permute-start.3 = (bf16[2,2,512,128]{3,2,1,0:T(8,128)(2,1)S(1)}, bf16[2,2,512,128]{3,2,1,0:T(8,128)(2,1)S(1)}, u32[]{:S(2)}, u32[]{:S(2)}) collective-permute-start(bf16[2,2,512,128]{3,2,1,0:T(8,128)(2,1)S(1)} %broadcast_select_fusion), channel_id=1, source_target_pairs={{0,8},{8,0},{16,24},{24,16},{32,40},{40,32},{48,56},{56,48},{64,72... | collective-permute-start | bytes 1572872 | tf_op jit(solution)/shard_map/ppermute | solution.py:322
  26.8 13.3 %collective-permute-start.2 = (bf16[168,512]{1,0:T(8,128)(2,1)S(1)}, bf16[168,512]{1,0:T(8,128)(2,1)}, u32[]{:S(2)}, u32[]{:S(2)}) collective-permute-start(bf16[168,512]{1,0:T(8,128)(2,1)S(1)} %get-tuple-element.15), channel_id=1, source_target_pairs={{0,0},{1,7},{2,6},{3,5},{4,4},{5,3},{6,2},{7,1},{8,8},{9,15},{10,1... | collective-permute-start | bytes 516104 | tf_op jit(solution)/shard_map/ppermute | solution.py:290
  41.7 10.9 %collective-permute-start.6 = (bf16[128,512]{1,0:T(8,128)(2,1)S(1)}, bf16[128,512]{1,0:T(8,128)(2,1)S(1)}, u32[]{:S(2)}, u32[]{:S(2)}) collective-permute-start(bf16[128,512]{1,0:T(8,128)(2,1)S(1)} %attend.7.refs_2_), channel_id=1, source_target_pairs={{0,1},{1,2},{2,3},{3,4},{4,5},{5,6},{6,7},{7,0},{8,15},{9,8},{10,9... | collective-permute-start | bytes 393224 | tf_op jit(solution)/shard_map/ppermute | solution.py:290
  49.0 9.1 %collective-permute-start.5 = (bf16[128,512]{1,0:T(8,128)(2,1)S(1)}, bf16[128,512]{1,0:T(8,128)(2,1)S(1)}, u32[]{:S(2)}, u32[]{:S(2)}) collective-permute-start(bf16[128,512]{1,0:T(8,128)(2,1)S(1)} %attend.6.refs_1_), channel_id=1, source_target_pairs={{0,1},{1,2},{2,3},{3,4},{4,5},{5,6},{6,7},{7,0},{8,15},{9,8},{10,9... | collective-permute-start | bytes 393224 | tf_op jit(solution)/shard_map/ppermute | solution.py:290
  51.8 6.5 %collective-permute-start.4 = (bf16[128,512]{1,0:T(8,128)(2,1)S(1)}, bf16[128,512]{1,0:T(8,128)(2,1)S(1)}, u32[]{:S(2)}, u32[]{:S(2)}) collective-permute-start(bf16[128,512]{1,0:T(8,128)(2,1)S(1)} %attend.5.refs_0_), channel_id=1, source_target_pairs={{0,1},{1,2},{2,3},{3,4},{4,5},{5,6},{6,7},{7,0},{8,15},{9,8},{10,9... | collective-permute-start | bytes 393224 | tf_op jit(solution)/shard_map/ppermute | solution.py:290
  51.9 7.6 %collective-permute-start.7 = (bf16[128,512]{1,0:T(8,128)(2,1)S(1)}, bf16[128,512]{1,0:T(8,128)(2,1)S(1)}, u32[]{:S(2)}, u32[]{:S(2)}) collective-permute-start(bf16[128,512]{1,0:T(8,128)(2,1)S(1)} %attend.4.refs_1_.refs_3_), channel_id=1, source_target_pairs={{0,1},{1,2},{2,3},{3,4},{4,5},{5,6},{6,7},{7,0},{8,15},{9,8},{10,9... | collective-permute-start | bytes 393224 | tf_op jit(solution)/shard_map/ppermute | solution.py:290
  52.6 8.3 %collective-permute-start.10 = (bf16[128,512]{1,0:T(8,128)(2,1)S(1)}, bf16[128,512]{1,0:T(8,128)(2,1)S(1)}, u32[]{:S(2)}, u32[]{:S(2)}) collective-permute-start(bf16[128,512]{1,0:T(8,128)(2,1)S(1)} %collective-permute-done.6.refs_6_), channel_id=1, source_target_pairs={{0,1},{1,2},{2,3},{3,4},{4,5},{5,6},{6,7},{7,0},{8,15},{9,8},{10,9... | collective-permute-start | bytes 393224 | tf_op jit(solution)/shard_map/ppermute | solution.py:290
  58.2 7.5 %collective-permute-start.8 = (bf16[128,512]{1,0:T(8,128)(2,1)S(1)}, bf16[128,512]{1,0:T(8,128)(2,1)S(1)}, u32[]{:S(2)}, u32[]{:S(2)}) collective-permute-start(bf16[128,512]{1,0:T(8,128)(2,1)S(1)} %collective-permute-done.4.refs_4_), channel_id=1, source_target_pairs={{0,1},{1,2},{2,3},{3,4},{4,5},{5,6},{6,7},{7,0},{8,15},{9,8},{10,9... | collective-permute-start | bytes 393224 | tf_op jit(solution)/shard_map/ppermute | solution.py:290
  59.4 7.7 %collective-permute-start.11 = (bf16[128,512]{1,0:T(8,128)(2,1)S(1)}, bf16[128,512]{1,0:T(8,128)(2,1)S(1)}, u32[]{:S(2)}, u32[]{:S(2)}) collective-permute-start(bf16[128,512]{1,0:T(8,128)(2,1)S(1)} %collective-permute-done.7.refs_7_), channel_id=1, source_target_pairs={{0,1},{1,2},{2,3},{3,4},{4,5},{5,6},{6,7},{7,0},{8,15},{9,8},{10,9... | collective-permute-start | bytes 393224 | tf_op jit(solution)/shard_map/ppermute | solution.py:290
  60.8 7.7 %collective-permute-start.14 = (bf16[128,512]{1,0:T(8,128)(2,1)S(1)}, bf16[128,512]{1,0:T(8,128)(2,1)S(1)}, u32[]{:S(2)}, u32[]{:S(2)}) collective-permute-start(bf16[128,512]{1,0:T(8,128)(2,1)S(1)} %collective-permute-done.10.refs_10_), channel_id=1, source_target_pairs={{0,1},{1,2},{2,3},{3,4},{4,5},{5,6},{6,7},{7,0},{8,15},{9,8},{10,9... | collective-permute-start | bytes 393224 | tf_op jit(solution)/shard_map/ppermute | solution.py:290
  76.7 6.3 %collective-permute-start.21 = (bf16[128,512]{1,0:T(8,128)(2,1)S(1)}, bf16[128,512]{1,0:T(8,128)(2,1)}, u32[]{:S(2)}, u32[]{:S(2)}) collective-permute-start(bf16[128,512]{1,0:T(8,128)(2,1)S(1)} %collective-permute-done.17.refs_17_), channel_id=1, source_target_pairs={{0,1},{1,2},{2,3},{3,4},{4,5},{5,6},{6,7},{7,0},{8,15},{9,8},{10,9... | collective-permute-start | bytes 393224 | tf_op jit(solution)/shard_map/ppermute | solution.py:290
  78.1 6.3 %collective-permute-start.20 = (bf16[128,512]{1,0:T(8,128)(2,1)S(1)}, bf16[128,512]{1,0:T(8,128)(2,1)}, u32[]{:S(2)}, u32[]{:S(2)}) collective-permute-start(bf16[128,512]{1,0:T(8,128)(2,1)S(1)} %collective-permute-done.16.refs_16_), channel_id=1, source_target_pairs={{0,1},{1,2},{2,3},{3,4},{4,5},{5,6},{6,7},{7,0},{8,15},{9,8},{10,9... | collective-permute-start | bytes 393224 | tf_op jit(solution)/shard_map/ppermute | solution.py:290
  79.5 6.3 %collective-permute-start.23 = (bf16[128,512]{1,0:T(8,128)(2,1)S(1)}, bf16[128,512]{1,0:T(8,128)(2,1)}, u32[]{:S(2)}, u32[]{:S(2)}) collective-permute-start(bf16[128,512]{1,0:T(8,128)(2,1)S(1)} %collective-permute-done.19.refs_19_), channel_id=1, source_target_pairs={{0,1},{1,2},{2,3},{3,4},{4,5},{5,6},{6,7},{7,0},{8,15},{9,8},{10,9... | collective-permute-start | bytes 393224 | tf_op jit(solution)/shard_map/ppermute | solution.py:290
  80.9 6.3 %collective-permute-start.26 = (bf16[128,512]{1,0:T(8,128)(2,1)S(1)}, bf16[128,512]{1,0:T(8,128)(2,1)}, u32[]{:S(2)}, u32[]{:S(2)}) collective-permute-start(bf16[128,512]{1,0:T(8,128)(2,1)S(1)} %collective-permute-done.22.refs_22_), channel_id=1, source_target_pairs={{0,1},{1,2},{2,3},{3,4},{4,5},{5,6},{6,7},{7,0},{8,15},{9,8},{10,9... | collective-permute-start | bytes 393224 | tf_op jit(solution)/shard_map/ppermute | solution.py:290
  83.0 6.5 %collective-permute-start.25 = (bf16[128,512]{1,0:T(8,128)(2,1)}, bf16[128,512]{1,0:T(8,128)(2,1)}, u32[]{:S(2)}, u32[]{:S(2)}) collective-permute-start(bf16[128,512]{1,0:T(8,128)(2,1)} %collective-permute-done.21.refs_21_), channel_id=1, source_target_pairs={{0,1},{1,2},{2,3},{3,4},{4,5},{5,6},{6,7},{7,0},{8,15},{9,8},{10,9... | collective-permute-start | bytes 393224 | tf_op jit(solution)/shard_map/ppermute | solution.py:290
  84.4 6.5 %collective-permute-start.24 = (bf16[128,512]{1,0:T(8,128)(2,1)}, bf16[128,512]{1,0:T(8,128)(2,1)}, u32[]{:S(2)}, u32[]{:S(2)}) collective-permute-start(bf16[128,512]{1,0:T(8,128)(2,1)} %collective-permute-done.20.refs_20_), channel_id=1, source_target_pairs={{0,1},{1,2},{2,3},{3,4},{4,5},{5,6},{6,7},{7,0},{8,15},{9,8},{10,9... | collective-permute-start | bytes 393224 | tf_op jit(solution)/shard_map/ppermute | solution.py:290
  85.8 6.5 %collective-permute-start.27 = (bf16[128,512]{1,0:T(8,128)(2,1)}, bf16[128,512]{1,0:T(8,128)(2,1)}, u32[]{:S(2)}, u32[]{:S(2)}) collective-permute-start(bf16[128,512]{1,0:T(8,128)(2,1)} %collective-permute-done.23.refs_23_), channel_id=1, source_target_pairs={{0,1},{1,2},{2,3},{3,4},{4,5},{5,6},{6,7},{7,0},{8,15},{9,8},{10,9... | collective-permute-start | bytes 393224 | tf_op jit(solution)/shard_map/ppermute | solution.py:290
  87.2 6.5 %collective-permute-start.30 = (bf16[128,512]{1,0:T(8,128)(2,1)}, bf16[128,512]{1,0:T(8,128)(2,1)}, u32[]{:S(2)}, u32[]{:S(2)}) collective-permute-start(bf16[128,512]{1,0:T(8,128)(2,1)} %collective-permute-done.26.refs_26_), channel_id=1, source_target_pairs={{0,1},{1,2},{2,3},{3,4},{4,5},{5,6},{6,7},{7,0},{8,15},{9,8},{10,9... | collective-permute-start | bytes 393224 | tf_op jit(solution)/shard_map/ppermute | solution.py:290
  89.5 6.5 %collective-permute-start.29 = (bf16[128,512]{1,0:T(8,128)(2,1)}, bf16[128,512]{1,0:T(8,128)(2,1)}, u32[]{:S(2)}, u32[]{:S(2)}) collective-permute-start(bf16[128,512]{1,0:T(8,128)(2,1)} %collective-permute-done.25.refs_25_), channel_id=1, source_target_pairs={{0,1},{1,2},{2,3},{3,4},{4,5},{5,6},{6,7},{7,0},{8,15},{9,8},{10,9... | collective-permute-start | bytes 393224 | tf_op jit(solution)/shard_map/ppermute | solution.py:290
  90.9 6.5 %collective-permute-start.28 = (bf16[128,512]{1,0:T(8,128)(2,1)}, bf16[128,512]{1,0:T(8,128)(2,1)}, u32[]{:S(2)}, u32[]{:S(2)}) collective-permute-start(bf16[128,512]{1,0:T(8,128)(2,1)} %collective-permute-done.24.refs_24_), channel_id=1, source_target_pairs={{0,1},{1,2},{2,3},{3,4},{4,5},{5,6},{6,7},{7,0},{8,15},{9,8},{10,9... | collective-permute-start | bytes 393224 | tf_op jit(solution)/shard_map/ppermute | solution.py:290
  92.3 6.5 %collective-permute-start.31 = (bf16[128,512]{1,0:T(8,128)(2,1)}, bf16[128,512]{1,0:T(8,128)(2,1)}, u32[]{:S(2)}, u32[]{:S(2)}) collective-permute-start(bf16[128,512]{1,0:T(8,128)(2,1)} %collective-permute-done.27.refs_27_), channel_id=1, source_target_pairs={{0,1},{1,2},{2,3},{3,4},{4,5},{5,6},{6,7},{7,0},{8,15},{9,8},{10,9... | collective-permute-start | bytes 393224 | tf_op jit(solution)/shard_map/ppermute | solution.py:290
  105.2 12.2 %all-to-all-start = ((f32[8,1,512]{2,1,0:T(1,128)}), f32[8,1,512]{2,1,0:T(1,128)S(1)}, u32[]{:S(2)}, u32[]{:S(2)}) async-start(f32[8,1,512]{2,1,0:T(1,128)} %get-tuple-element.18), calls=%async_computation | async-start | bytes 32768 | tf_op jit(solution)/shard_map/all_to_all | solution.py:339
  (34 other events, 883.9 us)
Sparse Core Ops, SparseCore 0:
  40.3 55.3 all-gather.2

commit v13 on v11

--- a/solution.py
+++ b/solution.py
@@ -132,7 +132,7 @@
     )(array, *after)
 
 
-def attend_kernel(place_ref, q_ref, own_ref, prev_ref, far_ref, *out_refs):
+def attend_kernel(first, place_ref, q_ref, own_ref, prev_ref, far_ref, *out_refs):
     place = place_ref[0]
     prev_bias = jnp.where(place >= 1, 0.0, LOW)
     far_bias = jnp.where(place >= 2, 0.0, LOW)
@@ -141,7 +141,7 @@
     col = lax.broadcasted_iota(jnp.int32, (QB, QB), 1)
     seen = row <= col
     blocks = ROWS // QB
-    for n in range(PIECES):
+    for n in range(first, first + GROUP):
         g = n // GROUP
         k_own, k_prev, k_far = own_ref[g, 0], prev_ref[g, 0], far_ref[g, 0]
         v_own = own_ref[g, 1].T
@@ -184,16 +184,16 @@
             context += jnp.dot(
                 v_far[:, lo:], jnp.concatenate(far_parts, 0), preferred_element_type=jnp.float32
             )
-            out_refs[n][:, lo:hi] = (context / total).astype(jnp.bfloat16)
-
-
-def attend(place, *arrays):
+            out_refs[n - first][:, lo:hi] = (context / total).astype(jnp.bfloat16)
+
+
+def attend(first, place, *arrays):
     arrays = [pltpu.with_memory_space_constraint(x, pltpu.VMEM) for x in arrays]
     return pl.pallas_call(
-        attend_kernel,
+        functools.partial(attend_kernel, first),
         in_specs=[pl.BlockSpec(memory_space=pltpu.SMEM)] + [VMEM] * len(arrays),
-        out_specs=[VMEM] * PIECES,
-        out_shape=[jax.ShapeDtypeStruct((PIECE, ROWS), jnp.bfloat16)] * PIECES,
+        out_specs=[VMEM] * GROUP,
+        out_shape=[jax.ShapeDtypeStruct((PIECE, ROWS), jnp.bfloat16)] * GROUP,
         compiler_params=pltpu.CompilerParams(vmem_limit_bytes=16 * 1024 * 1024),
         name="attend",
     )(place, *arrays)
@@ -324,13 +324,14 @@
 
     blocks = [[] for _ in range(N_HEAD)]
     place = seq.reshape(1)
-    for carried in attend(place, q, own, prev, far):
+    pieces = [x for n in range(0, PIECES, GROUP) for x in attend(n, place, q, own, prev, far)]
+    for carried in pieces:
         blocks[0].append(carried)
         for k in range(1, N_HEAD):
             carried = moved(carried, lambda x, y, core, head: (x, y, core, head + sense(core)))
             blocks[k].append(carried)
 
-    shard = held_alone(shard, after=blocks[0])
+    shard = held_alone(shard, after=blocks[0][-1:])
     weights = lax.all_gather(shard, "seq", axis=0).reshape(N_HEAD, 2, FEATURES // 2, WIDTH)
 
     source = (head - sense(seq % 2) * jnp.arange(N_HEAD, dtype=jnp.int32)) % N_HEAD

time: 126 us -> 126 us (level)
    all_gather x1, waiting for transfers between devices: 1.73 us -> 0.01 us  [on_device(): lax.all_gather(shard, 'seq', axis=0)]
    ppermute x30, waiting for transfers between devices: 10.2 us -> 11.8 us  [moved(): return lax.ppermute(array, ('seq', 'head'), pairs)]
    pallas_call x1 -> x2, Pallas kernels: 5.38 us -> 5.58 us  [attend(): pl.pallas_call(functools.partial(attend_kernel, first), in_specs=[pl.Bloc...]
where the time goes in v13:
time: 126 us; the launch traced here: 125 us
  starting transfers between devices  63.4 us (50%)
  waiting for transfers between devices  30.6 us (24%)
  Pallas kernels  13.9 us (11%)
  between operations  13.7 us (11%)
  local copies, waits for them, and re-layouts  3.14 us (2%)
    ppermute x30, starting transfers between devices, moved(): return lax.ppermute(array, ('seq', 'head'), pairs)  53.8 us
    ppermute x30, waiting for transfers between devices, moved(): return lax.ppermute(array, ('seq', 'head'), pairs)  11.8 us
    ppermute x1, waiting for transfers between devices, on_device(): far = lax.ppermute(own, 'seq', [(i, i + 2) for i in range(N_SEQ - 2)])  11.2 us
    all_to_all x1, waiting for transfers between devices, on_device(): squares = lax.all_to_all(squares, 'head', 0, 0, tiled=True)  7.62 us
    pallas_call x1, Pallas kernels, project(): pl.pallas_call(project_kernel, in_specs=[pl.BlockSpec(memory_space=pltpu....  6.3 us
    all_to_all x1, starting transfers between devices, on_device(): squares = lax.all_to_all(squares, 'head', 0, 0, tiled=True)  6 us
    pallas_call x2, Pallas kernels, attend(): pl.pallas_call(functools.partial(attend_kernel, first), in_specs=[pl.Bloc...  5.58 us
    ppermute x1, starting transfers between devices, on_device(): far = lax.ppermute(own, 'seq', [(i, i + 2) for i in range(N_SEQ - 2)])  3.48 us
  transfers between devices with their start and end apart: 34, of which 18 were waited for; matrix products, arithmetic and copies ran while one was open for 1% of the time, Pallas kernels for 5%

profile of v13, /device:TPU:6, one launch (start us, length us, event | category | flops | bytes accessed | tf_op | source)
XLA Modules:
  0.0 124.9 jit_solution(6858950549333737872)
XLA Ops:
  9.0 3.5 %collective-permute-start.1 = (bf16[2,2,512,128]{3,2,1,0:T(8,128)(2,1)S(1)}, bf16[2,2,512,128]{3,2,1,0:T(8,128)(2,1)S(1)}, u32[]{:S(2)}, u32[]{:S(2)}) collective-permute-start(bf16[2,2,512,128]{3,2,1,0:T(8,128)(2,1)S(1)} %get-tuple-element.16.own_ref), channel_id=1, source_target_pairs={{0,16},{8,24},{16,32},{24,40},{32,48},{40,56},{48,64},{56,72},{64,... | collective-permute-start | bytes 1572872 | tf_op jit(solution)/shard_map/ppermute | solution.py:318
  12.5 1.6 %collective-permute-start = (bf16[168,512]{1,0:T(8,128)(2,1)}, bf16[168,512]{1,0:T(8,128)(2,1)S(1)}, u32[]{:S(2)}, u32[]{:S(2)}) collective-permute-start(bf16[168,512]{1,0:T(8,128)(2,1)} %bitcast.21), channel_id=1, source_target_pairs={{0,0},{1,49},{2,66},{3,115},{4,132},{5,181},{6,198},{7,247},{8,8},... | collective-permute-start | bytes 516104 | tf_op jit(solution)/shard_map/ppermute | solution.py:291
  15.5 11.2 %collective-permute-done.1.refs_1_ = bf16[2,2,512,128]{3,2,1,0:T(8,128)(2,1)S(1)} collective-permute-done((bf16[2,2,512,128]{3,2,1,0:T(8,128)(2,1)S(1)}, bf16[2,2,512,128]{3,2,1,0:T(8,128)(2,1)S(1)}, u32[]{:S(2)}, u32[]{:S(2)}) %collective-permute-start.1) | collective-permute-done | bytes 524320 | tf_op jit(solution)/shard_map/ppermute | solution.py:318
  26.8 8.2 %collective-permute-start.2 = (bf16[168,512]{1,0:T(8,128)(2,1)S(1)}, bf16[168,512]{1,0:T(8,128)(2,1)}, u32[]{:S(2)}, u32[]{:S(2)}) collective-permute-start(bf16[168,512]{1,0:T(8,128)(2,1)S(1)} %get-tuple-element.19), channel_id=1, source_target_pairs={{0,0},{1,7},{2,6},{3,5},{4,4},{5,3},{6,2},{7,1},{8,8},{9,15},{10,1... | collective-permute-start | bytes 516104 | tf_op jit(solution)/shard_map/ppermute | solution.py:291
  35.0 2.8 %attend.2 = (bf16[128,512]{1,0:T(8,128)(2,1)S(1)}, bf16[128,512]{1,0:T(8,128)(2,1)S(1)}) custom-call(s32[1]{0:T(128)} %bitcast.5.place_ref, bf16[512,512]{1,0:T(8,128)(2,1)S(1)} %rotate.1.refs_2_.q_ref, bf16[2,2,512,128]{3,2,1,0:T(8,128)(2,1)S(1)} %get-tuple-element.16.own_ref, bf16[2,2,512,128]{3,2,1,0:T(8,128)(2,1)S(1)} %collective-permute-done.3.prev_ref, ...), custom_call_target="tpu_custom_call" | custom-call | tf_op jit(solution)/shard_map/attend/pallas_call | solution.py:192
  37.9 2.3 %collective-permute-done.2.refs_0_ = bf16[168,512]{1,0:T(8,128)(2,1)} collective-permute-done((bf16[168,512]{1,0:T(8,128)(2,1)S(1)}, bf16[168,512]{1,0:T(8,128)(2,1)}, u32[]{:S(2)}, u32[]{:S(2)}) %collective-permute-start.2) | collective-permute-done | bytes 172064 | tf_op jit(solution)/shard_map/ppermute | solution.py:291
  40.2 2.8 %attend.3 = (bf16[128,512]{1,0:T(8,128)(2,1)S(1)}, bf16[128,512]{1,0:T(8,128)(2,1)S(1)}) custom-call(s32[1]{0:T(128)} %bitcast.5.place_ref, bf16[512,512]{1,0:T(8,128)(2,1)S(1)} %rotate.1.refs_2_.q_ref, bf16[2,2,512,128]{3,2,1,0:T(8,128)(2,1)S(1)} %get-tuple-element.16.own_ref, bf16[2,2,512,128]{3,2,1,0:T(8,128)(2,1)S(1)} %collective-permute-done.3.prev_ref, ...), custom_call_target="tpu_custom_call" | custom-call | tf_op jit(solution)/shard_map/attend/pallas_call | solution.py:192
  43.0 5.8 %collective-permute-start.4 = (bf16[128,512]{1,0:T(8,128)(2,1)S(1)}, bf16[128,512]{1,0:T(8,128)(2,1)S(1)}, u32[]{:S(2)}, u32[]{:S(2)}) collective-permute-start(bf16[128,512]{1,0:T(8,128)(2,1)S(1)} %get-tuple-element.22.refs_0_), channel_id=1, source_target_pairs={{0,1},{1,2},{2,3},{3,4},{4,5},{5,6},{6,7},{7,0},{8,15},{9,8},{10,9... | collective-permute-start | bytes 393224 | tf_op jit(solution)/shard_map/ppermute | solution.py:291
  51.3 4.7 %collective-permute-start.8 = (bf16[128,512]{1,0:T(8,128)(2,1)S(1)}, bf16[128,512]{1,0:T(8,128)(2,1)S(1)}, u32[]{:S(2)}, u32[]{:S(2)}) collective-permute-start(bf16[128,512]{1,0:T(8,128)(2,1)S(1)} %collective-permute-done.4.refs_4_), channel_id=1, source_target_pairs={{0,1},{1,2},{2,3},{3,4},{4,5},{5,6},{6,7},{7,0},{8,15},{9,8},{10,9... | collective-permute-start | bytes 393224 | tf_op jit(solution)/shard_map/ppermute | solution.py:291
  59.2 3.0 %collective-permute-start.12 = (bf16[128,512]{1,0:T(8,128)(2,1)S(1)}, bf16[128,512]{1,0:T(8,128)(2,1)S(1)}, u32[]{:S(2)}, u32[]{:S(2)}) collective-permute-start(bf16[128,512]{1,0:T(8,128)(2,1)S(1)} %collective-permute-done.8.refs_8_), channel_id=1, source_target_pairs={{0,1},{1,2},{2,3},{3,4},{4,5},{5,6},{6,7},{7,0},{8,15},{9,8},{10,9... | collective-permute-start | bytes 393224 | tf_op jit(solution)/shard_map/ppermute | solution.py:291
  63.6 1.4 %collective-permute-start.14 = (bf16[128,512]{1,0:T(8,128)(2,1)S(1)}, bf16[128,512]{1,0:T(8,128)(2,1)S(1)}, u32[]{:S(2)}, u32[]{:S(2)}) collective-permute-start(bf16[128,512]{1,0:T(8,128)(2,1)S(1)} %collective-permute-done.10.refs_10_), channel_id=1, source_target_pairs={{0,1},{1,2},{2,3},{3,4},{4,5},{5,6},{6,7},{7,0},{8,15},{9,8},{10,9... | collective-permute-start | bytes 393224 | tf_op jit(solution)/shard_map/ppermute | solution.py:291
  66.4 2.0 %collective-permute-start.16 = (bf16[128,512]{1,0:T(8,128)(2,1)S(1)}, bf16[128,512]{1,0:T(8,128)(2,1)S(1)}, u32[]{:S(2)}, u32[]{:S(2)}) collective-permute-start(bf16[128,512]{1,0:T(8,128)(2,1)S(1)} %collective-permute-done.12.refs_12_), channel_id=1, source_target_pairs={{0,1},{1,2},{2,3},{3,4},{4,5},{5,6},{6,7},{7,0},{8,15},{9,8},{10,9... | collective-permute-start | bytes 393224 | tf_op jit(solution)/shard_map/ppermute | solution.py:291
  68.4 1.4 %collective-permute-start.17 = (bf16[128,512]{1,0:T(8,128)(2,1)S(1)}, bf16[128,512]{1,0:T(8,128)(2,1)S(1)}, u32[]{:S(2)}, u32[]{:S(2)}) collective-permute-start(bf16[128,512]{1,0:T(8,128)(2,1)S(1)} %collective-permute-done.13.refs_13_), channel_id=1, source_target_pairs={{0,1},{1,2},{2,3},{3,4},{4,5},{5,6},{6,7},{7,0},{8,15},{9,8},{10,9... | collective-permute-start | bytes 393224 | tf_op jit(solution)/shard_map/ppermute | solution.py:291
  69.8 1.4 %collective-permute-start.18 = (bf16[128,512]{1,0:T(8,128)(2,1)S(1)}, bf16[128,512]{1,0:T(8,128)(2,1)S(1)}, u32[]{:S(2)}, u32[]{:S(2)}) collective-permute-start(bf16[128,512]{1,0:T(8,128)(2,1)S(1)} %collective-permute-done.14.refs_14_), channel_id=1, source_target_pairs={{0,1},{1,2},{2,3},{3,4},{4,5},{5,6},{6,7},{7,0},{8,15},{9,8},{10,9... | collective-permute-start | bytes 393224 | tf_op jit(solution)/shard_map/ppermute | solution.py:291
  72.6 2.0 %collective-permute-start.20 = (bf16[128,512]{1,0:T(8,128)(2,1)S(1)}, bf16[128,512]{1,0:T(8,128)(2,1)S(1)}, u32[]{:S(2)}, u32[]{:S(2)}) collective-permute-start(bf16[128,512]{1,0:T(8,128)(2,1)S(1)} %collective-permute-done.16.refs_16_), channel_id=1, source_target_pairs={{0,1},{1,2},{2,3},{3,4},{4,5},{5,6},{6,7},{7,0},{8,15},{9,8},{10,9... | collective-permute-start | bytes 393224 | tf_op jit(solution)/shard_map/ppermute | solution.py:291
  74.6 1.4 %collective-permute-start.21 = (bf16[128,512]{1,0:T(8,128)(2,1)S(1)}, bf16[128,512]{1,0:T(8,128)(2,1)}, u32[]{:S(2)}, u32[]{:S(2)}) collective-permute-start(bf16[128,512]{1,0:T(8,128)(2,1)S(1)} %collective-permute-done.17.refs_17_), channel_id=1, source_target_pairs={{0,1},{1,2},{2,3},{3,4},{4,5},{5,6},{6,7},{7,0},{8,15},{9,8},{10,9... | collective-permute-start | bytes 393224 | tf_op jit(solution)/shard_map/ppermute | solution.py:291
  78.8 2.0 %collective-permute-start.24 = (bf16[128,512]{1,0:T(8,128)(2,1)S(1)}, bf16[128,512]{1,0:T(8,128)(2,1)}, u32[]{:S(2)}, u32[]{:S(2)}) collective-permute-start(bf16[128,512]{1,0:T(8,128)(2,1)S(1)} %collective-permute-done.20.refs_20_), channel_id=1, source_target_pairs={{0,1},{1,2},{2,3},{3,4},{4,5},{5,6},{6,7},{7,0},{8,15},{9,8},{10,9... | collective-permute-start | bytes 393224 | tf_op jit(solution)/shard_map/ppermute | solution.py:291
  85.1 2.0 %collective-permute-start.28 = (bf16[128,512]{1,0:T(8,128)(2,1)}, bf16[128,512]{1,0:T(8,128)(2,1)}, u32[]{:S(2)}, u32[]{:S(2)}) collective-permute-start(bf16[128,512]{1,0:T(8,128)(2,1)} %collective-permute-done.24.refs_24_), channel_id=1, source_target_pairs={{0,1},{1,2},{2,3},{3,4},{4,5},{5,6},{6,7},{7,0},{8,15},{9,8},{10,9... | collective-permute-start | bytes 393224 | tf_op jit(solution)/shard_map/ppermute | solution.py:291
  91.6 2.3 %collective-permute-done.29.refs_29_ = bf16[128,512]{1,0:T(8,128)(2,1)} collective-permute-done((bf16[128,512]{1,0:T(8,128)(2,1)}, bf16[128,512]{1,0:T(8,128)(2,1)}, u32[]{:S(2)}, u32[]{:S(2)}) %collective-permute-start.29) | collective-permute-done | bytes 131104 | tf_op jit(solution)/shard_map/ppermute | solution.py:291
  93.9 1.4 %collective-permute-done.30.refs_30_ = bf16[128,512]{1,0:T(8,128)(2,1)} collective-permute-done((bf16[128,512]{1,0:T(8,128)(2,1)}, bf16[128,512]{1,0:T(8,128)(2,1)}, u32[]{:S(2)}, u32[]{:S(2)}) %collective-permute-start.30) | collective-permute-done | bytes 131104 | tf_op jit(solution)/shard_map/ppermute | solution.py:291
  95.3 1.4 %collective-permute-done.31.refs_31_ = bf16[128,512]{1,0:T(8,128)(2,1)} collective-permute-done((bf16[128,512]{1,0:T(8,128)(2,1)}, bf16[128,512]{1,0:T(8,128)(2,1)}, u32[]{:S(2)}, u32[]{:S(2)}) %collective-permute-start.31) | collective-permute-done | bytes 131104 | tf_op jit(solution)/shard_map/ppermute | solution.py:291
  96.9 6.3 %project.1 = (f32[672,512]{1,0:T(8,128)S(1)}, f32[8,1,512]{2,1,0:T(1,128)}) custom-call(s32[2,8]{1,0:T(2,128)S(1)} %pad_add_fusion.order_ref, bf16[8,2,336,512]{3,2,1,0:T(8,128)(2,1)} %bitcast.19, bf16[128,512]{1,0:T(8,128)(2,1)} %copy-done.3, bf16[128,512]{1,0:T(8,128)(2,1)} %copy-done.4, bf16[128,512]{1,0:T(8,128)(2,1)} %copy-done.2, ...), custom_call_target="tpu_custom_call" | custom-call | tf_op jit(solution)/shard_map/project/pallas_call | solution.py:244
  103.2 6.0 %all-to-all-start = ((f32[8,1,512]{2,1,0:T(1,128)}), f32[8,1,512]{2,1,0:T(1,128)S(1)}, u32[]{:S(2)}, u32[]{:S(2)}) async-start(f32[8,1,512]{2,1,0:T(1,128)} %get-tuple-element.26), calls=%async_computation | async-start | bytes 32768 | tf_op jit(solution)/shard_map/all_to_all | solution.py:340
  109.3 7.6 %all-to-all-done.sq_ref = f32[8,1,512]{2,1,0:T(1,128)S(1)} async-done(((f32[8,1,512]{2,1,0:T(1,128)}), f32[8,1,512]{2,1,0:T(1,128)S(1)}, u32[]{:S(2)}, u32[]{:S(2)}) %all-to-all-start) | async-done | bytes 16416 | tf_op jit(solution)/shard_map/all_to_all | solution.py:340
  (109 shorter events, 26.9 us)
Async XLA Ops:
  6.5 90.1 %all-gather.3.cloned.1.call-start = ((), (), s32[]{:S(2)}) async-start(), calls=%async_computation.1 | async-start | bytes 5677056 | tf_op jit(solution)/shard_map/all_gather | solution.py:335
  9.0 17.7 %collective-permute-start.1 = (bf16[2,2,512,128]{3,2,1,0:T(8,128)(2,1)S(1)}, bf16[2,2,512,128]{3,2,1,0:T(8,128)(2,1)S(1)}, u32[]{:S(2)}, u32[]{:S(2)}) collective-permute-start(bf16[2,2,512,128]{3,2,1,0:T(8,128)(2,1)S(1)} %get-tuple-element.16.own_ref), channel_id=1, source_target_pairs={{0,16},{8,24},{16,32},{24,40},{32,48},{40,56},{48,64},{56,72},{64,... | collective-permute-start | bytes 1572872 | tf_op jit(solution)/shard_map/ppermute | solution.py:318
  26.7 8.3 %collective-permute-start.3 = (bf16[2,2,512,128]{3,2,1,0:T(8,128)(2,1)S(1)}, bf16[2,2,512,128]{3,2,1,0:T(8,128)(2,1)S(1)}, u32[]{:S(2)}, u32[]{:S(2)}) collective-permute-start(bf16[2,2,512,128]{3,2,1,0:T(8,128)(2,1)S(1)} %broadcast_select_fusion), channel_id=1, source_target_pairs={{0,8},{8,0},{16,24},{24,16},{32,40},{40,32},{48,56},{56,48},{64,72... | collective-permute-start | bytes 1572872 | tf_op jit(solution)/shard_map/ppermute | solution.py:323
  26.8 13.3 %collective-permute-start.2 = (bf16[168,512]{1,0:T(8,128)(2,1)S(1)}, bf16[168,512]{1,0:T(8,128)(2,1)}, u32[]{:S(2)}, u32[]{:S(2)}) collective-permute-start(bf16[168,512]{1,0:T(8,128)(2,1)S(1)} %get-tuple-element.19), channel_id=1, source_target_pairs={{0,0},{1,7},{2,6},{3,5},{4,4},{5,3},{6,2},{7,1},{8,8},{9,15},{10,1... | collective-permute-start | bytes 516104 | tf_op jit(solution)/shard_map/ppermute | solution.py:291
  43.0 8.3 %collective-permute-start.4 = (bf16[128,512]{1,0:T(8,128)(2,1)S(1)}, bf16[128,512]{1,0:T(8,128)(2,1)S(1)}, u32[]{:S(2)}, u32[]{:S(2)}) collective-permute-start(bf16[128,512]{1,0:T(8,128)(2,1)S(1)} %get-tuple-element.22.refs_0_), channel_id=1, source_target_pairs={{0,1},{1,2},{2,3},{3,4},{4,5},{5,6},{6,7},{7,0},{8,15},{9,8},{10,9... | collective-permute-start | bytes 393224 | tf_op jit(solution)/shard_map/ppermute | solution.py:291
  48.8 7.2 %collective-permute-start.5 = (bf16[128,512]{1,0:T(8,128)(2,1)S(1)}, bf16[128,512]{1,0:T(8,128)(2,1)S(1)}, u32[]{:S(2)}, u32[]{:S(2)}) collective-permute-start(bf16[128,512]{1,0:T(8,128)(2,1)S(1)} %get-tuple-element.23.refs_1_), channel_id=1, source_target_pairs={{0,1},{1,2},{2,3},{3,4},{4,5},{5,6},{6,7},{7,0},{8,15},{9,8},{10,9... | collective-permute-start | bytes 393224 | tf_op jit(solution)/shard_map/ppermute | solution.py:291
  50.0 6.4 %collective-permute-start.6 = (bf16[128,512]{1,0:T(8,128)(2,1)S(1)}, bf16[128,512]{1,0:T(8,128)(2,1)S(1)}, u32[]{:S(2)}, u32[]{:S(2)}) collective-permute-start(bf16[128,512]{1,0:T(8,128)(2,1)S(1)} %get-tuple-element.24.refs_2_), channel_id=1, source_target_pairs={{0,1},{1,2},{2,3},{3,4},{4,5},{5,6},{6,7},{7,0},{8,15},{9,8},{10,9... | collective-permute-start | bytes 393224 | tf_op jit(solution)/shard_map/ppermute | solution.py:291
  50.0 7.7 %collective-permute-start.7 = (bf16[128,512]{1,0:T(8,128)(2,1)S(1)}, bf16[128,512]{1,0:T(8,128)(2,1)S(1)}, u32[]{:S(2)}, u32[]{:S(2)}) collective-permute-start(bf16[128,512]{1,0:T(8,128)(2,1)S(1)} %get-tuple-element.21.refs_1_.refs_3_), channel_id=1, source_target_pairs={{0,1},{1,2},{2,3},{3,4},{4,5},{5,6},{6,7},{7,0},{8,15},{9,8},{10,9... | collective-permute-start | bytes 393224 | tf_op jit(solution)/shard_map/ppermute | solution.py:291
  51.3 7.9 %collective-permute-start.8 = (bf16[128,512]{1,0:T(8,128)(2,1)S(1)}, bf16[128,512]{1,0:T(8,128)(2,1)S(1)}, u32[]{:S(2)}, u32[]{:S(2)}) collective-permute-start(bf16[128,512]{1,0:T(8,128)(2,1)S(1)} %collective-permute-done.4.refs_4_), channel_id=1, source_target_pairs={{0,1},{1,2},{2,3},{3,4},{4,5},{5,6},{6,7},{7,0},{8,15},{9,8},{10,9... | collective-permute-start | bytes 393224 | tf_op jit(solution)/shard_map/ppermute | solution.py:291
  56.4 7.3 %collective-permute-start.10 = (bf16[128,512]{1,0:T(8,128)(2,1)S(1)}, bf16[128,512]{1,0:T(8,128)(2,1)S(1)}, u32[]{:S(2)}, u32[]{:S(2)}) collective-permute-start(bf16[128,512]{1,0:T(8,128)(2,1)S(1)} %collective-permute-done.6.refs_6_), channel_id=1, source_target_pairs={{0,1},{1,2},{2,3},{3,4},{4,5},{5,6},{6,7},{7,0},{8,15},{9,8},{10,9... | collective-permute-start | bytes 393224 | tf_op jit(solution)/shard_map/ppermute | solution.py:291
  57.8 7.3 %collective-permute-start.11 = (bf16[128,512]{1,0:T(8,128)(2,1)S(1)}, bf16[128,512]{1,0:T(8,128)(2,1)S(1)}, u32[]{:S(2)}, u32[]{:S(2)}) collective-permute-start(bf16[128,512]{1,0:T(8,128)(2,1)S(1)} %collective-permute-done.7.refs_7_), channel_id=1, source_target_pairs={{0,1},{1,2},{2,3},{3,4},{4,5},{5,6},{6,7},{7,0},{8,15},{9,8},{10,9... | collective-permute-start | bytes 393224 | tf_op jit(solution)/shard_map/ppermute | solution.py:291
  59.2 7.3 %collective-permute-start.12 = (bf16[128,512]{1,0:T(8,128)(2,1)S(1)}, bf16[128,512]{1,0:T(8,128)(2,1)S(1)}, u32[]{:S(2)}, u32[]{:S(2)}) collective-permute-start(bf16[128,512]{1,0:T(8,128)(2,1)S(1)} %collective-permute-done.8.refs_8_), channel_id=1, source_target_pairs={{0,1},{1,2},{2,3},{3,4},{4,5},{5,6},{6,7},{7,0},{8,15},{9,8},{10,9... | collective-permute-start | bytes 393224 | tf_op jit(solution)/shard_map/ppermute | solution.py:291
  74.6 6.3 %collective-permute-start.21 = (bf16[128,512]{1,0:T(8,128)(2,1)S(1)}, bf16[128,512]{1,0:T(8,128)(2,1)}, u32[]{:S(2)}, u32[]{:S(2)}) collective-permute-start(bf16[128,512]{1,0:T(8,128)(2,1)S(1)} %collective-permute-done.17.refs_17_), channel_id=1, source_target_pairs={{0,1},{1,2},{2,3},{3,4},{4,5},{5,6},{6,7},{7,0},{8,15},{9,8},{10,9... | collective-permute-start | bytes 393224 | tf_op jit(solution)/shard_map/ppermute | solution.py:291
  76.0 6.3 %collective-permute-start.22 = (bf16[128,512]{1,0:T(8,128)(2,1)S(1)}, bf16[128,512]{1,0:T(8,128)(2,1)}, u32[]{:S(2)}, u32[]{:S(2)}) collective-permute-start(bf16[128,512]{1,0:T(8,128)(2,1)S(1)} %collective-permute-done.18.refs_18_), channel_id=1, source_target_pairs={{0,1},{1,2},{2,3},{3,4},{4,5},{5,6},{6,7},{7,0},{8,15},{9,8},{10,9... | collective-permute-start | bytes 393224 | tf_op jit(solution)/shard_map/ppermute | solution.py:291
  77.4 6.3 %collective-permute-start.23 = (bf16[128,512]{1,0:T(8,128)(2,1)S(1)}, bf16[128,512]{1,0:T(8,128)(2,1)}, u32[]{:S(2)}, u32[]{:S(2)}) collective-permute-start(bf16[128,512]{1,0:T(8,128)(2,1)S(1)} %collective-permute-done.19.refs_19_), channel_id=1, source_target_pairs={{0,1},{1,2},{2,3},{3,4},{4,5},{5,6},{6,7},{7,0},{8,15},{9,8},{10,9... | collective-permute-start | bytes 393224 | tf_op jit(solution)/shard_map/ppermute | solution.py:291
  78.8 6.3 %collective-permute-start.24 = (bf16[128,512]{1,0:T(8,128)(2,1)S(1)}, bf16[128,512]{1,0:T(8,128)(2,1)}, u32[]{:S(2)}, u32[]{:S(2)}) collective-permute-start(bf16[128,512]{1,0:T(8,128)(2,1)S(1)} %collective-permute-done.20.refs_20_), channel_id=1, source_target_pairs={{0,1},{1,2},{2,3},{3,4},{4,5},{5,6},{6,7},{7,0},{8,15},{9,8},{10,9... | collective-permute-start | bytes 393224 | tf_op jit(solution)/shard_map/ppermute | solution.py:291
  80.9 6.5 %collective-permute-start.25 = (bf16[128,512]{1,0:T(8,128)(2,1)}, bf16[128,512]{1,0:T(8,128)(2,1)}, u32[]{:S(2)}, u32[]{:S(2)}) collective-permute-start(bf16[128,512]{1,0:T(8,128)(2,1)} %collective-permute-done.21.refs_21_), channel_id=1, source_target_pairs={{0,1},{1,2},{2,3},{3,4},{4,5},{5,6},{6,7},{7,0},{8,15},{9,8},{10,9... | collective-permute-start | bytes 393224 | tf_op jit(solution)/shard_map/ppermute | solution.py:291
  82.3 6.5 %collective-permute-start.26 = (bf16[128,512]{1,0:T(8,128)(2,1)}, bf16[128,512]{1,0:T(8,128)(2,1)}, u32[]{:S(2)}, u32[]{:S(2)}) collective-permute-start(bf16[128,512]{1,0:T(8,128)(2,1)} %collective-permute-done.22.refs_22_), channel_id=1, source_target_pairs={{0,1},{1,2},{2,3},{3,4},{4,5},{5,6},{6,7},{7,0},{8,15},{9,8},{10,9... | collective-permute-start | bytes 393224 | tf_op jit(solution)/shard_map/ppermute | solution.py:291
  83.7 6.5 %collective-permute-start.27 = (bf16[128,512]{1,0:T(8,128)(2,1)}, bf16[128,512]{1,0:T(8,128)(2,1)}, u32[]{:S(2)}, u32[]{:S(2)}) collective-permute-start(bf16[128,512]{1,0:T(8,128)(2,1)} %collective-permute-done.23.refs_23_), channel_id=1, source_target_pairs={{0,1},{1,2},{2,3},{3,4},{4,5},{5,6},{6,7},{7,0},{8,15},{9,8},{10,9... | collective-permute-start | bytes 393224 | tf_op jit(solution)/shard_map/ppermute | solution.py:291
  85.1 6.5 %collective-permute-start.28 = (bf16[128,512]{1,0:T(8,128)(2,1)}, bf16[128,512]{1,0:T(8,128)(2,1)}, u32[]{:S(2)}, u32[]{:S(2)}) collective-permute-start(bf16[128,512]{1,0:T(8,128)(2,1)} %collective-permute-done.24.refs_24_), channel_id=1, source_target_pairs={{0,1},{1,2},{2,3},{3,4},{4,5},{5,6},{6,7},{7,0},{8,15},{9,8},{10,9... | collective-permute-start | bytes 393224 | tf_op jit(solution)/shard_map/ppermute | solution.py:291
  87.4 6.5 %collective-permute-start.29 = (bf16[128,512]{1,0:T(8,128)(2,1)}, bf16[128,512]{1,0:T(8,128)(2,1)}, u32[]{:S(2)}, u32[]{:S(2)}) collective-permute-start(bf16[128,512]{1,0:T(8,128)(2,1)} %collective-permute-done.25.refs_25_), channel_id=1, source_target_pairs={{0,1},{1,2},{2,3},{3,4},{4,5},{5,6},{6,7},{7,0},{8,15},{9,8},{10,9... | collective-permute-start | bytes 393224 | tf_op jit(solution)/shard_map/ppermute | solution.py:291
  88.8 6.5 %collective-permute-start.30 = (bf16[128,512]{1,0:T(8,128)(2,1)}, bf16[128,512]{1,0:T(8,128)(2,1)}, u32[]{:S(2)}, u32[]{:S(2)}) collective-permute-start(bf16[128,512]{1,0:T(8,128)(2,1)} %collective-permute-done.26.refs_26_), channel_id=1, source_target_pairs={{0,1},{1,2},{2,3},{3,4},{4,5},{5,6},{6,7},{7,0},{8,15},{9,8},{10,9... | collective-permute-start | bytes 393224 | tf_op jit(solution)/shard_map/ppermute | solution.py:291
  90.2 6.5 %collective-permute-start.31 = (bf16[128,512]{1,0:T(8,128)(2,1)}, bf16[128,512]{1,0:T(8,128)(2,1)}, u32[]{:S(2)}, u32[]{:S(2)}) collective-permute-start(bf16[128,512]{1,0:T(8,128)(2,1)} %collective-permute-done.27.refs_27_), channel_id=1, source_target_pairs={{0,1},{1,2},{2,3},{3,4},{4,5},{5,6},{6,7},{7,0},{8,15},{9,8},{10,9... | collective-permute-start | bytes 393224 | tf_op jit(solution)/shard_map/ppermute | solution.py:291
  103.2 13.8 %all-to-all-start = ((f32[8,1,512]{2,1,0:T(1,128)}), f32[8,1,512]{2,1,0:T(1,128)S(1)}, u32[]{:S(2)}, u32[]{:S(2)}) async-start(f32[8,1,512]{2,1,0:T(1,128)} %get-tuple-element.26), calls=%async_computation | async-start | bytes 32768 | tf_op jit(solution)/shard_map/all_to_all | solution.py:340
  (34 other events, 945.7 us)
Sparse Core Ops, SparseCore 0:
  40.3 55.3 all-gather.2
